TPU v7x, 512 devices: a whole 4x4x16 slice. The times are simulated.
512 devices in a mesh: gx: 16 (over z), gy: 4 (over x), gz: 8 (over y, core).
Axes of the slice: x: 4, y: 4, z: 16, core: 2. Of those that a mesh axis runs over, the one named last changes fastest.
Arguments:
- right_side: float32 [256, 128, 1024], P('gx', 'gy', 'gz'), may hold values from -24 to 24
- conductivity: float32 [256, 128, 1024], P('gx', 'gy', 'gz'), may hold values from 0.1 to 10
Outputs:
- solution: float32 [256, 128, 1024], P('gx', 'gy', 'gz')
- residual: float32 [256, 128, 1024], P('gx', 'gy', 'gz')
All inputs are finite; a program needn't handle non-finite values.
Results may differ from a plain program's by a relative error of at most 0.0004.
Values sent between devices are 32-bit elements; how exact they have to be, the bound alone decides.
No kernel may reach another device: no remote copies, remote signals or barrier semaphores. Data moves between devices by JAX's collectives and lax.ppermute only.
A program may use at most 128 MiB of HBM per device.

v0:
```python
import jax
import jax.numpy as jnp
from jax import lax
from jax.sharding import PartitionSpec as P

LEVELS = 4
CSWEEPS = 6


absorption = 0.01
relaxation = 0.8


def padded_2(value, sides, width):
    for axis, dim in sides:
        count, length = (lax.axis_size(axis), value.shape[dim])
        up = [(i, (i + 1) % count) for i in range(count - 1)]
        down = [(j, i) for i, j in up]
        last = lax.slice_in_dim(value, length - width, length, axis=dim)
        initial = lax.slice_in_dim(value, 0, width, axis=dim)
        before = lax.ppermute(last, axis, up)
        after = lax.ppermute(initial, axis, down)
        value = jnp.concatenate([before, value, after], axis=dim)
    return value


def six_views(padded):
    return [
        padded[2:, 1:-1, 1:-1],
        padded[:-2, 1:-1, 1:-1],
        padded[1:-1, 2:, 1:-1],
        padded[1:-1, :-2, 1:-1],
        padded[1:-1, 1:-1, 2:],
        padded[1:-1, 1:-1, :-2],
    ]


def operator_parts(field, padded, kpadded, factor):
    center = kpadded[1:-1, 1:-1, 1:-1]
    total = None
    weight_sum = None
    for kother, fother in zip(six_views(kpadded), six_views(padded)):
        weight = 0.5 * (center + kother)
        term = weight * (field - fother)
        total = term if total is None else total + term
        weight_sum = weight if weight_sum is None else weight_sum + weight
    return (factor * total + absorption * field, factor * weight_sum + absorption)


def diagonal_only(kpadded, factor):
    center = kpadded[1:-1, 1:-1, 1:-1]
    weight_sum = None
    for kother in six_views(kpadded):
        weight = 0.5 * (center + kother)
        weight_sum = weight if weight_sum is None else weight_sum + weight
    return factor * weight_sum + absorption


def coarsen(values):
    values = 0.5 * (values[0::2] + values[1::2])
    values = 0.5 * (values[:, 0::2] + values[:, 1::2])
    return 0.5 * (values[:, :, 0::2] + values[:, :, 1::2])


def restrict_dim(padded, along):
    count = padded.shape[along] - 2
    first = lax.slice_in_dim(padded, 0, count, 2, along)
    second = lax.slice_in_dim(padded, 1, count + 1, 2, along)
    third = lax.slice_in_dim(padded, 2, count + 2, 2, along)
    fourth = lax.slice_in_dim(padded, 3, count + 2, 2, along)
    return (first + 3.0 * second + 3.0 * third + fourth) * 0.125


def prolong_dim(padded, along):
    count = padded.shape[along] - 2
    middle = lax.slice_in_dim(padded, 1, count + 1, 1, along)
    lower = lax.slice_in_dim(padded, 0, count, 1, along)
    upper = lax.slice_in_dim(padded, 2, count + 2, 1, along)
    even = (3.0 * middle + lower) * 0.25
    odd = (3.0 * middle + upper) * 0.25
    both = jnp.stack([even, odd], axis=along + 1)
    shape = list(middle.shape)
    shape[along] = 2 * count
    return both.reshape(shape)


def faces(values):
    return padded_2(values, (("gx", 0), ("gy", 1), ("gz", 2)), 1)


def rim_pad(values):
    return padded_2(values, (("gx", 0), ("gy", 1), ("gz", 2)), 1)


def sweep(field, source, kpadded, factor, padder):
    image, diagonal = operator_parts(field, padder(field), kpadded, factor)
    return field + relaxation * (source - image) / diagonal


def first_sweep(source, kpadded, factor):
    return relaxation * source / diagonal_only(kpadded, factor)


def restrict(residual_field):
    result = restrict_dim(rim_pad(residual_field), 0)
    result = restrict_dim(result, 1)
    return restrict_dim(result, 2)


def prolong_padded(padded):
    result = prolong_dim(padded, 0)
    result = prolong_dim(result, 1)
    return prolong_dim(result, 2)


def prolong(coarse_field):
    return prolong_padded(rim_pad(coarse_field))


def body(right_side, conductivity):
    coarse_factor = 0.25**LEVELS
    coefficient_pads = []
    values = conductivity
    for level in range(LEVELS + 1):
        if level == LEVELS:
            coefficient_pads.append(faces(values))
        else:
            coefficient_pads.append(faces(values))
            values = coarsen(values)

    def coarse_correction(coarse_source):
        kpadded = coefficient_pads[LEVELS]
        correction = first_sweep(coarse_source, kpadded, coarse_factor)
        for turn in range(CSWEEPS - 1):
            correction = sweep(correction, coarse_source, kpadded, coarse_factor, faces)
        return prolong(correction)

    def cycle(level, source, field):
        factor = 0.25**level
        kpadded = coefficient_pads[level]
        if field is None:
            field = first_sweep(source, kpadded, factor)
        else:
            field = sweep(field, source, kpadded, factor, faces)
        image, diagonal = operator_parts(field, faces(field), kpadded, factor)
        coarse_source = restrict(source - image)
        if level + 1 == LEVELS:
            increment = coarse_correction(coarse_source)
        else:
            increment = prolong(cycle(level + 1, coarse_source, None))
        field = field + increment
        return sweep(field, source, kpadded, factor, faces)

    solution = cycle(0, right_side, None)
    solution = cycle(0, right_side, solution)
    image, diagonal = operator_parts(solution, faces(solution), coefficient_pads[0], 1.0)
    return (solution, right_side - image)


def solution(mesh):
    placed = (P("gx", "gy", "gz"), P("gx", "gy", "gz"))
    return jax.shard_map(
        body,
        mesh=mesh,
        in_specs=placed,
        out_specs=(P("gx", "gy", "gz"), P("gx", "gy", "gz")),
        check_vma=False,
    )
```

profile of v0, /device:TPU:1, one launch (start us, length us, event | category | flops | bytes accessed | tf_op | source)
XLA Modules:
  0.0 1247.1 jit_solution(14312518835702964290)
XLA Ops:
  29.2 8.2 collective-permute-start.4
  40.9 5.1 collective-permute-start.55
  49.1 5.5 collective-permute-start.7
  123.1 6.4 collective-permute-start.25
  165.3 5.8 collective-permute-start.41
  182.4 5.5 collective-permute-start.43
  245.0 5.5 collective-permute-start.61
  269.7 5.1 collective-permute-start.66
  285.8 5.4 collective-permute-start.77
  300.8 5.5 collective-permute-start.79
  335.8 5.6 collective-permute-start.89
  357.4 5.9 collective-permute-start.95
  379.3 5.9 collective-permute-start.101
  387.3 5.4 collective-permute-start.103
  402.0 5.9 collective-permute-start.107
  408.8 5.1 collective-permute-start.108
  428.6 6.5 collective-permute-start.112
  441.8 5.7 collective-permute-start.115
  464.1 5.1 collective-permute-start.120
  483.1 6.8 collective-permute-start.124
  496.7 5.5 collective-permute-start.127
  516.5 5.1 collective-permute-start.132
  533.5 6.8 collective-permute-start.136
  547.6 5.5 collective-permute-start.139
  568.0 5.1 collective-permute-start.144
  587.4 6.9 collective-permute-start.148
  604.0 5.5 collective-permute-start.151
  628.7 5.8 collective-permute-start.157
  644.1 6.1 collective-permute-start.161
  656.5 5.5 collective-permute-start.163
  671.6 6.1 collective-permute-start.167
  702.5 6.7 collective-permute-start.172
  725.1 5.8 collective-permute-start.175
  746.0 5.1 collective-permute-start.180
  765.5 6.6 collective-permute-start.184
  781.3 5.5 collective-permute-start.187
  803.5 5.1 collective-permute-start.192
  822.9 6.5 collective-permute-start.196
  837.4 5.5 collective-permute-start.199
  858.1 5.1 collective-permute-start.204
  875.1 6.8 collective-permute-start.208
  889.4 5.5 collective-permute-start.211
  909.7 5.8 collective-permute-start.217
  925.0 5.6 collective-permute-start.221
  932.8 5.5 collective-permute-start.223
  947.6 5.9 collective-permute-start.227
  955.6 5.5 collective-permute-start.229
  970.4 5.9 collective-permute-start.233
  978.4 5.7 collective-permute-start.235
  993.4 5.9 collective-permute-start.239
  1000.2 5.1 collective-permute-start.240
  1020.0 6.5 collective-permute-start.244
  1033.1 5.7 collective-permute-start.247
  1055.4 5.1 collective-permute-start.252
  1074.5 6.8 collective-permute-start.256
  1088.0 5.5 collective-permute-start.259
  1107.7 5.1 collective-permute-start.264
  1124.8 6.8 collective-permute-start.268
  1138.9 5.5 collective-permute-start.271
  1159.2 5.1 collective-permute-start.276
  1178.6 6.9 collective-permute-start.280
  1195.2 5.5 collective-permute-start.283
  1219.9 5.7 collective-permute-start.289
  1235.2 6.1 collective-permute-start.293
  (1176 shorter events, 868.8 us)
Async XLA Ops:
  1.4 17.5 %collective-permute-start.1 = (f32[1,32,128]{2,1,0:T(8,128)S(1)}, f32[1,32,128]{2,1,0:T(8,128)S(1)}, u32[]{:S(2)}, u32[]{:S(2)}) collective-permute-start(f32[1,32,128]{2,1,0:T(8,128)S(1)} %get-tuple-element.110), channel_id=1, source_target_pairs={{0,32},{32,64},{64,96},{96,128},{128,160},{160,192},{192,224},{224... | collective-permute-start | bytes 49160 | tf_op jit(solution)/shard_map/ppermute | solution.py:21
  10.8 37.0 %collective-permute-start.72 = (f32[1,2,8]{2,1,0:T(2,128)S(1)}, f32[1,2,8]{2,1,0:T(2,128)S(1)}, u32[]{:S(2)}, u32[]{:S(2)}) collective-permute-start(f32[1,2,8]{2,1,0:T(2,128)S(1)} %add_multiply_fusion.23), channel_id=1, source_target_pairs={{32,0},{64,32},{96,64},{128,96},{160,128},{192,160},{224,192},{256... | collective-permute-start | bytes 200 | tf_op jit(solution)/shard_map/ppermute | solution.py:22
  12.1 37.0 %collective-permute-start.73 = (f32[1,2,8]{2,1,0:T(2,128)S(1)}, f32[1,2,8]{2,1,0:T(2,128)S(1)}, u32[]{:S(2)}, u32[]{:S(2)}) collective-permute-start(f32[1,2,8]{2,1,0:T(2,128)S(1)} %add_multiply_fusion.23), channel_id=1, source_target_pairs={{0,32},{32,64},{64,96},{96,128},{128,160},{160,192},{192,224},{224... | collective-permute-start | bytes 200 | tf_op jit(solution)/shard_map/ppermute | solution.py:21
  16.3 171.6 %collective-permute-start.54 = (f32[1,4,16]{2,1,0:T(4,128)}, f32[1,4,16]{2,1,0:T(4,128)S(1)}, u32[]{:S(2)}, u32[]{:S(2)}) collective-permute-start(f32[1,4,16]{2,1,0:T(4,128)} %get-tuple-element.370), channel_id=1, source_target_pairs={{32,0},{64,32},{96,64},{128,96},{160,128},{192,160},{224,192},{256... | collective-permute-start | bytes 776 | tf_op jit(solution)/shard_map/ppermute | solution.py:22
  29.2 11.7 collective-permute-start.4
  37.4 8.7 collective-permute-start.5
  40.9 147.0 %collective-permute-start.55 = (f32[1,4,16]{2,1,0:T(4,128)}, f32[1,4,16]{2,1,0:T(4,128)}, u32[]{:S(2)}, u32[]{:S(2)}) collective-permute-start(f32[1,4,16]{2,1,0:T(4,128)} %get-tuple-element.372), channel_id=1, source_target_pairs={{0,32},{32,64},{64,96},{96,128},{128,160},{160,192},{192,224},{224... | collective-permute-start | bytes 776 | tf_op jit(solution)/shard_map/ppermute | solution.py:21
  46.0 22.3 %collective-permute-start.36 = (f32[1,8,32]{2,1,0:T(8,128)S(1)}, f32[1,8,32]{2,1,0:T(8,128)S(1)}, u32[]{:S(2)}, u32[]{:S(2)}) collective-permute-start(f32[1,8,32]{2,1,0:T(8,128)S(1)} %get-tuple-element.252), channel_id=1, source_target_pairs={{32,0},{64,32},{96,64},{128,96},{160,128},{192,160},{224,192},{256... | collective-permute-start | bytes 3080 | tf_op jit(solution)/shard_map/ppermute | solution.py:22
  56.8 10.0 collective-permute-start.9
  62.0 8.3 collective-permute-start.37
  66.8 19.8 %collective-permute-start.18 = (f32[1,16,64]{2,1,0:T(8,128)S(1)}, f32[1,16,64]{2,1,0:T(8,128)S(1)}, u32[]{:S(2)}, u32[]{:S(2)}) collective-permute-start(f32[1,16,64]{2,1,0:T(8,128)S(1)} %get-tuple-element.177), channel_id=1, source_target_pairs={{32,0},{64,32},{96,64},{128,96},{160,128},{192,160},{224,192},{256... | collective-permute-start | bytes 12296 | tf_op jit(solution)/shard_map/ppermute | solution.py:22
  68.4 8.8 collective-permute-start.10
  70.3 11.2 collective-permute-start.11
  77.2 10.7 collective-permute-start.19
  88.0 9.0 collective-permute-start.20
  89.3 9.0 collective-permute-start.21
  101.6 8.9 collective-permute-start.16
  105.9 8.8 collective-permute-start.17
  108.6 11.9 collective-permute-start.22
  110.5 10.0 collective-permute-start.23
  121.7 11.0 collective-permute-start.24
  123.1 10.9 collective-permute-start.25
  132.6 21.9 %collective-permute-start.38 = (f32[6,1,32]{2,1,0:T(1,128)S(1)}, f32[6,1,32]{2,1,0:T(1,128)S(1)}, u32[]{:S(2)}, u32[]{:S(2)}) collective-permute-start(f32[6,1,32]{2,1,0:T(1,128)S(1)} %get-tuple-element.231), channel_id=1, source_target_pairs={{8,0},{16,8},{24,16},{9,1},{17,9},{25,17},{10,2},{18,10},{26,18},{... | collective-permute-start | bytes 2312 | tf_op jit(solution)/shard_map/ppermute | solution.py:22
  162.0 9.1 collective-permute-start.33
  163.4 10.3 collective-permute-start.40
  165.3 10.3 collective-permute-start.41
  197.6 10.7 collective-permute-start.46
  199.5 8.8 collective-permute-start.47
  203.4 10.3 collective-permute-start.57
  217.9 11.7 collective-permute-start.50
  221.9 16.2 %collective-permute-start.58 = (f32[4,6,1]{2,0,1:T(4,128)S(1)}, f32[4,6,1]{2,0,1:T(4,128)S(1)}, u32[]{:S(2)}, u32[]{:S(2)}) collective-permute-start(f32[4,6,1]{2,0,1:T(4,128)S(1)} %get-tuple-element.297), channel_id=1, source_target_pairs={{1,0},{2,1},{3,2},{4,3},{5,4},{6,5},{7,6},{9,8},{10,9},{11,10},{12... | collective-permute-start | bytes 296 | tf_op jit(solution)/shard_map/ppermute | solution.py:22
  224.2 14.0 %collective-permute-start.59 = (f32[4,6,1]{2,0,1:T(4,128)S(1)}, f32[4,6,1]{2,0,1:T(4,128)S(1)}, u32[]{:S(2)}, u32[]{:S(2)}) collective-permute-start(f32[4,6,1]{2,0,1:T(4,128)S(1)} %get-tuple-element.296), channel_id=1, source_target_pairs={{0,1},{1,2},{2,3},{3,4},{4,5},{5,6},{6,7},{8,9},{9,10},{10,11},{11... | collective-permute-start | bytes 296 | tf_op jit(solution)/shard_map/ppermute | solution.py:21
  243.7 12.1 collective-permute-start.60
  245.0 10.8 collective-permute-start.61
  250.5 8.6 collective-permute-start.74
  280.7 10.5 collective-permute-start.68
  282.4 8.9 collective-permute-start.69
  283.7 15.7 %collective-permute-start.76 = (f32[3,4,1]{2,1,0:T(4,128)S(1)}, f32[3,4,1]{2,1,0:T(4,128)S(1)}, u32[]{:S(2)}, u32[]{:S(2)}) collective-permute-start(f32[3,4,1]{2,1,0:T(4,128)S(1)} %get-tuple-element.345), channel_id=1, source_target_pairs={{1,0},{2,1},{3,2},{4,3},{5,4},{6,5},{7,6},{9,8},{10,9},{11,10},{12... | collective-permute-start | bytes 152 | tf_op jit(solution)/shard_map/ppermute | solution.py:22
  285.8 13.6 %collective-permute-start.77 = (f32[3,4,1]{2,1,0:T(4,128)S(1)}, f32[3,4,1]{2,1,0:T(4,128)S(1)}, u32[]{:S(2)}, u32[]{:S(2)}) collective-permute-start(f32[3,4,1]{2,1,0:T(4,128)S(1)} %get-tuple-element.344), channel_id=1, source_target_pairs={{0,1},{1,2},{2,3},{3,4},{4,5},{5,6},{6,7},{8,9},{9,10},{10,11},{11... | collective-permute-start | bytes 152 | tf_op jit(solution)/shard_map/ppermute | solution.py:21
  333.6 7.8 collective-permute-start.88
  428.6 8.4 collective-permute-start.112
  483.1 8.7 collective-permute-start.124
  533.5 8.7 collective-permute-start.136
  587.4 9.3 collective-permute-start.148
  616.7 9.0 collective-permute-start.154
  618.6 8.2 collective-permute-start.155
  642.2 11.3 collective-permute-start.160
  644.1 10.5 collective-permute-start.161
  669.7 11.3 collective-permute-start.166
  671.6 10.5 collective-permute-start.167
  702.5 11.1 collective-permute-start.172
  709.2 8.8 collective-permute-start.173
  765.5 8.8 collective-permute-start.184
  822.9 8.4 collective-permute-start.196
  875.1 8.7 collective-permute-start.208
  991.5 7.8 collective-permute-start.238
  1020.0 8.4 collective-permute-start.244
  1074.5 8.7 collective-permute-start.256
  1124.8 8.7 collective-permute-start.268
  1178.6 8.9 collective-permute-start.280
  1207.9 9.0 collective-permute-start.286
  1209.8 8.2 collective-permute-start.287
  1233.3 11.3 collective-permute-start.292
  1235.2 10.5 collective-permute-start.293
  (301 other events, 8574.1 us)
where the time goes:
time: 1270 us; the launch traced here: 1250 us
  starting transfers between devices  911 us (72%)
  waiting for transfers between devices  276 us (22%)
  local copies, waits for them, and re-layouts  32.9 us (3%)
  other arithmetic  19.8 us (2%)
    ppermute x147, starting transfers between devices, padded_2(): before = lax.ppermute(last, axis, up)  681 us
    ppermute x147, starting transfers between devices, padded_2(): after = lax.ppermute(initial, axis, down)  230 us
    ppermute x147, waiting for transfers between devices, padded_2(): after = lax.ppermute(initial, axis, down)  216 us
    ppermute x147, waiting for transfers between devices, padded_2(): before = lax.ppermute(last, axis, up)  60.5 us
  transfers between devices with their start and end apart: 294, of which 136 were waited for; matrix products, arithmetic and copies ran while one was open for 2% of the time, Pallas kernels for 0%

commit v1 on v0

v1 whole, which is shorter than its diff:
```python
import functools

import jax
import jax.numpy as jnp
import numpy as np
from jax import lax
from jax.experimental import pallas as pl
from jax.experimental.pallas import tpu as pltpu
from jax.sharding import PartitionSpec as P

LEVELS = 4
CSWEEPS = 6
absorption = 0.01
relaxation = 0.8
F32 = jnp.float32


def coords(n, b):
    at = np.arange(n)
    return np.where(at < (n + b) // 2, at, at - n)


def restriction(coarse, fine):
    gap = fine[None, :] - 2 * coarse[:, None]
    outer, inner = (gap == -1) | (gap == 2), (gap == 0) | (gap == 1)
    return np.where(outer, 0.125, np.where(inner, 0.375, 0.0)).astype(np.float32)


def halving(coarse, fine):
    return np.where(fine[None, :] // 2 == coarse[:, None], 0.5, 0.0).astype(np.float32)


def prolongation(fine, coarse):
    near = fine[:, None] // 2 == coarse[None, :]
    far = fine[:, None] // 2 + 2 * (fine[:, None] % 2) - 1 == coarse[None, :]
    return np.where(near, 0.75, np.where(far, 0.25, 0.0)).astype(np.float32)


def dot(a, b):
    return lax.dot_general(
        a, b, (((1,), (0,)), ((), ())),
        precision=lax.Precision.HIGHEST, preferred_element_type=F32,
    )


def planes(lo, hi, step, carry=0, unroll=1):
    whole = (hi - lo) // unroll

    def body(turn, carry):
        for j in range(unroll):
            carry = step(lo + turn * unroll + j, carry)
        return carry

    if whole > 1:
        carry = lax.fori_loop(0, whole, body, carry)
    elif whole == 1:
        carry = body(0, carry)
    for i in range(lo + whole * unroll, hi):
        carry = step(i, carry)
    return carry


class Open:
    def above(self, v, dim):
        return pltpu.roll(v, v.shape[dim] - 1, dim)

    def below(self, v, dim):
        return pltpu.roll(v, 1, dim)

    def closed(self, k):
        return None


class Closed(Open):
    def __init__(self, shape, counts):
        self.last, self.first = [], []
        for dim in range(2):
            at = lax.broadcasted_iota(jnp.int32, shape, dim)
            self.last.append(jnp.where(at == counts[dim] - 1, 0.0, 1.0))
            self.first.append(jnp.where(at == 0, 0.0, 1.0))

    def above(self, v, dim):
        return super().above(v, dim) * self.last[dim]

    def below(self, v, dim):
        return super().below(v, dim) * self.first[dim]

    def closed(self, k):
        return k * ((1.0 - self.first[0]) + (1.0 - self.first[1]))


def weigh(k, wx, wy, wz, lo, hi, factor, shifts, d=None, mask=None, b=None, unroll=1):
    half = 0.5 * factor
    first = half * (k[lo - 1] + k[lo])
    wx[lo - 1] = first

    def step(i, below):
        here = k[i]
        x = half * (here + k[i + 1])
        y = half * (here + shifts.above(here, 0))
        z = half * (here + shifts.above(here, 1))
        wx[i], wy[i], wz[i] = x, y, z
        ends = shifts.closed(half * here)
        if ends is not None:
            b[i] = ends
        if d is not None:
            total = (x + below) + (y + shifts.below(y, 0)) + (z + shifts.below(z, 1))
            if ends is not None:
                total = total + ends
            d[i] = mask(here, relaxation / (total + absorption))
        return x

    planes(lo, hi, step, first, unroll)


def image(v, wx, wy, wz, lo, hi, use, shifts, b=None, unroll=1):
    def step(i, below):
        here = v[i]
        x = wx[i] * (here - v[i + 1])
        y = wy[i] * (here - shifts.above(here, 0))
        z = wz[i] * (here - shifts.above(here, 1))
        total = (x - below) + (y - shifts.below(y, 0)) + (z - shifts.below(z, 1))
        if b is not None:
            total = total + b[i] * here
        use(i, here, total + absorption * here)
        return x

    planes(lo, hi, step, wx[lo - 1] * (v[lo - 1] - v[lo]), unroll)


def smooth(v, f, d, w, lo, hi, shifts, b=None, unroll=1):
    def use(i, here, im):
        v[i] = here + d[i] * (f[i] - im)

    image(v, *w, lo, hi, use, shifts, b, unroll)


def residual_of(v, f, r, w, lo, hi, shifts, mask=None, b=None, unroll=1):
    def use(i, here, im):
        value = f[i] - im
        r[i] = value if mask is None else jnp.where(mask[i] > 0.0, value, 0.0)

    image(v, *w, lo, hi, use, shifts, b, unroll)


def restrict_x(r, offset, count, rows):
    for i in range(count):
        at = 2 * i + offset
        outer, inner = r[at - 1] + r[at + 2], r[at] + r[at + 1]
        rows(i, 0.125 * outer + 0.375 * inner)


def restrict(r, offset, count, ry, rz, held):
    size = ry.shape[0]

    def rows(i, plane):
        held[i * size : (i + 1) * size, :] = dot(ry[...], plane)

    restrict_x(r, offset, count, rows)
    return dot(held[: count * size, :], rz[...])


def halve(k, offset, lo, hi, cy, cz, put):
    for i in range(lo, hi):
        plane = 0.5 * (k[2 * i + offset] + k[2 * i + 1 + offset])
        put(i, dot(dot(cy[...], plane), cz[...]))


def prolong(e, first, count, py, pz, finer, use):
    rows, fine = e.shape[1], py.shape[0]
    spread = dot(e[pl.ds(first, count)].reshape(count * rows, e.shape[2]), pz)
    for i in range(count):
        finer[i] = dot(py, spread[i * rows : (i + 1) * rows])

    def step(i, carry):
        below, here, above = finer[i - 1], finer[i], finer[i + 1]
        use(2 * (i - 1), 0.75 * here + 0.25 * below)
        use(2 * (i - 1) + 1, 0.75 * here + 0.25 * above)
        return carry

    planes(1, count - 1, step)


def inside(k, value):
    return jnp.where(k > 0.0, value, 0.0)


def down0(f, k, ry, rz, cy, cz, wx, wy, wz, d, g1, k1, d1, v, r, held, kc, wc):
    shifts = Open()
    weigh(k, wx, wy, wz, 1, 25, 1.0, shifts, d, inside)

    def start(i, carry):
        v[i] = f[i] * d[i]
        return carry

    planes(1, 25, start)
    residual_of(v, f, r, (wx, wy, wz), 4, 22, shifts, k)
    g1[...] = restrict(r, 5, 8, ry, rz, held).reshape(g1.shape)

    def put(i, value):
        kc[i + 1] = value

    halve(k, 5, -1, 9, cy, cz, put)
    coarse(kc, wc, k1, d1, 8, 0.25, shifts)


def coarse(kc, wc, kn, dn, count, factor, shifts):
    rows = kn.shape[1]
    dd = wc.at[3]
    weigh(kc, wc.at[0], wc.at[1], wc.at[2], 1, count + 1, factor, shifts, dd, lambda k, value: value)
    for i in range(count):
        kn[i] = kc[i + 1, :rows]
        dn[i] = dd[i + 1, :rows]


def start_level(g, k, d, v, w, factor):
    count, shifts = g.shape[0], Open()
    weigh(k, *w, 1, count - 1, factor, shifts, unroll=2)

    def start(i, carry):
        v[i] = g[i] * d[i]
        return carry

    planes(0, count, start, unroll=4)


def down(level, first, *refs):
    factor, shifts = 0.25**level, Open()
    block = 16 >> level
    g, k, d = refs[:3]
    if first:
        ry, rz, cy, cz, gn, kn, dn, v, r, held, w, kc, wc = refs[3:]
    else:
        ry, rz, gn, v, r, held, w = refs[3:]
    w = tuple(w.at[i] for i in range(3))
    start_level(g, k, d, v, w, factor)
    residual_of(v, g, r, w, 3, block + 5, shifts, d, unroll=2)
    gn[...] = restrict(r, 4, block // 2, ry, rz, held).reshape(gn.shape)
    if first:

        def put(i, value):
            kc[i + 1] = value

        halve(k, 4, -1, block // 2 + 1, cy, cz, put)
        coarse(kc, wc, kn, dn, block // 2, factor * 0.25, shifts)


def down2(first, *refs):
    g, k, d, ry, rz = refs[:5]
    if first:
        cy, cz = refs[5:7]
    gn, v, r, held, w = refs[-5:]
    w = tuple(w.at[i] for i in range(3))
    start_level(g, k, d, v, w, 0.25**2)
    residual_of(v, g, r, w, 3, 9, Open(), d, unroll=2)

    def rows(i, plane):
        held[i] = dot(ry[i], plane)

    restrict_x(r, 4, 2, rows)
    gn[0] = dot(held[0] + held[1], rz[...])
    if first:
        part = [dot(cy[i], 0.5 * (k[2 * i + 4] + k[2 * i + 5])) for i in range(2)]
        gn[1] = dot(part[0] + part[1], cz[...])


def repack(s, out):
    for field in range(s.shape[1]):
        total = s[0, field]
        for i in range(1, s.shape[0]):
            total = total + pltpu.roll(s[i, field], 16 * i, 1)
        for i in range(out.shape[0]):
            out[i, field] = total


def bottom(s, k3, scratch, mats):
    g3, v3, r3, w3, d3, b3, k4, g4, v4, w4, d4, b4, held, fine4 = scratch
    ry3, rz3, cy3, cz3, py3, pz3 = mats[:6]
    ny, nx = s.shape[:2]
    n3, n4 = 2 * nx, nx
    rows, lanes = g3.shape[1], g3.shape[2]
    for ref in (v3, r3, k4, v4):
        ref[...] = jnp.zeros(ref.shape, F32)
    for j in range(ny):
        for i in range(nx):
            for x in range(2):
                g3[2 * i + x + 3, 4 * j : 4 * j + 4] = s[j, i, 0, 4 * x : 4 * x + 4]
                if s.shape[2] == 2:
                    k3[2 * i + x + 3, 4 * j : 4 * j + 4] = s[j, i, 1, 4 * x : 4 * x + 4]
    if s.shape[2] == 2:
        for i in (0, 1, 2, n3 + 3, n3 + 4, n3 + 5):
            k3[i] = jnp.zeros((rows, lanes), F32)

    def put(i, value):
        k4[i + 1] = value

    halve(k3, 3, 0, n4, cy3, cz3, put)
    used = mats[6]
    shifts3 = Closed((rows, lanes), (rows, used))
    shifts4 = Closed((k4.shape[1], lanes), (k4.shape[1], used // 2))
    w3 = tuple(w3.at[i] for i in range(3))
    w4 = tuple(w4.at[i] for i in range(3))
    weigh(k3, *w3, 3, n3 + 3, 0.25**3, shifts3, d3, inside, b3, unroll=4)
    weigh(k4, *w4, 1, n4 + 1, 0.25**4, shifts4, d4, inside, b4, unroll=4)

    def start3(i, carry):
        v3[i] = g3[i] * d3[i]
        return carry

    planes(3, n3 + 3, start3, unroll=4)
    residual_of(v3, g3, r3, w3, 3, n3 + 3, shifts3, b=b3, unroll=4)
    g4[...] = restrict(r3, 3, n4, ry3, rz3, held).reshape(g4.shape)

    def start4(i, carry):
        v4[i + 1] = g4[i] * d4[i + 1]
        return carry

    planes(0, n4, start4, unroll=4)

    def turn(j, carry):
        def use(i, here, im):
            v4[i] = here + d4[i] * (g4[i - 1] - im)

        image(v4, *w4, 1, n4 + 1, use, shifts4, b4, unroll=n4)
        return carry

    lax.fori_loop(0, CSWEEPS - 1, turn, 0)

    def use(i, value):
        v3[i + 3] = v3[i + 3] + value

    prolong(v4, 0, n4 + 2, py3[...], pz3[...], fine4, use)
    smooth(v3, g3, d3, w3, 3, n3 + 3, shifts3, b3, unroll=4)
    return v3


def spread_matrix(shape, dim_fine, coarse_start, block_fine):
    fine = lax.broadcasted_iota(jnp.int32, shape, dim_fine)
    size = shape[dim_fine]
    fine = jnp.where(fine < (size + block_fine) // 2, fine, fine - size)
    whole = lax.broadcasted_iota(jnp.int32, shape, 1 - dim_fine)
    near = (fine >> 1) + coarse_start
    far = near + 2 * (fine & 1) - 1
    return jnp.where(whole == near, 0.75, jnp.where(whole == far, 0.25, 0.0))


def upward(index, e3, g2, k2, d2, g1, k1, d1, scratch, mats):
    v2, w2, v1, w1, fine2, fine1 = scratch
    py1, pz1 = mats
    shifts = Open()
    w2 = tuple(w2.at[i] for i in range(3))
    w1 = tuple(w1.at[i] for i in range(3))
    start_level(g2, k2, d2, v2, w2, 0.25**2)
    start_level(g1, k1, d1, v1, w1, 0.25)

    def use2(i, value):
        v2[i] = jnp.where(d2[i] > 0.0, v2[i] + value, 0.0)

    py2 = spread_matrix((g2.shape[1], e3.shape[1]), 0, index[1] * 4, 8)
    pz2 = spread_matrix((e3.shape[2], g2.shape[2]), 1, index[2] * 16, 32)
    prolong(e3, index[0] * 2, 8, py2, pz2, fine2, use2)
    smooth(v2, g2, d2, w2, 1, 11, shifts, unroll=2)

    def use1(i, value):
        v1[i] = jnp.where(d1[i] > 0.0, v1[i] + value, 0.0)

    prolong(v2, 1, 10, py1[...], pz1[...], fine1, use1)
    smooth(v1, g1, d1, w1, 1, 15, shifts, unroll=2)
    return v1


BOTTOM = 14
UP = 6


def middle(used, index, s, g2, k2, d2, g1, k1, d1, f, wx, wy, wz, d, k, *refs):
    m3, (py1, pz1, py0, pz0, ry, rz) = refs[:6] + (used,), refs[6:12]
    v, gn, k3 = refs[12:15]
    low, mid, (fine0, r, held0) = refs[15 : 15 + BOTTOM], refs[15 + BOTTOM : 15 + BOTTOM + UP], refs[15 + BOTTOM + UP :]
    e3 = bottom(s, k3, low, m3)
    e1 = upward(index, e3, g2, k2, d2, g1, k1, d1, mid, (py1, pz1))
    w, shifts = (wx, wy, wz), Open()

    def use(i, value):
        v[i + 1] = inside(k[i + 1], f[i + 1] * d[i + 1] + value)

    prolong(e1, 1, 14, py0[...], pz0[...], fine0, use)
    smooth(v, f, d, w, 2, 24, shifts)
    smooth(v, f, d, w, 3, 23, shifts)
    residual_of(v, f, r, w, 4, 22, shifts, k)
    gn[...] = restrict(r, 5, 8, ry, rz, held0).reshape(gn.shape)


def final(used, index, s, g2, k2, d2, g1, k1, d1, f, wx, wy, wz, d, k, *refs):
    m3, (py1, pz1, py0, pz0) = refs[:6] + (used,), refs[6:10]
    k3, v0, solution_, residual_ = refs[10:14]
    low, mid, (fine0, v) = refs[14 : 14 + BOTTOM], refs[14 + BOTTOM : 14 + BOTTOM + UP], refs[14 + BOTTOM + UP :]
    e3 = bottom(s, k3, low, m3)
    e1 = upward(index, e3, g2, k2, d2, g1, k1, d1, mid, (py1, pz1))
    w, shifts = (wx, wy, wz), Open()

    def use(i, value):
        v[i + 3] = inside(k[i + 3], v0[i + 3] + value)

    prolong(e1, 2, 12, py0[...], pz0[...], fine0, use)
    smooth(v, f, d, w, 4, 22, shifts)

    def out(i, here, im):
        solution_[i - 5] = here[:32, :128]
        residual_[i - 5] = (f[i] - im)[:32, :128]

    image(v, *w, 5, 21, out, shifts)


def call(kernel, outs, scratch, *args, name, scalars=0):
    vmem = pl.BlockSpec(memory_space=pltpu.VMEM)
    smem = pl.BlockSpec(memory_space=pltpu.SMEM)
    return pl.pallas_call(
        kernel,
        out_shape=[jax.ShapeDtypeStruct(o, F32) for o in outs],
        in_specs=[smem] * scalars + [vmem] * (len(args) - scalars),
        out_specs=[vmem] * len(outs),
        scratch_shapes=[pltpu.VMEM(s, F32) for s in scratch],
        compiler_params=pltpu.CompilerParams(vmem_limit_bytes=48 << 20),
        name=name,
    )(*args)


def neighbours(last, initial, axis):
    count = lax.axis_size(axis)
    if axis == "gz":
        up = [(i, (i + 1) % count) for i in range(count)]
    else:
        up = [(i, i + 1) for i in range(count - 1)]
    down = [(j, i) for i, j in up]
    before = lax.ppermute(last, axis, up)
    after = lax.ppermute(initial, axis, down)
    if axis == "gz":
        at = lax.axis_index(axis)
        before = jnp.where(at == 0, 0.0, before)
        after = jnp.where(at == count - 1, 0.0, after)
    return before, after


def exchange(fields, block, sizes, width):
    count = len(fields)
    for axis, dim in (("gz", 2), ("gy", 1), ("gx", 0)):
        along = 2 if dim == 2 else 0
        size = block[dim]
        last = [lax.slice_in_dim(f, size - width, size, axis=dim) for f in fields]
        initial = [lax.slice_in_dim(f, 0, width, axis=dim) for f in fields]
        before, after = neighbours(
            jnp.concatenate(last, along), jnp.concatenate(initial, along), axis
        )
        before = jnp.split(before, count, along)
        after = jnp.split(after, count, along)
        if dim == 0:
            fields = [jnp.concatenate([b, f, a], 0) for b, f, a in zip(before, fields, after)]
            continue
        own = [lax.slice_in_dim(f, 0, size, axis=dim) for f in fields]
        gap = list(own[0].shape)
        gap[dim] = sizes[dim - 1] - size - 2 * width
        parts = [[jnp.zeros(gap, F32)] if gap[dim] else []] * count
        fields = [
            jnp.concatenate([f, a] + z + [b], dim)
            for b, f, a, z in zip(before, own, after, parts)
        ]
    return fields


def gathered(piece):
    count = piece.shape[0]
    nx = lax.axis_size("gx")
    pieces = lax.all_gather(piece, "gz")
    (pieces,) = call(repack, [(nx, count, 8, 128)], [], pieces, name="repack")
    pieces = lax.all_to_all(pieces, "gx", 0, 0)
    return lax.all_gather(pieces, "gy")


def body(right_side, conductivity):
    nx, ny, nz = (lax.axis_size(axis) for axis in ("gx", "gy", "gz"))
    index = jnp.stack([lax.axis_index(axis) for axis in ("gx", "gy", "gz")]).astype(jnp.int32)
    y0, z0 = coords(48, 32), coords(256, 128)
    y1, z1 = coords(24, 16), coords(128, 64)
    y2, z2 = coords(16, 8), coords(128, 32)
    far = np.full(128, -1000)

    def ends(count):
        at = far.copy()
        at[:count] = np.arange(count)
        return at

    ry0, rz0 = restriction(np.arange(16), y0), restriction(ends(64), z0).T
    cy0, cz0 = halving(y1, y0), halving(z1, z0).T
    ry1, rz1 = restriction(np.arange(8), y1), restriction(ends(32), z1).T
    cy1, cz1 = halving(y2, y1), halving(z2, z1).T

    def both(matrix):
        zero = np.zeros_like(matrix)
        return np.stack([np.concatenate([matrix, zero]), np.concatenate([zero, matrix])])

    ry2, rz2 = both(restriction(np.arange(4), y2)), restriction(ends(16), z2).T
    cy2, cz2 = both(halving(np.arange(4), y2)), halving(ends(16), z2).T
    py0, pz0 = prolongation(y0, y1), prolongation(z0, z1).T
    py1, pz1 = prolongation(y1, y2), prolongation(z1, z2).T
    rows3, rows4, lanes3 = np.arange(4 * ny), np.arange(2 * ny), ends(16 * nz)
    lanes4 = np.where(ends(8 * nz) < 0, -5000, ends(8 * nz))
    ry3, rz3 = restriction(rows4, rows3), restriction(lanes4, lanes3).T
    cy3, cz3 = halving(rows4, rows3), halving(lanes4, lanes3).T
    py3, pz3 = prolongation(rows3, rows4), prolongation(lanes3, lanes4).T
    m3 = (ry3, rz3, cy3, cz3, py3, pz3)

    wide, l1, l2 = (26, 48, 256), (16, 24, 128), (12, 16, 128)
    n3, n4 = (2 * nx + 6, 4 * ny, 128), (nx + 2, 2 * ny, 128)
    low = [
        n3, n3, n3, (3,) + n3, n3, n3,
        n4, (nx, 2 * ny, 128), n4, (3,) + n4, n4, n4,
        (nx * 2 * ny, 128), (nx + 2, 4 * ny, 128),
    ]
    mid = [l2, (3,) + l2, l1, (3,) + l1, (8, 16, 128), (10, 24, 128)]

    f, k = exchange([right_side, conductivity], (16, 32, 128), (48, 256), 5)
    b1, b2 = (8, 16, 128), (4, 8, 128)
    wx, wy, wz, d, g1, k1, d1 = call(
        down0, [wide] * 4 + [b1] * 3,
        [wide, wide, (128, 256), (10, 24, 128), (4, 10, 24, 128)],
        f, k, ry0, rz0, cy0, cz0, name="down0",
    )
    g1, k1, d1 = exchange([g1, k1, d1], (8, 16, 64), (24, 128), 4)
    inner1 = [l1, l1, (32, 128), (3,) + l1]
    g2, k2, d2 = call(
        functools.partial(down, 1, True), [b2] * 3,
        inner1 + [(6, 16, 128), (4, 6, 16, 128)],
        g1, k1, d1, ry1, rz1, cy1, cz1, name="down1",
    )
    g2, k2, d2 = exchange([g2, k2, d2], (4, 8, 32), (16, 128), 4)
    inner2 = [l2, l2, (2, 8, 128), (3,) + l2]
    (piece,) = call(
        functools.partial(down2, True), [(2, 8, 128)], inner2,
        g2, k2, d2, ry2, rz2, cy2, cz2, name="down2",
    )
    s = gathered(piece)
    fields = (f, wx, wy, wz, d, k)
    v, g1b, k3 = call(
        functools.partial(middle, 16 * nz), [wide, b1, n3],
        low + mid + [(14, 48, 256), wide, (128, 256)],
        index, s, g2, k2, d2, g1, k1, d1, *fields, *m3, py1, pz1, py0, pz0, ry0, rz0,
        name="middle", scalars=1,
    )
    (g1,) = exchange([g1b], (8, 16, 64), (24, 128), 4)
    (g2b,) = call(
        functools.partial(down, 1, False), [b2], inner1, g1, k1, d1, ry1, rz1, name="again1"
    )
    (g2,) = exchange([g2b], (4, 8, 32), (16, 128), 4)
    (piece,) = call(
        functools.partial(down2, False), [(1, 8, 128)], inner2, g2, k2, d2, ry2, rz2, name="again2"
    )
    s = gathered(piece)
    return tuple(call(
        functools.partial(final, 16 * nz), [(16, 32, 128)] * 2,
        low + mid + [(12, 48, 256), wide],
        index, s, g2, k2, d2, g1, k1, d1, *fields, *m3, py1, pz1, py0, pz0, k3, v,
        name="final", scalars=1,
    ))


def solution(mesh):
    placed = P("gx", "gy", "gz")
    return jax.shard_map(
        body, mesh=mesh, in_specs=(placed, placed), out_specs=(placed, placed), check_vma=False
    )
```

time: 1270 us -> 321 us (0.25); the launches traced: 1250 us -> 318 us
  starting transfers between devices: 911 us -> 97.3 us
  waiting for transfers between devices: 276 us -> 52.5 us
  blocking collectives: 0 us -> 76.6 us
  Pallas kernels: 0 us -> 71.2 us
  local copies, waits for them, and re-layouts: 32.9 us -> 12.9 us
  other arithmetic: 19.8 us -> 5.47 us
    ppermute x294 -> x30, starting transfers between devices: 911 us -> 78.2 us  [the longest x15 49 us: neighbours(): before = lax.ppermute(last, axis, up)]
    ppermute x294 -> x30, waiting for transfers between devices: 276 us -> 40.9 us  [the longest x15 26.9 us: neighbours(): after = lax.ppermute(initial, axis, down)]
    pallas_call x0 -> x9, Pallas kernels: none -> 71.2 us  [call(): pl.pallas_call(kernel, out_shape=[jax.ShapeDtypeStruct(o, F32) for o in o...]
    all_gather x0 -> x4, blocking collectives: none -> 55.9 us  [the longest x2 32.9 us: gathered(): pieces = lax.all_gather(piece, 'gz')]
    slice x206 -> x25, local copies, waits for them, and re-layouts: 24.3 us -> 2.18 us  [the longest x19 2.07 us: exchange(): initial = [lax.slice_in_dim(f, 0, width, axis=dim) for f in fields]]
    all_to_all x0 -> x1, blocking collectives: none -> 20.7 us  [gathered(): pieces = lax.all_to_all(pieces, 'gx', 0, 0)]
    all_to_all x0 -> x1, starting transfers between devices: none -> 19.1 us  [gathered(): pieces = lax.all_to_all(pieces, 'gx', 0, 0)]
  transfers between devices with their start and end apart: 294 -> 31, of which waited for: 136 -> 24; matrix products, arithmetic and copies ran while one was open for 2% -> 1% of each run, Pallas kernels for 0% -> 0%
where the time goes in v1:
time: 321 us; the launch traced here: 318 us
  starting transfers between devices  97.3 us (30%)
  blocking collectives  76.6 us (24%)
  Pallas kernels  71.2 us (22%)
  waiting for transfers between devices  52.5 us (16%)
  local copies, waits for them, and re-layouts  12.9 us (4%)
  other arithmetic  5.47 us (2%)
    pallas_call x9, Pallas kernels, call(): pl.pallas_call(kernel, out_shape=[jax.ShapeDtypeStruct(o, F32) for o in o...  71.2 us
    ppermute x15, starting transfers between devices, neighbours(): before = lax.ppermute(last, axis, up)  49 us
    all_gather x2, blocking collectives, gathered(): pieces = lax.all_gather(piece, 'gz')  32.9 us
    ppermute x15, starting transfers between devices, neighbours(): after = lax.ppermute(initial, axis, down)  29.3 us
    ppermute x15, waiting for transfers between devices, neighbours(): after = lax.ppermute(initial, axis, down)  26.9 us
    all_gather x2, blocking collectives, gathered(): return lax.all_gather(pieces, 'gy')  23 us
    all_to_all x1, blocking collectives, gathered(): pieces = lax.all_to_all(pieces, 'gx', 0, 0)  20.7 us
    all_to_all x1, starting transfers between devices, gathered(): pieces = lax.all_to_all(pieces, 'gx', 0, 0)  19.1 us
  transfers between devices with their start and end apart: 31, of which 24 were waited for; matrix products, arithmetic and copies ran while one was open for 1% of the time, Pallas kernels for 0%

profile of v1, /device:TPU:1, one launch (start us, length us, event | category | flops | bytes accessed | tf_op | source)
XLA Modules:
  0.0 317.7 jit_solution(15784907659331652699)
XLA Ops:
  0.6 1.2 fusion.86
  2.5 6.9 %collective-permute-start = (f32[16,32,10]{2,1,0:T(8,128)S(1)}, f32[16,32,10]{2,1,0:T(8,128)S(1)}, u32[]{:S(2)}, u32[]{:S(2)}) collective-permute-start(f32[16,32,10]{2,1,0:T(8,128)S(1)} %copy.28), channel_id=1, source_target_pairs={{1,0},{2,1},{3,2},{4,3},{5,4},{6,5},{7,6},{0,7},{9,8},{10,9},{11,1... | collective-permute-start | bytes 61448 | tf_op jit(solution)/shard_map/ppermute | solution.py:437
  10.8 2.5 collective-permute-done.1
  13.9 1.3 collective-permute-start.3
  15.3 1.3 collective-permute-start.2
  16.6 1.9 collective-permute-done.3
  18.5 3.8 %collective-permute-done.2 = f32[32,5,256]{2,1,0:T(8,128)S(1)} collective-permute-done((f32[32,5,256]{2,1,0:T(8,128)S(1)}, f32[32,5,256]{2,1,0:T(8,128)S(1)}, u32[]{:S(2)}, u32[]{:S(2)}) %collective-permute-start.2) | collective-permute-done | bytes 163872 | tf_op jit(solution)/shard_map/ppermute | solution.py:437
  22.9 1.3 collective-permute-start.5
  24.2 4.0 %collective-permute-start.4 = (f32[10,48,256]{2,1,0:T(8,128)S(1)}, f32[10,48,256]{2,1,0:T(8,128)S(1)}, u32[]{:S(2)}, u32[]{:S(2)}) collective-permute-start(f32[10,48,256]{2,1,0:T(8,128)S(1)} %pad_maximum_fusion.10), channel_id=1, source_target_pairs={{0,32},{32,64},{64,96},{96,128},{128,160},{160,192},{192,224},{224... | collective-permute-start | bytes 1474568 | tf_op jit(solution)/shard_map/ppermute | solution.py:436
  28.3 4.2 %collective-permute-done.5 = f32[10,48,256]{2,1,0:T(8,128)S(1)} collective-permute-done((f32[10,48,256]{2,1,0:T(8,128)S(1)}, f32[10,48,256]{2,1,0:T(8,128)S(1)}, u32[]{:S(2)}, u32[]{:S(2)}) %collective-permute-start.5) | collective-permute-done | bytes 491552 | tf_op jit(solution)/shard_map/ppermute | solution.py:437
  32.5 1.5 collective-permute-done.4
  34.1 1.9 fusion.9
  36.0 12.8 %down0.1 = (f32[26,48,256]{2,1,0:T(8,128)S(1)}, f32[26,48,256]{2,1,0:T(8,128)S(1)}, f32[26,48,256]{2,1,0:T(8,128)S(1)}, f32[26,48,256]{2,1,0:T(8,128)S(1)}, f32[...) custom-call(f32[26,48,256]{2,1,0:T(8,128)} %get-tuple-element.41.f, ...), custom_call_target="tpu_custom_call" | custom-call | tf_op jit(solution)/shard_map/down0/pallas_call | solution.py:418
  48.8 1.1 copy-done.4
  50.2 8.2 %collective-permute-start.7 = (f32[8,16,12]{2,1,0:T(8,128)S(1)}, f32[8,16,12]{2,1,0:T(8,128)S(1)}, u32[]{:S(2)}, u32[]{:S(2)}) collective-permute-start(f32[8,16,12]{2,1,0:T(8,128)S(1)} %pad_maximum_fusion.36), channel_id=1, source_target_pairs={{0,1},{1,2},{2,3},{3,4},{4,5},{5,6},{6,7},{7,0},{8,9},{9,10},{10,1... | collective-permute-start | bytes 18440 | tf_op jit(solution)/shard_map/ppermute | solution.py:436
  58.6 1.2 collective-permute-done.7
  59.9 2.4 collective-permute-done.6
  62.7 3.1 collective-permute-start.9
  65.9 1.3 collective-permute-start.8
  67.2 3.5 %collective-permute-done.8 = f32[24,4,128]{2,1,0:T(4,128)S(1)} collective-permute-done((f32[24,4,128]{2,1,0:T(4,128)S(1)}, f32[24,4,128]{2,1,0:T(4,128)S(1)}, u32[]{:S(2)}, u32[]{:S(2)}) %collective-permute-start.8) | collective-permute-done | bytes 49184 | tf_op jit(solution)/shard_map/ppermute | solution.py:437
  71.0 1.3 collective-permute-start.11
  72.3 4.9 %collective-permute-start.10 = (f32[12,24,128]{2,1,0:T(8,128)S(1)}, f32[12,24,128]{2,1,0:T(8,128)S(1)}, u32[]{:S(2)}, u32[]{:S(2)}) collective-permute-start(f32[12,24,128]{2,1,0:T(8,128)S(1)} %pad_maximum_fusion.30), channel_id=1, source_target_pairs={{0,32},{32,64},{64,96},{96,128},{128,160},{160,192},{192,224},{224... | collective-permute-start | bytes 442376 | tf_op jit(solution)/shard_map/ppermute | solution.py:436
  77.6 1.7 collective-permute-done.10
  79.6 3.0 down1.1
  83.0 3.4 %collective-permute-start.13 = (f32[4,8,12]{2,1,0:T(8,128)S(1)}, f32[4,8,12]{2,1,0:T(8,128)S(1)}, u32[]{:S(2)}, u32[]{:S(2)}) collective-permute-start(f32[4,8,12]{2,1,0:T(8,128)S(1)} %pad_maximum_fusion.47), channel_id=1, source_target_pairs={{0,1},{1,2},{2,3},{3,4},{4,5},{5,6},{6,7},{7,0},{8,9},{9,10},{10,1... | collective-permute-start | bytes 4616 | tf_op jit(solution)/shard_map/ppermute | solution.py:436
  87.3 2.3 collective-permute-done.12
  89.9 2.8 collective-permute-start.15
  92.7 1.3 collective-permute-start.14
  94.0 3.2 %collective-permute-done.14 = f32[12,4,128]{2,1,0:T(4,128)S(1)} collective-permute-done((f32[12,4,128]{2,1,0:T(4,128)S(1)}, f32[12,4,128]{2,1,0:T(4,128)S(1)}, u32[]{:S(2)}, u32[]{:S(2)}) %collective-permute-start.14) | collective-permute-done | bytes 24608 | tf_op jit(solution)/shard_map/ppermute | solution.py:437
  97.4 1.3 collective-permute-start.17
  98.7 4.7 %collective-permute-start.16 = (f32[12,16,128]{2,1,0:T(8,128)S(1)}, f32[12,16,128]{2,1,0:T(8,128)S(1)}, u32[]{:S(2)}, u32[]{:S(2)}) collective-permute-start(f32[12,16,128]{2,1,0:T(8,128)S(1)} %maximum_maximum_fusion), channel_id=1, source_target_pairs={{0,32},{32,64},{64,96},{96,128},{128,160},{160,192},{192,224},{224... | collective-permute-start | bytes 294920 | tf_op jit(solution)/shard_map/ppermute | solution.py:436
  103.6 1.5 collective-permute-done.16
  105.3 1.2 down2.1
  106.5 15.1 %all-gather = f32[16,8,128]{2,1,0:T(8,128)S(1)} all-gather(f32[2,8,128]{2,1,0:T(8,128)S(1)} %down2.1), channel_id=2, replica_groups=mesh['gx'=16,'gy'=4,'gz'=8] {'gz'}, dimensions={0}, use_global_device_ids=true | all-gather | bytes 73728 | tf_op jit(solution)/shard_map/all_gather | solution.py:474
  122.4 19.1 %all-to-all-start = ((f32[16,2,8,128]{3,2,1,0:T(8,128)}), f32[16,2,8,128]{3,2,1,0:T(8,128)}, u32[]{:S(2)}, u32[]{:S(2)}) async-start(f32[16,2,8,128]{3,2,1,0:T(8,128)} %copy-done.8), calls=%async_computation | async-start | bytes 262144 | tf_op jit(solution)/shard_map/all_to_all | solution.py:476
  142.0 11.6 %all-to-all-done = f32[16,2,8,128]{3,2,1,0:T(8,128)} async-done(((f32[16,2,8,128]{3,2,1,0:T(8,128)}), f32[16,2,8,128]{3,2,1,0:T(8,128)}, u32[]{:S(2)}, u32[]{:S(2)}) %all-to-all-start) | async-done | bytes 131104 | tf_op jit(solution)/shard_map/all_to_all | solution.py:476
  153.7 11.3 %all-gather.1 = f32[64,2,8,128]{3,2,1,0:T(8,128)S(1)} all-gather(f32[16,2,8,128]{3,2,1,0:T(8,128)} %all-to-all-done), channel_id=3, replica_groups=mesh['gx'=16,'gy'=4,'gz'=8] {'gy'}, dimensions={0}, use_global_device_ids=true | all-gather | bytes 655360 | tf_op jit(solution)/shard_map/all_gather | solution.py:477
  165.0 0.9 copy-done.6
  165.9 0.9 copy-done.10
  166.8 0.8 copy-done.12
  167.7 0.8 copy-done.13
  168.5 0.8 copy-done.14
  172.0 28.0 %middle.1 = (f32[26,48,256]{2,1,0:T(8,128)S(1)}, f32[8,16,128]{2,1,0:T(8,128)S(1)}, f32[38,16,128]{2,1,0:T(8,128)S(1)}) custom-call(s32[3]{0:T(128)S(1)} %copy-done.35, f32[4,16,2,8,128]{4,3,2,1,0:T(8,128)S(1)} %bitcast.15, f32[12,16,128]{2,1,0:T(8,128)S(1)} %get-tuple-element.125.refs_0_.g2, f32[12,16,128]{2,1,0:T(8,128)S(1)} %pad_maximum_fusion.32.refs_1_.k2, ...), custom_call_target="tpu_custom_call" | custom-call | tf_op jit(solution)/shard_map/middle/pallas_call | solution.py:418
  200.2 4.7 %collective-permute-start.18 = (f32[8,16,4]{2,1,0:T(8,128)S(1)}, f32[8,16,4]{2,1,0:T(8,128)S(1)}, u32[]{:S(2)}, u32[]{:S(2)}) collective-permute-start(f32[8,16,4]{2,1,0:T(8,128)S(1)} %get-tuple-element.80), channel_id=1, source_target_pairs={{1,0},{2,1},{3,2},{4,3},{5,4},{6,5},{7,6},{0,7},{9,8},{10,9},{11,1... | collective-permute-start | bytes 6152 | tf_op jit(solution)/shard_map/ppermute | solution.py:437
  205.6 1.9 collective-permute-done.18
  207.7 1.3 collective-permute-start.20
  209.0 4.0 %collective-permute-start.21 = (f32[8,4,128]{2,1,0:T(4,128)S(1)}, f32[8,4,128]{2,1,0:T(4,128)S(1)}, u32[]{:S(2)}, u32[]{:S(2)}) collective-permute-start(f32[8,4,128]{2,1,0:T(4,128)S(1)} %get-tuple-element.79), channel_id=1, source_target_pairs={{0,8},{8,16},{16,24},{1,9},{9,17},{17,25},{2,10},{10,18},{18,26},{... | collective-permute-start | bytes 49160 | tf_op jit(solution)/shard_map/ppermute | solution.py:436
  213.0 0.8 collective-permute-done.21
  214.0 3.2 %collective-permute-start.22 = (f32[4,24,128]{2,1,0:T(8,128)S(1)}, f32[4,24,128]{2,1,0:T(8,128)S(1)}, u32[]{:S(2)}, u32[]{:S(2)}) collective-permute-start(f32[4,24,128]{2,1,0:T(8,128)S(1)} %get-tuple-element.64), channel_id=1, source_target_pairs={{0,32},{32,64},{64,96},{96,128},{128,160},{160,192},{192,224},{224... | collective-permute-start | bytes 147464 | tf_op jit(solution)/shard_map/ppermute | solution.py:436
  217.2 1.3 collective-permute-start.23
  218.5 3.5 %collective-permute-done.23 = f32[4,24,128]{2,1,0:T(8,128)S(1)} collective-permute-done((f32[4,24,128]{2,1,0:T(8,128)S(1)}, f32[4,24,128]{2,1,0:T(8,128)S(1)}, u32[]{:S(2)}, u32[]{:S(2)}) %collective-permute-start.23) | collective-permute-done | bytes 49184 | tf_op jit(solution)/shard_map/ppermute | solution.py:437
  222.2 1.6 again1.1
  223.9 4.8 %collective-permute-start.24 = (f32[4,8,4]{2,1,0:T(8,128)S(1)}, f32[4,8,4]{2,1,0:T(8,128)S(1)}, u32[]{:S(2)}, u32[]{:S(2)}) collective-permute-start(f32[4,8,4]{2,1,0:T(8,128)S(1)} %get-tuple-element.122), channel_id=1, source_target_pairs={{1,0},{2,1},{3,2},{4,3},{5,4},{6,5},{7,6},{0,7},{9,8},{10,9},{11,1... | collective-permute-start | bytes 1544 | tf_op jit(solution)/shard_map/ppermute | solution.py:437
  228.7 0.9 collective-permute-done.24
  230.0 1.3 collective-permute-start.26
  231.3 4.5 %collective-permute-start.27 = (f32[4,4,128]{2,1,0:T(4,128)S(1)}, f32[4,4,128]{2,1,0:T(4,128)S(1)}, u32[]{:S(2)}, u32[]{:S(2)}) collective-permute-start(f32[4,4,128]{2,1,0:T(4,128)S(1)} %get-tuple-element.121), channel_id=1, source_target_pairs={{0,8},{8,16},{16,24},{1,9},{9,17},{17,25},{2,10},{10,18},{18,26},{... | collective-permute-start | bytes 24584 | tf_op jit(solution)/shard_map/ppermute | solution.py:436
  236.7 1.3 collective-permute-start.29
  238.0 4.0 %collective-permute-start.28 = (f32[4,16,128]{2,1,0:T(8,128)S(1)}, f32[4,16,128]{2,1,0:T(8,128)S(1)}, u32[]{:S(2)}, u32[]{:S(2)}) collective-permute-start(f32[4,16,128]{2,1,0:T(8,128)S(1)} %pad_maximum_fusion.43), channel_id=1, source_target_pairs={{0,32},{32,64},{64,96},{96,128},{128,160},{160,192},{192,224},{224... | collective-permute-start | bytes 98312 | tf_op jit(solution)/shard_map/ppermute | solution.py:436
  242.0 1.0 collective-permute-done.28
  243.1 1.1 again2.1
  244.3 17.8 %all-gather.2 = f32[8,8,128]{2,1,0:T(8,128)S(1)} all-gather(f32[1,8,128]{2,1,0:T(8,128)S(1)} %again2.1), channel_id=4, replica_groups=mesh['gx'=16,'gy'=4,'gz'=8] {'gz'}, dimensions={0}, use_global_device_ids=true | all-gather | bytes 36864 | tf_op jit(solution)/shard_map/all_gather | solution.py:474
  262.2 20.7 %all_to_all.10 = f32[16,1,8,128]{3,2,1,0:T(8,128)S(1)} all-to-all(f32[16,1,8,128]{3,2,1,0:T(8,128)S(1)} %repack.3), channel_id=1, replica_groups=mesh['gx'=16,'gy'=4,'gz'=8] {'gx'}, dimensions={0} | all-to-all | bytes 131072 | tf_op jit(solution)/shard_map/all_to_all | solution.py:476
  282.8 11.7 %all-gather.3 = f32[64,1,8,128]{3,2,1,0:T(8,128)S(1)} all-gather(f32[16,1,8,128]{3,2,1,0:T(8,128)S(1)} %all_to_all.10), channel_id=5, replica_groups=mesh['gx'=16,'gy'=4,'gz'=8] {'gy'}, dimensions={0}, use_global_device_ids=true | all-gather | bytes 327680 | tf_op jit(solution)/shard_map/all_gather | solution.py:477
  294.5 23.2 %final.1 = (f32[16,32,128]{2,1,0:T(8,128)}, f32[16,32,128]{2,1,0:T(8,128)}) custom-call(s32[3]{0:T(128)S(1)} %copy-done.36, f32[4,16,1,8,128]{4,3,2,1,0:T(8,128)S(1)} %bitcast.28, f32[12,16,128]{2,1,0:T(8,128)S(1)} %fusion.55.refs_0_.g2, f32[12,16,128]{2,1,0:T(8,128)S(1)} %pad_maximum_fusion.32.refs_1_.k2, f32[12,16,128]{2,1,0:T(8,128)S(1)} %get-tuple-element.124.refs_2_.d2, ...), custom_call_target="tpu_custom_call" | custom-call | tf_op jit(solution)/shard_map/final/pallas_call | solution.py:418
  (195 shorter events, 13.7 us)
Async XLA Ops:
  0.6 1.4 copy-start.37
  2.5 8.0 %collective-permute-start = (f32[16,32,10]{2,1,0:T(8,128)S(1)}, f32[16,32,10]{2,1,0:T(8,128)S(1)}, u32[]{:S(2)}, u32[]{:S(2)}) collective-permute-start(f32[16,32,10]{2,1,0:T(8,128)S(1)} %copy.28), channel_id=1, source_target_pairs={{1,0},{2,1},{3,2},{4,3},{5,4},{6,5},{7,6},{0,7},{9,8},{10,9},{11,1... | collective-permute-start | bytes 61448 | tf_op jit(solution)/shard_map/ppermute | solution.py:437
  10.0 3.3 %collective-permute-start.1 = (f32[16,32,10]{2,1,0:T(8,128)S(1)}, f32[16,32,10]{2,1,0:T(8,128)S(1)}, u32[]{:S(2)}, u32[]{:S(2)}) collective-permute-start(f32[16,32,10]{2,1,0:T(8,128)S(1)} %copy.31), channel_id=1, source_target_pairs={{0,1},{1,2},{2,3},{3,4},{4,5},{5,6},{6,7},{7,0},{8,9},{9,10},{10,1... | collective-permute-start | bytes 61448 | tf_op jit(solution)/shard_map/ppermute | solution.py:436
  10.6 2.9 copy-start.38
  13.9 4.6 %collective-permute-start.3 = (f32[32,5,256]{2,1,0:T(8,128)S(1)}, f32[32,5,256]{2,1,0:T(8,128)S(1)}, u32[]{:S(2)}, u32[]{:S(2)}) collective-permute-start(f32[32,5,256]{2,1,0:T(8,128)S(1)} %pad_maximum_fusion.17), channel_id=1, source_target_pairs={{0,8},{8,16},{16,24},{1,9},{9,17},{17,25},{2,10},{10,18},{18,26},{... | collective-permute-start | bytes 491528 | tf_op jit(solution)/shard_map/ppermute | solution.py:436
  15.3 7.1 %collective-permute-start.2 = (f32[32,5,256]{2,1,0:T(8,128)S(1)}, f32[32,5,256]{2,1,0:T(8,128)S(1)}, u32[]{:S(2)}, u32[]{:S(2)}) collective-permute-start(f32[32,5,256]{2,1,0:T(8,128)S(1)} %pad_maximum_fusion.16), channel_id=1, source_target_pairs={{8,0},{16,8},{24,16},{9,1},{17,9},{25,17},{10,2},{18,10},{26,18},{... | collective-permute-start | bytes 491528 | tf_op jit(solution)/shard_map/ppermute | solution.py:437
  22.9 9.6 %collective-permute-start.5 = (f32[10,48,256]{2,1,0:T(8,128)S(1)}, f32[10,48,256]{2,1,0:T(8,128)S(1)}, u32[]{:S(2)}, u32[]{:S(2)}) collective-permute-start(f32[10,48,256]{2,1,0:T(8,128)S(1)} %pad_maximum_fusion.11), channel_id=1, source_target_pairs={{32,0},{64,32},{96,64},{128,96},{160,128},{192,160},{224,192},{256... | collective-permute-start | bytes 1474568 | tf_op jit(solution)/shard_map/ppermute | solution.py:437
  24.2 9.8 %collective-permute-start.4 = (f32[10,48,256]{2,1,0:T(8,128)S(1)}, f32[10,48,256]{2,1,0:T(8,128)S(1)}, u32[]{:S(2)}, u32[]{:S(2)}) collective-permute-start(f32[10,48,256]{2,1,0:T(8,128)S(1)} %pad_maximum_fusion.10), channel_id=1, source_target_pairs={{0,32},{32,64},{64,96},{96,128},{128,160},{160,192},{192,224},{224... | collective-permute-start | bytes 1474568 | tf_op jit(solution)/shard_map/ppermute | solution.py:436
  34.0 2.0 copy-start.9
  34.0 1.9 copy-start.19
  34.0 1.9 copy-start.26
  34.1 1.9 copy-start.32
  48.8 1.1 copy-start.4
  49.9 12.8 %copy-start.1 = (f32[26,48,256]{2,1,0:T(8,128)}, f32[26,48,256]{2,1,0:T(8,128)S(1)}, u32[]{:S(2)}) copy-start(f32[26,48,256]{2,1,0:T(8,128)S(1)} %get-tuple-element.22.wy) | copy-start | bytes 3833860
  49.9 12.8 %copy-start.3 = (f32[26,48,256]{2,1,0:T(8,128)}, f32[26,48,256]{2,1,0:T(8,128)S(1)}, u32[]{:S(2)}) copy-start(f32[26,48,256]{2,1,0:T(8,128)S(1)} %get-tuple-element.23.wz) | copy-start | bytes 3833860
  50.2 9.6 %collective-permute-start.7 = (f32[8,16,12]{2,1,0:T(8,128)S(1)}, f32[8,16,12]{2,1,0:T(8,128)S(1)}, u32[]{:S(2)}, u32[]{:S(2)}) collective-permute-start(f32[8,16,12]{2,1,0:T(8,128)S(1)} %pad_maximum_fusion.36), channel_id=1, source_target_pairs={{0,1},{1,2},{2,3},{3,4},{4,5},{5,6},{6,7},{7,0},{8,9},{9,10},{10,1... | collective-permute-start | bytes 18440 | tf_op jit(solution)/shard_map/ppermute | solution.py:436
  58.6 3.7 %collective-permute-start.6 = (f32[8,16,12]{2,1,0:T(8,128)S(1)}, f32[8,16,12]{2,1,0:T(8,128)S(1)}, u32[]{:S(2)}, u32[]{:S(2)}) collective-permute-start(f32[8,16,12]{2,1,0:T(8,128)S(1)} %pad_maximum_fusion.35), channel_id=1, source_target_pairs={{1,0},{2,1},{3,2},{4,3},{5,4},{6,5},{7,6},{0,7},{9,8},{10,9},{11,1... | collective-permute-start | bytes 18440 | tf_op jit(solution)/shard_map/ppermute | solution.py:437
  62.4 17.0 %copy-start.39 = (f32[8,16,56]{2,1,0:T(8,128)}, f32[8,16,56]{2,1,0:T(8,128)S(1)}, u32[]{:S(2)}) copy-start(f32[8,16,56]{2,1,0:T(8,128)S(1)} %broadcast.6) | copy-start | bytes 86020
  62.7 4.5 %collective-permute-start.9 = (f32[24,4,128]{2,1,0:T(4,128)S(1)}, f32[24,4,128]{2,1,0:T(4,128)S(1)}, u32[]{:S(2)}, u32[]{:S(2)}) collective-permute-start(f32[24,4,128]{2,1,0:T(4,128)S(1)} %pad_maximum_fusion.38), channel_id=1, source_target_pairs={{0,8},{8,16},{16,24},{1,9},{9,17},{17,25},{2,10},{10,18},{18,26},{... | collective-permute-start | bytes 147464 | tf_op jit(solution)/shard_map/ppermute | solution.py:436
  65.9 4.8 %collective-permute-start.8 = (f32[24,4,128]{2,1,0:T(4,128)S(1)}, f32[24,4,128]{2,1,0:T(4,128)S(1)}, u32[]{:S(2)}, u32[]{:S(2)}) collective-permute-start(f32[24,4,128]{2,1,0:T(4,128)S(1)} %pad_maximum_fusion.37), channel_id=1, source_target_pairs={{8,0},{16,8},{24,16},{9,1},{17,9},{25,17},{10,2},{18,10},{26,18},{... | collective-permute-start | bytes 147464 | tf_op jit(solution)/shard_map/ppermute | solution.py:437
  71.0 6.6 %collective-permute-start.11 = (f32[12,24,128]{2,1,0:T(8,128)S(1)}, f32[12,24,128]{2,1,0:T(8,128)S(1)}, u32[]{:S(2)}, u32[]{:S(2)}) collective-permute-start(f32[12,24,128]{2,1,0:T(8,128)S(1)} %pad_maximum_fusion.31), channel_id=1, source_target_pairs={{32,0},{64,32},{96,64},{128,96},{160,128},{192,160},{224,192},{256... | collective-permute-start | bytes 442376 | tf_op jit(solution)/shard_map/ppermute | solution.py:437
  72.3 7.3 %copy-start.17 = (f32[128,128]{1,0:T(8,128)S(1)}, f32[128,128]{1,0:T(8,128)}, u32[]{:S(2)}) copy-start(f32[128,128]{1,0:T(8,128)} %constant.73.clone.refs_4_) | copy-start | bytes 196612
  72.3 7.3 %copy-start.22 = (f32[128,128]{1,0:T(8,128)S(1)}, f32[128,128]{1,0:T(8,128)}, u32[]{:S(2)}) copy-start(f32[128,128]{1,0:T(8,128)} %constant.75.clone.refs_6_) | copy-start | bytes 196612
  72.3 7.3 %copy-start.30 = (f32[8,24]{1,0:T(8,128)S(1)}, f32[8,24]{1,0:T(8,128)}, u32[]{:S(2)}) copy-start(f32[8,24]{1,0:T(8,128)} %constant.72.clone.refs_3_) | copy-start | bytes 2308
  72.3 7.3 %copy-start.34 = (f32[16,24]{1,0:T(8,128)S(1)}, f32[16,24]{1,0:T(8,128)}, u32[]{:S(2)}) copy-start(f32[16,24]{1,0:T(8,128)} %constant.74.clone.refs_5_) | copy-start | bytes 4612
  72.3 6.9 %collective-permute-start.10 = (f32[12,24,128]{2,1,0:T(8,128)S(1)}, f32[12,24,128]{2,1,0:T(8,128)S(1)}, u32[]{:S(2)}, u32[]{:S(2)}) collective-permute-start(f32[12,24,128]{2,1,0:T(8,128)S(1)} %pad_maximum_fusion.30), channel_id=1, source_target_pairs={{0,32},{32,64},{64,96},{96,128},{128,160},{160,192},{192,224},{224... | collective-permute-start | bytes 442376 | tf_op jit(solution)/shard_map/ppermute | solution.py:436
  82.8 22.5 %copy-start.15 = (f32[128,128]{1,0:T(8,128)S(1)}, f32[128,128]{1,0:T(8,128)}, u32[]{:S(2)}) copy-start(f32[128,128]{1,0:T(8,128)} %constant.77.clone.refs_4_) | copy-start | bytes 196612
  82.8 22.5 %copy-start.21 = (f32[128,128]{1,0:T(8,128)S(1)}, f32[128,128]{1,0:T(8,128)}, u32[]{:S(2)}) copy-start(f32[128,128]{1,0:T(8,128)} %constant.79.clone.refs_6_) | copy-start | bytes 196612
  82.8 22.5 %copy-start.24 = (f32[2,8,16]{2,1,0:T(8,128)S(1)}, f32[2,8,16]{2,1,0:T(8,128)}, u32[]{:S(2)}) copy-start(f32[2,8,16]{2,1,0:T(8,128)} %constant.76.clone.refs_3_) | copy-start | bytes 3076
  82.8 22.5 %copy-start.33 = (f32[2,8,16]{2,1,0:T(8,128)S(1)}, f32[2,8,16]{2,1,0:T(8,128)}, u32[]{:S(2)}) copy-start(f32[2,8,16]{2,1,0:T(8,128)} %constant.78.clone.refs_5_) | copy-start | bytes 3076
  83.0 4.2 %collective-permute-start.13 = (f32[4,8,12]{2,1,0:T(8,128)S(1)}, f32[4,8,12]{2,1,0:T(8,128)S(1)}, u32[]{:S(2)}, u32[]{:S(2)}) collective-permute-start(f32[4,8,12]{2,1,0:T(8,128)S(1)} %pad_maximum_fusion.47), channel_id=1, source_target_pairs={{0,1},{1,2},{2,3},{3,4},{4,5},{5,6},{6,7},{7,0},{8,9},{9,10},{10,1... | collective-permute-start | bytes 4616 | tf_op jit(solution)/shard_map/ppermute | solution.py:436
  86.4 3.2 collective-permute-start.12
  89.7 15.6 %copy-start.41 = (f32[4,8,88]{2,1,0:T(8,128)}, f32[4,8,88]{2,1,0:T(8,128)S(1)}, u32[]{:S(2)}) copy-start(f32[4,8,88]{2,1,0:T(8,128)S(1)} %broadcast.7) | copy-start | bytes 33796
  89.9 4.2 %collective-permute-start.15 = (f32[12,4,128]{2,1,0:T(4,128)S(1)}, f32[12,4,128]{2,1,0:T(4,128)S(1)}, u32[]{:S(2)}, u32[]{:S(2)}) collective-permute-start(f32[12,4,128]{2,1,0:T(4,128)S(1)} %pad_maximum_fusion.45), channel_id=1, source_target_pairs={{0,8},{8,16},{16,24},{1,9},{9,17},{17,25},{2,10},{10,18},{18,26},{... | collective-permute-start | bytes 73736 | tf_op jit(solution)/shard_map/ppermute | solution.py:436
  92.7 4.6 %collective-permute-start.14 = (f32[12,4,128]{2,1,0:T(4,128)S(1)}, f32[12,4,128]{2,1,0:T(4,128)S(1)}, u32[]{:S(2)}, u32[]{:S(2)}) collective-permute-start(f32[12,4,128]{2,1,0:T(4,128)S(1)} %pad_maximum_fusion.44), channel_id=1, source_target_pairs={{8,0},{16,8},{24,16},{9,1},{17,9},{25,17},{10,2},{18,10},{26,18},{... | collective-permute-start | bytes 73736 | tf_op jit(solution)/shard_map/ppermute | solution.py:437
  97.4 6.1 %collective-permute-start.17 = (f32[12,16,128]{2,1,0:T(8,128)S(1)}, f32[12,16,128]{2,1,0:T(8,128)S(1)}, u32[]{:S(2)}, u32[]{:S(2)}) collective-permute-start(f32[12,16,128]{2,1,0:T(8,128)S(1)} %maximum_maximum_fusion), channel_id=1, source_target_pairs={{32,0},{64,32},{96,64},{128,96},{160,128},{192,160},{224,192},{256... | collective-permute-start | bytes 294920 | tf_op jit(solution)/shard_map/ppermute | solution.py:437
  98.7 6.4 %collective-permute-start.16 = (f32[12,16,128]{2,1,0:T(8,128)S(1)}, f32[12,16,128]{2,1,0:T(8,128)S(1)}, u32[]{:S(2)}, u32[]{:S(2)}) collective-permute-start(f32[12,16,128]{2,1,0:T(8,128)S(1)} %maximum_maximum_fusion), channel_id=1, source_target_pairs={{0,32},{32,64},{64,96},{96,128},{128,160},{160,192},{192,224},{224... | collective-permute-start | bytes 294920 | tf_op jit(solution)/shard_map/ppermute | solution.py:436
  103.5 61.4 %copy-start = (f32[26,48,256]{2,1,0:T(8,128)S(1)}, f32[26,48,256]{2,1,0:T(8,128)}, u32[]{:S(2)}) copy-start(f32[26,48,256]{2,1,0:T(8,128)} %get-tuple-element.41.f) | copy-start | bytes 3833860
  103.5 61.4 %copy-start.11 = (f32[128,128]{1,0:T(8,128)S(1)}, f32[128,128]{1,0:T(8,128)}, u32[]{:S(2)}) copy-start(f32[128,128]{1,0:T(8,128)} %constant.87.clone.refs_7_) | copy-start | bytes 196612
  103.6 61.4 %copy-start.20 = (f32[48,24]{1,0:T(8,128)S(1)}, f32[48,24]{1,0:T(8,128)}, u32[]{:S(2)}) copy-start(f32[48,24]{1,0:T(8,128)} %constant.88.clone.refs_8_) | copy-start | bytes 13828
  103.6 61.4 %copy-start.23 = (f32[24,16]{1,0:T(8,128)S(1)}, f32[24,16]{1,0:T(8,128)}, u32[]{:S(2)}) copy-start(f32[24,16]{1,0:T(8,128)} %constant.86.clone.refs_6_) | copy-start | bytes 4612
  103.6 61.4 %copy-start.28 = (f32[8,16]{1,0:T(8,128)S(1)}, f32[8,16]{1,0:T(8,128)}, u32[]{:S(2)}) copy-start(f32[8,16]{1,0:T(8,128)} %constant.82.clone.refs_2_) | copy-start | bytes 1540
  122.4 31.3 %all-to-all-start = ((f32[16,2,8,128]{3,2,1,0:T(8,128)}), f32[16,2,8,128]{3,2,1,0:T(8,128)}, u32[]{:S(2)}, u32[]{:S(2)}) async-start(f32[16,2,8,128]{3,2,1,0:T(8,128)} %copy-done.8), calls=%async_computation | async-start | bytes 262144 | tf_op jit(solution)/shard_map/all_to_all | solution.py:476
  172.0 35.5 %copy-start.40 = (f32[8,16,56]{2,1,0:T(8,128)S(1)}, f32[8,16,56]{2,1,0:T(8,128)}, u32[]{:S(2)}) copy-start(f32[8,16,56]{2,1,0:T(8,128)} %copy-done.39) | copy-start | bytes 86020
  200.0 18.5 %copy-start.5 = (f32[26,48,256]{2,1,0:T(8,128)}, f32[26,48,256]{2,1,0:T(8,128)S(1)}, u32[]{:S(2)}) copy-start(f32[26,48,256]{2,1,0:T(8,128)S(1)} %get-tuple-element.27.refs_11_) | copy-start | bytes 3833860
  200.0 22.1 %copy-start.18 = (f32[128,128]{1,0:T(8,128)S(1)}, f32[128,128]{1,0:T(8,128)}, u32[]{:S(2)}) copy-start(f32[128,128]{1,0:T(8,128)} %constant.73.clone.refs_4_) | copy-start | bytes 196612
  200.1 22.1 %copy-start.31 = (f32[8,24]{1,0:T(8,128)S(1)}, f32[8,24]{1,0:T(8,128)}, u32[]{:S(2)}) copy-start(f32[8,24]{1,0:T(8,128)} %constant.72.clone.refs_3_) | copy-start | bytes 2308
  200.2 7.3 %collective-permute-start.18 = (f32[8,16,4]{2,1,0:T(8,128)S(1)}, f32[8,16,4]{2,1,0:T(8,128)S(1)}, u32[]{:S(2)}, u32[]{:S(2)}) collective-permute-start(f32[8,16,4]{2,1,0:T(8,128)S(1)} %get-tuple-element.80), channel_id=1, source_target_pairs={{1,0},{2,1},{3,2},{4,3},{5,4},{6,5},{7,6},{0,7},{9,8},{10,9},{11,1... | collective-permute-start | bytes 6152 | tf_op jit(solution)/shard_map/ppermute | solution.py:437
  204.8 2.7 collective-permute-start.19
  207.5 22.4 %copy-start.42 = (f32[4,8,88]{2,1,0:T(8,128)S(1)}, f32[4,8,88]{2,1,0:T(8,128)}, u32[]{:S(2)}) copy-start(f32[4,8,88]{2,1,0:T(8,128)} %copy-done.41) | copy-start | bytes 33796
  207.7 35.5 %copy-start.16 = (f32[128,128]{1,0:T(8,128)S(1)}, f32[128,128]{1,0:T(8,128)}, u32[]{:S(2)}) copy-start(f32[128,128]{1,0:T(8,128)} %constant.77.clone.refs_4_) | copy-start | bytes 196612
  207.7 5.3 %collective-permute-start.20 = (f32[8,4,128]{2,1,0:T(4,128)S(1)}, f32[8,4,128]{2,1,0:T(4,128)S(1)}, u32[]{:S(2)}, u32[]{:S(2)}) collective-permute-start(f32[8,4,128]{2,1,0:T(4,128)S(1)} %get-tuple-element.78), channel_id=1, source_target_pairs={{8,0},{16,8},{24,16},{9,1},{17,9},{25,17},{10,2},{18,10},{26,18},{... | collective-permute-start | bytes 49160 | tf_op jit(solution)/shard_map/ppermute | solution.py:437
  209.0 4.8 %collective-permute-start.21 = (f32[8,4,128]{2,1,0:T(4,128)S(1)}, f32[8,4,128]{2,1,0:T(4,128)S(1)}, u32[]{:S(2)}, u32[]{:S(2)}) collective-permute-start(f32[8,4,128]{2,1,0:T(4,128)S(1)} %get-tuple-element.79), channel_id=1, source_target_pairs={{0,8},{8,16},{16,24},{1,9},{9,17},{17,25},{2,10},{10,18},{18,26},{... | collective-permute-start | bytes 49160 | tf_op jit(solution)/shard_map/ppermute | solution.py:436
  214.0 4.5 %collective-permute-start.22 = (f32[4,24,128]{2,1,0:T(8,128)S(1)}, f32[4,24,128]{2,1,0:T(8,128)S(1)}, u32[]{:S(2)}, u32[]{:S(2)}) collective-permute-start(f32[4,24,128]{2,1,0:T(8,128)S(1)} %get-tuple-element.64), channel_id=1, source_target_pairs={{0,32},{32,64},{64,96},{96,128},{128,160},{160,192},{192,224},{224... | collective-permute-start | bytes 147464 | tf_op jit(solution)/shard_map/ppermute | solution.py:436
  217.2 4.8 %collective-permute-start.23 = (f32[4,24,128]{2,1,0:T(8,128)S(1)}, f32[4,24,128]{2,1,0:T(8,128)S(1)}, u32[]{:S(2)}, u32[]{:S(2)}) collective-permute-start(f32[4,24,128]{2,1,0:T(8,128)S(1)} %get-tuple-element.65), channel_id=1, source_target_pairs={{32,0},{64,32},{96,64},{128,96},{160,128},{192,160},{224,192},{256... | collective-permute-start | bytes 147464 | tf_op jit(solution)/shard_map/ppermute | solution.py:437
  222.2 72.3 %copy-start.2 = (f32[26,48,256]{2,1,0:T(8,128)S(1)}, f32[26,48,256]{2,1,0:T(8,128)}, u32[]{:S(2)}) copy-start(f32[26,48,256]{2,1,0:T(8,128)} %copy-done.1) | copy-start | bytes 3833860
  222.2 72.3 %copy-start.7 = (f32[128,256]{1,0:T(8,128)S(1)}, f32[128,256]{1,0:T(8,128)}, u32[]{:S(2)}) copy-start(f32[128,256]{1,0:T(8,128)} %constant.89.clone.refs_9_) | copy-start | bytes 393220
  222.2 72.3 %copy-start.36 = (s32[3]{0:T(128)S(1)}, s32[3]{0:T(128)}, u32[]{:S(2)}) copy-start(s32[3]{0:T(128)} %pad_add_fusion.index) | copy-start | bytes 40
  223.9 5.7 %collective-permute-start.24 = (f32[4,8,4]{2,1,0:T(8,128)S(1)}, f32[4,8,4]{2,1,0:T(8,128)S(1)}, u32[]{:S(2)}, u32[]{:S(2)}) collective-permute-start(f32[4,8,4]{2,1,0:T(8,128)S(1)} %get-tuple-element.122), channel_id=1, source_target_pairs={{1,0},{2,1},{3,2},{4,3},{5,4},{6,5},{7,6},{0,7},{9,8},{10,9},{11,1... | collective-permute-start | bytes 1544 | tf_op jit(solution)/shard_map/ppermute | solution.py:437
  228.7 1.2 collective-permute-start.25
  230.0 5.9 %collective-permute-start.26 = (f32[4,4,128]{2,1,0:T(4,128)S(1)}, f32[4,4,128]{2,1,0:T(4,128)S(1)}, u32[]{:S(2)}, u32[]{:S(2)}) collective-permute-start(f32[4,4,128]{2,1,0:T(4,128)S(1)} %get-tuple-element.120), channel_id=1, source_target_pairs={{8,0},{16,8},{24,16},{9,1},{17,9},{25,17},{10,2},{18,10},{26,18},{... | collective-permute-start | bytes 24584 | tf_op jit(solution)/shard_map/ppermute | solution.py:437
  231.3 5.3 %collective-permute-start.27 = (f32[4,4,128]{2,1,0:T(4,128)S(1)}, f32[4,4,128]{2,1,0:T(4,128)S(1)}, u32[]{:S(2)}, u32[]{:S(2)}) collective-permute-start(f32[4,4,128]{2,1,0:T(4,128)S(1)} %get-tuple-element.121), channel_id=1, source_target_pairs={{0,8},{8,16},{16,24},{1,9},{9,17},{17,25},{2,10},{10,18},{18,26},{... | collective-permute-start | bytes 24584 | tf_op jit(solution)/shard_map/ppermute | solution.py:436
  236.7 5.3 %collective-permute-start.29 = (f32[4,16,128]{2,1,0:T(8,128)S(1)}, f32[4,16,128]{2,1,0:T(8,128)S(1)}, u32[]{:S(2)}, u32[]{:S(2)}) collective-permute-start(f32[4,16,128]{2,1,0:T(8,128)S(1)} %pad_maximum_fusion.43), channel_id=1, source_target_pairs={{32,0},{64,32},{96,64},{128,96},{160,128},{192,160},{224,192},{256... | collective-permute-start | bytes 98312 | tf_op jit(solution)/shard_map/ppermute | solution.py:437
  238.0 5.0 %collective-permute-start.28 = (f32[4,16,128]{2,1,0:T(8,128)S(1)}, f32[4,16,128]{2,1,0:T(8,128)S(1)}, u32[]{:S(2)}, u32[]{:S(2)}) collective-permute-start(f32[4,16,128]{2,1,0:T(8,128)S(1)} %pad_maximum_fusion.43), channel_id=1, source_target_pairs={{0,32},{32,64},{64,96},{96,128},{128,160},{160,192},{192,224},{224... | collective-permute-start | bytes 98312 | tf_op jit(solution)/shard_map/ppermute | solution.py:436
  (10 other events, 7.7 us)

commit v2 on v1

v2 whole, which is shorter than its diff:
```python
import functools

import jax
import jax.numpy as jnp
import numpy as np
from jax import lax
from jax.experimental import pallas as pl
from jax.experimental.pallas import tpu as pltpu
from jax.sharding import PartitionSpec as P

LEVELS = 4
CSWEEPS = 6
absorption = 0.01
relaxation = 0.8
F32 = jnp.float32


def coords(n, b):
    at = np.arange(n)
    return np.where(at < (n + b) // 2, at, at - n)


def restriction(coarse, fine):
    gap = fine[None, :] - 2 * coarse[:, None]
    outer, inner = (gap == -1) | (gap == 2), (gap == 0) | (gap == 1)
    return np.where(outer, 0.125, np.where(inner, 0.375, 0.0)).astype(np.float32)


def halving(coarse, fine):
    return np.where(fine[None, :] // 2 == coarse[:, None], 0.5, 0.0).astype(np.float32)


def prolongation(fine, coarse):
    near = fine[:, None] // 2 == coarse[None, :]
    far = fine[:, None] // 2 + 2 * (fine[:, None] % 2) - 1 == coarse[None, :]
    return np.where(near, 0.75, np.where(far, 0.25, 0.0)).astype(np.float32)


def dot(a, b):
    return lax.dot_general(
        a, b, (((1,), (0,)), ((), ())),
        precision=lax.Precision.HIGHEST, preferred_element_type=F32,
    )


def planes(lo, hi, step, carry=0, unroll=1):
    whole = (hi - lo) // unroll
    if whole > 1:
        carry = lax.fori_loop(0, whole, lambda t, c: step(lo + t * unroll, unroll, c), carry)
    elif whole == 1:
        carry = step(lo, unroll, carry)
    rest = (hi - lo) % unroll
    return step(hi - rest, rest, carry) if rest else carry


class Open:
    def above(self, v, dim):
        return pltpu.roll(v, v.shape[dim] - 1, dim)

    def below(self, v, dim):
        return pltpu.roll(v, 1, dim)

    def closed(self, k):
        return None


class Closed(Open):
    def __init__(self, shape, counts):
        self.last, self.first = [], []
        for dim in range(2):
            at = lax.broadcasted_iota(jnp.int32, shape, dim)
            self.last.append(jnp.where(at == counts[dim] - 1, 0.0, 1.0))
            self.first.append(jnp.where(at == 0, 0.0, 1.0))

    def above(self, v, dim):
        return super().above(v, dim) * self.last[dim]

    def below(self, v, dim):
        return super().below(v, dim) * self.first[dim]

    def closed(self, k):
        return k * ((1.0 - self.first[0]) + (1.0 - self.first[1]))


def weigh(k, wx, wy, wz, lo, hi, factor, shifts, d=None, mask=None, b=None, unroll=1):
    half = 0.5 * factor
    first = half * (k[lo - 1] + k[lo])
    wx[lo - 1] = first

    def step(i, n, below):
        here = [k[i + j] for j in range(n + 1)]
        outs = []
        for j in range(n):
            x = half * (here[j] + here[j + 1])
            y = half * (here[j] + shifts.above(here[j], 0))
            z = half * (here[j] + shifts.above(here[j], 1))
            ends, value = shifts.closed(half * here[j]), None
            if d is not None:
                value = (x + below) + (y + shifts.below(y, 0)) + (z + shifts.below(z, 1))
                if ends is not None:
                    value = value + ends
                value = relaxation / (value + absorption)
                if mask is not None:
                    value = mask(here[j], value)
            outs.append((x, y, z, ends, value))
            below = x
        for j, (x, y, z, ends, value) in enumerate(outs):
            wx[i + j], wy[i + j], wz[i + j] = x, y, z
            if ends is not None:
                b[i + j] = ends
            if value is not None:
                d[i + j] = value
        return below

    planes(lo, hi, step, first, unroll)


def image(v, wx, wy, wz, lo, hi, use, put, shifts, b=None, unroll=1):
    def step(i, n, below):
        here = [v[i + j] for j in range(n + 1)]
        outs = []
        for j in range(n):
            x = wx[i + j] * (here[j] - here[j + 1])
            y = wy[i + j] * (here[j] - shifts.above(here[j], 0))
            z = wz[i + j] * (here[j] - shifts.above(here[j], 1))
            total = (x - below) + (y - shifts.below(y, 0)) + (z - shifts.below(z, 1))
            if b is not None:
                total = total + b[i + j] * here[j]
            outs.append(use(i + j, here[j], total + absorption * here[j]))
            below = x
        for j, value in enumerate(outs):
            put(i + j, value)
        return below

    planes(lo, hi, step, wx[lo - 1] * (v[lo - 1] - v[lo]), unroll)


def into(ref, by=0):
    def put(i, value):
        ref[i + by] = value

    return put


def smooth(v, f, d, w, lo, hi, shifts, b=None, unroll=1, by=0):
    def use(i, here, im):
        return here + d[i] * (f[i + by] - im)

    image(v, *w, lo, hi, use, into(v), shifts, b, unroll)


def residual_of(v, f, r, w, lo, hi, shifts, mask=None, b=None, unroll=1):
    def use(i, here, im):
        value = f[i] - im
        return value if mask is None else jnp.where(mask[i] > 0.0, value, 0.0)

    image(v, *w, lo, hi, use, into(r), shifts, b, unroll)


def first_sweep(g, d, v, lo, hi, unroll, by=0):
    def step(i, n, carry):
        values = [g[i + j + by] * d[i + j] for j in range(n)]
        for j, value in enumerate(values):
            v[i + j] = value
        return carry

    planes(lo, hi, step, unroll=unroll)


def restrict(r, offset, lo, hi, ry, rz, held):
    size = ry.shape[0]
    for i in range(lo, hi):
        at = 2 * i + offset
        plane = 0.125 * (r[at - 1] + r[at + 2]) + 0.375 * (r[at] + r[at + 1])
        held[(i - lo) * size : (i - lo + 1) * size, :] = dot(ry[...], plane)
    return dot(held[: (hi - lo) * size, :], rz[...])


def halve(k, offset, lo, hi, cy, cz, held):
    size = cy.shape[0]
    for i in range(lo, hi):
        plane = 0.5 * (k[2 * i + offset] + k[2 * i + 1 + offset])
        held[(i - lo) * size : (i - lo + 1) * size, :] = dot(cy[...], plane)
    return dot(held[: (hi - lo) * size, :], cz[...])


def prolong(e, first, count, py, pz, finer, use):
    rows = e.shape[1]
    spread = dot(e[pl.ds(first, count)].reshape(count * rows, e.shape[2]), pz)
    for i in range(count):
        finer[i] = dot(py, spread[i * rows : (i + 1) * rows])

    def step(i, n, carry):
        below, here, above = finer[i - 1], finer[i], finer[i + 1]
        use(2 * (i - 1), 0.75 * here + 0.25 * below)
        use(2 * (i - 1) + 1, 0.75 * here + 0.25 * above)
        return carry

    planes(1, count - 1, step)


def three(w):
    return tuple(w.at[i] for i in range(3))


def inside(k, value):
    return jnp.where(k > 0.0, value, 0.0)


U0, U1, U2, U3 = 2, 4, 2, 4


def down0(f, k, ry, rz, cy, cz, wx, wy, wz, d, g1, k1, d1, v, r, held, kc, wc):
    shifts = Open()
    weigh(k, wx, wy, wz, 1, 25, 1.0, shifts, d, inside, unroll=U0)
    first_sweep(f, d, v, 1, 25, U0)
    residual_of(v, f, r, (wx, wy, wz), 4, 22, shifts, k, unroll=U0)
    g1[...] = restrict(r, 5, 0, 8, ry, rz, held).reshape(g1.shape)
    kc[...] = halve(k, 5, -1, 9, cy, cz, held).reshape(kc.shape)
    coarse(kc, wc, 8, 0.25)
    for i in range(8):
        k1[i] = kc[i + 1, :16]
        d1[i] = wc[3, i + 1, :16]


def coarse(kc, wc, count, factor):
    weigh(kc, *three(wc), 1, count + 1, factor, Open(), wc.at[3], unroll=U1)


def tile_of(values):
    total = None
    for i, value in enumerate(values):
        if value is None:
            continue
        lane = lax.broadcasted_iota(jnp.int32, value.shape, 1)
        part = jnp.where(lane < 32, value, 0.0)
        part = pltpu.roll(part, 32 * i, 1) if i else part
        total = part if total is None else total + part
    return total


def down1(first, *refs):
    shifts = Open()
    g, k, d, ry, rz = refs[:5]
    if first:
        cy, cz, out, v, r, held, w, kc, wc = refs[5:]
    else:
        out, v, r, held, w = refs[5:]
    w = three(w)
    weigh(k, *w, 1, 23, 0.25, shifts, unroll=U1)
    first_sweep(g, d, v, 0, 24, U1)
    if first:
        residual_of(v, g, r, w, 7, 17, shifts, d, unroll=U1)
        value = restrict(r, 8, 0, 4, ry, rz, held).reshape(4, 8, 128)
        kc[...] = halve(k, 8, -1, 5, cy, cz, held).reshape(kc.shape)
        coarse(kc, wc, 4, 0.25**2)
        tiles = [
            tile_of([value[i] for i in range(4)]),
            tile_of([kc[i + 1, :8] for i in range(4)]),
            tile_of([wc[3, i + 1, :8] for i in range(4)]),
        ]
    else:
        residual_of(v, g, r, w, 1, 23, shifts, d, unroll=U1)
        value = restrict(r, 8, -3, 7, ry, rz, held).reshape(10, 8, 128)
        tiles = [
            tile_of([None] + [value[i] for i in range(3)]),
            tile_of([value[i + 3] for i in range(4)]),
            tile_of([value[i + 7] for i in range(3)]),
        ]
    for i in range(out.shape[0]):
        for t in range(3):
            out[i, t] = tiles[t]


def unpack(s, t, nz, put):
    lane = lax.broadcasted_iota(jnp.int32, (8, 128), 1) // 32
    for j in range(s.shape[0] // nz):
        for x in range(4):
            for half in range(2):
                total = jnp.zeros((8, 128), F32)
                for q in range(4):
                    if half * 4 + q < nz:
                        part = s[j * nz + half * 4 + q, t]
                        if q != x:
                            part = pltpu.roll(part, (32 * (q - x)) % 128, 1)
                        total = jnp.where(lane == q, part, total)
                put(x, pl.ds(8 * j, 8), pl.ds(128 * half, 128), total)


def arrange(nz, s, out):
    for t in range(3):

        def put(x, rows, lanes, value):
            out[t, x, rows, lanes] = value

        unpack(s, t, nz, put)


def closed2(shape, nz):
    return Closed(shape, (shape[0], 32 * nz))


def down2(nz, first, *refs):
    if first:
        before, own, after, ry, rz, cy, cz, out, g, k, d, v, r, held, w, b = refs
        for part, at in ((before, 0), (own, 4), (after, 8)):
            for ref, field in ((g, 0), (k, 1), (d, 2)):
                for i in range(4):
                    ref[at + i] = part[field, i]
    else:
        s, k, d, ry, rz, out, g, v, r, held, w, b = refs
        for t in range(3):

            def put(x, rows, lanes, value):
                g[4 * t + x, rows, lanes] = value

            unpack(s, t, nz, put)
    shifts, w = closed2(g.shape[1:], nz), three(w)
    weigh(k, *w, 3, 9, 0.25**2, shifts, b=b, unroll=U2)
    first_sweep(g, d, v, 2, 10, U2)
    residual_of(v, g, r, w, 3, 9, shifts, d, b, unroll=U2)
    value = restrict(r, 4, 0, 2, ry, rz, held)
    rows = ry.shape[0]
    parts = [value]
    if first:
        parts.append(halve(k, 4, 0, 2, cy, cz, held))
    for i in range(out.shape[0]):
        for j, part in enumerate(parts):
            for x in range(2):
                out[i, j, x] = part[x * rows : (x + 1) * rows]


def bottom(nz, s, k3, scratch, mats):
    g3, v3, r3, w3, d3, b3, k4, g4, v4, w4, d4, b4, held, fine4 = scratch
    ry3, rz3, cy3, cz3, py3, pz3 = mats
    nx = s.shape[0]
    n3, n4 = 2 * nx, nx
    rows, lanes = g3.shape[1], g3.shape[2]
    zero = jnp.zeros((rows, lanes), F32)
    for i in (0, 1, 2, n3 + 3, n3 + 4, n3 + 5):
        v3[i], r3[i] = zero, zero
        if s.shape[1] == 2:
            k3[i] = zero
    for ref in (k4, v4):
        for i in (0, n4 + 1):
            ref[i] = jnp.zeros(ref.shape[1:], F32)
    for i in range(nx):
        for x in range(2):
            g3[2 * i + x + 3] = s[i, 0, x]
            if s.shape[1] == 2:
                k3[2 * i + x + 3] = s[i, 1, x]
    k4[1 : n4 + 1] = halve(k3, 3, 0, n4, cy3, cz3, held).reshape(g4.shape)
    shifts3 = Closed((rows, lanes), (rows, 16 * nz))
    shifts4 = Closed((k4.shape[1], lanes), (k4.shape[1], 8 * nz))
    w3, w4 = three(w3), three(w4)
    weigh(k3, *w3, 3, n3 + 3, 0.25**3, shifts3, d3, inside, b3, U3)
    weigh(k4, *w4, 1, n4 + 1, 0.25**4, shifts4, d4, inside, b4, U3)
    first_sweep(g3, d3, v3, 3, n3 + 3, U3)
    residual_of(v3, g3, r3, w3, 3, n3 + 3, shifts3, b=b3, unroll=U3)
    g4[...] = restrict(r3, 3, 0, n4, ry3, rz3, held).reshape(g4.shape)
    first_sweep(g4, d4, v4, 1, n4 + 1, U3, by=-1)

    def turn(j, carry):
        smooth(v4, g4, d4, w4, 1, n4 + 1, shifts4, b4, n4, by=-1)
        return carry

    lax.fori_loop(0, CSWEEPS - 1, turn, 0)

    def use(i, value):
        v3[i + 3] = v3[i + 3] + value

    prolong(v4, 0, n4 + 2, py3[...], pz3[...], fine4, use)
    smooth(v3, g3, d3, w3, 3, n3 + 3, shifts3, b3, U3)
    return v3


def spread_matrix(shape, dim_fine, coarse_start, block_fine):
    fine = lax.broadcasted_iota(jnp.int32, shape, dim_fine)
    size = shape[dim_fine]
    fine = jnp.where(fine < (size + block_fine) // 2, fine, fine - size)
    whole = lax.broadcasted_iota(jnp.int32, shape, 1 - dim_fine)
    near = (fine >> 1) + coarse_start
    far = near + 2 * (fine & 1) - 1
    return jnp.where(whole == near, 0.75, jnp.where(whole == far, 0.25, 0.0))


def upward(nz, index, e3, g2, k2, d2, g1, k1, d1, scratch, mats):
    v2, w2, b2, v1, w1, fine2, fine1 = scratch
    py2, pz2 = mats
    open_, closed, w2, w1 = Open(), closed2(g2.shape[1:], nz), three(w2), three(w1)
    weigh(k2, *w2, 1, 11, 0.25**2, closed, b=b2, unroll=U2)
    first_sweep(g2, d2, v2, 0, 12, U2)
    weigh(k1, *w1, 5, 19, 0.25, open_, unroll=U1)
    first_sweep(g1, d1, v1, 4, 20, U1)

    def use2(i, value):
        v2[i] = jnp.where(d2[i] > 0.0, v2[i] + value, 0.0)

    prolong(e3, index[0] * 2, 8, py2[...], pz2[...], fine2, use2)
    smooth(v2, g2, d2, w2, 1, 11, closed, b2, U2)

    def use1(i, value):
        v1[i + 4] = jnp.where(d1[i + 4] > 0.0, v1[i + 4] + value, 0.0)

    py1 = spread_matrix((g1.shape[1], g2.shape[1]), 0, index[1] * 8, 16)
    pz1 = spread_matrix((g2.shape[2], g1.shape[2]), 1, index[2] * 32, 64)
    prolong(v2, 1, 10, py1, pz1, fine1, use1)
    smooth(v1, g1, d1, w1, 5, 19, open_, unroll=U1)
    return v1


BOTTOM = 14
UP = 7


def middle(nz, index, s, g2, k2, d2, g1, k1, d1, f, wx, wy, wz, d, k, *refs):
    m3, m2, (py0, pz0, ry, rz) = refs[:6], refs[6:8], refs[8:12]
    v, gn, k3 = refs[12:15]
    low, mid, (fine0, r, held0) = refs[15 : 15 + BOTTOM], refs[15 + BOTTOM : 15 + BOTTOM + UP], refs[15 + BOTTOM + UP :]
    e3 = bottom(nz, s, k3, low, m3)
    e1 = upward(nz, index, e3, g2, k2, d2, g1, k1, d1, mid, m2)
    w, shifts = (wx, wy, wz), Open()

    def use(i, value):
        v[i + 1] = inside(k[i + 1], f[i + 1] * d[i + 1] + value)

    prolong(e1, 5, 14, py0[...], pz0[...], fine0, use)
    smooth(v, f, d, w, 2, 24, shifts, unroll=U0)
    smooth(v, f, d, w, 3, 23, shifts, unroll=U0)
    residual_of(v, f, r, w, 4, 22, shifts, k, unroll=U0)
    gn[...] = restrict(r, 5, 0, 8, ry, rz, held0).reshape(gn.shape)


def final(nz, index, s, g2, k2, d2, g1, k1, d1, f, wx, wy, wz, d, k, *refs):
    m3, m2, (py0, pz0) = refs[:6], refs[6:8], refs[8:10]
    k3, v0, solution_, residual_ = refs[10:14]
    low, mid, (fine0, v) = refs[14 : 14 + BOTTOM], refs[14 + BOTTOM : 14 + BOTTOM + UP], refs[14 + BOTTOM + UP :]
    e3 = bottom(nz, s, k3, low, m3)
    e1 = upward(nz, index, e3, g2, k2, d2, g1, k1, d1, mid, m2)
    w, shifts = (wx, wy, wz), Open()

    def use(i, value):
        v[i + 3] = inside(k[i + 3], v0[i + 3] + value)

    prolong(e1, 6, 12, py0[...], pz0[...], fine0, use)
    smooth(v, f, d, w, 4, 22, shifts, unroll=U0)

    def last(i, here, im):
        return here[:32, :128], (f[i] - im)[:32, :128]

    def out(i, values):
        solution_[i - 5], residual_[i - 5] = values

    image(v, *w, 5, 21, last, out, shifts, unroll=U0)


def call(kernel, outs, scratch, *args, name, scalars=0):
    vmem = pl.BlockSpec(memory_space=pltpu.VMEM)
    smem = pl.BlockSpec(memory_space=pltpu.SMEM)
    return pl.pallas_call(
        kernel,
        out_shape=[jax.ShapeDtypeStruct(o, F32) for o in outs],
        in_specs=[smem] * scalars + [vmem] * (len(args) - scalars),
        out_specs=[vmem] * len(outs),
        scratch_shapes=[pltpu.VMEM(s, F32) for s in scratch],
        compiler_params=pltpu.CompilerParams(vmem_limit_bytes=48 << 20),
        name=name,
    )(*args)


def neighbours(last, initial, axis):
    count = lax.axis_size(axis)
    if axis == "gz":
        up = [(i, (i + 1) % count) for i in range(count)]
    else:
        up = [(i, i + 1) for i in range(count - 1)]
    down = [(j, i) for i, j in up]
    before = lax.ppermute(last, axis, up)
    after = lax.ppermute(initial, axis, down)
    if axis == "gz":
        at = lax.axis_index(axis)
        before = jnp.where(at == 0, 0.0, before)
        after = jnp.where(at == count - 1, 0.0, after)
    return before, after


def exchange(fields, block, sizes, widths):
    count = len(fields)
    for axis, dim in (("gz", 2), ("gy", 1), ("gx", 0)):
        along = 2 if dim == 2 else 0
        size, width = block[dim], widths[dim]
        last = [lax.slice_in_dim(f, size - width, size, axis=dim) for f in fields]
        initial = [lax.slice_in_dim(f, 0, width, axis=dim) for f in fields]
        before, after = neighbours(
            jnp.concatenate(last, along), jnp.concatenate(initial, along), axis
        )
        before = jnp.split(before, count, along)
        after = jnp.split(after, count, along)
        if dim == 0:
            fields = [jnp.concatenate([b, f, a], 0) for b, f, a in zip(before, fields, after)]
            continue
        own = [lax.slice_in_dim(f, 0, size, axis=dim) for f in fields]
        gap = list(own[0].shape)
        gap[dim] = sizes[dim - 1] - size - 2 * width
        parts = [[jnp.zeros(gap, F32)] if gap[dim] else []] * count
        fields = [
            jnp.concatenate([f, a] + z + [b], dim)
            for b, f, a, z in zip(before, own, after, parts)
        ]
    return fields


def everyone(pieces, axes):
    return lax.all_to_all(pieces, axes, 0, 0)


def body(right_side, conductivity):
    nx, ny, nz = (lax.axis_size(axis) for axis in ("gx", "gy", "gz"))
    index = jnp.stack([lax.axis_index(axis) for axis in ("gx", "gy", "gz")]).astype(jnp.int32)

    def ends(size, count, away=-1000):
        return np.where(np.arange(size) < count, np.arange(size), away)

    y0, z0 = coords(48, 32), coords(256, 128)
    y1, z1 = coords(24, 16), coords(128, 64)
    y2, z2 = coords(16, 8), coords(128, 32)
    rows2, rows3, rows4 = np.arange(8 * ny), np.arange(4 * ny), np.arange(2 * ny)
    lanes2, lanes3, lanes4 = ends(256, 32 * nz), ends(128, 16 * nz, -3000), ends(128, 8 * nz, -9000)
    ry0, rz0 = restriction(np.arange(16), y0), restriction(ends(128, 64), z0).T
    cy0, cz0 = halving(y1, y0), halving(z1, z0).T
    ry1, rz1 = restriction(np.arange(8), y1), restriction(ends(128, 32), z1).T
    cy1, cz1 = halving(y2, y1), halving(z2, z1).T
    ry2, rz2 = restriction(rows3, rows2), restriction(lanes3, lanes2).T
    cy2, cz2 = halving(rows3, rows2), halving(lanes3, lanes2).T
    ry3, rz3 = restriction(rows4, rows3), restriction(lanes4, lanes3).T
    cy3, cz3 = halving(rows4, rows3), halving(lanes4, lanes3).T
    py0, pz0 = prolongation(y0, y1), prolongation(z0, z1).T
    py2, pz2 = prolongation(rows2, rows3), prolongation(lanes2, lanes3).T
    py3, pz3 = prolongation(rows3, rows4), prolongation(lanes3, lanes4).T
    m3, m2 = (ry3, rz3, cy3, cz3, py3, pz3), (py2, pz2)

    wide, l1, l2 = (26, 48, 256), (24, 24, 128), (12, 8 * ny, 256)
    n3, n4 = (2 * nx + 6, 4 * ny, 128), (nx + 2, 2 * ny, 128)
    low = [
        n3, n3, n3, (3,) + n3, n3, n3,
        n4, (nx, 2 * ny, 128), n4, (3,) + n4, n4, n4,
        (nx * 2 * ny, 128), (nx + 2, 4 * ny, 128),
    ]
    mid = [l2, (3,) + l2, l2, l1, (3,) + l1, (8, 8 * ny, 256), (10, 24, 128)]

    f, k = exchange([right_side, conductivity], (16, 32, 128), (48, 256), (5, 5, 5))
    b1 = (8, 16, 128)
    wx, wy, wz, d, g1, k1, d1 = call(
        down0, [wide] * 4 + [b1] * 3,
        [wide, wide, (240, 256), (10, 24, 128), (4, 10, 24, 128)],
        f, k, ry0, rz0, cy0, cz0, name="down0",
    )
    ring1 = ((8, 16, 64), (24, 128), (8, 4, 4))
    g1, k1, d1 = exchange([g1, k1, d1], *ring1)
    inner1 = [l1, l1, (96, 128), (3,) + l1]
    (pieces,) = call(
        functools.partial(down1, True), [(ny * nz, 3, 8, 128)],
        inner1 + [(6, 16, 128), (4, 6, 16, 128)],
        g1, k1, d1, ry1, rz1, cy1, cz1, name="down1",
    )
    pieces = everyone(pieces, ("gy", "gz"))
    (own,) = call(
        functools.partial(arrange, nz), [(3, 4, 8 * ny, 256)], [], pieces, name="arrange"
    )
    before, after = neighbours(own, own, "gx")
    inner2 = [l2, l2, (8 * ny, 256), (3,) + l2, l2]
    pieces, g2, k2, d2 = call(
        functools.partial(down2, nz, True), [(nx, 2, 2, 4 * ny, 128), l2, l2, l2], inner2,
        before, own, after, ry2, rz2, cy2, cz2, name="down2",
    )
    s = everyone(pieces, "gx")
    fields = (f, wx, wy, wz, d, k)
    v, g1b, k3 = call(
        functools.partial(middle, nz), [wide, b1, n3],
        low + mid + [(14, 48, 256), wide, (128, 256)],
        index, s, g2, k2, d2, g1, k1, d1, *fields, *m3, *m2, py0, pz0, ry0, rz0,
        name="middle", scalars=1,
    )
    (g1,) = exchange([g1b], *ring1)
    (pieces,) = call(
        functools.partial(down1, False), [(ny * nz, 3, 8, 128)], inner1,
        g1, k1, d1, ry1, rz1, name="again1",
    )
    pieces = everyone(pieces, ("gy", "gz"))
    pieces, g2 = call(
        functools.partial(down2, nz, False), [(nx, 1, 2, 4 * ny, 128), l2], inner2,
        pieces, k2, d2, ry2, rz2, name="again2",
    )
    s = everyone(pieces, "gx")
    return tuple(call(
        functools.partial(final, nz), [(16, 32, 128)] * 2,
        low + mid + [(12, 48, 256), wide],
        index, s, g2, k2, d2, g1, k1, d1, *fields, *m3, *m2, py0, pz0, k3, v,
        name="final", scalars=1,
    ))


def solution(mesh):
    placed = P("gx", "gy", "gz")
    return jax.shard_map(
        body, mesh=mesh, in_specs=(placed, placed), out_specs=(placed, placed), check_vma=False
    )
```

time: 321 us -> 285 us (0.89)
  starting transfers between devices: 97.3 us -> 76.6 us
  Pallas kernels: 71.2 us -> 56.7 us
  blocking collectives: 76.6 us -> 63 us
  waiting for transfers between devices: 52.5 us -> 61.6 us
  local copies, waits for them, and re-layouts: 12.9 us -> 17.3 us
    all_gather x4 -> x0, blocking collectives: 55.9 us -> none  [the longest x2 32.9 us: gathered(): pieces = lax.all_gather(piece, 'gz')]
    all_to_all x1 -> x3, blocking collectives: 20.7 us -> 63 us  [everyone(): return lax.all_to_all(pieces, axes, 0, 0)]
    ppermute x15 -> x10, starting transfers between devices: 49 us -> 34 us  [neighbours(): before = lax.ppermute(last, axis, up)]
    pallas_call x9 -> x8, Pallas kernels: 71.2 us -> 56.7 us  [call(): pl.pallas_call(kernel, out_shape=[jax.ShapeDtypeStruct(o, F32) for o in o...]
    all_to_all x1, waiting for transfers between devices: 11.6 us -> 22.2 us  [everyone(): return lax.all_to_all(pieces, axes, 0, 0)]
    ppermute x15 -> x10, starting transfers between devices: 29.3 us -> 23.5 us  [neighbours(): after = lax.ppermute(initial, axis, down)]
    unnamed x90 -> x104, local copies, waits for them, and re-layouts: 9.56 us -> 14.5 us
    ppermute x15 -> x10, waiting for transfers between devices: 14 us -> 11.3 us  [neighbours(): before = lax.ppermute(last, axis, up)]
  transfers between devices with their start and end apart: 31 -> 21, of which waited for: 24 -> 18; matrix products, arithmetic and copies ran while one was open for 1% -> 1% of each run, Pallas kernels for 0% -> 0%
where the time goes in v2:
time: 285 us; the launch traced here: 281 us
  starting transfers between devices  76.6 us (27%)
  blocking collectives  63 us (22%)
  waiting for transfers between devices  61.6 us (22%)
  Pallas kernels  56.7 us (20%)
  local copies, waits for them, and re-layouts  17.3 us (6%)
  other arithmetic  4.64 us (2%)
    all_to_all x3, blocking collectives, everyone(): return lax.all_to_all(pieces, axes, 0, 0)  63 us
    pallas_call x8, Pallas kernels, call(): pl.pallas_call(kernel, out_shape=[jax.ShapeDtypeStruct(o, F32) for o in o...  56.7 us
    ppermute x10, starting transfers between devices, neighbours(): before = lax.ppermute(last, axis, up)  34 us
    ppermute x10, waiting for transfers between devices, neighbours(): after = lax.ppermute(initial, axis, down)  28 us
    ppermute x10, starting transfers between devices, neighbours(): after = lax.ppermute(initial, axis, down)  23.5 us
    all_to_all x1, waiting for transfers between devices, everyone(): return lax.all_to_all(pieces, axes, 0, 0)  22.2 us
    all_to_all x1, starting transfers between devices, everyone(): return lax.all_to_all(pieces, axes, 0, 0)  19.1 us
    unnamed x104, local copies, waits for them, and re-layouts  14.5 us
  transfers between devices with their start and end apart: 21, of which 18 were waited for; matrix products, arithmetic and copies ran while one was open for 1% of the time, Pallas kernels for 0%

profile of v2, /device:TPU:1, one launch (start us, length us, event | category | flops | bytes accessed | tf_op | source)
XLA Modules:
  0.0 281.4 jit_solution(8818127413627261678)
XLA Ops:
  0.6 1.2 fusion.52
  2.5 6.9 %collective-permute-start = (f32[16,32,10]{2,1,0:T(8,128)S(1)}, f32[16,32,10]{2,1,0:T(8,128)S(1)}, u32[]{:S(2)}, u32[]{:S(2)}) collective-permute-start(f32[16,32,10]{2,1,0:T(8,128)S(1)} %copy.28), channel_id=1, source_target_pairs={{1,0},{2,1},{3,2},{4,3},{5,4},{6,5},{7,6},{0,7},{9,8},{10,9},{11,1... | collective-permute-start | bytes 61448 | tf_op jit(solution)/shard_map/ppermute | solution.py:479
  10.0 0.6 collective-permute-done
  10.8 2.5 collective-permute-done.1
  13.9 1.3 collective-permute-start.3
  15.2 1.3 collective-permute-start.2
  16.5 1.9 collective-permute-done.3
  18.5 3.8 %collective-permute-done.2 = f32[32,5,256]{2,1,0:T(8,128)S(1)} collective-permute-done((f32[32,5,256]{2,1,0:T(8,128)S(1)}, f32[32,5,256]{2,1,0:T(8,128)S(1)}, u32[]{:S(2)}, u32[]{:S(2)}) %collective-permute-start.2) | collective-permute-done | bytes 163872 | tf_op jit(solution)/shard_map/ppermute | solution.py:479
  22.9 1.3 collective-permute-start.5
  24.2 4.0 %collective-permute-start.4 = (f32[10,48,256]{2,1,0:T(8,128)S(1)}, f32[10,48,256]{2,1,0:T(8,128)S(1)}, u32[]{:S(2)}, u32[]{:S(2)}) collective-permute-start(f32[10,48,256]{2,1,0:T(8,128)S(1)} %pad_maximum_fusion.14), channel_id=1, source_target_pairs={{0,32},{32,64},{64,96},{96,128},{128,160},{160,192},{192,224},{224... | collective-permute-start | bytes 1474568 | tf_op jit(solution)/shard_map/ppermute | solution.py:478
  28.2 4.2 %collective-permute-done.5 = f32[10,48,256]{2,1,0:T(8,128)S(1)} collective-permute-done((f32[10,48,256]{2,1,0:T(8,128)S(1)}, f32[10,48,256]{2,1,0:T(8,128)S(1)}, u32[]{:S(2)}, u32[]{:S(2)}) %collective-permute-start.5) | collective-permute-done | bytes 491552 | tf_op jit(solution)/shard_map/ppermute | solution.py:479
  32.5 1.5 collective-permute-done.4
  34.1 1.9 fusion.9
  36.0 7.2 %down0.1 = (f32[26,48,256]{2,1,0:T(8,128)S(1)}, f32[26,48,256]{2,1,0:T(8,128)S(1)}, f32[26,48,256]{2,1,0:T(8,128)S(1)}, f32[26,48,256]{2,1,0:T(8,128)S(1)}, f32[...) custom-call(f32[26,48,256]{2,1,0:T(8,128)} %get-tuple-element.47.f, ...), custom_call_target="tpu_custom_call" | custom-call | tf_op jit(solution)/shard_map/down0/pallas_call | solution.py:460
  43.2 1.0 copy-done.4
  44.2 1.0 copy-done.5
  45.7 8.2 %collective-permute-start.7 = (f32[8,16,12]{2,1,0:T(8,128)S(1)}, f32[8,16,12]{2,1,0:T(8,128)S(1)}, u32[]{:S(2)}, u32[]{:S(2)}) collective-permute-start(f32[8,16,12]{2,1,0:T(8,128)S(1)} %pad_maximum_fusion.27), channel_id=1, source_target_pairs={{0,1},{1,2},{2,3},{3,4},{4,5},{5,6},{6,7},{7,0},{8,9},{9,10},{10,1... | collective-permute-start | bytes 18440 | tf_op jit(solution)/shard_map/ppermute | solution.py:478
  54.0 1.2 collective-permute-done.7
  55.3 2.4 collective-permute-done.6
  58.1 3.1 %collective-permute-start.9 = (f32[24,4,128]{2,1,0:T(4,128)S(1)}, f32[24,4,128]{2,1,0:T(4,128)S(1)}, u32[]{:S(2)}, u32[]{:S(2)}) collective-permute-start(f32[24,4,128]{2,1,0:T(4,128)S(1)} %pad_maximum_fusion.29), channel_id=1, source_target_pairs={{0,8},{8,16},{16,24},{1,9},{9,17},{17,25},{2,10},{10,18},{18,26},{... | collective-permute-start | bytes 147464 | tf_op jit(solution)/shard_map/ppermute | solution.py:478
  61.3 1.3 collective-permute-start.8
  62.6 3.5 %collective-permute-done.8 = f32[24,4,128]{2,1,0:T(4,128)S(1)} collective-permute-done((f32[24,4,128]{2,1,0:T(4,128)S(1)}, f32[24,4,128]{2,1,0:T(4,128)S(1)}, u32[]{:S(2)}, u32[]{:S(2)}) %collective-permute-start.8) | collective-permute-done | bytes 49184 | tf_op jit(solution)/shard_map/ppermute | solution.py:479
  66.4 1.3 collective-permute-start.11
  67.7 4.7 %collective-permute-start.10 = (f32[24,24,128]{2,1,0:T(8,128)S(1)}, f32[24,24,128]{2,1,0:T(8,128)S(1)}, u32[]{:S(2)}, u32[]{:S(2)}) collective-permute-start(f32[24,24,128]{2,1,0:T(8,128)S(1)} %maximum_maximum_fusion), channel_id=1, source_target_pairs={{0,32},{32,64},{64,96},{96,128},{128,160},{160,192},{192,224},{224... | collective-permute-start | bytes 884744 | tf_op jit(solution)/shard_map/ppermute | solution.py:478
  72.4 3.9 %collective-permute-done.11 = f32[24,24,128]{2,1,0:T(8,128)S(1)} collective-permute-done((f32[24,24,128]{2,1,0:T(8,128)S(1)}, f32[24,24,128]{2,1,0:T(8,128)S(1)}, u32[]{:S(2)}, u32[]{:S(2)}) %collective-permute-start.11) | collective-permute-done | bytes 294944 | tf_op jit(solution)/shard_map/ppermute | solution.py:479
  76.3 0.9 collective-permute-done.10
  78.1 1.9 down1.1
  80.0 18.1 %all_to_all.20.s = f32[32,3,8,128]{3,2,1,0:T(8,128)S(1)} all-to-all(f32[32,3,8,128]{3,2,1,0:T(8,128)S(1)} %down1.1), channel_id=1, replica_groups=mesh['gx'=16,'gy'=4,'gz'=8] {'gy','gz'}, dimensions={0} | all-to-all | bytes 786432 | tf_op jit(solution)/shard_map/all_to_all | solution.py:514
  98.5 1.4 collective-permute-start.13
  99.9 4.5 %collective-permute-start.12 = (f32[3,4,32,256]{3,2,1,0:T(8,128)S(1)}, f32[3,4,32,256]{3,2,1,0:T(8,128)S(1)}, u32[]{:S(2)}, u32[]{:S(2)}) collective-permute-start(f32[3,4,32,256]{3,2,1,0:T(8,128)S(1)} %arrange.1.refs_1_), channel_id=1, source_target_pairs={{0,32},{32,64},{64,96},{96,128},{128,160},{160,192},{192,224},{224... | collective-permute-start | bytes 1179656 | tf_op jit(solution)/shard_map/ppermute | solution.py:478
  104.5 7.6 %collective-permute-done.13.refs_2_ = f32[3,4,32,256]{3,2,1,0:T(8,128)S(1)} collective-permute-done((f32[3,4,32,256]{3,2,1,0:T(8,128)S(1)}, f32[3,4,32,256]{3,2,1,0:T(8,128)S(1)}, u32[]{:S(2)}, u32[]{:S(2)}) %collective-permute-start.13) | collective-permute-done | bytes 393248 | tf_op jit(solution)/shard_map/ppermute | solution.py:479
  112.1 0.9 collective-permute-done.12.refs_0_
  113.0 1.5 down2.1
  114.5 0.8 copy-done.15
  115.3 0.7 copy-done.16
  116.0 19.1 %all-to-all-start.1 = ((f32[16,2,2,16,128]{4,3,2,1,0:T(8,128)}), f32[16,2,2,16,128]{4,3,2,1,0:T(8,128)S(1)}, u32[]{:S(2)}, u32[]{:S(2)}) async-start(f32[16,2,2,16,128]{4,3,2,1,0:T(8,128)} %copy-done.15), calls=%async_computation.1 | async-start | bytes 1048576 | tf_op jit(solution)/shard_map/all_to_all | solution.py:514
  135.2 0.6 pad_add_fusion.index
  135.7 22.2 %all-to-all-done.1.s = f32[16,2,2,16,128]{4,3,2,1,0:T(8,128)S(1)} async-done(((f32[16,2,2,16,128]{4,3,2,1,0:T(8,128)}), f32[16,2,2,16,128]{4,3,2,1,0:T(8,128)S(1)}, u32[]{:S(2)}, u32[]{:S(2)}) %all-to-all-start.1) | async-done | bytes 524320 | tf_op jit(solution)/shard_map/all_to_all | solution.py:514
  158.0 0.9 copy-done.7
  158.9 0.9 copy-done.8
  159.8 0.9 copy-done.11
  160.7 1.0 copy-done.17
  161.7 0.8 copy-done.19
  162.5 0.8 copy-done.21
  163.4 0.7 copy-done.25
  164.1 0.7 copy-done.32
  164.8 0.7 copy-done.33
  165.5 0.7 copy-done.35
  166.2 0.7 copy-done.37
  166.9 0.6 copy-done.44
  167.5 22.5 %middle.1 = (f32[26,48,256]{2,1,0:T(8,128)S(1)}, f32[8,16,128]{2,1,0:T(8,128)S(1)}, f32[38,16,128]{2,1,0:T(8,128)S(1)}) custom-call(s32[3]{0:T(128)S(1)} %copy-done.44, f32[16,2,2,16,128]{4,3,2,1,0:T(8,128)S(1)} %all-to-all-done.1.s, f32[12,32,256]{2,1,0:T(8,128)S(1)} %copy-done.17, f32[12,32,256]{2,1,0:T(8,128)S(1)} %get-tuple-element.23.k2.refs_1_, ...), custom_call_target="tpu_custom_call" | custom-call | tf_op jit(solution)/shard_map/middle/pallas_call | solution.py:460
  190.1 7.3 %collective-permute-start.14 = (f32[8,16,4]{2,1,0:T(8,128)S(1)}, f32[8,16,4]{2,1,0:T(8,128)S(1)}, u32[]{:S(2)}, u32[]{:S(2)}) collective-permute-start(f32[8,16,4]{2,1,0:T(8,128)S(1)} %get-tuple-element.72), channel_id=1, source_target_pairs={{1,0},{2,1},{3,2},{4,3},{5,4},{6,5},{7,6},{0,7},{9,8},{10,9},{11,1... | collective-permute-start | bytes 6152 | tf_op jit(solution)/shard_map/ppermute | solution.py:479
  197.5 1.9 collective-permute-done.14
  199.6 1.3 collective-permute-start.16
  200.9 4.0 %collective-permute-start.17 = (f32[8,4,128]{2,1,0:T(4,128)S(1)}, f32[8,4,128]{2,1,0:T(4,128)S(1)}, u32[]{:S(2)}, u32[]{:S(2)}) collective-permute-start(f32[8,4,128]{2,1,0:T(4,128)S(1)} %get-tuple-element.71), channel_id=1, source_target_pairs={{0,8},{8,16},{16,24},{1,9},{9,17},{17,25},{2,10},{10,18},{18,26},{... | collective-permute-start | bytes 49160 | tf_op jit(solution)/shard_map/ppermute | solution.py:478
  204.9 0.8 collective-permute-done.17
  205.9 1.4 collective-permute-start.19
  207.3 4.0 %collective-permute-start.18 = (f32[8,24,128]{2,1,0:T(8,128)S(1)}, f32[8,24,128]{2,1,0:T(8,128)S(1)}, u32[]{:S(2)}, u32[]{:S(2)}) collective-permute-start(f32[8,24,128]{2,1,0:T(8,128)S(1)} %pad_maximum_fusion.23), channel_id=1, source_target_pairs={{0,32},{32,64},{64,96},{96,128},{128,160},{160,192},{192,224},{224... | collective-permute-start | bytes 294920 | tf_op jit(solution)/shard_map/ppermute | solution.py:478
  211.4 1.6 collective-permute-done.18
  213.1 1.9 again1.1
  215.1 19.6 %all_to_all.21.refs_0_ = f32[32,3,8,128]{3,2,1,0:T(8,128)S(1)} all-to-all(f32[32,3,8,128]{3,2,1,0:T(8,128)S(1)} %again1.1), channel_id=1, replica_groups=mesh['gx'=16,'gy'=4,'gz'=8] {'gy','gz'}, dimensions={0} | all-to-all | bytes 786432 | tf_op jit(solution)/shard_map/all_to_all | solution.py:514
  234.7 1.6 again2.1
  236.3 25.2 %all_to_all.22.s = f32[16,1,2,16,128]{4,3,2,1,0:T(8,128)S(1)} all-to-all(f32[16,1,2,16,128]{4,3,2,1,0:T(8,128)S(1)} %get-tuple-element.30), channel_id=1, replica_groups=mesh['gx'=16,'gy'=4,'gz'=8] {'gx'}, dimensions={0} | all-to-all | bytes 524288 | tf_op jit(solution)/shard_map/all_to_all | solution.py:514
  261.6 19.8 %final.1 = (f32[16,32,128]{2,1,0:T(8,128)}, f32[16,32,128]{2,1,0:T(8,128)}) custom-call(s32[3]{0:T(128)S(1)} %copy-done.45, f32[16,1,2,16,128]{4,3,2,1,0:T(8,128)S(1)} %all_to_all.22.s, f32[12,32,256]{2,1,0:T(8,128)S(1)} %get-tuple-element.31.g2, f32[12,32,256]{2,1,0:T(8,128)S(1)} %get-tuple-element.23.k2.refs_1_, ...), custom_call_target="tpu_custom_call" | custom-call | tf_op jit(solution)/shard_map/final/pallas_call | solution.py:460
  (150 shorter events, 5.7 us)
Async XLA Ops:
  0.6 1.4 copy-start.46
  2.5 8.0 %collective-permute-start = (f32[16,32,10]{2,1,0:T(8,128)S(1)}, f32[16,32,10]{2,1,0:T(8,128)S(1)}, u32[]{:S(2)}, u32[]{:S(2)}) collective-permute-start(f32[16,32,10]{2,1,0:T(8,128)S(1)} %copy.28), channel_id=1, source_target_pairs={{1,0},{2,1},{3,2},{4,3},{5,4},{6,5},{7,6},{0,7},{9,8},{10,9},{11,1... | collective-permute-start | bytes 61448 | tf_op jit(solution)/shard_map/ppermute | solution.py:479
  10.0 3.3 %collective-permute-start.1 = (f32[16,32,10]{2,1,0:T(8,128)S(1)}, f32[16,32,10]{2,1,0:T(8,128)S(1)}, u32[]{:S(2)}, u32[]{:S(2)}) collective-permute-start(f32[16,32,10]{2,1,0:T(8,128)S(1)} %copy.31), channel_id=1, source_target_pairs={{0,1},{1,2},{2,3},{3,4},{4,5},{5,6},{6,7},{7,0},{8,9},{9,10},{10,1... | collective-permute-start | bytes 61448 | tf_op jit(solution)/shard_map/ppermute | solution.py:478
  10.6 2.9 %copy-start.47 = (f32[16,32,128]{2,1,0:T(8,128)S(1)}, f32[16,32,128]{2,1,0:T(8,128)}, u32[]{:S(2)}) copy-start(f32[16,32,128]{2,1,0:T(8,128)} %param.24) | copy-start | bytes 786436
  13.9 4.6 %collective-permute-start.3 = (f32[32,5,256]{2,1,0:T(8,128)S(1)}, f32[32,5,256]{2,1,0:T(8,128)S(1)}, u32[]{:S(2)}, u32[]{:S(2)}) collective-permute-start(f32[32,5,256]{2,1,0:T(8,128)S(1)} %pad_maximum_fusion.18), channel_id=1, source_target_pairs={{0,8},{8,16},{16,24},{1,9},{9,17},{17,25},{2,10},{10,18},{18,26},{... | collective-permute-start | bytes 491528 | tf_op jit(solution)/shard_map/ppermute | solution.py:478
  15.2 7.1 %collective-permute-start.2 = (f32[32,5,256]{2,1,0:T(8,128)S(1)}, f32[32,5,256]{2,1,0:T(8,128)S(1)}, u32[]{:S(2)}, u32[]{:S(2)}) collective-permute-start(f32[32,5,256]{2,1,0:T(8,128)S(1)} %pad_maximum_fusion.17), channel_id=1, source_target_pairs={{8,0},{16,8},{24,16},{9,1},{17,9},{25,17},{10,2},{18,10},{26,18},{... | collective-permute-start | bytes 491528 | tf_op jit(solution)/shard_map/ppermute | solution.py:479
  22.9 9.6 %collective-permute-start.5 = (f32[10,48,256]{2,1,0:T(8,128)S(1)}, f32[10,48,256]{2,1,0:T(8,128)S(1)}, u32[]{:S(2)}, u32[]{:S(2)}) collective-permute-start(f32[10,48,256]{2,1,0:T(8,128)S(1)} %pad_maximum_fusion.15), channel_id=1, source_target_pairs={{32,0},{64,32},{96,64},{128,96},{160,128},{192,160},{224,192},{256... | collective-permute-start | bytes 1474568 | tf_op jit(solution)/shard_map/ppermute | solution.py:479
  24.2 9.8 %collective-permute-start.4 = (f32[10,48,256]{2,1,0:T(8,128)S(1)}, f32[10,48,256]{2,1,0:T(8,128)S(1)}, u32[]{:S(2)}, u32[]{:S(2)}) collective-permute-start(f32[10,48,256]{2,1,0:T(8,128)S(1)} %pad_maximum_fusion.14), channel_id=1, source_target_pairs={{0,32},{32,64},{64,96},{96,128},{128,160},{160,192},{192,224},{224... | collective-permute-start | bytes 1474568 | tf_op jit(solution)/shard_map/ppermute | solution.py:478
  34.0 2.0 copy-start.10
  34.0 2.0 copy-start.14
  34.0 2.0 copy-start.31
  34.0 1.9 copy-start.41
  43.2 1.0 copy-start.4
  44.2 1.0 copy-start.5
  45.3 12.8 %copy-start.1 = (f32[26,48,256]{2,1,0:T(8,128)}, f32[26,48,256]{2,1,0:T(8,128)S(1)}, u32[]{:S(2)}) copy-start(f32[26,48,256]{2,1,0:T(8,128)S(1)} %get-tuple-element.25.wx) | copy-start | bytes 3833860
  45.3 12.8 %copy-start.3 = (f32[26,48,256]{2,1,0:T(8,128)}, f32[26,48,256]{2,1,0:T(8,128)S(1)}, u32[]{:S(2)}) copy-start(f32[26,48,256]{2,1,0:T(8,128)S(1)} %get-tuple-element.26.wy) | copy-start | bytes 3833860
  45.7 9.6 %collective-permute-start.7 = (f32[8,16,12]{2,1,0:T(8,128)S(1)}, f32[8,16,12]{2,1,0:T(8,128)S(1)}, u32[]{:S(2)}, u32[]{:S(2)}) collective-permute-start(f32[8,16,12]{2,1,0:T(8,128)S(1)} %pad_maximum_fusion.27), channel_id=1, source_target_pairs={{0,1},{1,2},{2,3},{3,4},{4,5},{5,6},{6,7},{7,0},{8,9},{9,10},{10,1... | collective-permute-start | bytes 18440 | tf_op jit(solution)/shard_map/ppermute | solution.py:478
  54.0 3.7 %collective-permute-start.6 = (f32[8,16,12]{2,1,0:T(8,128)S(1)}, f32[8,16,12]{2,1,0:T(8,128)S(1)}, u32[]{:S(2)}, u32[]{:S(2)}) collective-permute-start(f32[8,16,12]{2,1,0:T(8,128)S(1)} %pad_maximum_fusion.26), channel_id=1, source_target_pairs={{1,0},{2,1},{3,2},{4,3},{5,4},{6,5},{7,6},{0,7},{9,8},{10,9},{11,1... | collective-permute-start | bytes 18440 | tf_op jit(solution)/shard_map/ppermute | solution.py:479
  57.8 19.5 %copy-start.48 = (f32[8,16,56]{2,1,0:T(8,128)}, f32[8,16,56]{2,1,0:T(8,128)S(1)}, u32[]{:S(2)}) copy-start(f32[8,16,56]{2,1,0:T(8,128)S(1)} %broadcast.3) | copy-start | bytes 86020
  58.1 4.5 %collective-permute-start.9 = (f32[24,4,128]{2,1,0:T(4,128)S(1)}, f32[24,4,128]{2,1,0:T(4,128)S(1)}, u32[]{:S(2)}, u32[]{:S(2)}) collective-permute-start(f32[24,4,128]{2,1,0:T(4,128)S(1)} %pad_maximum_fusion.29), channel_id=1, source_target_pairs={{0,8},{8,16},{16,24},{1,9},{9,17},{17,25},{2,10},{10,18},{18,26},{... | collective-permute-start | bytes 147464 | tf_op jit(solution)/shard_map/ppermute | solution.py:478
  61.3 4.8 %collective-permute-start.8 = (f32[24,4,128]{2,1,0:T(4,128)S(1)}, f32[24,4,128]{2,1,0:T(4,128)S(1)}, u32[]{:S(2)}, u32[]{:S(2)}) collective-permute-start(f32[24,4,128]{2,1,0:T(4,128)S(1)} %pad_maximum_fusion.28), channel_id=1, source_target_pairs={{8,0},{16,8},{24,16},{9,1},{17,9},{25,17},{10,2},{18,10},{26,18},{... | collective-permute-start | bytes 147464 | tf_op jit(solution)/shard_map/ppermute | solution.py:479
  66.4 9.9 %collective-permute-start.11 = (f32[24,24,128]{2,1,0:T(8,128)S(1)}, f32[24,24,128]{2,1,0:T(8,128)S(1)}, u32[]{:S(2)}, u32[]{:S(2)}) collective-permute-start(f32[24,24,128]{2,1,0:T(8,128)S(1)} %maximum_maximum_fusion), channel_id=1, source_target_pairs={{32,0},{64,32},{96,64},{128,96},{160,128},{192,160},{224,192},{256... | collective-permute-start | bytes 884744 | tf_op jit(solution)/shard_map/ppermute | solution.py:479
  67.7 9.5 %collective-permute-start.10 = (f32[24,24,128]{2,1,0:T(8,128)S(1)}, f32[24,24,128]{2,1,0:T(8,128)S(1)}, u32[]{:S(2)}, u32[]{:S(2)}) collective-permute-start(f32[24,24,128]{2,1,0:T(8,128)S(1)} %maximum_maximum_fusion), channel_id=1, source_target_pairs={{0,32},{32,64},{64,96},{96,128},{128,160},{160,192},{192,224},{224... | collective-permute-start | bytes 884744 | tf_op jit(solution)/shard_map/ppermute | solution.py:478
  77.2 0.8 copy-start.23
  77.2 0.9 copy-start.28
  77.2 0.9 copy-start.39
  77.2 0.8 copy-start.43
  78.1 34.9 %copy-start.12 = (f32[256,128]{1,0:T(8,128)S(1)}, f32[256,128]{1,0:T(8,128)}, u32[]{:S(2)}) copy-start(f32[256,128]{1,0:T(8,128)} %constant.74.clone.refs_4_) | copy-start | bytes 393220
  78.1 34.9 %copy-start.29 = (f32[16,32]{1,0:T(8,128)S(1)}, f32[16,32]{1,0:T(8,128)}, u32[]{:S(2)}) copy-start(f32[16,32]{1,0:T(8,128)} %constant.73.clone.refs_3_) | copy-start | bytes 6148
  78.1 34.9 %copy-start.42 = (f32[16,32]{1,0:T(8,128)S(1)}, f32[16,32]{1,0:T(8,128)}, u32[]{:S(2)}) copy-start(f32[16,32]{1,0:T(8,128)} %constant.75.clone.refs_5_) | copy-start | bytes 6148
  98.5 59.5 %copy-start = (f32[26,48,256]{2,1,0:T(8,128)S(1)}, f32[26,48,256]{2,1,0:T(8,128)}, u32[]{:S(2)}) copy-start(f32[26,48,256]{2,1,0:T(8,128)} %get-tuple-element.47.f) | copy-start | bytes 3833860
  98.5 59.5 %copy-start.18 = (f32[128,128]{1,0:T(8,128)S(1)}, f32[128,128]{1,0:T(8,128)}, u32[]{:S(2)}) copy-start(f32[128,128]{1,0:T(8,128)} %constant.81.clone.refs_5_) | copy-start | bytes 196612
  98.5 59.5 %copy-start.27 = (f32[32,16]{1,0:T(8,128)S(1)}, f32[32,16]{1,0:T(8,128)}, u32[]{:S(2)}) copy-start(f32[32,16]{1,0:T(8,128)} %constant.82.clone.refs_6_) | copy-start | bytes 6148
  98.5 13.6 %collective-permute-start.13 = (f32[3,4,32,256]{3,2,1,0:T(8,128)S(1)}, f32[3,4,32,256]{3,2,1,0:T(8,128)S(1)}, u32[]{:S(2)}, u32[]{:S(2)}) collective-permute-start(f32[3,4,32,256]{3,2,1,0:T(8,128)S(1)} %arrange.1.refs_1_), channel_id=1, source_target_pairs={{32,0},{64,32},{96,64},{128,96},{160,128},{192,160},{224,192},{256... | collective-permute-start | bytes 1179656 | tf_op jit(solution)/shard_map/ppermute | solution.py:479
  99.9 13.1 %collective-permute-start.12 = (f32[3,4,32,256]{3,2,1,0:T(8,128)S(1)}, f32[3,4,32,256]{3,2,1,0:T(8,128)S(1)}, u32[]{:S(2)}, u32[]{:S(2)}) collective-permute-start(f32[3,4,32,256]{3,2,1,0:T(8,128)S(1)} %arrange.1.refs_1_), channel_id=1, source_target_pairs={{0,32},{32,64},{64,96},{96,128},{128,160},{160,192},{192,224},{224... | collective-permute-start | bytes 1179656 | tf_op jit(solution)/shard_map/ppermute | solution.py:478
  114.5 0.8 copy-start.15
  116.0 41.9 %all-to-all-start.1 = ((f32[16,2,2,16,128]{4,3,2,1,0:T(8,128)}), f32[16,2,2,16,128]{4,3,2,1,0:T(8,128)S(1)}, u32[]{:S(2)}, u32[]{:S(2)}) async-start(f32[16,2,2,16,128]{4,3,2,1,0:T(8,128)} %copy-done.15), calls=%async_computation.1 | async-start | bytes 1048576 | tf_op jit(solution)/shard_map/all_to_all | solution.py:514
  158.0 0.9 copy-start.7
  158.9 0.9 copy-start.8
  159.8 0.9 copy-start.11
  160.7 1.0 copy-start.17
  161.7 0.8 copy-start.19
  162.5 0.8 copy-start.21
  167.5 32.0 %copy-start.49 = (f32[8,16,56]{2,1,0:T(8,128)S(1)}, f32[8,16,56]{2,1,0:T(8,128)}, u32[]{:S(2)}) copy-start(f32[8,16,56]{2,1,0:T(8,128)} %copy-done.48) | copy-start | bytes 86020
  190.0 21.4 %copy-start.6 = (f32[26,48,256]{2,1,0:T(8,128)}, f32[26,48,256]{2,1,0:T(8,128)S(1)}, u32[]{:S(2)}) copy-start(f32[26,48,256]{2,1,0:T(8,128)S(1)} %get-tuple-element.33.refs_11_) | copy-start | bytes 3833860
  190.0 23.0 %copy-start.24 = (f32[128,128]{1,0:T(8,128)S(1)}, f32[128,128]{1,0:T(8,128)}, u32[]{:S(2)}) copy-start(f32[128,128]{1,0:T(8,128)} %constant.70.clone.refs_4_) | copy-start | bytes 196612
  190.0 23.0 %copy-start.40 = (f32[8,24]{1,0:T(8,128)S(1)}, f32[8,24]{1,0:T(8,128)}, u32[]{:S(2)}) copy-start(f32[8,24]{1,0:T(8,128)} %constant.69.clone.refs_3_) | copy-start | bytes 2308
  190.1 9.3 %collective-permute-start.14 = (f32[8,16,4]{2,1,0:T(8,128)S(1)}, f32[8,16,4]{2,1,0:T(8,128)S(1)}, u32[]{:S(2)}, u32[]{:S(2)}) collective-permute-start(f32[8,16,4]{2,1,0:T(8,128)S(1)} %get-tuple-element.72), channel_id=1, source_target_pairs={{1,0},{2,1},{3,2},{4,3},{5,4},{6,5},{7,6},{0,7},{9,8},{10,9},{11,1... | collective-permute-start | bytes 6152 | tf_op jit(solution)/shard_map/ppermute | solution.py:479
  197.4 2.0 collective-permute-start.15
  199.6 5.3 %collective-permute-start.16 = (f32[8,4,128]{2,1,0:T(4,128)S(1)}, f32[8,4,128]{2,1,0:T(4,128)S(1)}, u32[]{:S(2)}, u32[]{:S(2)}) collective-permute-start(f32[8,4,128]{2,1,0:T(4,128)S(1)} %get-tuple-element.70), channel_id=1, source_target_pairs={{8,0},{16,8},{24,16},{9,1},{17,9},{25,17},{10,2},{18,10},{26,18},{... | collective-permute-start | bytes 49160 | tf_op jit(solution)/shard_map/ppermute | solution.py:479
  200.9 4.8 %collective-permute-start.17 = (f32[8,4,128]{2,1,0:T(4,128)S(1)}, f32[8,4,128]{2,1,0:T(4,128)S(1)}, u32[]{:S(2)}, u32[]{:S(2)}) collective-permute-start(f32[8,4,128]{2,1,0:T(4,128)S(1)} %get-tuple-element.71), channel_id=1, source_target_pairs={{0,8},{8,16},{16,24},{1,9},{9,17},{17,25},{2,10},{10,18},{18,26},{... | collective-permute-start | bytes 49160 | tf_op jit(solution)/shard_map/ppermute | solution.py:478
  205.9 28.9 %copy-start.13 = (f32[256,128]{1,0:T(8,128)S(1)}, f32[256,128]{1,0:T(8,128)}, u32[]{:S(2)}) copy-start(f32[256,128]{1,0:T(8,128)} %constant.74.clone.refs_4_) | copy-start | bytes 393220
  205.9 28.9 %copy-start.30 = (f32[16,32]{1,0:T(8,128)S(1)}, f32[16,32]{1,0:T(8,128)}, u32[]{:S(2)}) copy-start(f32[16,32]{1,0:T(8,128)} %constant.73.clone.refs_3_) | copy-start | bytes 6148
  205.9 5.5 %collective-permute-start.19 = (f32[8,24,128]{2,1,0:T(8,128)S(1)}, f32[8,24,128]{2,1,0:T(8,128)S(1)}, u32[]{:S(2)}, u32[]{:S(2)}) collective-permute-start(f32[8,24,128]{2,1,0:T(8,128)S(1)} %pad_maximum_fusion.23), channel_id=1, source_target_pairs={{32,0},{64,32},{96,64},{128,96},{160,128},{192,160},{224,192},{256... | collective-permute-start | bytes 294920 | tf_op jit(solution)/shard_map/ppermute | solution.py:479
  207.3 5.6 %collective-permute-start.18 = (f32[8,24,128]{2,1,0:T(8,128)S(1)}, f32[8,24,128]{2,1,0:T(8,128)S(1)}, u32[]{:S(2)}, u32[]{:S(2)}) collective-permute-start(f32[8,24,128]{2,1,0:T(8,128)S(1)} %pad_maximum_fusion.23), channel_id=1, source_target_pairs={{0,32},{32,64},{64,96},{96,128},{128,160},{160,192},{192,224},{224... | collective-permute-start | bytes 294920 | tf_op jit(solution)/shard_map/ppermute | solution.py:478
  215.0 46.6 %copy-start.2 = (f32[26,48,256]{2,1,0:T(8,128)S(1)}, f32[26,48,256]{2,1,0:T(8,128)}, u32[]{:S(2)}) copy-start(f32[26,48,256]{2,1,0:T(8,128)} %copy-done.1) | copy-start | bytes 3833860
  215.0 46.6 %copy-start.9 = (f32[128,256]{1,0:T(8,128)S(1)}, f32[128,256]{1,0:T(8,128)}, u32[]{:S(2)}) copy-start(f32[128,256]{1,0:T(8,128)} %constant.83.clone.refs_7_) | copy-start | bytes 393220
  215.0 46.5 %copy-start.20 = (f32[128,128]{1,0:T(8,128)S(1)}, f32[128,128]{1,0:T(8,128)}, u32[]{:S(2)}) copy-start(f32[128,128]{1,0:T(8,128)} %constant.79.clone.refs_3_) | copy-start | bytes 196612
  215.0 46.5 %copy-start.22 = (f32[128,128]{1,0:T(8,128)S(1)}, f32[128,128]{1,0:T(8,128)}, u32[]{:S(2)}) copy-start(f32[128,128]{1,0:T(8,128)} %constant.77.clone.refs_1_) | copy-start | bytes 196612
  215.0 46.5 %copy-start.26 = (f32[48,24]{1,0:T(8,128)S(1)}, f32[48,24]{1,0:T(8,128)}, u32[]{:S(2)}) copy-start(f32[48,24]{1,0:T(8,128)} %constant.84.clone.refs_8_) | copy-start | bytes 13828
  215.0 46.5 %copy-start.34 = (f32[16,8]{1,0:T(8,128)S(1)}, f32[16,8]{1,0:T(8,128)}, u32[]{:S(2)}) copy-start(f32[16,8]{1,0:T(8,128)} %constant.80.clone.refs_4_) | copy-start | bytes 1540
  215.1 46.5 %copy-start.36 = (f32[8,16]{1,0:T(8,128)S(1)}, f32[8,16]{1,0:T(8,128)}, u32[]{:S(2)}) copy-start(f32[8,16]{1,0:T(8,128)} %constant.78.clone.refs_2_) | copy-start | bytes 1540
  215.1 46.5 %copy-start.38 = (f32[8,16]{1,0:T(8,128)S(1)}, f32[8,16]{1,0:T(8,128)}, u32[]{:S(2)}) copy-start(f32[8,16]{1,0:T(8,128)} %constant.76.clone.refs_0_) | copy-start | bytes 1540
  215.1 46.5 %copy-start.45 = (s32[3]{0:T(128)S(1)}, s32[3]{0:T(128)}, u32[]{:S(2)}) copy-start(s32[3]{0:T(128)} %pad_add_fusion.index) | copy-start | bytes 40
  (7 other events, 4.8 us)

commit v3 on v2

v3 whole, which is shorter than its diff:
```python
import functools

import jax
import jax.numpy as jnp
import numpy as np
from jax import lax
from jax.experimental import pallas as pl
from jax.experimental.pallas import tpu as pltpu
from jax.sharding import PartitionSpec as P

LEVELS = 4
CSWEEPS = 6
absorption = 0.01
relaxation = 0.8
F32 = jnp.float32


def coords(n, b):
    at = np.arange(n)
    return np.where(at < (n + b) // 2, at, at - n)


def restriction(coarse, fine):
    gap = fine[None, :] - 2 * coarse[:, None]
    outer, inner = (gap == -1) | (gap == 2), (gap == 0) | (gap == 1)
    return np.where(outer, 0.125, np.where(inner, 0.375, 0.0)).astype(np.float32)


def halving(coarse, fine):
    return np.where(fine[None, :] // 2 == coarse[:, None], 0.5, 0.0).astype(np.float32)


def prolongation(fine, coarse):
    near = fine[:, None] // 2 == coarse[None, :]
    far = fine[:, None] // 2 + 2 * (fine[:, None] % 2) - 1 == coarse[None, :]
    return np.where(near, 0.75, np.where(far, 0.25, 0.0)).astype(np.float32)


def dot(a, b):
    return lax.dot_general(
        a, b, (((1,), (0,)), ((), ())),
        precision=lax.Precision.HIGHEST, preferred_element_type=F32,
    )


def planes(lo, hi, step, carry=0, unroll=1):
    whole = (hi - lo) // unroll
    if whole > 1:
        carry = lax.fori_loop(0, whole, lambda t, c: step(lo + t * unroll, unroll, c), carry)
    elif whole == 1:
        carry = step(lo, unroll, carry)
    rest = (hi - lo) % unroll
    return step(hi - rest, rest, carry) if rest else carry


class Open:
    def above(self, v, dim):
        return pltpu.roll(v, v.shape[dim] - 1, dim)

    def below(self, v, dim):
        return pltpu.roll(v, 1, dim)

    def closed(self, k):
        return None


class Closed(Open):
    def __init__(self, shape, counts):
        self.last, self.first = [], []
        for dim in range(2):
            at = lax.broadcasted_iota(jnp.int32, shape, dim)
            self.last.append(jnp.where(at == counts[dim] - 1, 0.0, 1.0))
            self.first.append(jnp.where(at == 0, 0.0, 1.0))

    def above(self, v, dim):
        return super().above(v, dim) * self.last[dim]

    def below(self, v, dim):
        return super().below(v, dim) * self.first[dim]

    def closed(self, k):
        return k * ((1.0 - self.first[0]) + (1.0 - self.first[1]))


def weigh(k, wx, wy, wz, lo, hi, factor, shifts, d=None, mask=None, b=None, unroll=1):
    half = 0.5 * factor
    first = half * (k[lo - 1] + k[lo])
    wx[lo - 1] = first

    def step(i, n, below):
        here = [k[i + j] for j in range(n + 1)]
        outs = []
        for j in range(n):
            x = half * (here[j] + here[j + 1])
            y = half * (here[j] + shifts.above(here[j], 0))
            z = half * (here[j] + shifts.above(here[j], 1))
            ends, value = shifts.closed(half * here[j]), None
            if d is not None:
                value = (x + below) + (y + shifts.below(y, 0)) + (z + shifts.below(z, 1))
                if ends is not None:
                    value = value + ends
                value = relaxation / (value + absorption)
                if mask is not None:
                    value = mask(here[j], value)
            outs.append((x, y, z, ends, value))
            below = x
        for j, (x, y, z, ends, value) in enumerate(outs):
            wx[i + j], wy[i + j], wz[i + j] = x, y, z
            if ends is not None:
                b[i + j] = ends
            if value is not None:
                d[i + j] = value
        return below

    planes(lo, hi, step, first, unroll)


def image(v, wx, wy, wz, lo, hi, use, put, shifts, b=None, unroll=1):
    def step(i, n, below):
        here = [v[i + j] for j in range(n + 1)]
        outs = []
        for j in range(n):
            x = wx[i + j] * (here[j] - here[j + 1])
            y = wy[i + j] * (here[j] - shifts.above(here[j], 0))
            z = wz[i + j] * (here[j] - shifts.above(here[j], 1))
            total = (x - below) + (y - shifts.below(y, 0)) + (z - shifts.below(z, 1))
            if b is not None:
                total = total + b[i + j] * here[j]
            outs.append(use(i + j, here[j], total + absorption * here[j]))
            below = x
        for j, value in enumerate(outs):
            put(i + j, value)
        return below

    planes(lo, hi, step, wx[lo - 1] * (v[lo - 1] - v[lo]), unroll)


def into(ref, by=0):
    def put(i, value):
        ref[i + by] = value

    return put


def smooth(v, f, d, w, lo, hi, shifts, b=None, unroll=1, by=0):
    def use(i, here, im):
        return here + d[i] * (f[i + by] - im)

    image(v, *w, lo, hi, use, into(v), shifts, b, unroll)


def residual_of(v, f, r, w, lo, hi, shifts, mask=None, b=None, unroll=1):
    def use(i, here, im):
        value = f[i] - im
        return value if mask is None else jnp.where(mask[i] > 0.0, value, 0.0)

    image(v, *w, lo, hi, use, into(r), shifts, b, unroll)


def first_sweep(g, d, v, lo, hi, unroll, by=0):
    def step(i, n, carry):
        values = [g[i + j + by] * d[i + j] for j in range(n)]
        for j, value in enumerate(values):
            v[i + j] = value
        return carry

    planes(lo, hi, step, unroll=unroll)


def restrict(r, offset, lo, hi, ry, rz, held):
    size = ry.shape[0]
    for i in range(lo, hi):
        at = 2 * i + offset
        plane = 0.125 * (r[at - 1] + r[at + 2]) + 0.375 * (r[at] + r[at + 1])
        held[(i - lo) * size : (i - lo + 1) * size, :] = dot(ry[...], plane)
    return dot(held[: (hi - lo) * size, :], rz[...])


def halve(k, offset, lo, hi, cy, cz, held):
    size = cy.shape[0]
    for i in range(lo, hi):
        plane = 0.5 * (k[2 * i + offset] + k[2 * i + 1 + offset])
        held[(i - lo) * size : (i - lo + 1) * size, :] = dot(cy[...], plane)
    return dot(held[: (hi - lo) * size, :], cz[...])


def prolong(e, first, count, py, pz, finer, use):
    rows = e.shape[1]
    spread = dot(e[pl.ds(first, count)].reshape(count * rows, e.shape[2]), pz)
    for i in range(count):
        finer[i] = dot(py, spread[i * rows : (i + 1) * rows])

    def step(i, n, carry):
        below, here, above = finer[i - 1], finer[i], finer[i + 1]
        use(2 * (i - 1), 0.75 * here + 0.25 * below)
        use(2 * (i - 1) + 1, 0.75 * here + 0.25 * above)
        return carry

    planes(1, count - 1, step)


def three(w):
    return tuple(w.at[i] for i in range(3))


def inside(k, value):
    return jnp.where(k > 0.0, value, 0.0)


U0, U1, U2, U3 = 2, 2, 4, 4


def down0(f, k, ry, rz, cy, cz, wx_, wy_, wz_, d_, g1, k1, wx, wy, wz, d, v, r, held, sem):
    shifts = Open()
    weigh(k, wx, wy, wz, 1, 25, 1.0, shifts, d, inside, unroll=U0)
    copies = [
        pltpu.make_async_copy(here, there, sem.at[i])
        for i, (here, there) in enumerate(((wx, wx_), (wy, wy_), (wz, wz_), (d, d_)))
    ]
    for copy in copies:
        copy.start()
    first_sweep(f, d, v, 1, 25, U0)
    residual_of(v, f, r, (wx, wy, wz), 2, 24, shifts, k, unroll=U0)
    g1[...] = restrict(r, 5, -1, 9, ry, rz, held).reshape(g1.shape)
    k1[...] = halve(k, 5, -1, 9, cy, cz, held).reshape(k1.shape)
    for copy in copies:
        copy.wait()


def descend(first, *refs):
    shifts = Open()
    if first:
        g1, k1, ry1, rz1, ry2, rz2, cy1, cz1, cy2, cz2 = refs[:10]
        out, d1, g2, k2, d2 = refs[10:15]
    else:
        g1, k1, d1, k2, d2, ry1, rz1, ry2, rz2 = refs[:9]
        out, g2 = refs[9:11]
    v1, r1, held, w1, v2, r2, w2, part = refs[-8:]
    w1, w2 = three(w1), three(w2)
    rows = g2.shape[1]
    if first:
        zero = jnp.zeros(d1.shape[1:], F32)
        d1[0], d1[25] = zero, zero
        weigh(k1, *w1, 1, 25, 0.25, shifts, d1, inside, unroll=U1)
    else:
        weigh(k1, *w1, 1, 25, 0.25, shifts, unroll=U1)
    first_sweep(g1, d1, v1, 1, 25, U1)
    residual_of(v1, g1, r1, w1, 2, 24, shifts, d1, unroll=U1)
    zero = jnp.zeros(g2.shape[1:], F32)
    g2[0], g2[11] = zero, zero
    g2[1:11] = restrict(r1, 9, -3, 7, ry1, rz1, held).reshape(10, rows, 128)
    if first:
        d2[0], d2[11] = zero, zero
        k2[...] = halve(k1, 9, -4, 8, cy1, cz1, held).reshape(k2.shape)
        weigh(k2, *w2, 1, 11, 0.25**2, shifts, d2, inside, unroll=U2)
    else:
        weigh(k2, *w2, 1, 11, 0.25**2, shifts, unroll=U2)
    first_sweep(g2, d2, v2, 1, 11, U2)
    residual_of(v2, g2, r2, w2, 3, 9, shifts, d2, unroll=U2)
    total = None
    for i in range(2):
        at = 2 * i + 4
        plane = 0.125 * (r2[at - 1] + r2[at + 2]) + 0.375 * (r2[at] + r2[at + 1])
        value = dot(ry2[i], plane)
        total = value if total is None else total + value
    tile = dot(total, rz2[...])
    if first:
        total = dot(cy2[0], 0.5 * (k2[4] + k2[5])) + dot(cy2[1], 0.5 * (k2[6] + k2[7]))
        tile = tile + dot(total, cz2[...])
    for i in range(out.shape[0]):
        out[i] = tile


def repack(s, out):
    tiles = 2 * s.shape[0] // 16
    lane = lax.broadcasted_iota(jnp.int32, (8, 128), 1) // 16
    row = lax.broadcasted_iota(jnp.int32, (8, 128), 0) // 4
    for field in range(out.shape[1] // tiles):
        for t in range(tiles):
            total = jnp.zeros((8, 128), F32)
            for half in range(2):
                for p in range(8):
                    plane = 16 * t + 8 * half + p
                    part = s[plane // 2]
                    if plane % 2 != half:
                        part = pltpu.roll(part, 4, 0)
                    if p != field:
                        part = pltpu.roll(part, (16 * (p - field)) % 128, 1)
                    total = jnp.where((lane == p) & (row == half), part, total)
            for i in range(out.shape[0]):
                out[i, field * tiles + t] = total


def unpack(s, first, tiles, nz, whole):
    lane = lax.broadcasted_iota(jnp.int32, (8, 128), 1) // 16
    for j in range(s.shape[0] // nz):
        for t in range(tiles):
            for p in range(8):
                total = jnp.zeros((8, 128), F32)
                for q in range(nz):
                    part = s[j * nz + q, first + t]
                    if p != q:
                        part = pltpu.roll(part, (16 * (q - p)) % 128, 1)
                    total = jnp.where(lane == q, part, total)
                whole[16 * t + p + 3, 4 * j : 4 * j + 4] = total[:4]
                whole[16 * t + p + 11, 4 * j : 4 * j + 4] = total[4:]


def bottom(nz, s, k3, scratch, mats):
    g3, v3, r3, w3, d3, b3, k4, g4, v4, w4, d4, b4, held, fine4 = scratch
    ry3, rz3, cy3, cz3, py3, pz3 = mats
    n4 = g4.shape[0]
    n3, two = 2 * n4, s.shape[1] == n4 // 4
    rows, lanes = g3.shape[1], g3.shape[2]
    zero = jnp.zeros((rows, lanes), F32)
    for i in (0, 1, 2, n3 + 3, n3 + 4, n3 + 5):
        v3[i], r3[i] = zero, zero
        if two:
            k3[i] = zero
    for ref in (k4, v4):
        for i in (0, n4 + 1):
            ref[i] = jnp.zeros(ref.shape[1:], F32)
    unpack(s, 0, n3 // 16, nz, g3)
    if two:
        unpack(s, n3 // 16, n3 // 16, nz, k3)
    k4[1 : n4 + 1] = halve(k3, 3, 0, n4, cy3, cz3, held).reshape(g4.shape)
    shifts3 = Closed((rows, lanes), (rows, 16 * nz))
    shifts4 = Closed((k4.shape[1], lanes), (k4.shape[1], 8 * nz))
    w3, w4 = three(w3), three(w4)
    weigh(k3, *w3, 3, n3 + 3, 0.25**3, shifts3, d3, inside, b3, U3)
    weigh(k4, *w4, 1, n4 + 1, 0.25**4, shifts4, d4, inside, b4, U3)
    first_sweep(g3, d3, v3, 3, n3 + 3, U3)
    residual_of(v3, g3, r3, w3, 3, n3 + 3, shifts3, b=b3, unroll=U3)
    g4[...] = restrict(r3, 3, 0, n4, ry3, rz3, held).reshape(g4.shape)
    first_sweep(g4, d4, v4, 1, n4 + 1, U3, by=-1)

    def turn(j, carry):
        smooth(v4, g4, d4, w4, 1, n4 + 1, shifts4, b4, n4, by=-1)
        return carry

    lax.fori_loop(0, CSWEEPS - 1, turn, 0)

    def use(i, value):
        v3[i + 3] = v3[i + 3] + value

    prolong(v4, 0, n4 + 2, py3[...], pz3[...], fine4, use)
    smooth(v3, g3, d3, w3, 3, n3 + 3, shifts3, b3, U3)
    return v3


def spread_matrix(shape, dim_fine, coarse_start, block_fine):
    fine = lax.broadcasted_iota(jnp.int32, shape, dim_fine)
    size = shape[dim_fine]
    fine = jnp.where(fine < (size + block_fine) // 2, fine, fine - size)
    whole = lax.broadcasted_iota(jnp.int32, shape, 1 - dim_fine)
    near = (fine >> 1) + coarse_start
    far = near + 2 * (fine & 1) - 1
    return jnp.where(whole == near, 0.75, jnp.where(whole == far, 0.25, 0.0))


def upward(index, e3, g2, k2, d2, g1, k1, d1, ends, scratch, mats):
    v2, w2, m2, v1, w1, fine2, fine1 = scratch
    py1, pz1 = mats
    shifts, w2, w1 = Open(), three(w2), three(w1)
    weigh(k2, *w2, 1, 11, 0.25**2, shifts, unroll=U2)
    weigh(k1, *w1, 6, 20, 0.25, shifts, unroll=U1)
    first_sweep(g2, d2, v2, 0, 12, U2)
    first_sweep(g1, d1, v1, 5, 21, U1)
    m2[...] = d2[...]
    if ends is not None:
        for ref, i in zip(ends, (0, 11)):
            v2[i], m2[i] = ref[0] * ref[1], ref[1]

    def use2(i, value):
        v2[i] = jnp.where(m2[i] > 0.0, v2[i] + value, 0.0)

    py2 = spread_matrix((g2.shape[1], e3.shape[1]), 0, index[1] * 4, 8)
    pz2 = spread_matrix((e3.shape[2], g2.shape[2]), 1, index[2] * 16, 32)
    prolong(e3, index[0] * 2, 8, py2, pz2, fine2, use2)
    smooth(v2, g2, d2, w2, 1, 11, shifts, unroll=U2)

    def use1(i, value):
        v1[i + 5] = jnp.where(d1[i + 5] > 0.0, v1[i + 5] + value, 0.0)

    prolong(v2, 1, 10, py1[...], pz1[...], fine1, use1)
    smooth(v1, g1, d1, w1, 6, 20, shifts, unroll=U1)
    return v1


BOTTOM = 14
UP = 7


def fetch(sources, targets, sem):
    copies = [
        pltpu.make_async_copy(there, here, sem.at[i])
        for i, (there, here) in enumerate(zip(sources, targets))
    ]
    for copy in copies:
        copy.start()
    return copies


def middle(nz, index, f_, wx_, wy_, wz_, d_, k_, s, g2, k2, d2, g1, k1, d1, *refs):
    ends, m3, m1, (py0, pz0, ry, rz), (v_, gn, k3) = refs[:2], refs[2:8], refs[8:10], refs[10:14], refs[14:17]
    low, mid, (fine0, r, held0, f, wx, wy, wz, d, k, v, sem) = refs[17:31], refs[31:38], refs[38:]
    copies = fetch((f_, wx_, wy_, wz_, d_, k_), (f, wx, wy, wz, d, k), sem)
    e3 = bottom(nz, s, k3, low, m3)
    e1 = upward(index, e3, g2, k2, d2, g1, k1, d1, ends, mid, m1)
    for copy in copies:
        copy.wait()
    w, shifts = (wx, wy, wz), Open()

    def use(i, value):
        v[i + 1] = inside(k[i + 1], f[i + 1] * d[i + 1] + value)

    prolong(e1, 6, 14, py0[...], pz0[...], fine0, use)
    smooth(v, f, d, w, 2, 24, shifts, unroll=U0)
    smooth(v, f, d, w, 3, 23, shifts, unroll=U0)
    copy = pltpu.make_async_copy(v, v_, sem.at[0])
    copy.start()
    residual_of(v, f, r, w, 4, 22, shifts, k, unroll=U0)
    gn[...] = restrict(r, 5, 0, 8, ry, rz, held0).reshape(gn.shape)
    copy.wait()


def final(nz, index, f_, wx_, wy_, wz_, d_, k_, v_, s, g2, k2, d2, g1, k1, d1, *refs):
    m3, m1, (py0, pz0, k3), (solution_, residual_) = refs[:6], refs[6:8], refs[8:11], refs[11:13]
    low, mid, (fine0, f, wx, wy, wz, d, k, v, sem) = refs[13:27], refs[27:34], refs[34:]
    copies = fetch((f_, wx_, wy_, wz_, d_, k_, v_), (f, wx, wy, wz, d, k, v), sem)
    e3 = bottom(nz, s, k3, low, m3)
    e1 = upward(index, e3, g2, k2, d2, g1, k1, d1, None, mid, m1)
    for copy in copies:
        copy.wait()
    w, shifts = (wx, wy, wz), Open()

    def use(i, value):
        v[i + 3] = inside(k[i + 3], v[i + 3] + value)

    prolong(e1, 7, 12, py0[...], pz0[...], fine0, use)
    smooth(v, f, d, w, 4, 22, shifts, unroll=U0)

    def last(i, here, im):
        return here[:32, :128], (f[i] - im)[:32, :128]

    def out(i, values):
        solution_[i - 5], residual_[i - 5] = values

    image(v, *w, 5, 21, last, out, shifts, unroll=U0)


def call(kernel, outs, scratch, *args, name, scalars=0, loose=0, away=0, sems=0):
    vmem = pl.BlockSpec(memory_space=pltpu.VMEM)
    smem = pl.BlockSpec(memory_space=pltpu.SMEM)
    hbm = pl.BlockSpec(memory_space=pl.ANY)
    return pl.pallas_call(
        kernel,
        out_shape=[jax.ShapeDtypeStruct(o, F32) for o in outs],
        in_specs=[smem] * scalars + [hbm] * loose + [vmem] * (len(args) - scalars - loose),
        out_specs=[hbm] * away + [vmem] * (len(outs) - away),
        scratch_shapes=[pltpu.VMEM(s, F32) for s in scratch]
        + ([pltpu.SemaphoreType.DMA((sems,))] if sems else []),
        compiler_params=pltpu.CompilerParams(vmem_limit_bytes=56 << 20),
        name=name,
    )(*args)


def neighbours(last, initial, axis):
    count = lax.axis_size(axis)
    if axis == "gz":
        up = [(i, (i + 1) % count) for i in range(count)]
    else:
        up = [(i, i + 1) for i in range(count - 1)]
    down = [(j, i) for i, j in up]
    before = lax.ppermute(last, axis, up)
    after = lax.ppermute(initial, axis, down)
    if axis == "gz":
        at = lax.axis_index(axis)
        before = jnp.where(at == 0, 0.0, before)
        after = jnp.where(at == count - 1, 0.0, after)
    return before, after


def exchange(fields, block, sizes, widths, extra=0):
    count = len(fields)
    for axis, dim in (("gz", 2), ("gy", 1), ("gx", 0)):
        along = 2 if dim == 2 else 0
        size, width, shift = block[dim], widths[dim], extra if dim == 0 else 0
        last = [lax.slice_in_dim(f, size + shift - width, size + shift, axis=dim) for f in fields]
        initial = [lax.slice_in_dim(f, shift, shift + width, axis=dim) for f in fields]
        before, after = neighbours(
            jnp.concatenate(last, along), jnp.concatenate(initial, along), axis
        )
        before = jnp.split(before, count, along)
        after = jnp.split(after, count, along)
        own = [lax.slice_in_dim(f, shift, shift + size, axis=dim) for f in fields]
        if dim == 0:
            fields = [jnp.concatenate([b, f, a], 0) for b, f, a in zip(before, own, after)]
            continue
        gap = list(own[0].shape)
        gap[dim] = sizes[dim - 1] - size - 2 * width
        parts = [[jnp.zeros(gap, F32)] if gap[dim] else []] * count
        fields = [
            jnp.concatenate([f, a] + z + [b], dim)
            for b, f, a, z in zip(before, own, after, parts)
        ]
    return fields


def everyone(pieces, axes):
    return lax.all_to_all(pieces, axes, 0, 0)


def body(right_side, conductivity):
    nx, ny, nz = (lax.axis_size(axis) for axis in ("gx", "gy", "gz"))
    index = jnp.stack([lax.axis_index(axis) for axis in ("gx", "gy", "gz")]).astype(jnp.int32)

    def ends(size, count, away=-1000, start=0):
        at = np.arange(size)
        return np.where((at >= start) & (at < start + count), at - start, away)

    y0, z0 = coords(48, 32), coords(256, 128)
    y1, z1 = coords(40, 16), coords(128, 64)
    y2, z2 = coords(24, 8), coords(128, 32)
    rows3, rows4 = np.arange(4 * ny), np.arange(2 * ny)
    lanes3, lanes4 = ends(128, 16 * nz, -3000), ends(128, 8 * nz, -9000)
    ry0, rz0 = restriction(np.arange(16), y0), restriction(ends(128, 64), z0).T
    cy0, cz0 = halving(np.arange(16), y0), halving(ends(128, 64), z0).T
    ry1, rz1 = restriction(y2, y1), restriction(z2, z1).T
    cy1, cz1 = halving(y2, y1), halving(z2, z1).T

    def both(matrix):
        zero = np.zeros_like(matrix)
        return np.stack([np.concatenate([matrix, zero]), np.concatenate([zero, matrix])])

    ry2, rz2 = both(restriction(np.arange(4), y2)), restriction(ends(128, 16), z2).T
    cy2, cz2 = both(halving(np.arange(4), y2)), halving(ends(128, 16, start=16), z2).T
    ry3, rz3 = restriction(rows4, rows3), restriction(lanes4, lanes3).T
    cy3, cz3 = halving(rows4, rows3), halving(lanes4, lanes3).T
    py0, pz0 = prolongation(y0, y1), prolongation(z0, z1).T
    py1, pz1 = prolongation(y1, y2), prolongation(z1, z2).T
    py3, pz3 = prolongation(rows3, rows4), prolongation(lanes3, lanes4).T
    m3, m1 = (ry3, rz3, cy3, cz3, py3, pz3), (py1, pz1)

    wide, l1, l2 = (26, 48, 256), (26, 40, 128), (12, 24, 128)
    n3, n4 = (2 * nx + 6, 4 * ny, 128), (nx + 2, 2 * ny, 128)
    low = [
        n3, n3, n3, (3,) + n3, n3, n3,
        n4, (nx, 2 * ny, 128), n4, (3,) + n4, n4, n4,
        (nx * 2 * ny, 128), (nx + 2, 4 * ny, 128),
    ]
    mid = [l2, (3,) + l2, l2, l1, (3,) + l1, (8, 24, 128), (10, 40, 128)]
    tiles = nx // 8

    f, k = exchange([right_side, conductivity], (16, 32, 128), (48, 256), (5, 5, 5))
    b1 = (10, 16, 128)
    wx, wy, wz, d, g1, k1 = call(
        down0, [wide] * 4 + [b1] * 2, [wide] * 6 + [(160, 256)],
        f, k, ry0, rz0, cy0, cz0, name="down0", away=4, sems=4,
    )
    size1 = ((8, 16, 64), (40, 128))
    g1, k1 = exchange([g1, k1], *size1, (9, 11, 11), 1)
    inner = [l1, l1, (288, 128), (3,) + l1, l2, l2, (3,) + l2, (8, 128)]
    pieces, d1, g2, k2, d2 = call(
        functools.partial(descend, True), [(nx, 8, 128), l1, l2, l2, l2], inner,
        g1, k1, ry1, rz1, ry2, rz2, cy1, cz1, cy2, cz2, name="descend",
    )
    first, last = jnp.stack([g2[4], d2[4]]), jnp.stack([g2[7], d2[7]])
    outer = neighbours(first, last, "gx")
    pieces = everyone(pieces, "gx")
    (pieces,) = call(repack, [(ny * nz, 2 * tiles, 8, 128)], [], pieces, name="repack")
    s = everyone(pieces, ("gy", "gz"))
    fields = (f, wx, wy, wz, d, k)
    v, g1b, k3 = call(
        functools.partial(middle, nz), [wide, (8, 16, 128), n3],
        low + mid + [(14, 48, 256), wide, (128, 256)] + [wide] * 7,
        index, *fields, s, g2, k2, d2, g1, k1, d1, *outer, *m3, *m1, py0, pz0, ry0, rz0,
        name="middle", scalars=1, loose=6, away=1, sems=6,
    )
    (g1,) = exchange([g1b], *size1, (8, 11, 11))
    g1 = jnp.pad(g1, ((1, 1), (0, 0), (0, 0)))
    pieces, g2 = call(
        functools.partial(descend, False), [(nx, 8, 128), l2], inner,
        g1, k1, d1, k2, d2, ry1, rz1, ry2, rz2, name="again",
    )
    pieces = everyone(pieces, "gx")
    (pieces,) = call(repack, [(ny * nz, tiles, 8, 128)], [], pieces, name="repack2")
    s = everyone(pieces, ("gy", "gz"))
    return tuple(call(
        functools.partial(final, nz), [(16, 32, 128)] * 2,
        low + mid + [(12, 48, 256)] + [wide] * 7,
        index, *fields, v, s, g2, k2, d2, g1, k1, d1, *m3, *m1, py0, pz0, k3,
        name="final", scalars=1, loose=7, sems=7,
    ))


def solution(mesh):
    placed = P("gx", "gy", "gz")
    return jax.shard_map(
        body, mesh=mesh, in_specs=(placed, placed), out_specs=(placed, placed), check_vma=False
    )
```

time: 285 us -> 258 us (0.905)
  blocking collectives: 63 us -> 38.6 us
  Pallas kernels: 56.7 us -> 68.2 us
  waiting for transfers between devices: 61.6 us -> 53.6 us
  local copies, waits for them, and re-layouts: 17.3 us -> 10.2 us
  other arithmetic: 4.64 us -> 7.77 us
    all_to_all x3 -> x2, blocking collectives: 63 us -> 38.6 us  [everyone(): return lax.all_to_all(pieces, axes, 0, 0)]
    unnamed x104 -> x22, local copies, waits for them, and re-layouts: 14.5 us -> 2.13 us
    pallas_call x8 -> x7, Pallas kernels: 56.7 us -> 68.2 us  [call(): pl.pallas_call(kernel, out_shape=[jax.ShapeDtypeStruct(o, F32) for o in o...]
    all_to_all x1 -> x2, waiting for transfers between devices: 22.2 us -> 14.5 us  [everyone(): return lax.all_to_all(pieces, axes, 0, 0)]
    all_to_all x1 -> x2, starting transfers between devices: 19.1 us -> 26.8 us  [everyone(): return lax.all_to_all(pieces, axes, 0, 0)]
    ppermute x10, starting transfers between devices: 23.5 us -> 16.1 us  [neighbours(): after = lax.ppermute(initial, axis, down)]
    slice x13 -> x17, local copies, waits for them, and re-layouts: 1.82 us -> 6.19 us  [the longest x9 4.58 us: exchange(): lax.slice_in_dim(f, shift, shift + width, axis=dim)]
  transfers between devices with their start and end apart: 21 -> 22, of which waited for: 18 -> 19; matrix products, arithmetic and copies ran while one was open for 1% -> 1% of each run, Pallas kernels for 0% -> 0%
where the time goes in v3:
time: 258 us; the launch traced here: 256 us
  starting transfers between devices  76.5 us (30%)
  Pallas kernels  68.2 us (26%)
  waiting for transfers between devices  53.6 us (21%)
  blocking collectives  38.6 us (15%)
  local copies, waits for them, and re-layouts  10.2 us (4%)
  other arithmetic  7.77 us (3%)
    pallas_call x7, Pallas kernels, call(): pl.pallas_call(kernel, out_shape=[jax.ShapeDtypeStruct(o, F32) for o in o...  68.2 us
    all_to_all x2, blocking collectives, everyone(): return lax.all_to_all(pieces, axes, 0, 0)  38.6 us
    ppermute x10, starting transfers between devices, neighbours(): before = lax.ppermute(last, axis, up)  33.6 us
    all_to_all x2, starting transfers between devices, everyone(): return lax.all_to_all(pieces, axes, 0, 0)  26.8 us
    ppermute x10, waiting for transfers between devices, neighbours(): after = lax.ppermute(initial, axis, down)  25.9 us
    ppermute x10, starting transfers between devices, neighbours(): after = lax.ppermute(initial, axis, down)  16.1 us
    all_to_all x2, waiting for transfers between devices, everyone(): return lax.all_to_all(pieces, axes, 0, 0)  14.5 us
    ppermute x10, waiting for transfers between devices, neighbours(): before = lax.ppermute(last, axis, up)  13.2 us
  transfers between devices with their start and end apart: 22, of which 19 were waited for; matrix products, arithmetic and copies ran while one was open for 1% of the time, Pallas kernels for 0%

profile of v3, /device:TPU:1, one launch (start us, length us, event | category | flops | bytes accessed | tf_op | source)
XLA Modules:
  0.0 256.4 jit_solution(3855515661101814710)
XLA Ops:
  0.6 1.2 fusion.40
  2.5 6.9 %collective-permute-start = (f32[16,32,10]{2,1,0:T(8,128)S(1)}, f32[16,32,10]{2,1,0:T(8,128)S(1)}, u32[]{:S(2)}, u32[]{:S(2)}) collective-permute-start(f32[16,32,10]{2,1,0:T(8,128)S(1)} %copy.28), channel_id=1, source_target_pairs={{1,0},{2,1},{3,2},{4,3},{5,4},{6,5},{7,6},{0,7},{9,8},{10,9},{11,1... | collective-permute-start | bytes 61448 | tf_op jit(solution)/shard_map/ppermute | solution.py:476
  10.0 0.6 collective-permute-done
  10.8 2.5 collective-permute-done.1
  13.5 0.3 fusion.16
  13.9 1.3 collective-permute-start.3
  15.2 1.3 collective-permute-start.2
  16.5 1.9 collective-permute-done.3
  18.5 3.8 %collective-permute-done.2 = f32[32,5,256]{2,1,0:T(8,128)S(1)} collective-permute-done((f32[32,5,256]{2,1,0:T(8,128)S(1)}, f32[32,5,256]{2,1,0:T(8,128)S(1)}, u32[]{:S(2)}, u32[]{:S(2)}) %collective-permute-start.2) | collective-permute-done | bytes 163872 | tf_op jit(solution)/shard_map/ppermute | solution.py:476
  22.4 0.3 fusion.14
  22.9 1.3 collective-permute-start.5
  24.2 4.0 %collective-permute-start.4 = (f32[10,48,256]{2,1,0:T(8,128)S(1)}, f32[10,48,256]{2,1,0:T(8,128)S(1)}, u32[]{:S(2)}, u32[]{:S(2)}) collective-permute-start(f32[10,48,256]{2,1,0:T(8,128)S(1)} %pad_maximum_fusion.12), channel_id=1, source_target_pairs={{0,32},{32,64},{64,96},{96,128},{128,160},{160,192},{192,224},{224... | collective-permute-start | bytes 1474568 | tf_op jit(solution)/shard_map/ppermute | solution.py:475
  28.3 4.1 %collective-permute-done.5 = f32[10,48,256]{2,1,0:T(8,128)S(1)} collective-permute-done((f32[10,48,256]{2,1,0:T(8,128)S(1)}, f32[10,48,256]{2,1,0:T(8,128)S(1)}, u32[]{:S(2)}, u32[]{:S(2)}) %collective-permute-start.5) | collective-permute-done | bytes 491552 | tf_op jit(solution)/shard_map/ppermute | solution.py:476
  32.5 1.5 collective-permute-done.4
  34.0 1.9 fusion.9
  35.9 8.2 %down0.1 = (f32[26,48,256]{2,1,0:T(8,128)}, f32[26,48,256]{2,1,0:T(8,128)}, f32[26,48,256]{2,1,0:T(8,128)}, f32[26,48,256]{2,1,0:T(8,128)}, f32[10,16,128]{2,1,0:T(8,128)}, /*index=5*/f32[10,16,128]{2,1,0:T(8,128)}) custom-call(f32[26,48,256]{2,1,0:T(8,128)} %get-tuple-element.47.f.f_, f32[26,48,256]{2,1,0:T(8,128)} %get-tuple-element.46.k.k_, ...), custom_call_target="tpu_custom_call" | custom-call | tf_op jit(solution)/shard_map/down0/pallas_call | solution.py:456
  44.2 1.1 fusion.52
  45.3 1.0 fusion.53
  46.4 8.3 %collective-permute-start.7 = (f32[10,16,22]{2,1,0:T(8,128)S(1)}, f32[10,16,22]{2,1,0:T(8,128)S(1)}, u32[]{:S(2)}, u32[]{:S(2)}) collective-permute-start(f32[10,16,22]{2,1,0:T(8,128)S(1)} %pad_maximum_fusion.29), channel_id=1, source_target_pairs={{0,1},{1,2},{2,3},{3,4},{4,5},{5,6},{6,7},{7,0},{8,9},{9,10},{10,1... | collective-permute-start | bytes 42248 | tf_op jit(solution)/shard_map/ppermute | solution.py:475
  54.8 1.4 collective-permute-done.7
  56.3 2.4 collective-permute-done.6
  59.0 3.1 %collective-permute-start.9 = (f32[20,11,128]{2,1,0:T(8,128)S(1)}, f32[20,11,128]{2,1,0:T(8,128)S(1)}, u32[]{:S(2)}, u32[]{:S(2)}) collective-permute-start(f32[20,11,128]{2,1,0:T(8,128)S(1)} %pad_maximum_fusion.22), channel_id=1, source_target_pairs={{0,8},{8,16},{16,24},{1,9},{9,17},{17,25},{2,10},{10,18},{18,26},{... | collective-permute-start | bytes 337928 | tf_op jit(solution)/shard_map/ppermute | solution.py:475
  62.2 1.3 collective-permute-start.8
  63.5 2.2 collective-permute-done.9
  65.7 3.8 %collective-permute-done.8 = f32[20,11,128]{2,1,0:T(8,128)S(1)} collective-permute-done((f32[20,11,128]{2,1,0:T(8,128)S(1)}, f32[20,11,128]{2,1,0:T(8,128)S(1)}, u32[]{:S(2)}, u32[]{:S(2)}) %collective-permute-start.8) | collective-permute-done | bytes 112672 | tf_op jit(solution)/shard_map/ppermute | solution.py:476
  69.8 1.3 collective-permute-start.11
  71.2 4.7 %collective-permute-start.10 = (f32[18,40,128]{2,1,0:T(8,128)S(1)}, f32[18,40,128]{2,1,0:T(8,128)S(1)}, u32[]{:S(2)}, u32[]{:S(2)}) collective-permute-start(f32[18,40,128]{2,1,0:T(8,128)S(1)} %pad_maximum_fusion.15), channel_id=1, source_target_pairs={{0,32},{32,64},{64,96},{96,128},{128,160},{160,192},{192,224},{224... | collective-permute-start | bytes 1105928 | tf_op jit(solution)/shard_map/ppermute | solution.py:475
  76.0 5.7 %collective-permute-done.11 = f32[18,40,128]{2,1,0:T(8,128)S(1)} collective-permute-done((f32[18,40,128]{2,1,0:T(8,128)S(1)}, f32[18,40,128]{2,1,0:T(8,128)S(1)}, u32[]{:S(2)}, u32[]{:S(2)}) %collective-permute-start.11) | collective-permute-done | bytes 368672 | tf_op jit(solution)/shard_map/ppermute | solution.py:476
  81.7 0.9 collective-permute-done.10
  82.6 0.8 pad_maximum_fusion.11.refs_1_.k1
  83.4 0.8 pad_maximum_fusion.10.refs_0_.g1
  84.3 7.9 %descend.1 = (f32[16,8,128]{2,1,0:T(8,128)}, f32[26,40,128]{2,1,0:T(8,128)}, f32[12,24,128]{2,1,0:T(8,128)}, f32[12,24,128]{2,1,0:T(8,128)}, f32[12,24,128]{2,1,0:T(8,128)}) custom-call(f32[26,40,128]{2,1,0:T(8,128)} %pad_maximum_fusion.10.refs_0_.g1, f32[26,40,128]{2,1,0:T(8,128)} %pad_maximum_fusion.11.refs_1_.k1, ...), custom_call_target="tpu_custom_call" | custom-call | tf_op jit(solution)/shard_map/descend/pallas_call | solution.py:456
  92.2 17.9 %all-to-all-start = ((f32[16,8,128]{2,1,0:T(8,128)}), f32[16,8,128]{2,1,0:T(8,128)S(1)}, u32[]{:S(2)}, u32[]{:S(2)}) async-start(f32[16,8,128]{2,1,0:T(8,128)} %get-tuple-element.24), calls=%async_computation | async-start | bytes 131072 | tf_op jit(solution)/shard_map/all_to_all | solution.py:511
  110.1 0.7 fusion.46
  110.9 10.9 %all-to-all-done.s = f32[16,8,128]{2,1,0:T(8,128)S(1)} async-done(((f32[16,8,128]{2,1,0:T(8,128)}), f32[16,8,128]{2,1,0:T(8,128)S(1)}, u32[]{:S(2)}, u32[]{:S(2)}) %all-to-all-start) | async-done | bytes 65568 | tf_op jit(solution)/shard_map/all_to_all | solution.py:511
  121.8 0.6 copy-done.6
  122.4 1.9 repack.1
  124.3 8.9 %all-to-all-start.1 = ((f32[32,4,8,128]{3,2,1,0:T(8,128)}), f32[32,4,8,128]{3,2,1,0:T(8,128)S(1)}, u32[]{:S(2)}, u32[]{:S(2)}) async-start(f32[32,4,8,128]{3,2,1,0:T(8,128)} %repack.1), calls=%async_computation.1 | async-start | bytes 1048576 | tf_op jit(solution)/shard_map/all_to_all | solution.py:511
  133.2 0.7 fusion.47
  133.9 2.4 collective-permute-start.12
  136.3 1.5 collective-permute-start.13
  137.8 0.6 pad_add_fusion.index
  138.4 2.7 %collective-permute-done.13.refs_1_ = f32[2,24,128]{2,1,0:T(8,128)S(1)} collective-permute-done((f32[2,24,128]{2,1,0:T(8,128)S(1)}, f32[2,24,128]{2,1,0:T(8,128)S(1)}, u32[]{:S(2)}, u32[]{:S(2)}) %collective-permute-start.13) | collective-permute-done | bytes 24608 | tf_op jit(solution)/shard_map/ppermute | solution.py:476
  141.2 3.6 %all-to-all-done.1.s = f32[32,4,8,128]{3,2,1,0:T(8,128)S(1)} async-done(((f32[32,4,8,128]{3,2,1,0:T(8,128)}), f32[32,4,8,128]{3,2,1,0:T(8,128)S(1)}, u32[]{:S(2)}, u32[]{:S(2)}) %all-to-all-start.1) | async-done | bytes 524320 | tf_op jit(solution)/shard_map/all_to_all | solution.py:511
  144.8 0.8 copy-done.2
  145.6 23.4 %middle.1 = (f32[26,48,256]{2,1,0:T(8,128)}, f32[8,16,128]{2,1,0:T(8,128)}, f32[38,16,128]{2,1,0:T(8,128)}) custom-call(s32[3]{0:T(128)} %pad_add_fusion.index, f32[26,48,256]{2,1,0:T(8,128)} %get-tuple-element.47.f.f_, f32[26,48,256]{2,1,0:T(8,128)} %get-tuple-element.18.wx_, f32[26,48,256]{2,1,0:T(8,128)} %get-tuple-element.19.wy_, ...), custom_call_target="tpu_custom_call" | custom-call | tf_op jit(solution)/shard_map/middle/pallas_call | solution.py:456
  168.9 1.0 fusion.55
  170.0 1.7 collective-permute-start.15
  171.7 1.9 collective-permute-done.14
  173.7 1.0 pad_maximum_fusion.30
  174.7 1.3 collective-permute-start.16
  176.0 4.0 %collective-permute-start.17 = (f32[8,11,128]{2,1,0:T(8,128)S(1)}, f32[8,11,128]{2,1,0:T(8,128)S(1)}, u32[]{:S(2)}, u32[]{:S(2)}) collective-permute-start(f32[8,11,128]{2,1,0:T(8,128)S(1)} %get-tuple-element.97), channel_id=1, source_target_pairs={{0,8},{8,16},{16,24},{1,9},{9,17},{17,25},{2,10},{10,18},{18,26},{... | collective-permute-start | bytes 135176 | tf_op jit(solution)/shard_map/ppermute | solution.py:475
  180.0 1.3 collective-permute-done.17
  181.3 1.0 pad_maximum_fusion.23
  182.3 1.3 collective-permute-start.19
  183.6 4.0 %collective-permute-start.18 = (f32[8,40,128]{2,1,0:T(8,128)S(1)}, f32[8,40,128]{2,1,0:T(8,128)S(1)}, u32[]{:S(2)}, u32[]{:S(2)}) collective-permute-start(f32[8,40,128]{2,1,0:T(8,128)S(1)} %pad_maximum_fusion.23), channel_id=1, source_target_pairs={{0,32},{32,64},{64,96},{96,128},{128,160},{160,192},{192,224},{224... | collective-permute-start | bytes 491528 | tf_op jit(solution)/shard_map/ppermute | solution.py:475
  187.6 0.8 collective-permute-done.19
  188.4 1.5 collective-permute-done.18
  190.0 0.8 pad.4.refs_0_.g1
  190.8 6.2 %again.1 = (f32[16,8,128]{2,1,0:T(8,128)}, f32[12,24,128]{2,1,0:T(8,128)}) custom-call(f32[26,40,128]{2,1,0:T(8,128)} %pad.4.refs_0_.g1, f32[26,40,128]{2,1,0:T(8,128)} %pad_maximum_fusion.11.refs_1_.k1, f32[26,40,128]{2,1,0:T(8,128)} %get-tuple-element.28.d1.refs_2_, f32[12,24,128]{2,1,0:T(8,128)} %get-tuple-element.26.k2.refs_3_, ...), custom_call_target="tpu_custom_call" | custom-call | tf_op jit(solution)/shard_map/again/pallas_call | solution.py:456
  197.0 18.3 %all_to_all.20.s = f32[16,8,128]{2,1,0:T(8,128)} all-to-all(f32[16,8,128]{2,1,0:T(8,128)} %get-tuple-element.31), channel_id=1, replica_groups=mesh['gx'=16,'gy'=4,'gz'=8] {'gx'}, dimensions={0} | all-to-all | bytes 131072 | tf_op jit(solution)/shard_map/all_to_all | solution.py:511
  215.4 1.7 repack2.1
  217.0 20.3 %all_to_all.21.s = f32[32,2,8,128]{3,2,1,0:T(8,128)} all-to-all(f32[32,2,8,128]{3,2,1,0:T(8,128)} %repack2.1), channel_id=1, replica_groups=mesh['gx'=16,'gy'=4,'gz'=8] {'gy','gz'}, dimensions={0} | all-to-all | bytes 524288 | tf_op jit(solution)/shard_map/all_to_all | solution.py:511
  237.3 18.9 %final.1 = (f32[16,32,128]{2,1,0:T(8,128)}, f32[16,32,128]{2,1,0:T(8,128)}) custom-call(s32[3]{0:T(128)} %pad_add_fusion.index, f32[26,48,256]{2,1,0:T(8,128)} %get-tuple-element.47.f.f_, f32[26,48,256]{2,1,0:T(8,128)} %get-tuple-element.18.wx_, f32[26,48,256]{2,1,0:T(8,128)} %get-tuple-element.19.wy_, f32[26,48,256]{2,1,0:T(8,128)} %get-tuple-element.20.wz_, ...), custom_call_target="tpu_custom_call" | custom-call | tf_op jit(solution)/shard_map/final/pallas_call | solution.py:456
  (81 shorter events, 3.2 us)
Async XLA Ops:
  0.6 1.4 copy-start
  2.5 8.0 %collective-permute-start = (f32[16,32,10]{2,1,0:T(8,128)S(1)}, f32[16,32,10]{2,1,0:T(8,128)S(1)}, u32[]{:S(2)}, u32[]{:S(2)}) collective-permute-start(f32[16,32,10]{2,1,0:T(8,128)S(1)} %copy.28), channel_id=1, source_target_pairs={{1,0},{2,1},{3,2},{4,3},{5,4},{6,5},{7,6},{0,7},{9,8},{10,9},{11,1... | collective-permute-start | bytes 61448 | tf_op jit(solution)/shard_map/ppermute | solution.py:476
  10.0 3.3 %collective-permute-start.1 = (f32[16,32,10]{2,1,0:T(8,128)S(1)}, f32[16,32,10]{2,1,0:T(8,128)S(1)}, u32[]{:S(2)}, u32[]{:S(2)}) collective-permute-start(f32[16,32,10]{2,1,0:T(8,128)S(1)} %copy.31), channel_id=1, source_target_pairs={{0,1},{1,2},{2,3},{3,4},{4,5},{5,6},{6,7},{7,0},{8,9},{9,10},{10,1... | collective-permute-start | bytes 61448 | tf_op jit(solution)/shard_map/ppermute | solution.py:475
  10.6 2.9 %copy-start.1 = (f32[16,32,128]{2,1,0:T(8,128)S(1)}, f32[16,32,128]{2,1,0:T(8,128)}, u32[]{:S(2)}) copy-start(f32[16,32,128]{2,1,0:T(8,128)} %param.24) | copy-start | bytes 786436
  13.9 4.6 %collective-permute-start.3 = (f32[32,5,256]{2,1,0:T(8,128)S(1)}, f32[32,5,256]{2,1,0:T(8,128)S(1)}, u32[]{:S(2)}, u32[]{:S(2)}) collective-permute-start(f32[32,5,256]{2,1,0:T(8,128)S(1)} %pad_maximum_fusion.20), channel_id=1, source_target_pairs={{0,8},{8,16},{16,24},{1,9},{9,17},{17,25},{2,10},{10,18},{18,26},{... | collective-permute-start | bytes 491528 | tf_op jit(solution)/shard_map/ppermute | solution.py:475
  15.2 7.1 %collective-permute-start.2 = (f32[32,5,256]{2,1,0:T(8,128)S(1)}, f32[32,5,256]{2,1,0:T(8,128)S(1)}, u32[]{:S(2)}, u32[]{:S(2)}) collective-permute-start(f32[32,5,256]{2,1,0:T(8,128)S(1)} %pad_maximum_fusion.19), channel_id=1, source_target_pairs={{8,0},{16,8},{24,16},{9,1},{17,9},{25,17},{10,2},{18,10},{26,18},{... | collective-permute-start | bytes 491528 | tf_op jit(solution)/shard_map/ppermute | solution.py:476
  22.9 9.6 %collective-permute-start.5 = (f32[10,48,256]{2,1,0:T(8,128)S(1)}, f32[10,48,256]{2,1,0:T(8,128)S(1)}, u32[]{:S(2)}, u32[]{:S(2)}) collective-permute-start(f32[10,48,256]{2,1,0:T(8,128)S(1)} %pad_maximum_fusion.13), channel_id=1, source_target_pairs={{32,0},{64,32},{96,64},{128,96},{160,128},{192,160},{224,192},{256... | collective-permute-start | bytes 1474568 | tf_op jit(solution)/shard_map/ppermute | solution.py:476
  24.2 9.8 %collective-permute-start.4 = (f32[10,48,256]{2,1,0:T(8,128)S(1)}, f32[10,48,256]{2,1,0:T(8,128)S(1)}, u32[]{:S(2)}, u32[]{:S(2)}) collective-permute-start(f32[10,48,256]{2,1,0:T(8,128)S(1)} %pad_maximum_fusion.12), channel_id=1, source_target_pairs={{0,32},{32,64},{64,96},{96,128},{128,160},{160,192},{192,224},{224... | collective-permute-start | bytes 1474568 | tf_op jit(solution)/shard_map/ppermute | solution.py:475
  44.1 14.6 %copy-start.4 = (f32[10,16,128]{2,1,0:T(8,128)S(1)}, f32[10,16,128]{2,1,0:T(8,128)}, u32[]{:S(2)}) copy-start(f32[10,16,128]{2,1,0:T(8,128)} %get-tuple-element.22) | copy-start | bytes 245764
  44.2 14.6 %copy-start.5 = (f32[10,16,128]{2,1,0:T(8,128)S(1)}, f32[10,16,128]{2,1,0:T(8,128)}, u32[]{:S(2)}) copy-start(f32[10,16,128]{2,1,0:T(8,128)} %get-tuple-element.23) | copy-start | bytes 245764
  46.4 9.7 %collective-permute-start.7 = (f32[10,16,22]{2,1,0:T(8,128)S(1)}, f32[10,16,22]{2,1,0:T(8,128)S(1)}, u32[]{:S(2)}, u32[]{:S(2)}) collective-permute-start(f32[10,16,22]{2,1,0:T(8,128)S(1)} %pad_maximum_fusion.29), channel_id=1, source_target_pairs={{0,1},{1,2},{2,3},{3,4},{4,5},{5,6},{6,7},{7,0},{8,9},{9,10},{10,1... | collective-permute-start | bytes 42248 | tf_op jit(solution)/shard_map/ppermute | solution.py:475
  54.8 3.9 %collective-permute-start.6 = (f32[10,16,22]{2,1,0:T(8,128)S(1)}, f32[10,16,22]{2,1,0:T(8,128)S(1)}, u32[]{:S(2)}, u32[]{:S(2)}) collective-permute-start(f32[10,16,22]{2,1,0:T(8,128)S(1)} %pad_maximum_fusion.28), channel_id=1, source_target_pairs={{1,0},{2,1},{3,2},{4,3},{5,4},{6,5},{7,6},{0,7},{9,8},{10,9},{11,1... | collective-permute-start | bytes 42248 | tf_op jit(solution)/shard_map/ppermute | solution.py:476
  59.0 6.7 %collective-permute-start.9 = (f32[20,11,128]{2,1,0:T(8,128)S(1)}, f32[20,11,128]{2,1,0:T(8,128)S(1)}, u32[]{:S(2)}, u32[]{:S(2)}) collective-permute-start(f32[20,11,128]{2,1,0:T(8,128)S(1)} %pad_maximum_fusion.22), channel_id=1, source_target_pairs={{0,8},{8,16},{16,24},{1,9},{9,17},{17,25},{2,10},{10,18},{18,26},{... | collective-permute-start | bytes 337928 | tf_op jit(solution)/shard_map/ppermute | solution.py:475
  62.2 7.3 %collective-permute-start.8 = (f32[20,11,128]{2,1,0:T(8,128)S(1)}, f32[20,11,128]{2,1,0:T(8,128)S(1)}, u32[]{:S(2)}, u32[]{:S(2)}) collective-permute-start(f32[20,11,128]{2,1,0:T(8,128)S(1)} %pad_maximum_fusion.21), channel_id=1, source_target_pairs={{8,0},{16,8},{24,16},{9,1},{17,9},{25,17},{10,2},{18,10},{26,18},{... | collective-permute-start | bytes 337928 | tf_op jit(solution)/shard_map/ppermute | solution.py:476
  69.8 11.8 %collective-permute-start.11 = (f32[18,40,128]{2,1,0:T(8,128)S(1)}, f32[18,40,128]{2,1,0:T(8,128)S(1)}, u32[]{:S(2)}, u32[]{:S(2)}) collective-permute-start(f32[18,40,128]{2,1,0:T(8,128)S(1)} %pad_maximum_fusion.16), channel_id=1, source_target_pairs={{32,0},{64,32},{96,64},{128,96},{160,128},{192,160},{224,192},{256... | collective-permute-start | bytes 1105928 | tf_op jit(solution)/shard_map/ppermute | solution.py:476
  71.2 11.4 %collective-permute-start.10 = (f32[18,40,128]{2,1,0:T(8,128)S(1)}, f32[18,40,128]{2,1,0:T(8,128)S(1)}, u32[]{:S(2)}, u32[]{:S(2)}) collective-permute-start(f32[18,40,128]{2,1,0:T(8,128)S(1)} %pad_maximum_fusion.15), channel_id=1, source_target_pairs={{0,32},{32,64},{64,96},{96,128},{128,160},{160,192},{192,224},{224... | collective-permute-start | bytes 1105928 | tf_op jit(solution)/shard_map/ppermute | solution.py:475
  92.2 29.6 %all-to-all-start = ((f32[16,8,128]{2,1,0:T(8,128)}), f32[16,8,128]{2,1,0:T(8,128)S(1)}, u32[]{:S(2)}, u32[]{:S(2)}) async-start(f32[16,8,128]{2,1,0:T(8,128)} %get-tuple-element.24), calls=%async_computation | async-start | bytes 131072 | tf_op jit(solution)/shard_map/all_to_all | solution.py:511
  121.8 0.6 copy-start.6
  124.3 20.5 %all-to-all-start.1 = ((f32[32,4,8,128]{3,2,1,0:T(8,128)}), f32[32,4,8,128]{3,2,1,0:T(8,128)S(1)}, u32[]{:S(2)}, u32[]{:S(2)}) async-start(f32[32,4,8,128]{3,2,1,0:T(8,128)} %repack.1), calls=%async_computation.1 | async-start | bytes 1048576 | tf_op jit(solution)/shard_map/all_to_all | solution.py:511
  133.9 4.5 %collective-permute-start.12 = (f32[2,24,128]{2,1,0:T(8,128)S(1)}, f32[2,24,128]{2,1,0:T(8,128)S(1)}, u32[]{:S(2)}, u32[]{:S(2)}) collective-permute-start(f32[2,24,128]{2,1,0:T(8,128)S(1)} %pad_maximum_fusion.31), channel_id=1, source_target_pairs={{0,32},{32,64},{64,96},{96,128},{128,160},{160,192},{192,224},{224... | collective-permute-start | bytes 73736 | tf_op jit(solution)/shard_map/ppermute | solution.py:475
  136.3 4.9 %collective-permute-start.13 = (f32[2,24,128]{2,1,0:T(8,128)S(1)}, f32[2,24,128]{2,1,0:T(8,128)S(1)}, u32[]{:S(2)}, u32[]{:S(2)}) collective-permute-start(f32[2,24,128]{2,1,0:T(8,128)S(1)} %pad_maximum_fusion.32), channel_id=1, source_target_pairs={{32,0},{64,32},{96,64},{128,96},{160,128},{192,160},{224,192},{256... | collective-permute-start | bytes 73736 | tf_op jit(solution)/shard_map/ppermute | solution.py:476
  138.4 6.4 %copy-start.7 = (f32[2,24,128]{2,1,0:T(8,128)}, f32[2,24,128]{2,1,0:T(8,128)S(1)}, u32[]{:S(2)}) copy-start(f32[2,24,128]{2,1,0:T(8,128)S(1)} %collective-permute-done.12.refs_0_) | copy-start | bytes 73732
  141.2 3.6 %copy-start.8 = (f32[2,24,128]{2,1,0:T(8,128)}, f32[2,24,128]{2,1,0:T(8,128)S(1)}, u32[]{:S(2)}) copy-start(f32[2,24,128]{2,1,0:T(8,128)S(1)} %collective-permute-done.13.refs_1_) | copy-start | bytes 73732
  144.8 0.8 copy-start.2
  168.9 20.9 %copy-start.3 = (f32[8,16,128]{2,1,0:T(8,128)S(1)}, f32[8,16,128]{2,1,0:T(8,128)}, u32[]{:S(2)}) copy-start(f32[8,16,128]{2,1,0:T(8,128)} %get-tuple-element.30) | copy-start | bytes 196612
  170.0 3.7 %collective-permute-start.14 = (f32[8,16,11]{2,1,0:T(8,128)S(1)}, f32[8,16,11]{2,1,0:T(8,128)S(1)}, u32[]{:S(2)}, u32[]{:S(2)}) collective-permute-start(f32[8,16,11]{2,1,0:T(8,128)S(1)} %get-tuple-element.98), channel_id=1, source_target_pairs={{1,0},{2,1},{3,2},{4,3},{5,4},{6,5},{7,6},{0,7},{9,8},{10,9},{11,1... | collective-permute-start | bytes 16904 | tf_op jit(solution)/shard_map/ppermute | solution.py:476
  170.0 3.7 %collective-permute-start.15 = (f32[8,16,11]{2,1,0:T(8,128)S(1)}, f32[8,16,11]{2,1,0:T(8,128)S(1)}, u32[]{:S(2)}, u32[]{:S(2)}) collective-permute-start(f32[8,16,11]{2,1,0:T(8,128)S(1)} %get-tuple-element.99), channel_id=1, source_target_pairs={{0,1},{1,2},{2,3},{3,4},{4,5},{5,6},{6,7},{7,0},{8,9},{9,10},{10,1... | collective-permute-start | bytes 16904 | tf_op jit(solution)/shard_map/ppermute | solution.py:475
  174.7 5.3 %collective-permute-start.16 = (f32[8,11,128]{2,1,0:T(8,128)S(1)}, f32[8,11,128]{2,1,0:T(8,128)S(1)}, u32[]{:S(2)}, u32[]{:S(2)}) collective-permute-start(f32[8,11,128]{2,1,0:T(8,128)S(1)} %get-tuple-element.96), channel_id=1, source_target_pairs={{8,0},{16,8},{24,16},{9,1},{17,9},{25,17},{10,2},{18,10},{26,18},{... | collective-permute-start | bytes 135176 | tf_op jit(solution)/shard_map/ppermute | solution.py:476
  176.0 5.3 %collective-permute-start.17 = (f32[8,11,128]{2,1,0:T(8,128)S(1)}, f32[8,11,128]{2,1,0:T(8,128)S(1)}, u32[]{:S(2)}, u32[]{:S(2)}) collective-permute-start(f32[8,11,128]{2,1,0:T(8,128)S(1)} %get-tuple-element.97), channel_id=1, source_target_pairs={{0,8},{8,16},{16,24},{1,9},{9,17},{17,25},{2,10},{10,18},{18,26},{... | collective-permute-start | bytes 135176 | tf_op jit(solution)/shard_map/ppermute | solution.py:475
  182.3 6.1 %collective-permute-start.19 = (f32[8,40,128]{2,1,0:T(8,128)S(1)}, f32[8,40,128]{2,1,0:T(8,128)S(1)}, u32[]{:S(2)}, u32[]{:S(2)}) collective-permute-start(f32[8,40,128]{2,1,0:T(8,128)S(1)} %pad_maximum_fusion.23), channel_id=1, source_target_pairs={{32,0},{64,32},{96,64},{128,96},{160,128},{192,160},{224,192},{256... | collective-permute-start | bytes 491528 | tf_op jit(solution)/shard_map/ppermute | solution.py:476
  183.6 6.2 %collective-permute-start.18 = (f32[8,40,128]{2,1,0:T(8,128)S(1)}, f32[8,40,128]{2,1,0:T(8,128)S(1)}, u32[]{:S(2)}, u32[]{:S(2)}) collective-permute-start(f32[8,40,128]{2,1,0:T(8,128)S(1)} %pad_maximum_fusion.23), channel_id=1, source_target_pairs={{0,32},{32,64},{64,96},{96,128},{128,160},{160,192},{192,224},{224... | collective-permute-start | bytes 491528 | tf_op jit(solution)/shard_map/ppermute | solution.py:475

commit v4 on v3

--- a/solution.py
+++ b/solution.py
@@ -207,34 +207,57 @@
     return jnp.where(k > 0.0, value, 0.0)
 
 
-U0, U1, U2, U3 = 2, 2, 4, 4
-
-
-def down0(f, k, ry, rz, cy, cz, wx_, wy_, wz_, d_, g1, k1, wx, wy, wz, d, v, r, held, sem):
+U0, U1, U2, U3 = 6, 12, 10, 16
+
+
+def place(target, at, source, start, count, unroll=4):
+    def step(i, n, carry):
+        values = [source[start + i + j] for j in range(n)]
+        for j, value in enumerate(values):
+            target[at + i + j] = value
+        return carry
+
+    planes(0, count, step, unroll=unroll)
+
+
+def down0(before, fo, ko, after, ry, rz, cy, cz, f_, k_, wx_, wy_, wz_, d_, out, f, k, wx, wy, wz, d, v, r, held, sem):
     shifts = Open()
+    for ref, own, at in ((f, fo, 0), (k, ko, 5)):
+        place(ref, 0, before, at, 5, 5)
+        place(ref, 5, own, 0, 16)
+        place(ref, 21, after, at, 5, 5)
     weigh(k, wx, wy, wz, 1, 25, 1.0, shifts, d, inside, unroll=U0)
     copies = [
         pltpu.make_async_copy(here, there, sem.at[i])
-        for i, (here, there) in enumerate(((wx, wx_), (wy, wy_), (wz, wz_), (d, d_)))
+        for i, (here, there) in enumerate(((f, f_), (k, k_), (wx, wx_), (wy, wy_), (wz, wz_), (d, d_)))
     ]
     for copy in copies:
         copy.start()
     first_sweep(f, d, v, 1, 25, U0)
     residual_of(v, f, r, (wx, wy, wz), 2, 24, shifts, k, unroll=U0)
-    g1[...] = restrict(r, 5, -1, 9, ry, rz, held).reshape(g1.shape)
-    k1[...] = halve(k, 5, -1, 9, cy, cz, held).reshape(k1.shape)
+    out[:10] = restrict(r, 5, -1, 9, ry, rz, held).reshape(10, 16, 128)
+    out[10:] = halve(k, 5, -1, 9, cy, cz, held).reshape(10, 16, 128)
     for copy in copies:
         copy.wait()
 
 
 def descend(first, *refs):
     shifts = Open()
+    before, own, after = refs[:3]
     if first:
-        g1, k1, ry1, rz1, ry2, rz2, cy1, cz1, cy2, cz2 = refs[:10]
-        out, d1, g2, k2, d2 = refs[10:15]
+        ry1, rz1, ry2, rz2, cy1, cz1, cy2, cz2 = refs[3:11]
+        out, g1, k1, d1, g2, k2, d2 = refs[11:18]
+        for ref, at in ((g1, 0), (k1, 1)):
+            place(ref, 0, before, 9 * at, 9, 9)
+            place(ref, 9, own, 10 * at + 1, 8, 8)
+            place(ref, 17, after, 9 * at, 9, 9)
     else:
-        g1, k1, d1, k2, d2, ry1, rz1, ry2, rz2 = refs[:9]
-        out, g2 = refs[9:11]
+        k1, d1, k2, d2, ry1, rz1, ry2, rz2 = refs[3:11]
+        out, g1, g2 = refs[11:14]
+        zero = jnp.zeros(g1.shape[1:], F32)
+        g1[0], g1[25] = zero, zero
+        for ref, at in ((before, 1), (own, 9), (after, 17)):
+            place(g1, at, ref, 0, 8, 8)
     v1, r1, held, w1, v2, r2, w2, part = refs[-8:]
     w1, w2 = three(w1), three(w2)
     rows = g2.shape[1]
@@ -402,8 +425,8 @@
 
 
 def middle(nz, index, f_, wx_, wy_, wz_, d_, k_, s, g2, k2, d2, g1, k1, d1, *refs):
-    ends, m3, m1, (py0, pz0, ry, rz), (v_, gn, k3) = refs[:2], refs[2:8], refs[8:10], refs[10:14], refs[14:17]
-    low, mid, (fine0, r, held0, f, wx, wy, wz, d, k, v, sem) = refs[17:31], refs[31:38], refs[38:]
+    ends, m3, m1, (py0, pz0, ry, rz), (v_, gn, turned, k3) = refs[:2], refs[2:8], refs[8:10], refs[10:14], refs[14:18]
+    low, mid, (fine0, r, held0, f, wx, wy, wz, d, k, v, sem) = refs[18:32], refs[32:39], refs[39:]
     copies = fetch((f_, wx_, wy_, wz_, d_, k_), (f, wx, wy, wz, d, k), sem)
     e3 = bottom(nz, s, k3, low, m3)
     e1 = upward(index, e3, g2, k2, d2, g1, k1, d1, ends, mid, m1)
@@ -420,7 +443,9 @@
     copy = pltpu.make_async_copy(v, v_, sem.at[0])
     copy.start()
     residual_of(v, f, r, w, 4, 22, shifts, k, unroll=U0)
-    gn[...] = restrict(r, 5, 0, 8, ry, rz, held0).reshape(gn.shape)
+    value = restrict(r, 5, 0, 8, ry, rz, held0)
+    gn[...] = value.reshape(gn.shape)
+    turned[...] = pltpu.roll(value, 64, 1).reshape(gn.shape)
     copy.wait()
 
 
@@ -481,30 +506,38 @@
     return before, after
 
 
-def exchange(fields, block, sizes, widths, extra=0):
-    count = len(fields)
-    for axis, dim in (("gz", 2), ("gy", 1), ("gx", 0)):
+def finest(fields):
+    for axis, dim, size, count, width in (("gz", 2, 128, 256, 25), ("gy", 1, 32, 48, 5)):
         along = 2 if dim == 2 else 0
-        size, width, shift = block[dim], widths[dim], extra if dim == 0 else 0
-        last = [lax.slice_in_dim(f, size + shift - width, size + shift, axis=dim) for f in fields]
-        initial = [lax.slice_in_dim(f, shift, shift + width, axis=dim) for f in fields]
+        last = [lax.slice_in_dim(v, size - width, size, axis=dim) for v in fields]
+        initial = [lax.slice_in_dim(v, 0, width, axis=dim) for v in fields]
         before, after = neighbours(
             jnp.concatenate(last, along), jnp.concatenate(initial, along), axis
         )
-        before = jnp.split(before, count, along)
-        after = jnp.split(after, count, along)
-        own = [lax.slice_in_dim(f, shift, shift + size, axis=dim) for f in fields]
-        if dim == 0:
-            fields = [jnp.concatenate([b, f, a], 0) for b, f, a in zip(before, own, after)]
-            continue
-        gap = list(own[0].shape)
-        gap[dim] = sizes[dim - 1] - size - 2 * width
-        parts = [[jnp.zeros(gap, F32)] if gap[dim] else []] * count
+        before, after = jnp.split(before, 2, along), jnp.split(after, 2, along)
+        gap = list(fields[0].shape)
+        gap[dim] = count - size - 2 * width
+        gap = jnp.zeros(gap, F32)
         fields = [
-            jnp.concatenate([f, a] + z + [b], dim)
-            for b, f, a, z in zip(before, own, after, parts)
+            jnp.concatenate([v, a, gap, b], dim) for b, v, a in zip(before, fields, after)
         ]
-    return fields
+    last = jnp.concatenate([v[11:] for v in fields])
+    initial = jnp.concatenate([v[:5] for v in fields])
+    before, after = neighbours(last, initial, "gx")
+    return before, *fields, after
+
+
+def rows1(values):
+    before, after = neighbours(values, values, "gy")
+    gap = jnp.zeros((values.shape[0], 2, 128), F32)
+    return jnp.concatenate([values, after[:, :11], gap, before[:, 5:]], 1)
+
+
+def lanes1(values, turned):
+    before, after = neighbours(turned, turned, "gz")
+    lane = jnp.arange(128)
+    zero = jnp.where(lane >= 117, before, 0.0)
+    return jnp.where(lane < 64, values, jnp.where(lane < 75, after, zero))
 
 
 def everyone(pieces, axes):
@@ -524,8 +557,8 @@
     y2, z2 = coords(24, 8), coords(128, 32)
     rows3, rows4 = np.arange(4 * ny), np.arange(2 * ny)
     lanes3, lanes4 = ends(128, 16 * nz, -3000), ends(128, 8 * nz, -9000)
-    ry0, rz0 = restriction(np.arange(16), y0), restriction(ends(128, 64), z0).T
-    cy0, cz0 = halving(np.arange(16), y0), halving(ends(128, 64), z0).T
+    ry0, rz0 = restriction(np.arange(16), y0), restriction(z1, z0).T
+    cy0, cz0 = halving(np.arange(16), y0), halving(z1, z0).T
     ry1, rz1 = restriction(y2, y1), restriction(z2, z1).T
     cy1, cz1 = halving(y2, y1), halving(z2, z1).T
 
@@ -552,18 +585,18 @@
     mid = [l2, (3,) + l2, l2, l1, (3,) + l1, (8, 24, 128), (10, 40, 128)]
     tiles = nx // 8
 
-    f, k = exchange([right_side, conductivity], (16, 32, 128), (48, 256), (5, 5, 5))
-    b1 = (10, 16, 128)
-    wx, wy, wz, d, g1, k1 = call(
-        down0, [wide] * 4 + [b1] * 2, [wide] * 6 + [(160, 256)],
-        f, k, ry0, rz0, cy0, cz0, name="down0", away=4, sems=4,
+    f, k, wx, wy, wz, d, both1 = call(
+        down0, [wide] * 6 + [(20, 16, 128)], [wide] * 8 + [(160, 256)],
+        *finest([right_side, conductivity]), ry0, rz0, cy0, cz0, name="down0", away=6, sems=6,
     )
-    size1 = ((8, 16, 64), (40, 128))
-    g1, k1 = exchange([g1, k1], *size1, (9, 11, 11), 1)
+    own = rows1(both1)
+    last = jnp.concatenate([own[0:9], own[10:19]])
+    initial = jnp.concatenate([own[1:10], own[11:20]])
+    before, after = neighbours(last, initial, "gx")
     inner = [l1, l1, (288, 128), (3,) + l1, l2, l2, (3,) + l2, (8, 128)]
-    pieces, d1, g2, k2, d2 = call(
-        functools.partial(descend, True), [(nx, 8, 128), l1, l2, l2, l2], inner,
-        g1, k1, ry1, rz1, ry2, rz2, cy1, cz1, cy2, cz2, name="descend",
+    pieces, g1, k1, d1, g2, k2, d2 = call(
+        functools.partial(descend, True), [(nx, 8, 128), l1, l1, l1, l2, l2, l2], inner,
+        before, own, after, ry1, rz1, ry2, rz2, cy1, cz1, cy2, cz2, name="descend",
     )
     first, last = jnp.stack([g2[4], d2[4]]), jnp.stack([g2[7], d2[7]])
     outer = neighbours(first, last, "gx")
@@ -571,17 +604,17 @@
     (pieces,) = call(repack, [(ny * nz, 2 * tiles, 8, 128)], [], pieces, name="repack")
     s = everyone(pieces, ("gy", "gz"))
     fields = (f, wx, wy, wz, d, k)
-    v, g1b, k3 = call(
-        functools.partial(middle, nz), [wide, (8, 16, 128), n3],
+    v, value, turned, k3 = call(
+        functools.partial(middle, nz), [wide, (8, 16, 128), (8, 16, 128), n3],
         low + mid + [(14, 48, 256), wide, (128, 256)] + [wide] * 7,
         index, *fields, s, g2, k2, d2, g1, k1, d1, *outer, *m3, *m1, py0, pz0, ry0, rz0,
         name="middle", scalars=1, loose=6, away=1, sems=6,
     )
-    (g1,) = exchange([g1b], *size1, (8, 11, 11))
-    g1 = jnp.pad(g1, ((1, 1), (0, 0), (0, 0)))
-    pieces, g2 = call(
-        functools.partial(descend, False), [(nx, 8, 128), l2], inner,
-        g1, k1, d1, k2, d2, ry1, rz1, ry2, rz2, name="again",
+    own = rows1(lanes1(value, turned))
+    before, after = neighbours(own, own, "gx")
+    pieces, g1, g2 = call(
+        functools.partial(descend, False), [(nx, 8, 128), l1, l2], inner,
+        before, own, after, k1, d1, k2, d2, ry1, rz1, ry2, rz2, name="again",
     )
     pieces = everyone(pieces, "gx")
     (pieces,) = call(repack, [(ny * nz, tiles, 8, 128)], [], pieces, name="repack2")

time: 258 us -> 227 us (0.88)
  Pallas kernels: 68.2 us -> 47.5 us
  starting transfers between devices: 76.5 us -> 66.8 us
  waiting for transfers between devices: 53.6 us -> 58.8 us
  other arithmetic: 7.77 us -> 3.66 us
    pallas_call x7, Pallas kernels: 68.2 us -> 47.5 us  [call(): pl.pallas_call(kernel, out_shape=[jax.ShapeDtypeStruct(o, F32) for o in o...]
    ppermute x10 -> x9, starting transfers between devices: 33.6 us -> 26.3 us  [neighbours(): before = lax.ppermute(last, axis, up)]
    concatenate x22 -> x12, other arithmetic: 7.04 us -> 2.18 us  [the longest x2 1.09 us: rows1(): return jnp.concatenate([values, after[:, :11], gap, before[:, 5:]], 1)]
    ppermute x10 -> x9, waiting for transfers between devices: 13.2 us -> 17 us  [neighbours(): before = lax.ppermute(last, axis, up)]
    slice x15 -> x8, local copies, waits for them, and re-layouts: 4.73 us -> 1.59 us  [the longest x3 1.45 us: finest(): initial = [lax.slice_in_dim(v, 0, width, axis=dim) for v in fields]]
    unnamed x22 -> x32, local copies, waits for them, and re-layouts: 2.13 us -> 4.85 us
    ppermute x10 -> x9, starting transfers between devices: 16.1 us -> 13.8 us  [neighbours(): after = lax.ppermute(initial, axis, down)]
    ppermute x10 -> x9, waiting for transfers between devices: 25.9 us -> 27.5 us  [neighbours(): after = lax.ppermute(initial, axis, down)]
  transfers between devices with their start and end apart: 22 -> 20, of which waited for: 19 -> 18; matrix products, arithmetic and copies ran while one was open for 1% -> 1% of each run, Pallas kernels for 0% -> 0%
where the time goes in v4:
time: 227 us; the launch traced here: 226 us
  starting transfers between devices  66.8 us (29%)
  waiting for transfers between devices  58.8 us (26%)
  Pallas kernels  47.5 us (21%)
  blocking collectives  39.1 us (17%)
  local copies, waits for them, and re-layouts  8.38 us (4%)
  other arithmetic  3.66 us (2%)
    pallas_call x7, Pallas kernels, call(): pl.pallas_call(kernel, out_shape=[jax.ShapeDtypeStruct(o, F32) for o in o...  47.5 us
    all_to_all x2, blocking collectives, everyone(): return lax.all_to_all(pieces, axes, 0, 0)  39.1 us
    ppermute x9, waiting for transfers between devices, neighbours(): after = lax.ppermute(initial, axis, down)  27.5 us
    all_to_all x2, starting transfers between devices, everyone(): return lax.all_to_all(pieces, axes, 0, 0)  26.7 us
    ppermute x9, starting transfers between devices, neighbours(): before = lax.ppermute(last, axis, up)  26.3 us
    ppermute x9, waiting for transfers between devices, neighbours(): before = lax.ppermute(last, axis, up)  17 us
    all_to_all x2, waiting for transfers between devices, everyone(): return lax.all_to_all(pieces, axes, 0, 0)  14.3 us
    ppermute x9, starting transfers between devices, neighbours(): after = lax.ppermute(initial, axis, down)  13.8 us
  transfers between devices with their start and end apart: 20, of which 18 were waited for; matrix products, arithmetic and copies ran while one was open for 1% of the time, Pallas kernels for 0%

profile of v4, /device:TPU:1, one launch (start us, length us, event | category | flops | bytes accessed | tf_op | source)
XLA Modules:
  0.0 225.5 jit_solution(10585791891723238158)
XLA Ops:
  0.6 1.4 fusion.19
  2.0 0.1 pad_maximum_fusion.10
  2.2 2.7 %collective-permute-start.1 = (f32[16,32,50]{2,1,0:T(8,128)S(1)}, f32[16,32,50]{2,1,0:T(8,128)S(1)}, u32[]{:S(2)}, u32[]{:S(2)}) collective-permute-start(f32[16,32,50]{2,1,0:T(8,128)S(1)} %pad_maximum_fusion.10), channel_id=1, source_target_pairs={{0,1},{1,2},{2,3},{3,4},{4,5},{5,6},{6,7},{7,0},{8,9},{9,10},{10,1... | collective-permute-start | bytes 307208 | tf_op jit(solution)/shard_map/ppermute | solution.py:500
  4.9 0.1 pad_maximum_fusion.9
  5.0 4.2 %collective-permute-start = (f32[16,32,50]{2,1,0:T(8,128)S(1)}, f32[16,32,50]{2,1,0:T(8,128)S(1)}, u32[]{:S(2)}, u32[]{:S(2)}) collective-permute-start(f32[16,32,50]{2,1,0:T(8,128)S(1)} %pad_maximum_fusion.9), channel_id=1, source_target_pairs={{1,0},{2,1},{3,2},{4,3},{5,4},{6,5},{7,6},{0,7},{9,8},{10,9},{11,1... | collective-permute-start | bytes 307208 | tf_op jit(solution)/shard_map/ppermute | solution.py:501
  9.2 0.9 collective-permute-done.1
  10.3 0.5 collective-permute-done
  11.2 0.3 fusion.8
  11.6 3.0 %collective-permute-start.3 = (f32[32,5,256]{2,1,0:T(8,128)S(1)}, f32[32,5,256]{2,1,0:T(8,128)S(1)}, u32[]{:S(2)}, u32[]{:S(2)}) collective-permute-start(f32[32,5,256]{2,1,0:T(8,128)S(1)} %pad_maximum_fusion.12), channel_id=1, source_target_pairs={{0,8},{8,16},{16,24},{1,9},{9,17},{17,25},{2,10},{10,18},{18,26},{... | collective-permute-start | bytes 491528 | tf_op jit(solution)/shard_map/ppermute | solution.py:500
  14.7 1.3 collective-permute-start.2
  16.0 1.9 collective-permute-done.3
  17.9 3.9 %collective-permute-done.2 = f32[32,5,256]{2,1,0:T(8,128)S(1)} collective-permute-done((f32[32,5,256]{2,1,0:T(8,128)S(1)}, f32[32,5,256]{2,1,0:T(8,128)S(1)}, u32[]{:S(2)}, u32[]{:S(2)}) %collective-permute-start.2) | collective-permute-done | bytes 163872 | tf_op jit(solution)/shard_map/ppermute | solution.py:501
  21.8 0.3 fusion.3
  22.3 0.8 copy-done.1
  23.1 0.2 copy-done.2
  23.4 5.1 %collective-permute-start.4 = (f32[10,48,256]{2,1,0:T(8,128)S(1)}, f32[10,48,256]{2,1,0:T(8,128)S(1)}, u32[]{:S(2)}, u32[]{:S(2)}) collective-permute-start(f32[10,48,256]{2,1,0:T(8,128)S(1)} %pad_maximum_fusion.4), channel_id=1, source_target_pairs={{0,32},{32,64},{64,96},{96,128},{128,160},{160,192},{192,224},{224... | collective-permute-start | bytes 1474568 | tf_op jit(solution)/shard_map/ppermute | solution.py:500
  28.6 1.3 collective-permute-start.5
  29.9 7.2 %collective-permute-done.4.before = f32[10,48,256]{2,1,0:T(8,128)S(1)} collective-permute-done((f32[10,48,256]{2,1,0:T(8,128)S(1)}, f32[10,48,256]{2,1,0:T(8,128)S(1)}, u32[]{:S(2)}, u32[]{:S(2)}) %collective-permute-start.4) | collective-permute-done | bytes 491552 | tf_op jit(solution)/shard_map/ppermute | solution.py:500
  37.1 4.2 %collective-permute-done.5.after = f32[10,48,256]{2,1,0:T(8,128)S(1)} collective-permute-done((f32[10,48,256]{2,1,0:T(8,128)S(1)}, f32[10,48,256]{2,1,0:T(8,128)S(1)}, u32[]{:S(2)}, u32[]{:S(2)}) %collective-permute-start.5) | collective-permute-done | bytes 491552 | tf_op jit(solution)/shard_map/ppermute | solution.py:501
  41.3 0.8 copy-done.8
  42.1 6.6 %down0.1 = (f32[26,48,256]{2,1,0:T(8,128)}, f32[26,48,256]{2,1,0:T(8,128)}, f32[26,48,256]{2,1,0:T(8,128)}, f32[26,48,256]{2,1,0:T(8,128)}, f32[26,48,256]{2,1,0...) custom-call(f32[10,48,256]{2,1,0:T(8,128)} %copy-done.7, f32[16,48,256]{2,1,0:T(8,128)} %copy-done.1, ...), custom_call_target="tpu_custom_call" | custom-call | tf_op jit(solution)/shard_map/down0/pallas_call | solution.py:481
  48.8 3.1 %collective-permute-start.7 = (f32[20,16,128]{2,1,0:T(8,128)}, f32[20,16,128]{2,1,0:T(8,128)S(1)}, u32[]{:S(2)}, u32[]{:S(2)}) collective-permute-start(f32[20,16,128]{2,1,0:T(8,128)} %get-tuple-element.29), channel_id=1, source_target_pairs={{0,8},{8,16},{16,24},{1,9},{9,17},{17,25},{2,10},{10,18},{18,26},{... | collective-permute-start | bytes 491528 | tf_op jit(solution)/shard_map/ppermute | solution.py:500
  51.9 1.3 collective-permute-start.6
  53.3 1.2 collective-permute-done.7
  54.4 3.7 %collective-permute-done.6 = f32[20,16,128]{2,1,0:T(8,128)S(1)} collective-permute-done((f32[20,16,128]{2,1,0:T(8,128)}, f32[20,16,128]{2,1,0:T(8,128)S(1)}, u32[]{:S(2)}, u32[]{:S(2)}) %collective-permute-start.6) | collective-permute-done | bytes 163872 | tf_op jit(solution)/shard_map/ppermute | solution.py:501
  58.2 1.0 pad_maximum_fusion.6.refs_1_
  59.3 3.6 %collective-permute-start.8 = (f32[18,40,128]{2,1,0:T(8,128)S(1)}, f32[18,40,128]{2,1,0:T(8,128)S(1)}, u32[]{:S(2)}, u32[]{:S(2)}) collective-permute-start(f32[18,40,128]{2,1,0:T(8,128)S(1)} %pad_maximum_fusion.7), channel_id=1, source_target_pairs={{0,32},{32,64},{64,96},{96,128},{128,160},{160,192},{192,224},{224... | collective-permute-start | bytes 1105928 | tf_op jit(solution)/shard_map/ppermute | solution.py:500
  62.9 1.3 collective-permute-start.9
  64.2 3.1 %collective-permute-done.8.refs_0_ = f32[18,40,128]{2,1,0:T(8,128)S(1)} collective-permute-done((f32[18,40,128]{2,1,0:T(8,128)S(1)}, f32[18,40,128]{2,1,0:T(8,128)S(1)}, u32[]{:S(2)}, u32[]{:S(2)}) %collective-permute-start.8) | collective-permute-done | bytes 368672 | tf_op jit(solution)/shard_map/ppermute | solution.py:500
  67.3 5.4 %collective-permute-done.9.refs_2_ = f32[18,40,128]{2,1,0:T(8,128)S(1)} collective-permute-done((f32[18,40,128]{2,1,0:T(8,128)S(1)}, f32[18,40,128]{2,1,0:T(8,128)S(1)}, u32[]{:S(2)}, u32[]{:S(2)}) %collective-permute-start.9) | collective-permute-done | bytes 368672 | tf_op jit(solution)/shard_map/ppermute | solution.py:501
  72.7 0.7 copy-done.10
  73.4 4.9 %descend.1 = (f32[16,8,128]{2,1,0:T(8,128)}, f32[26,40,128]{2,1,0:T(8,128)}, f32[26,40,128]{2,1,0:T(8,128)}, f32[26,40,128]{2,1,0:T(8,128)}, f32[12,24,128]{2,1,...) custom-call(f32[18,40,128]{2,1,0:T(8,128)} %copy-done.9, f32[20,40,128]{2,1,0:T(8,128)} %copy-done, ...), custom_call_target="tpu_custom_call" | custom-call | tf_op jit(solution)/shard_map/descend/pallas_call | solution.py:481
  78.2 12.5 %all-to-all-start = ((f32[16,8,128]{2,1,0:T(8,128)}), f32[16,8,128]{2,1,0:T(8,128)S(1)}, u32[]{:S(2)}, u32[]{:S(2)}) async-start(f32[16,8,128]{2,1,0:T(8,128)} %get-tuple-element.30), calls=%async_computation | async-start | bytes 131072 | tf_op jit(solution)/shard_map/all_to_all | solution.py:544
  90.8 0.7 fusion.21
  91.5 10.8 %all-to-all-done.s = f32[16,8,128]{2,1,0:T(8,128)S(1)} async-done(((f32[16,8,128]{2,1,0:T(8,128)}), f32[16,8,128]{2,1,0:T(8,128)S(1)}, u32[]{:S(2)}, u32[]{:S(2)}) %all-to-all-start) | async-done | bytes 65568 | tf_op jit(solution)/shard_map/all_to_all | solution.py:544
  102.3 0.6 copy-done.11
  103.0 1.8 repack.1
  104.8 14.2 %all-to-all-start.1 = ((f32[32,4,8,128]{3,2,1,0:T(8,128)}), f32[32,4,8,128]{3,2,1,0:T(8,128)S(1)}, u32[]{:S(2)}, u32[]{:S(2)}) async-start(f32[32,4,8,128]{3,2,1,0:T(8,128)} %repack.1), calls=%async_computation.1 | async-start | bytes 1048576 | tf_op jit(solution)/shard_map/all_to_all | solution.py:544
  119.0 0.7 fusion.22
  119.7 2.5 %collective-permute-start.10 = (f32[2,24,128]{2,1,0:T(8,128)S(1)}, f32[2,24,128]{2,1,0:T(8,128)S(1)}, u32[]{:S(2)}, u32[]{:S(2)}) collective-permute-start(f32[2,24,128]{2,1,0:T(8,128)S(1)} %pad_maximum_fusion.14), channel_id=1, source_target_pairs={{0,32},{32,64},{64,96},{96,128},{128,160},{160,192},{192,224},{224... | collective-permute-start | bytes 73736 | tf_op jit(solution)/shard_map/ppermute | solution.py:500
  122.2 1.5 collective-permute-start.11
  123.7 0.6 pad_add_fusion.index
  124.3 2.8 %collective-permute-done.11.refs_1_ = f32[2,24,128]{2,1,0:T(8,128)S(1)} collective-permute-done((f32[2,24,128]{2,1,0:T(8,128)S(1)}, f32[2,24,128]{2,1,0:T(8,128)S(1)}, u32[]{:S(2)}, u32[]{:S(2)}) %collective-permute-start.11) | collective-permute-done | bytes 24608 | tf_op jit(solution)/shard_map/ppermute | solution.py:501
  127.1 3.5 %all-to-all-done.1.s = f32[32,4,8,128]{3,2,1,0:T(8,128)S(1)} async-done(((f32[32,4,8,128]{3,2,1,0:T(8,128)}), f32[32,4,8,128]{3,2,1,0:T(8,128)S(1)}, u32[]{:S(2)}, u32[]{:S(2)}) %all-to-all-start.1) | async-done | bytes 524320 | tf_op jit(solution)/shard_map/all_to_all | solution.py:544
  130.6 0.8 copy-done.5
  131.4 16.2 %middle.1 = (f32[26,48,256]{2,1,0:T(8,128)}, f32[8,16,128]{2,1,0:T(8,128)}, f32[8,16,128]{2,1,0:T(8,128)}, f32[38,16,128]{2,1,0:T(8,128)}) custom-call(s32[3]{0:T(128)} %pad_add_fusion.index, f32[26,48,256]{2,1,0:T(8,128)} %get-tuple-element.23.f_, f32[26,48,256]{2,1,0:T(8,128)} %get-tuple-element.24.wx_, f32[26,48,256]{2,1,0:T(8,128)} %get-tuple-element.25.wy_, ...), custom_call_target="tpu_custom_call" | custom-call | tf_op jit(solution)/shard_map/middle/pallas_call | solution.py:481
  147.5 0.2 collective-permute-start.13
  147.7 0.4 collective-permute-start.12
  148.1 1.3 collective-permute-done.13
  149.4 2.5 %collective-permute-done.12 = f32[8,16,128]{2,1,0:T(8,128)S(1)} collective-permute-done((f32[8,16,128]{2,1,0:T(8,128)}, f32[8,16,128]{2,1,0:T(8,128)S(1)}, u32[]{:S(2)}, u32[]{:S(2)}) %collective-permute-start.12) | collective-permute-done | bytes 65568 | tf_op jit(solution)/shard_map/ppermute | solution.py:501
  151.9 0.9 select_select_fusion
  152.8 2.1 collective-permute-start.15
  154.9 1.3 collective-permute-start.14
  156.2 3.7 %collective-permute-done.14 = f32[8,16,128]{2,1,0:T(8,128)S(1)} collective-permute-done((f32[8,16,128]{2,1,0:T(8,128)S(1)}, f32[8,16,128]{2,1,0:T(8,128)S(1)}, u32[]{:S(2)}, u32[]{:S(2)}) %collective-permute-start.14) | collective-permute-done | bytes 65568 | tf_op jit(solution)/shard_map/ppermute | solution.py:501
  160.0 1.3 collective-permute-start.17
  161.3 4.0 %collective-permute-start.16 = (f32[8,40,128]{2,1,0:T(8,128)S(1)}, f32[8,40,128]{2,1,0:T(8,128)S(1)}, u32[]{:S(2)}, u32[]{:S(2)}) collective-permute-start(f32[8,40,128]{2,1,0:T(8,128)S(1)} %pad_maximum_fusion.13.refs_1_), channel_id=1, source_target_pairs={{0,32},{32,64},{64,96},{96,128},{128,160},{160,192},{192,224},{224... | collective-permute-start | bytes 491528 | tf_op jit(solution)/shard_map/ppermute | solution.py:500
  165.3 0.8 collective-permute-done.17.refs_2_
  166.0 1.5 collective-permute-done.16.refs_0_
  167.5 0.7 copy-done.13
  168.2 4.0 %again.1 = (f32[16,8,128]{2,1,0:T(8,128)}, f32[26,40,128]{2,1,0:T(8,128)}, f32[12,24,128]{2,1,0:T(8,128)}) custom-call(f32[8,40,128]{2,1,0:T(8,128)} %copy-done.13, f32[8,40,128]{2,1,0:T(8,128)} %copy-done.6, f32[8,40,128]{2,1,0:T(8,128)} %copy-done.12, f32[26,40,128]{2,1,0:T(8,128)} %get-tuple-element.35.k1.refs_3_, ...), custom_call_target="tpu_custom_call" | custom-call | tf_op jit(solution)/shard_map/again/pallas_call | solution.py:481
  172.2 19.1 %all_to_all.20.s = f32[16,8,128]{2,1,0:T(8,128)} all-to-all(f32[16,8,128]{2,1,0:T(8,128)} %get-tuple-element.40), channel_id=1, replica_groups=mesh['gx'=16,'gy'=4,'gz'=8] {'gx'}, dimensions={0} | all-to-all | bytes 131072 | tf_op jit(solution)/shard_map/all_to_all | solution.py:544
  191.2 1.7 repack2.1
  192.9 20.1 %all_to_all.21.s = f32[32,2,8,128]{3,2,1,0:T(8,128)} all-to-all(f32[32,2,8,128]{3,2,1,0:T(8,128)} %repack2.1), channel_id=1, replica_groups=mesh['gx'=16,'gy'=4,'gz'=8] {'gy','gz'}, dimensions={0} | all-to-all | bytes 524288 | tf_op jit(solution)/shard_map/all_to_all | solution.py:544
  212.9 12.4 %final.1 = (f32[16,32,128]{2,1,0:T(8,128)}, f32[16,32,128]{2,1,0:T(8,128)}) custom-call(s32[3]{0:T(128)} %pad_add_fusion.index, f32[26,48,256]{2,1,0:T(8,128)} %get-tuple-element.23.f_, f32[26,48,256]{2,1,0:T(8,128)} %get-tuple-element.24.wx_, f32[26,48,256]{2,1,0:T(8,128)} %get-tuple-element.25.wy_, f32[26,48,256]{2,1,0:T(8,128)} %get-tuple-element.26.wz_, ...), custom_call_target="tpu_custom_call" | custom-call | tf_op jit(solution)/shard_map/final/pallas_call | solution.py:481
  (56 shorter events, 1.2 us)
Async XLA Ops:
  2.2 7.9 %collective-permute-start.1 = (f32[16,32,50]{2,1,0:T(8,128)S(1)}, f32[16,32,50]{2,1,0:T(8,128)S(1)}, u32[]{:S(2)}, u32[]{:S(2)}) collective-permute-start(f32[16,32,50]{2,1,0:T(8,128)S(1)} %pad_maximum_fusion.10), channel_id=1, source_target_pairs={{0,1},{1,2},{2,3},{3,4},{4,5},{5,6},{6,7},{7,0},{8,9},{9,10},{10,1... | collective-permute-start | bytes 307208 | tf_op jit(solution)/shard_map/ppermute | solution.py:500
  5.0 5.8 %collective-permute-start = (f32[16,32,50]{2,1,0:T(8,128)S(1)}, f32[16,32,50]{2,1,0:T(8,128)S(1)}, u32[]{:S(2)}, u32[]{:S(2)}) collective-permute-start(f32[16,32,50]{2,1,0:T(8,128)S(1)} %pad_maximum_fusion.9), channel_id=1, source_target_pairs={{1,0},{2,1},{3,2},{4,3},{5,4},{6,5},{7,6},{0,7},{9,8},{10,9},{11,1... | collective-permute-start | bytes 307208 | tf_op jit(solution)/shard_map/ppermute | solution.py:501
  10.1 1.0 copy-start.3
  10.1 1.0 copy-start.4
  11.6 6.3 %collective-permute-start.3 = (f32[32,5,256]{2,1,0:T(8,128)S(1)}, f32[32,5,256]{2,1,0:T(8,128)S(1)}, u32[]{:S(2)}, u32[]{:S(2)}) collective-permute-start(f32[32,5,256]{2,1,0:T(8,128)S(1)} %pad_maximum_fusion.12), channel_id=1, source_target_pairs={{0,8},{8,16},{16,24},{1,9},{9,17},{17,25},{2,10},{10,18},{18,26},{... | collective-permute-start | bytes 491528 | tf_op jit(solution)/shard_map/ppermute | solution.py:500
  14.7 7.1 %collective-permute-start.2 = (f32[32,5,256]{2,1,0:T(8,128)S(1)}, f32[32,5,256]{2,1,0:T(8,128)S(1)}, u32[]{:S(2)}, u32[]{:S(2)}) collective-permute-start(f32[32,5,256]{2,1,0:T(8,128)S(1)} %pad_maximum_fusion.11), channel_id=1, source_target_pairs={{8,0},{16,8},{24,16},{9,1},{17,9},{25,17},{10,2},{18,10},{26,18},{... | collective-permute-start | bytes 491528 | tf_op jit(solution)/shard_map/ppermute | solution.py:501
  22.2 0.9 copy-start.1
  22.2 1.2 copy-start.2
  23.4 13.7 %collective-permute-start.4 = (f32[10,48,256]{2,1,0:T(8,128)S(1)}, f32[10,48,256]{2,1,0:T(8,128)S(1)}, u32[]{:S(2)}, u32[]{:S(2)}) collective-permute-start(f32[10,48,256]{2,1,0:T(8,128)S(1)} %pad_maximum_fusion.4), channel_id=1, source_target_pairs={{0,32},{32,64},{64,96},{96,128},{128,160},{160,192},{192,224},{224... | collective-permute-start | bytes 1474568 | tf_op jit(solution)/shard_map/ppermute | solution.py:500
  28.6 12.7 %collective-permute-start.5 = (f32[10,48,256]{2,1,0:T(8,128)S(1)}, f32[10,48,256]{2,1,0:T(8,128)S(1)}, u32[]{:S(2)}, u32[]{:S(2)}) collective-permute-start(f32[10,48,256]{2,1,0:T(8,128)S(1)} %pad_maximum_fusion.5), channel_id=1, source_target_pairs={{32,0},{64,32},{96,64},{128,96},{160,128},{192,160},{224,192},{256... | collective-permute-start | bytes 1474568 | tf_op jit(solution)/shard_map/ppermute | solution.py:501
  37.1 4.2 %copy-start.7 = (f32[10,48,256]{2,1,0:T(8,128)}, f32[10,48,256]{2,1,0:T(8,128)S(1)}, u32[]{:S(2)}) copy-start(f32[10,48,256]{2,1,0:T(8,128)S(1)} %collective-permute-done.4.before) | copy-start | bytes 1474564
  41.3 0.8 copy-start.8
  48.8 5.7 %collective-permute-start.7 = (f32[20,16,128]{2,1,0:T(8,128)}, f32[20,16,128]{2,1,0:T(8,128)S(1)}, u32[]{:S(2)}, u32[]{:S(2)}) collective-permute-start(f32[20,16,128]{2,1,0:T(8,128)} %get-tuple-element.29), channel_id=1, source_target_pairs={{0,8},{8,16},{16,24},{1,9},{9,17},{17,25},{2,10},{10,18},{18,26},{... | collective-permute-start | bytes 491528 | tf_op jit(solution)/shard_map/ppermute | solution.py:500
  51.9 6.3 %collective-permute-start.6 = (f32[20,16,128]{2,1,0:T(8,128)}, f32[20,16,128]{2,1,0:T(8,128)S(1)}, u32[]{:S(2)}, u32[]{:S(2)}) collective-permute-start(f32[20,16,128]{2,1,0:T(8,128)} %get-tuple-element.29), channel_id=1, source_target_pairs={{8,0},{16,8},{24,16},{9,1},{17,9},{25,17},{10,2},{18,10},{26,18},{... | collective-permute-start | bytes 491528 | tf_op jit(solution)/shard_map/ppermute | solution.py:501
  59.2 3.7 %copy-start = (f32[20,40,128]{2,1,0:T(8,128)}, f32[20,40,128]{2,1,0:T(8,128)S(1)}, u32[]{:S(2)}) copy-start(f32[20,40,128]{2,1,0:T(8,128)S(1)} %pad_maximum_fusion.6.refs_1_) | copy-start | bytes 1228804
  59.3 8.0 %collective-permute-start.8 = (f32[18,40,128]{2,1,0:T(8,128)S(1)}, f32[18,40,128]{2,1,0:T(8,128)S(1)}, u32[]{:S(2)}, u32[]{:S(2)}) collective-permute-start(f32[18,40,128]{2,1,0:T(8,128)S(1)} %pad_maximum_fusion.7), channel_id=1, source_target_pairs={{0,32},{32,64},{64,96},{96,128},{128,160},{160,192},{192,224},{224... | collective-permute-start | bytes 1105928 | tf_op jit(solution)/shard_map/ppermute | solution.py:500
  62.9 9.7 %collective-permute-start.9 = (f32[18,40,128]{2,1,0:T(8,128)S(1)}, f32[18,40,128]{2,1,0:T(8,128)S(1)}, u32[]{:S(2)}, u32[]{:S(2)}) collective-permute-start(f32[18,40,128]{2,1,0:T(8,128)S(1)} %pad_maximum_fusion.8), channel_id=1, source_target_pairs={{32,0},{64,32},{96,64},{128,96},{160,128},{192,160},{224,192},{256... | collective-permute-start | bytes 1105928 | tf_op jit(solution)/shard_map/ppermute | solution.py:501
  67.3 5.4 %copy-start.9 = (f32[18,40,128]{2,1,0:T(8,128)}, f32[18,40,128]{2,1,0:T(8,128)S(1)}, u32[]{:S(2)}) copy-start(f32[18,40,128]{2,1,0:T(8,128)S(1)} %collective-permute-done.8.refs_0_) | copy-start | bytes 1105924
  72.6 0.7 copy-start.10
  78.2 24.1 %all-to-all-start = ((f32[16,8,128]{2,1,0:T(8,128)}), f32[16,8,128]{2,1,0:T(8,128)S(1)}, u32[]{:S(2)}, u32[]{:S(2)}) async-start(f32[16,8,128]{2,1,0:T(8,128)} %get-tuple-element.30), calls=%async_computation | async-start | bytes 131072 | tf_op jit(solution)/shard_map/all_to_all | solution.py:544
  102.3 0.6 copy-start.11
  104.8 25.8 %all-to-all-start.1 = ((f32[32,4,8,128]{3,2,1,0:T(8,128)}), f32[32,4,8,128]{3,2,1,0:T(8,128)S(1)}, u32[]{:S(2)}, u32[]{:S(2)}) async-start(f32[32,4,8,128]{3,2,1,0:T(8,128)} %repack.1), calls=%async_computation.1 | async-start | bytes 1048576 | tf_op jit(solution)/shard_map/all_to_all | solution.py:544
  119.7 4.6 %collective-permute-start.10 = (f32[2,24,128]{2,1,0:T(8,128)S(1)}, f32[2,24,128]{2,1,0:T(8,128)S(1)}, u32[]{:S(2)}, u32[]{:S(2)}) collective-permute-start(f32[2,24,128]{2,1,0:T(8,128)S(1)} %pad_maximum_fusion.14), channel_id=1, source_target_pairs={{0,32},{32,64},{64,96},{96,128},{128,160},{160,192},{192,224},{224... | collective-permute-start | bytes 73736 | tf_op jit(solution)/shard_map/ppermute | solution.py:500
  122.2 4.9 %collective-permute-start.11 = (f32[2,24,128]{2,1,0:T(8,128)S(1)}, f32[2,24,128]{2,1,0:T(8,128)S(1)}, u32[]{:S(2)}, u32[]{:S(2)}) collective-permute-start(f32[2,24,128]{2,1,0:T(8,128)S(1)} %pad_maximum_fusion.15), channel_id=1, source_target_pairs={{32,0},{64,32},{96,64},{128,96},{160,128},{192,160},{224,192},{256... | collective-permute-start | bytes 73736 | tf_op jit(solution)/shard_map/ppermute | solution.py:501
  124.3 6.3 %copy-start.14 = (f32[2,24,128]{2,1,0:T(8,128)}, f32[2,24,128]{2,1,0:T(8,128)S(1)}, u32[]{:S(2)}) copy-start(f32[2,24,128]{2,1,0:T(8,128)S(1)} %collective-permute-done.10.refs_0_) | copy-start | bytes 73732
  127.1 3.5 %copy-start.15 = (f32[2,24,128]{2,1,0:T(8,128)}, f32[2,24,128]{2,1,0:T(8,128)S(1)}, u32[]{:S(2)}) copy-start(f32[2,24,128]{2,1,0:T(8,128)S(1)} %collective-permute-done.11.refs_1_) | copy-start | bytes 73732
  130.6 0.8 copy-start.5
  147.5 1.8 collective-permute-start.13
  147.7 4.2 %collective-permute-start.12 = (f32[8,16,128]{2,1,0:T(8,128)}, f32[8,16,128]{2,1,0:T(8,128)S(1)}, u32[]{:S(2)}, u32[]{:S(2)}) collective-permute-start(f32[8,16,128]{2,1,0:T(8,128)} %get-tuple-element.39), channel_id=1, source_target_pairs={{1,0},{2,1},{3,2},{4,3},{5,4},{6,5},{7,6},{0,7},{9,8},{10,9},{11,1... | collective-permute-start | bytes 196616 | tf_op jit(solution)/shard_map/ppermute | solution.py:501
  152.8 3.4 %collective-permute-start.15 = (f32[8,16,128]{2,1,0:T(8,128)S(1)}, f32[8,16,128]{2,1,0:T(8,128)S(1)}, u32[]{:S(2)}, u32[]{:S(2)}) collective-permute-start(f32[8,16,128]{2,1,0:T(8,128)S(1)} %select_select_fusion), channel_id=1, source_target_pairs={{0,8},{8,16},{16,24},{1,9},{9,17},{17,25},{2,10},{10,18},{18,26},{... | collective-permute-start | bytes 196616 | tf_op jit(solution)/shard_map/ppermute | solution.py:500
  154.9 5.0 %collective-permute-start.14 = (f32[8,16,128]{2,1,0:T(8,128)S(1)}, f32[8,16,128]{2,1,0:T(8,128)S(1)}, u32[]{:S(2)}, u32[]{:S(2)}) collective-permute-start(f32[8,16,128]{2,1,0:T(8,128)S(1)} %select_select_fusion), channel_id=1, source_target_pairs={{8,0},{16,8},{24,16},{9,1},{17,9},{25,17},{10,2},{18,10},{26,18},{... | collective-permute-start | bytes 196616 | tf_op jit(solution)/shard_map/ppermute | solution.py:501
  160.0 7.6 %copy-start.6 = (f32[8,40,128]{2,1,0:T(8,128)}, f32[8,40,128]{2,1,0:T(8,128)S(1)}, u32[]{:S(2)}) copy-start(f32[8,40,128]{2,1,0:T(8,128)S(1)} %pad_maximum_fusion.13.refs_1_) | copy-start | bytes 491524
  160.0 6.1 %collective-permute-start.17 = (f32[8,40,128]{2,1,0:T(8,128)S(1)}, f32[8,40,128]{2,1,0:T(8,128)S(1)}, u32[]{:S(2)}, u32[]{:S(2)}) collective-permute-start(f32[8,40,128]{2,1,0:T(8,128)S(1)} %pad_maximum_fusion.13.refs_1_), channel_id=1, source_target_pairs={{32,0},{64,32},{96,64},{128,96},{160,128},{192,160},{224,192},{256... | collective-permute-start | bytes 491528 | tf_op jit(solution)/shard_map/ppermute | solution.py:501
  161.3 6.2 %collective-permute-start.16 = (f32[8,40,128]{2,1,0:T(8,128)S(1)}, f32[8,40,128]{2,1,0:T(8,128)S(1)}, u32[]{:S(2)}, u32[]{:S(2)}) collective-permute-start(f32[8,40,128]{2,1,0:T(8,128)S(1)} %pad_maximum_fusion.13.refs_1_), channel_id=1, source_target_pairs={{0,32},{32,64},{64,96},{96,128},{128,160},{160,192},{192,224},{224... | collective-permute-start | bytes 491528 | tf_op jit(solution)/shard_map/ppermute | solution.py:500
  166.0 1.5 copy-start.12
  167.5 0.7 copy-start.13

commit v5 on v4

--- a/solution.py
+++ b/solution.py
@@ -220,25 +220,17 @@
     planes(0, count, step, unroll=unroll)
 
 
-def down0(before, fo, ko, after, ry, rz, cy, cz, f_, k_, wx_, wy_, wz_, d_, out, f, k, wx, wy, wz, d, v, r, held, sem):
+def down0(before, fo, ko, after, ry, rz, cy, cz, f, k, wx, wy, wz, d, out, v, r, held):
     shifts = Open()
     for ref, own, at in ((f, fo, 0), (k, ko, 5)):
         place(ref, 0, before, at, 5, 5)
         place(ref, 5, own, 0, 16)
         place(ref, 21, after, at, 5, 5)
     weigh(k, wx, wy, wz, 1, 25, 1.0, shifts, d, inside, unroll=U0)
-    copies = [
-        pltpu.make_async_copy(here, there, sem.at[i])
-        for i, (here, there) in enumerate(((f, f_), (k, k_), (wx, wx_), (wy, wy_), (wz, wz_), (d, d_)))
-    ]
-    for copy in copies:
-        copy.start()
     first_sweep(f, d, v, 1, 25, U0)
     residual_of(v, f, r, (wx, wy, wz), 2, 24, shifts, k, unroll=U0)
     out[:10] = restrict(r, 5, -1, 9, ry, rz, held).reshape(10, 16, 128)
     out[10:] = halve(k, 5, -1, 9, cy, cz, held).reshape(10, 16, 128)
-    for copy in copies:
-        copy.wait()
 
 
 def descend(first, *refs):
@@ -414,24 +406,11 @@
 UP = 7
 
 
-def fetch(sources, targets, sem):
-    copies = [
-        pltpu.make_async_copy(there, here, sem.at[i])
-        for i, (there, here) in enumerate(zip(sources, targets))
-    ]
-    for copy in copies:
-        copy.start()
-    return copies
-
-
-def middle(nz, index, f_, wx_, wy_, wz_, d_, k_, s, g2, k2, d2, g1, k1, d1, *refs):
-    ends, m3, m1, (py0, pz0, ry, rz), (v_, gn, turned, k3) = refs[:2], refs[2:8], refs[8:10], refs[10:14], refs[14:18]
-    low, mid, (fine0, r, held0, f, wx, wy, wz, d, k, v, sem) = refs[18:32], refs[32:39], refs[39:]
-    copies = fetch((f_, wx_, wy_, wz_, d_, k_), (f, wx, wy, wz, d, k), sem)
+def middle(nz, index, f, wx, wy, wz, d, k, s, g2, k2, d2, g1, k1, d1, *refs):
+    ends, m3, m1, (py0, pz0, ry, rz), (v, gn, turned, k3) = refs[:2], refs[2:8], refs[8:10], refs[10:14], refs[14:18]
+    low, mid, (fine0, r, held0) = refs[18:32], refs[32:39], refs[39:]
     e3 = bottom(nz, s, k3, low, m3)
     e1 = upward(index, e3, g2, k2, d2, g1, k1, d1, ends, mid, m1)
-    for copy in copies:
-        copy.wait()
     w, shifts = (wx, wy, wz), Open()
 
     def use(i, value):
@@ -440,27 +419,21 @@
     prolong(e1, 6, 14, py0[...], pz0[...], fine0, use)
     smooth(v, f, d, w, 2, 24, shifts, unroll=U0)
     smooth(v, f, d, w, 3, 23, shifts, unroll=U0)
-    copy = pltpu.make_async_copy(v, v_, sem.at[0])
-    copy.start()
     residual_of(v, f, r, w, 4, 22, shifts, k, unroll=U0)
     value = restrict(r, 5, 0, 8, ry, rz, held0)
     gn[...] = value.reshape(gn.shape)
     turned[...] = pltpu.roll(value, 64, 1).reshape(gn.shape)
-    copy.wait()
-
-
-def final(nz, index, f_, wx_, wy_, wz_, d_, k_, v_, s, g2, k2, d2, g1, k1, d1, *refs):
+
+
+def final(nz, index, f, wx, wy, wz, d, k, v0, s, g2, k2, d2, g1, k1, d1, *refs):
     m3, m1, (py0, pz0, k3), (solution_, residual_) = refs[:6], refs[6:8], refs[8:11], refs[11:13]
-    low, mid, (fine0, f, wx, wy, wz, d, k, v, sem) = refs[13:27], refs[27:34], refs[34:]
-    copies = fetch((f_, wx_, wy_, wz_, d_, k_, v_), (f, wx, wy, wz, d, k, v), sem)
+    low, mid, (fine0, v) = refs[13:27], refs[27:34], refs[34:]
     e3 = bottom(nz, s, k3, low, m3)
     e1 = upward(index, e3, g2, k2, d2, g1, k1, d1, None, mid, m1)
-    for copy in copies:
-        copy.wait()
     w, shifts = (wx, wy, wz), Open()
 
     def use(i, value):
-        v[i + 3] = inside(k[i + 3], v[i + 3] + value)
+        v[i + 3] = inside(k[i + 3], v0[i + 3] + value)
 
     prolong(e1, 7, 12, py0[...], pz0[...], fine0, use)
     smooth(v, f, d, w, 4, 22, shifts, unroll=U0)
@@ -474,18 +447,16 @@
     image(v, *w, 5, 21, last, out, shifts, unroll=U0)
 
 
-def call(kernel, outs, scratch, *args, name, scalars=0, loose=0, away=0, sems=0):
+def call(kernel, outs, scratch, *args, name, scalars=0, room=4):
     vmem = pl.BlockSpec(memory_space=pltpu.VMEM)
     smem = pl.BlockSpec(memory_space=pltpu.SMEM)
-    hbm = pl.BlockSpec(memory_space=pl.ANY)
     return pl.pallas_call(
         kernel,
         out_shape=[jax.ShapeDtypeStruct(o, F32) for o in outs],
-        in_specs=[smem] * scalars + [hbm] * loose + [vmem] * (len(args) - scalars - loose),
-        out_specs=[hbm] * away + [vmem] * (len(outs) - away),
-        scratch_shapes=[pltpu.VMEM(s, F32) for s in scratch]
-        + ([pltpu.SemaphoreType.DMA((sems,))] if sems else []),
-        compiler_params=pltpu.CompilerParams(vmem_limit_bytes=56 << 20),
+        in_specs=[smem] * scalars + [vmem] * (len(args) - scalars),
+        out_specs=[vmem] * len(outs),
+        scratch_shapes=[pltpu.VMEM(s, F32) for s in scratch],
+        compiler_params=pltpu.CompilerParams(vmem_limit_bytes=room << 20),
         name=name,
     )(*args)
 
@@ -586,8 +557,8 @@
     tiles = nx // 8
 
     f, k, wx, wy, wz, d, both1 = call(
-        down0, [wide] * 6 + [(20, 16, 128)], [wide] * 8 + [(160, 256)],
-        *finest([right_side, conductivity]), ry0, rz0, cy0, cz0, name="down0", away=6, sems=6,
+        down0, [wide] * 6 + [(20, 16, 128)], [wide] * 2 + [(160, 256)],
+        *finest([right_side, conductivity]), ry0, rz0, cy0, cz0, name="down0", room=6,
     )
     own = rows1(both1)
     last = jnp.concatenate([own[0:9], own[10:19]])
@@ -596,7 +567,7 @@
     inner = [l1, l1, (288, 128), (3,) + l1, l2, l2, (3,) + l2, (8, 128)]
     pieces, g1, k1, d1, g2, k2, d2 = call(
         functools.partial(descend, True), [(nx, 8, 128), l1, l1, l1, l2, l2, l2], inner,
-        before, own, after, ry1, rz1, ry2, rz2, cy1, cz1, cy2, cz2, name="descend",
+        before, own, after, ry1, rz1, ry2, rz2, cy1, cz1, cy2, cz2, name="descend", room=14,
     )
     first, last = jnp.stack([g2[4], d2[4]]), jnp.stack([g2[7], d2[7]])
     outer = neighbours(first, last, "gx")
@@ -606,24 +577,24 @@
     fields = (f, wx, wy, wz, d, k)
     v, value, turned, k3 = call(
         functools.partial(middle, nz), [wide, (8, 16, 128), (8, 16, 128), n3],
-        low + mid + [(14, 48, 256), wide, (128, 256)] + [wide] * 7,
+        low + mid + [(14, 48, 256), wide, (128, 256)],
         index, *fields, s, g2, k2, d2, g1, k1, d1, *outer, *m3, *m1, py0, pz0, ry0, rz0,
-        name="middle", scalars=1, loose=6, away=1, sems=6,
+        name="middle", room=14, scalars=1,
     )
     own = rows1(lanes1(value, turned))
     before, after = neighbours(own, own, "gx")
     pieces, g1, g2 = call(
         functools.partial(descend, False), [(nx, 8, 128), l1, l2], inner,
-        before, own, after, k1, d1, k2, d2, ry1, rz1, ry2, rz2, name="again",
+        before, own, after, k1, d1, k2, d2, ry1, rz1, ry2, rz2, name="again", room=14,
     )
     pieces = everyone(pieces, "gx")
     (pieces,) = call(repack, [(ny * nz, tiles, 8, 128)], [], pieces, name="repack2")
     s = everyone(pieces, ("gy", "gz"))
     return tuple(call(
         functools.partial(final, nz), [(16, 32, 128)] * 2,
-        low + mid + [(12, 48, 256)] + [wide] * 7,
+        low + mid + [(12, 48, 256), wide],
         index, *fields, v, s, g2, k2, d2, g1, k1, d1, *m3, *m1, py0, pz0, k3,
-        name="final", scalars=1, loose=7, sems=7,
+        name="final", room=14, scalars=1,
     ))
 
 

time: 227 us -> 236 us (1.040)
  local copies, waits for them, and re-layouts: 8.38 us -> 30.3 us
  Pallas kernels: 47.5 us -> 35.8 us
  waiting for transfers between devices: 58.8 us -> 55.5 us
    unnamed x32 -> x116, local copies, waits for them, and re-layouts: 4.85 us -> 26.9 us
    pallas_call x7, Pallas kernels: 47.5 us -> 35.8 us  [call(): pl.pallas_call(kernel, out_shape=[jax.ShapeDtypeStruct(o, F32) for o in o...]
    all_to_all x2, waiting for transfers between devices: 14.3 us -> 11.8 us  [everyone(): return lax.all_to_all(pieces, axes, 0, 0)]
  transfers between devices with their start and end apart: 20 -> 20, of which waited for: 18 -> 18; matrix products, arithmetic and copies ran while one was open for 1% -> 2% of each run, Pallas kernels for 0% -> 0%
where the time goes in v5:
time: 236 us; the launch traced here: 234 us
  starting transfers between devices  68.5 us (29%)
  waiting for transfers between devices  55.5 us (24%)
  blocking collectives  38.9 us (16%)
  Pallas kernels  35.8 us (15%)
  local copies, waits for them, and re-layouts  30.3 us (13%)
  other arithmetic  3.94 us (2%)
    all_to_all x2, blocking collectives, everyone(): return lax.all_to_all(pieces, axes, 0, 0)  38.9 us
    pallas_call x7, Pallas kernels, call(): pl.pallas_call(kernel, out_shape=[jax.ShapeDtypeStruct(o, F32) for o in o...  35.8 us
    ppermute x9, starting transfers between devices, neighbours(): before = lax.ppermute(last, axis, up)  27.9 us
    ppermute x9, waiting for transfers between devices, neighbours(): after = lax.ppermute(initial, axis, down)  27 us
    all_to_all x2, starting transfers between devices, everyone(): return lax.all_to_all(pieces, axes, 0, 0)  26.9 us
    unnamed x116, local copies, waits for them, and re-layouts  26.9 us
    ppermute x9, waiting for transfers between devices, neighbours(): before = lax.ppermute(last, axis, up)  16.7 us
    ppermute x9, starting transfers between devices, neighbours(): after = lax.ppermute(initial, axis, down)  13.7 us
  transfers between devices with their start and end apart: 20, of which 18 were waited for; matrix products, arithmetic and copies ran while one was open for 2% of the time, Pallas kernels for 0%

profile of v5, /device:TPU:1, one launch (start us, length us, event | category | flops | bytes accessed | tf_op | source)
XLA Modules:
  0.0 234.2 jit_solution(15994180747624818966)
XLA Ops:
  0.6 1.4 fusion.19
  2.2 2.7 %collective-permute-start.1 = (f32[16,32,50]{2,1,0:T(8,128)S(1)}, f32[16,32,50]{2,1,0:T(8,128)S(1)}, u32[]{:S(2)}, u32[]{:S(2)}) collective-permute-start(f32[16,32,50]{2,1,0:T(8,128)S(1)} %pad_maximum_fusion.10), channel_id=1, source_target_pairs={{0,1},{1,2},{2,3},{3,4},{4,5},{5,6},{6,7},{7,0},{8,9},{9,10},{10,1... | collective-permute-start | bytes 307208 | tf_op jit(solution)/shard_map/ppermute | solution.py:471
  5.0 4.2 %collective-permute-start = (f32[16,32,50]{2,1,0:T(8,128)S(1)}, f32[16,32,50]{2,1,0:T(8,128)S(1)}, u32[]{:S(2)}, u32[]{:S(2)}) collective-permute-start(f32[16,32,50]{2,1,0:T(8,128)S(1)} %pad_maximum_fusion.9), channel_id=1, source_target_pairs={{1,0},{2,1},{3,2},{4,3},{5,4},{6,5},{7,6},{0,7},{9,8},{10,9},{11,1... | collective-permute-start | bytes 307208 | tf_op jit(solution)/shard_map/ppermute | solution.py:472
  9.2 0.9 collective-permute-done.1
  11.5 3.0 %collective-permute-start.3 = (f32[32,5,256]{2,1,0:T(8,128)S(1)}, f32[32,5,256]{2,1,0:T(8,128)S(1)}, u32[]{:S(2)}, u32[]{:S(2)}) collective-permute-start(f32[32,5,256]{2,1,0:T(8,128)S(1)} %pad_maximum_fusion.12), channel_id=1, source_target_pairs={{0,8},{8,16},{16,24},{1,9},{9,17},{17,25},{2,10},{10,18},{18,26},{... | collective-permute-start | bytes 491528 | tf_op jit(solution)/shard_map/ppermute | solution.py:471
  14.7 1.3 collective-permute-start.2
  16.0 1.9 collective-permute-done.3
  17.9 3.9 %collective-permute-done.2 = f32[32,5,256]{2,1,0:T(8,128)S(1)} collective-permute-done((f32[32,5,256]{2,1,0:T(8,128)S(1)}, f32[32,5,256]{2,1,0:T(8,128)S(1)}, u32[]{:S(2)}, u32[]{:S(2)}) %collective-permute-start.2) | collective-permute-done | bytes 163872 | tf_op jit(solution)/shard_map/ppermute | solution.py:472
  22.3 5.3 %collective-permute-start.4 = (f32[10,48,256]{2,1,0:T(8,128)S(1)}, f32[10,48,256]{2,1,0:T(8,128)S(1)}, u32[]{:S(2)}, u32[]{:S(2)}) collective-permute-start(f32[10,48,256]{2,1,0:T(8,128)S(1)} %pad_maximum_fusion.4), channel_id=1, source_target_pairs={{0,32},{32,64},{64,96},{96,128},{128,160},{160,192},{192,224},{224... | collective-permute-start | bytes 1474568 | tf_op jit(solution)/shard_map/ppermute | solution.py:471
  27.7 1.3 collective-permute-start.5
  29.0 7.2 %collective-permute-done.4.before = f32[10,48,256]{2,1,0:T(8,128)S(1)} collective-permute-done((f32[10,48,256]{2,1,0:T(8,128)S(1)}, f32[10,48,256]{2,1,0:T(8,128)S(1)}, u32[]{:S(2)}, u32[]{:S(2)}) %collective-permute-start.4) | collective-permute-done | bytes 491552 | tf_op jit(solution)/shard_map/ppermute | solution.py:471
  36.2 4.2 %collective-permute-done.5.after = f32[10,48,256]{2,1,0:T(8,128)S(1)} collective-permute-done((f32[10,48,256]{2,1,0:T(8,128)S(1)}, f32[10,48,256]{2,1,0:T(8,128)S(1)}, u32[]{:S(2)}, u32[]{:S(2)}) %collective-permute-start.5) | collective-permute-done | bytes 491552 | tf_op jit(solution)/shard_map/ppermute | solution.py:472
  40.4 4.1 %down0.1 = (f32[26,48,256]{2,1,0:T(8,128)S(1)}, f32[26,48,256]{2,1,0:T(8,128)S(1)}, f32[26,48,256]{2,1,0:T(8,128)S(1)}, f32[26,48,256]{2,1,0:T(8,128)S(1)}, f32[...) custom-call(f32[10,48,256]{2,1,0:T(8,128)S(1)} %collective-permute-done.4.before, ...), custom_call_target="tpu_custom_call" | custom-call | tf_op jit(solution)/shard_map/down0/pallas_call | solution.py:453
  44.6 1.1 copy-done
  45.6 1.0 copy-done.3
  46.7 1.0 copy-done.6
  47.7 1.1 copy-done.9
  48.8 3.1 %collective-permute-start.7 = (f32[20,16,128]{2,1,0:T(8,128)S(1)}, f32[20,16,128]{2,1,0:T(8,128)S(1)}, u32[]{:S(2)}, u32[]{:S(2)}) collective-permute-start(f32[20,16,128]{2,1,0:T(8,128)S(1)} %get-tuple-element.29), channel_id=1, source_target_pairs={{0,8},{8,16},{16,24},{1,9},{9,17},{17,25},{2,10},{10,18},{18,26},{... | collective-permute-start | bytes 491528 | tf_op jit(solution)/shard_map/ppermute | solution.py:471
  51.9 1.3 collective-permute-start.6
  53.3 0.8 collective-permute-done.7
  54.2 3.8 %collective-permute-done.6 = f32[20,16,128]{2,1,0:T(8,128)S(1)} collective-permute-done((f32[20,16,128]{2,1,0:T(8,128)S(1)}, f32[20,16,128]{2,1,0:T(8,128)S(1)}, u32[]{:S(2)}, u32[]{:S(2)}) %collective-permute-start.6) | collective-permute-done | bytes 163872 | tf_op jit(solution)/shard_map/ppermute | solution.py:472
  58.3 3.6 %collective-permute-start.8 = (f32[18,40,128]{2,1,0:T(8,128)S(1)}, f32[18,40,128]{2,1,0:T(8,128)S(1)}, u32[]{:S(2)}, u32[]{:S(2)}) collective-permute-start(f32[18,40,128]{2,1,0:T(8,128)S(1)} %pad_maximum_fusion.7), channel_id=1, source_target_pairs={{0,32},{32,64},{64,96},{96,128},{128,160},{160,192},{192,224},{224... | collective-permute-start | bytes 1105928 | tf_op jit(solution)/shard_map/ppermute | solution.py:471
  62.0 1.3 collective-permute-start.9
  63.3 3.1 %collective-permute-done.8.refs_0_ = f32[18,40,128]{2,1,0:T(8,128)S(1)} collective-permute-done((f32[18,40,128]{2,1,0:T(8,128)S(1)}, f32[18,40,128]{2,1,0:T(8,128)S(1)}, u32[]{:S(2)}, u32[]{:S(2)}) %collective-permute-start.8) | collective-permute-done | bytes 368672 | tf_op jit(solution)/shard_map/ppermute | solution.py:471
  66.4 5.3 %collective-permute-done.9.refs_2_ = f32[18,40,128]{2,1,0:T(8,128)S(1)} collective-permute-done((f32[18,40,128]{2,1,0:T(8,128)S(1)}, f32[18,40,128]{2,1,0:T(8,128)S(1)}, u32[]{:S(2)}, u32[]{:S(2)}) %collective-permute-start.9) | collective-permute-done | bytes 368672 | tf_op jit(solution)/shard_map/ppermute | solution.py:472
  71.8 3.0 %descend.1 = (f32[16,8,128]{2,1,0:T(8,128)S(1)}, f32[26,40,128]{2,1,0:T(8,128)S(1)}, f32[26,40,128]{2,1,0:T(8,128)S(1)}, f32[26,40,128]{2,1,0:T(8,128)S(1)}, f32...) custom-call(f32[18,40,128]{2,1,0:T(8,128)S(1)} %collective-permute-done.8.refs_0_, ...), custom_call_target="tpu_custom_call" | custom-call | tf_op jit(solution)/shard_map/descend/pallas_call | solution.py:453
  74.8 0.9 copy-done.11
  75.6 0.8 copy-done.15
  77.7 12.6 %all-to-all-start = ((f32[16,8,128]{2,1,0:T(8,128)}), f32[16,8,128]{2,1,0:T(8,128)}, u32[]{:S(2)}, u32[]{:S(2)}) async-start(f32[16,8,128]{2,1,0:T(8,128)} %copy-done.35), calls=%async_computation | async-start | bytes 131072 | tf_op jit(solution)/shard_map/all_to_all | solution.py:515
  90.9 1.3 fusion.21
  92.3 9.7 %all-to-all-done.s = f32[16,8,128]{2,1,0:T(8,128)} async-done(((f32[16,8,128]{2,1,0:T(8,128)}), f32[16,8,128]{2,1,0:T(8,128)}, u32[]{:S(2)}, u32[]{:S(2)}) %all-to-all-start) | async-done | bytes 65568 | tf_op jit(solution)/shard_map/all_to_all | solution.py:515
  102.0 1.0 repack.1
  103.0 0.8 copy-done.14
  103.8 14.3 %all-to-all-start.1 = ((f32[32,4,8,128]{3,2,1,0:T(8,128)}), f32[32,4,8,128]{3,2,1,0:T(8,128)}, u32[]{:S(2)}, u32[]{:S(2)}) async-start(f32[32,4,8,128]{3,2,1,0:T(8,128)} %copy-done.14), calls=%async_computation.1 | async-start | bytes 1048576 | tf_op jit(solution)/shard_map/all_to_all | solution.py:515
  118.8 2.5 %collective-permute-start.10 = (f32[2,24,128]{2,1,0:T(8,128)S(1)}, f32[2,24,128]{2,1,0:T(8,128)S(1)}, u32[]{:S(2)}, u32[]{:S(2)}) collective-permute-start(f32[2,24,128]{2,1,0:T(8,128)S(1)} %pad_maximum_fusion.14), channel_id=1, source_target_pairs={{0,32},{32,64},{64,96},{96,128},{128,160},{160,192},{192,224},{224... | collective-permute-start | bytes 73736 | tf_op jit(solution)/shard_map/ppermute | solution.py:471
  122.1 1.5 collective-permute-start.11
  124.8 2.3 collective-permute-done.11.refs_1_
  127.7 2.1 all-to-all-done.1.s
  129.8 1.3 copy-done.1
  131.1 1.3 copy-done.4
  132.4 1.3 copy-done.7
  133.7 1.3 copy-done.10
  135.0 1.0 copy-done.12
  136.1 1.0 copy-done.16
  137.1 0.9 copy-done.19
  138.0 0.8 copy-done.20
  138.8 0.8 copy-done.21
  139.7 0.8 copy-done.22
  140.5 0.8 copy-done.23
  141.4 0.9 copy-done.29
  147.2 14.7 %middle.1 = (f32[26,48,256]{2,1,0:T(8,128)S(1)}, f32[8,16,128]{2,1,0:T(8,128)S(1)}, f32[8,16,128]{2,1,0:T(8,128)S(1)}, f32[38,16,128]{2,1,0:T(8,128)S(1)}) custom-call(s32[3]{0:T(128)S(1)} %copy-done.51, f32[26,48,256]{2,1,0:T(8,128)S(1)} %get-tuple-element.23.f, f32[26,48,256]{2,1,0:T(8,128)S(1)} %copy-done.1, f32[26,48,256]{2,1,0:T(8,128)S(1)} %copy-done.4, ...), custom_call_target="tpu_custom_call" | custom-call | tf_op jit(solution)/shard_map/middle/pallas_call | solution.py:453
  162.5 1.3 collective-permute-done.13
  163.8 2.4 %collective-permute-done.12 = f32[8,16,128]{2,1,0:T(8,128)S(1)} collective-permute-done((f32[8,16,128]{2,1,0:T(8,128)S(1)}, f32[8,16,128]{2,1,0:T(8,128)S(1)}, u32[]{:S(2)}, u32[]{:S(2)}) %collective-permute-start.12) | collective-permute-done | bytes 65568 | tf_op jit(solution)/shard_map/ppermute | solution.py:472
  166.3 3.0 %collective-permute-start.15 = (f32[8,16,128]{2,1,0:T(8,128)S(1)}, f32[8,16,128]{2,1,0:T(8,128)S(1)}, u32[]{:S(2)}, u32[]{:S(2)}) collective-permute-start(f32[8,16,128]{2,1,0:T(8,128)S(1)} %select_select_fusion), channel_id=1, source_target_pairs={{0,8},{8,16},{16,24},{1,9},{9,17},{17,25},{2,10},{10,18},{18,26},{... | collective-permute-start | bytes 196616 | tf_op jit(solution)/shard_map/ppermute | solution.py:471
  169.3 1.3 collective-permute-start.14
  170.6 3.7 %collective-permute-done.14 = f32[8,16,128]{2,1,0:T(8,128)S(1)} collective-permute-done((f32[8,16,128]{2,1,0:T(8,128)S(1)}, f32[8,16,128]{2,1,0:T(8,128)S(1)}, u32[]{:S(2)}, u32[]{:S(2)}) %collective-permute-start.14) | collective-permute-done | bytes 65568 | tf_op jit(solution)/shard_map/ppermute | solution.py:472
  174.4 1.6 collective-permute-start.17
  176.0 4.0 %collective-permute-start.16 = (f32[8,40,128]{2,1,0:T(8,128)S(1)}, f32[8,40,128]{2,1,0:T(8,128)S(1)}, u32[]{:S(2)}, u32[]{:S(2)}) collective-permute-start(f32[8,40,128]{2,1,0:T(8,128)S(1)} %pad_maximum_fusion.13.refs_1_), channel_id=1, source_target_pairs={{0,32},{32,64},{64,96},{96,128},{128,160},{160,192},{192,224},{224... | collective-permute-start | bytes 491528 | tf_op jit(solution)/shard_map/ppermute | solution.py:471
  180.0 0.8 collective-permute-done.17.refs_2_
  180.7 1.5 collective-permute-done.16.refs_0_
  182.2 1.9 again.1
  184.1 18.9 %all_to_all.20.s = f32[16,8,128]{2,1,0:T(8,128)S(1)} all-to-all(f32[16,8,128]{2,1,0:T(8,128)S(1)} %get-tuple-element.40), channel_id=1, replica_groups=mesh['gx'=16,'gy'=4,'gz'=8] {'gx'}, dimensions={0} | all-to-all | bytes 131072 | tf_op jit(solution)/shard_map/all_to_all | solution.py:515
  203.1 20.1 %all_to_all.21.s = f32[32,2,8,128]{3,2,1,0:T(8,128)S(1)} all-to-all(f32[32,2,8,128]{3,2,1,0:T(8,128)S(1)} %repack2.1), channel_id=1, replica_groups=mesh['gx'=16,'gy'=4,'gz'=8] {'gy','gz'}, dimensions={0} | all-to-all | bytes 524288 | tf_op jit(solution)/shard_map/all_to_all | solution.py:515
  223.2 11.0 %final.1 = (f32[16,32,128]{2,1,0:T(8,128)}, f32[16,32,128]{2,1,0:T(8,128)}) custom-call(s32[3]{0:T(128)S(1)} %copy-done.51, f32[26,48,256]{2,1,0:T(8,128)S(1)} %get-tuple-element.23.f, f32[26,48,256]{2,1,0:T(8,128)S(1)} %copy-done.2, f32[26,48,256]{2,1,0:T(8,128)S(1)} %copy-done.5, f32[26,48,256]{2,1,0:T(8,128)S(1)} %copy-done.8, ...), custom_call_target="tpu_custom_call" | custom-call | tf_op jit(solution)/shard_map/final/pallas_call | solution.py:453
  (140 shorter events, 13.6 us)
Async XLA Ops:
  2.2 7.9 %collective-permute-start.1 = (f32[16,32,50]{2,1,0:T(8,128)S(1)}, f32[16,32,50]{2,1,0:T(8,128)S(1)}, u32[]{:S(2)}, u32[]{:S(2)}) collective-permute-start(f32[16,32,50]{2,1,0:T(8,128)S(1)} %pad_maximum_fusion.10), channel_id=1, source_target_pairs={{0,1},{1,2},{2,3},{3,4},{4,5},{5,6},{6,7},{7,0},{8,9},{9,10},{10,1... | collective-permute-start | bytes 307208 | tf_op jit(solution)/shard_map/ppermute | solution.py:471
  5.0 5.8 %collective-permute-start = (f32[16,32,50]{2,1,0:T(8,128)S(1)}, f32[16,32,50]{2,1,0:T(8,128)S(1)}, u32[]{:S(2)}, u32[]{:S(2)}) collective-permute-start(f32[16,32,50]{2,1,0:T(8,128)S(1)} %pad_maximum_fusion.9), channel_id=1, source_target_pairs={{1,0},{2,1},{3,2},{4,3},{5,4},{6,5},{7,6},{0,7},{9,8},{10,9},{11,1... | collective-permute-start | bytes 307208 | tf_op jit(solution)/shard_map/ppermute | solution.py:472
  10.1 1.0 copy-start.52
  10.1 1.0 copy-start.53
  11.5 6.3 %collective-permute-start.3 = (f32[32,5,256]{2,1,0:T(8,128)S(1)}, f32[32,5,256]{2,1,0:T(8,128)S(1)}, u32[]{:S(2)}, u32[]{:S(2)}) collective-permute-start(f32[32,5,256]{2,1,0:T(8,128)S(1)} %pad_maximum_fusion.12), channel_id=1, source_target_pairs={{0,8},{8,16},{16,24},{1,9},{9,17},{17,25},{2,10},{10,18},{18,26},{... | collective-permute-start | bytes 491528 | tf_op jit(solution)/shard_map/ppermute | solution.py:471
  14.7 7.1 %collective-permute-start.2 = (f32[32,5,256]{2,1,0:T(8,128)S(1)}, f32[32,5,256]{2,1,0:T(8,128)S(1)}, u32[]{:S(2)}, u32[]{:S(2)}) collective-permute-start(f32[32,5,256]{2,1,0:T(8,128)S(1)} %pad_maximum_fusion.11), channel_id=1, source_target_pairs={{8,0},{16,8},{24,16},{9,1},{17,9},{25,17},{10,2},{18,10},{26,18},{... | collective-permute-start | bytes 491528 | tf_op jit(solution)/shard_map/ppermute | solution.py:472
  22.2 18.2 %copy-start.18 = (f32[256,128]{1,0:T(8,128)S(1)}, f32[256,128]{1,0:T(8,128)}, u32[]{:S(2)}) copy-start(f32[256,128]{1,0:T(8,128)} %constant.75.clone.rz.refs_13_) | copy-start | bytes 393220
  22.2 18.2 %copy-start.30 = (f32[256,128]{1,0:T(8,128)S(1)}, f32[256,128]{1,0:T(8,128)}, u32[]{:S(2)}) copy-start(f32[256,128]{1,0:T(8,128)} %constant.77.clone.cz) | copy-start | bytes 393220
  22.2 18.2 %copy-start.39 = (f32[16,48]{1,0:T(8,128)S(1)}, f32[16,48]{1,0:T(8,128)}, u32[]{:S(2)}) copy-start(f32[16,48]{1,0:T(8,128)} %constant.74.clone.ry.refs_12_) | copy-start | bytes 9220
  22.2 18.2 %copy-start.50 = (f32[16,48]{1,0:T(8,128)S(1)}, f32[16,48]{1,0:T(8,128)}, u32[]{:S(2)}) copy-start(f32[16,48]{1,0:T(8,128)} %constant.76.clone.cy) | copy-start | bytes 9220
  22.3 13.8 %collective-permute-start.4 = (f32[10,48,256]{2,1,0:T(8,128)S(1)}, f32[10,48,256]{2,1,0:T(8,128)S(1)}, u32[]{:S(2)}, u32[]{:S(2)}) collective-permute-start(f32[10,48,256]{2,1,0:T(8,128)S(1)} %pad_maximum_fusion.4), channel_id=1, source_target_pairs={{0,32},{32,64},{64,96},{96,128},{128,160},{160,192},{192,224},{224... | collective-permute-start | bytes 1474568 | tf_op jit(solution)/shard_map/ppermute | solution.py:471
  27.7 12.7 %collective-permute-start.5 = (f32[10,48,256]{2,1,0:T(8,128)S(1)}, f32[10,48,256]{2,1,0:T(8,128)S(1)}, u32[]{:S(2)}, u32[]{:S(2)}) collective-permute-start(f32[10,48,256]{2,1,0:T(8,128)S(1)} %pad_maximum_fusion.5), channel_id=1, source_target_pairs={{32,0},{64,32},{96,64},{128,96},{160,128},{192,160},{224,192},{256... | collective-permute-start | bytes 1474568 | tf_op jit(solution)/shard_map/ppermute | solution.py:472
  44.6 1.1 copy-start
  45.6 1.0 copy-start.3
  46.7 1.0 copy-start.6
  47.7 1.1 copy-start.9
  48.8 5.3 %collective-permute-start.7 = (f32[20,16,128]{2,1,0:T(8,128)S(1)}, f32[20,16,128]{2,1,0:T(8,128)S(1)}, u32[]{:S(2)}, u32[]{:S(2)}) collective-permute-start(f32[20,16,128]{2,1,0:T(8,128)S(1)} %get-tuple-element.29), channel_id=1, source_target_pairs={{0,8},{8,16},{16,24},{1,9},{9,17},{17,25},{2,10},{10,18},{18,26},{... | collective-permute-start | bytes 491528 | tf_op jit(solution)/shard_map/ppermute | solution.py:471
  51.9 6.1 %collective-permute-start.6 = (f32[20,16,128]{2,1,0:T(8,128)S(1)}, f32[20,16,128]{2,1,0:T(8,128)S(1)}, u32[]{:S(2)}, u32[]{:S(2)}) collective-permute-start(f32[20,16,128]{2,1,0:T(8,128)S(1)} %get-tuple-element.29), channel_id=1, source_target_pairs={{8,0},{16,8},{24,16},{9,1},{17,9},{25,17},{10,2},{18,10},{26,18},{... | collective-permute-start | bytes 491528 | tf_op jit(solution)/shard_map/ppermute | solution.py:472
  53.3 4.7 %copy-start.54 = (f32[40]{0:T(128)}, f32[40]{0:T(128)S(1)}, u32[]{:S(2)}) copy-start(f32[40]{0:T(128)S(1)} %pad.14.clone) | copy-start | bytes 484
  58.1 13.6 %copy-start.24 = (f32[128,128]{1,0:T(8,128)S(1)}, f32[128,128]{1,0:T(8,128)}, u32[]{:S(2)}) copy-start(f32[128,128]{1,0:T(8,128)} %constant.81.clone.refs_6_.refs_10_) | copy-start | bytes 196612
  58.1 13.6 %copy-start.26 = (f32[128,128]{1,0:T(8,128)S(1)}, f32[128,128]{1,0:T(8,128)}, u32[]{:S(2)}) copy-start(f32[128,128]{1,0:T(8,128)} %constant.79.clone.refs_4_.refs_8_) | copy-start | bytes 196612
  58.1 13.6 %copy-start.33 = (f32[128,128]{1,0:T(8,128)S(1)}, f32[128,128]{1,0:T(8,128)}, u32[]{:S(2)}) copy-start(f32[128,128]{1,0:T(8,128)} %constant.85.clone.refs_10_) | copy-start | bytes 196612
  58.1 13.6 %copy-start.34 = (f32[128,128]{1,0:T(8,128)S(1)}, f32[128,128]{1,0:T(8,128)}, u32[]{:S(2)}) copy-start(f32[128,128]{1,0:T(8,128)} %constant.83.clone.refs_8_) | copy-start | bytes 196612
  58.2 13.6 %copy-start.36 = (f32[24,40]{1,0:T(8,128)S(1)}, f32[24,40]{1,0:T(8,128)}, u32[]{:S(2)}) copy-start(f32[24,40]{1,0:T(8,128)} %constant.78.clone.refs_3_.refs_7_) | copy-start | bytes 11524
  58.2 13.6 %copy-start.37 = (f32[2,8,24]{2,1,0:T(8,128)S(1)}, f32[2,8,24]{2,1,0:T(8,128)}, u32[]{:S(2)}) copy-start(f32[2,8,24]{2,1,0:T(8,128)} %constant.80.clone.refs_5_.refs_9_) | copy-start | bytes 4612
  58.2 13.6 %copy-start.48 = (f32[24,40]{1,0:T(8,128)S(1)}, f32[24,40]{1,0:T(8,128)}, u32[]{:S(2)}) copy-start(f32[24,40]{1,0:T(8,128)} %constant.82.clone.refs_7_) | copy-start | bytes 11524
  58.2 13.6 %copy-start.49 = (f32[2,8,24]{2,1,0:T(8,128)S(1)}, f32[2,8,24]{2,1,0:T(8,128)}, u32[]{:S(2)}) copy-start(f32[2,8,24]{2,1,0:T(8,128)} %constant.84.clone.refs_9_) | copy-start | bytes 4612
  58.3 8.1 %collective-permute-start.8 = (f32[18,40,128]{2,1,0:T(8,128)S(1)}, f32[18,40,128]{2,1,0:T(8,128)S(1)}, u32[]{:S(2)}, u32[]{:S(2)}) collective-permute-start(f32[18,40,128]{2,1,0:T(8,128)S(1)} %pad_maximum_fusion.7), channel_id=1, source_target_pairs={{0,32},{32,64},{64,96},{96,128},{128,160},{160,192},{192,224},{224... | collective-permute-start | bytes 1105928 | tf_op jit(solution)/shard_map/ppermute | solution.py:471
  62.0 9.7 %collective-permute-start.9 = (f32[18,40,128]{2,1,0:T(8,128)S(1)}, f32[18,40,128]{2,1,0:T(8,128)S(1)}, u32[]{:S(2)}, u32[]{:S(2)}) collective-permute-start(f32[18,40,128]{2,1,0:T(8,128)S(1)} %pad_maximum_fusion.8), channel_id=1, source_target_pairs={{32,0},{64,32},{96,64},{128,96},{160,128},{192,160},{224,192},{256... | collective-permute-start | bytes 1105928 | tf_op jit(solution)/shard_map/ppermute | solution.py:472
  74.8 0.9 copy-start.11
  77.7 52.1 %copy-start.17 = (f32[128,256]{1,0:T(8,128)S(1)}, f32[128,256]{1,0:T(8,128)}, u32[]{:S(2)}) copy-start(f32[128,256]{1,0:T(8,128)} %constant.95.clone.refs_11_.refs_9_) | copy-start | bytes 393220
  77.7 52.1 %copy-start.31 = (f32[48,40]{1,0:T(8,128)S(1)}, f32[48,40]{1,0:T(8,128)}, u32[]{:S(2)}) copy-start(f32[48,40]{1,0:T(8,128)} %constant.94.clone.refs_10_.refs_8_) | copy-start | bytes 23044
  77.7 52.1 %copy-start.46 = (f32[8,16]{1,0:T(8,128)S(1)}, f32[8,16]{1,0:T(8,128)}, u32[]{:S(2)}) copy-start(f32[8,16]{1,0:T(8,128)} %constant.88.clone.refs_4_.refs_2_) | copy-start | bytes 1540
  77.7 24.3 %all-to-all-start = ((f32[16,8,128]{2,1,0:T(8,128)}), f32[16,8,128]{2,1,0:T(8,128)}, u32[]{:S(2)}, u32[]{:S(2)}) async-start(f32[16,8,128]{2,1,0:T(8,128)} %copy-done.35), calls=%async_computation | async-start | bytes 131072 | tf_op jit(solution)/shard_map/all_to_all | solution.py:515
  103.0 0.9 copy-start.14
  103.8 26.0 %all-to-all-start.1 = ((f32[32,4,8,128]{3,2,1,0:T(8,128)}), f32[32,4,8,128]{3,2,1,0:T(8,128)}, u32[]{:S(2)}, u32[]{:S(2)}) async-start(f32[32,4,8,128]{3,2,1,0:T(8,128)} %copy-done.14), calls=%async_computation.1 | async-start | bytes 1048576 | tf_op jit(solution)/shard_map/all_to_all | solution.py:515
  118.8 5.3 %collective-permute-start.10 = (f32[2,24,128]{2,1,0:T(8,128)S(1)}, f32[2,24,128]{2,1,0:T(8,128)S(1)}, u32[]{:S(2)}, u32[]{:S(2)}) collective-permute-start(f32[2,24,128]{2,1,0:T(8,128)S(1)} %pad_maximum_fusion.14), channel_id=1, source_target_pairs={{0,32},{32,64},{64,96},{96,128},{128,160},{160,192},{192,224},{224... | collective-permute-start | bytes 73736 | tf_op jit(solution)/shard_map/ppermute | solution.py:471
  122.1 5.0 %collective-permute-start.11 = (f32[2,24,128]{2,1,0:T(8,128)S(1)}, f32[2,24,128]{2,1,0:T(8,128)S(1)}, u32[]{:S(2)}, u32[]{:S(2)}) collective-permute-start(f32[2,24,128]{2,1,0:T(8,128)S(1)} %pad_maximum_fusion.15), channel_id=1, source_target_pairs={{32,0},{64,32},{96,64},{128,96},{160,128},{192,160},{224,192},{256... | collective-permute-start | bytes 73736 | tf_op jit(solution)/shard_map/ppermute | solution.py:472
  129.8 1.3 copy-start.1
  131.1 1.3 copy-start.4
  132.4 1.3 copy-start.7
  133.7 1.3 copy-start.10
  135.0 1.0 copy-start.12
  136.1 1.0 copy-start.16
  137.1 0.9 copy-start.19
  138.0 0.8 copy-start.20
  138.8 0.8 copy-start.21
  141.4 0.9 copy-start.29
  147.2 19.0 %copy-start.56 = (pred[128]{0:T(512)(128)(4,1)S(1)}, pred[128]{0:T(512)(128)(4,1)}, u32[]{:S(2)}) copy-start(pred[128]{0:T(512)(128)(4,1)} %get-tuple-element.78) | copy-start | bytes 388
  147.2 19.0 %copy-start.57 = (pred[128]{0:T(512)(128)(4,1)S(1)}, pred[128]{0:T(512)(128)(4,1)}, u32[]{:S(2)}) copy-start(pred[128]{0:T(512)(128)(4,1)} %get-tuple-element.79) | copy-start | bytes 388
  147.2 27.1 %copy-start.55 = (f32[40]{0:T(128)S(1)}, f32[40]{0:T(128)}, u32[]{:S(2)}) copy-start(f32[40]{0:T(128)} %copy-done.54) | copy-start | bytes 484
  147.2 35.0 %copy-start.25 = (f32[128,128]{1,0:T(8,128)S(1)}, f32[128,128]{1,0:T(8,128)}, u32[]{:S(2)}) copy-start(f32[128,128]{1,0:T(8,128)} %constant.81.clone.refs_6_.refs_10_) | copy-start | bytes 196612
  147.2 35.0 %copy-start.27 = (f32[128,128]{1,0:T(8,128)S(1)}, f32[128,128]{1,0:T(8,128)}, u32[]{:S(2)}) copy-start(f32[128,128]{1,0:T(8,128)} %constant.79.clone.refs_4_.refs_8_) | copy-start | bytes 196612
  147.2 35.0 %copy-start.38 = (f32[2,8,24]{2,1,0:T(8,128)S(1)}, f32[2,8,24]{2,1,0:T(8,128)}, u32[]{:S(2)}) copy-start(f32[2,8,24]{2,1,0:T(8,128)} %constant.80.clone.refs_5_.refs_9_) | copy-start | bytes 4612
  147.2 75.9 %copy-start.8 = (f32[26,48,256]{2,1,0:T(8,128)S(1)}, f32[26,48,256]{2,1,0:T(8,128)}, u32[]{:S(2)}) copy-start(f32[26,48,256]{2,1,0:T(8,128)} %copy-done.6) | copy-start | bytes 3833860
  161.9 1.9 collective-permute-start.13
  162.5 3.8 %collective-permute-start.12 = (f32[8,16,128]{2,1,0:T(8,128)S(1)}, f32[8,16,128]{2,1,0:T(8,128)S(1)}, u32[]{:S(2)}, u32[]{:S(2)}) collective-permute-start(f32[8,16,128]{2,1,0:T(8,128)S(1)} %get-tuple-element.39), channel_id=1, source_target_pairs={{1,0},{2,1},{3,2},{4,3},{5,4},{6,5},{7,6},{0,7},{9,8},{10,9},{11,1... | collective-permute-start | bytes 196616 | tf_op jit(solution)/shard_map/ppermute | solution.py:472
  166.3 4.4 %collective-permute-start.15 = (f32[8,16,128]{2,1,0:T(8,128)S(1)}, f32[8,16,128]{2,1,0:T(8,128)S(1)}, u32[]{:S(2)}, u32[]{:S(2)}) collective-permute-start(f32[8,16,128]{2,1,0:T(8,128)S(1)} %select_select_fusion), channel_id=1, source_target_pairs={{0,8},{8,16},{16,24},{1,9},{9,17},{17,25},{2,10},{10,18},{18,26},{... | collective-permute-start | bytes 196616 | tf_op jit(solution)/shard_map/ppermute | solution.py:471
  169.3 5.0 %collective-permute-start.14 = (f32[8,16,128]{2,1,0:T(8,128)S(1)}, f32[8,16,128]{2,1,0:T(8,128)S(1)}, u32[]{:S(2)}, u32[]{:S(2)}) collective-permute-start(f32[8,16,128]{2,1,0:T(8,128)S(1)} %select_select_fusion), channel_id=1, source_target_pairs={{8,0},{16,8},{24,16},{9,1},{17,9},{25,17},{10,2},{18,10},{26,18},{... | collective-permute-start | bytes 196616 | tf_op jit(solution)/shard_map/ppermute | solution.py:472
  174.3 48.9 %copy-start.13 = (f32[26,40,128]{2,1,0:T(8,128)S(1)}, f32[26,40,128]{2,1,0:T(8,128)}, u32[]{:S(2)}) copy-start(f32[26,40,128]{2,1,0:T(8,128)} %copy-done.11) | copy-start | bytes 1597444
  174.4 48.8 %copy-start.2 = (f32[26,48,256]{2,1,0:T(8,128)S(1)}, f32[26,48,256]{2,1,0:T(8,128)}, u32[]{:S(2)}) copy-start(f32[26,48,256]{2,1,0:T(8,128)} %copy-done) | copy-start | bytes 3833860
  174.4 48.8 %copy-start.5 = (f32[26,48,256]{2,1,0:T(8,128)S(1)}, f32[26,48,256]{2,1,0:T(8,128)}, u32[]{:S(2)}) copy-start(f32[26,48,256]{2,1,0:T(8,128)} %copy-done.3) | copy-start | bytes 3833860
  174.4 6.3 %collective-permute-start.17 = (f32[8,40,128]{2,1,0:T(8,128)S(1)}, f32[8,40,128]{2,1,0:T(8,128)S(1)}, u32[]{:S(2)}, u32[]{:S(2)}) collective-permute-start(f32[8,40,128]{2,1,0:T(8,128)S(1)} %pad_maximum_fusion.13.refs_1_), channel_id=1, source_target_pairs={{32,0},{64,32},{96,64},{128,96},{160,128},{192,160},{224,192},{256... | collective-permute-start | bytes 491528 | tf_op jit(solution)/shard_map/ppermute | solution.py:472
  176.0 6.2 %collective-permute-start.16 = (f32[8,40,128]{2,1,0:T(8,128)S(1)}, f32[8,40,128]{2,1,0:T(8,128)S(1)}, u32[]{:S(2)}, u32[]{:S(2)}) collective-permute-start(f32[8,40,128]{2,1,0:T(8,128)S(1)} %pad_maximum_fusion.13.refs_1_), channel_id=1, source_target_pairs={{0,32},{32,64},{64,96},{96,128},{128,160},{160,192},{192,224},{224... | collective-permute-start | bytes 491528 | tf_op jit(solution)/shard_map/ppermute | solution.py:471
  (14 other events, 9.9 us)

commit v6 on v5

--- a/solution.py
+++ b/solution.py
@@ -2,7 +2,6 @@
 
 import jax
 import jax.numpy as jnp
-import numpy as np
 from jax import lax
 from jax.experimental import pallas as pl
 from jax.experimental.pallas import tpu as pltpu
@@ -15,25 +14,46 @@
 F32 = jnp.float32
 
 
-def coords(n, b):
-    at = np.arange(n)
-    return np.where(at < (n + b) // 2, at, at - n)
-
-
-def restriction(coarse, fine):
-    gap = fine[None, :] - 2 * coarse[:, None]
-    outer, inner = (gap == -1) | (gap == 2), (gap == 0) | (gap == 1)
-    return np.where(outer, 0.125, np.where(inner, 0.375, 0.0)).astype(np.float32)
-
-
-def halving(coarse, fine):
-    return np.where(fine[None, :] // 2 == coarse[:, None], 0.5, 0.0).astype(np.float32)
-
-
-def prolongation(fine, coarse):
-    near = fine[:, None] // 2 == coarse[None, :]
-    far = fine[:, None] // 2 + 2 * (fine[:, None] % 2) - 1 == coarse[None, :]
-    return np.where(near, 0.75, np.where(far, 0.25, 0.0)).astype(np.float32)
+def ring(n, b):
+    return lambda at: jnp.where(at < (n + b) // 2, at, at - n)
+
+
+def span(count, away=-1000, start=0):
+    return lambda at: jnp.where((at >= start) & (at < start + count), at - start, away)
+
+
+def matrix(shape, rows, columns, turned, values):
+    a = rows(lax.broadcasted_iota(jnp.int32, shape, 0))
+    b = columns(lax.broadcasted_iota(jnp.int32, shape, 1))
+    return values(b, a) if turned else values(a, b)
+
+
+def restriction(shape, rows, columns, turned=False):
+    def values(coarse, fine):
+        gap = fine - 2 * coarse
+        outer, inner = (gap == -1) | (gap == 2), (gap == 0) | (gap == 1)
+        return jnp.where(outer, 0.125, jnp.where(inner, 0.375, 0.0))
+
+    return matrix(shape, rows, columns, turned, values)
+
+
+def halving(shape, rows, columns, turned=False):
+    def values(coarse, fine):
+        return jnp.where((fine >> 1) == coarse, 0.5, 0.0)
+
+    return matrix(shape, rows, columns, turned, values)
+
+
+def prolongation(shape, rows, columns, turned=False):
+    def values(fine, coarse):
+        near = (fine >> 1) == coarse
+        far = (fine >> 1) + 2 * (fine & 1) - 1 == coarse
+        return jnp.where(near, 0.75, jnp.where(far, 0.25, 0.0))
+
+    return matrix(shape, rows, columns, turned, values)
+
+
+Y0, Z0, Y1, Z1, Y2, Z2 = ring(48, 32), ring(256, 128), ring(40, 16), ring(128, 64), ring(24, 8), ring(128, 32)
 
 
 def dot(a, b):
@@ -172,16 +192,16 @@
     for i in range(lo, hi):
         at = 2 * i + offset
         plane = 0.125 * (r[at - 1] + r[at + 2]) + 0.375 * (r[at] + r[at + 1])
-        held[(i - lo) * size : (i - lo + 1) * size, :] = dot(ry[...], plane)
-    return dot(held[: (hi - lo) * size, :], rz[...])
+        held[(i - lo) * size : (i - lo + 1) * size, :] = dot(ry, plane)
+    return dot(held[: (hi - lo) * size, :], rz)
 
 
 def halve(k, offset, lo, hi, cy, cz, held):
     size = cy.shape[0]
     for i in range(lo, hi):
         plane = 0.5 * (k[2 * i + offset] + k[2 * i + 1 + offset])
-        held[(i - lo) * size : (i - lo + 1) * size, :] = dot(cy[...], plane)
-    return dot(held[: (hi - lo) * size, :], cz[...])
+        held[(i - lo) * size : (i - lo + 1) * size, :] = dot(cy, plane)
+    return dot(held[: (hi - lo) * size, :], cz)
 
 
 def prolong(e, first, count, py, pz, finer, use):
@@ -220,7 +240,7 @@
     planes(0, count, step, unroll=unroll)
 
 
-def down0(before, fo, ko, after, ry, rz, cy, cz, f, k, wx, wy, wz, d, out, v, r, held):
+def down0(before, fo, ko, after, f, k, out, wx, wy, wz, d, v, r, held):
     shifts = Open()
     for ref, own, at in ((f, fo, 0), (k, ko, 5)):
         place(ref, 0, before, at, 5, 5)
@@ -229,7 +249,9 @@
     weigh(k, wx, wy, wz, 1, 25, 1.0, shifts, d, inside, unroll=U0)
     first_sweep(f, d, v, 1, 25, U0)
     residual_of(v, f, r, (wx, wy, wz), 2, 24, shifts, k, unroll=U0)
+    ry, rz = restriction((16, 48), span(16), Y0), restriction((256, 128), Z0, Z1, True)
     out[:10] = restrict(r, 5, -1, 9, ry, rz, held).reshape(10, 16, 128)
+    cy, cz = halving((16, 48), span(16), Y0), halving((256, 128), Z0, Z1, True)
     out[10:] = halve(k, 5, -1, 9, cy, cz, held).reshape(10, 16, 128)
 
 
@@ -237,51 +259,48 @@
     shifts = Open()
     before, own, after = refs[:3]
     if first:
-        ry1, rz1, ry2, rz2, cy1, cz1, cy2, cz2 = refs[3:11]
-        out, g1, k1, d1, g2, k2, d2 = refs[11:18]
+        out, g1, k1, g2, k2, below, above = refs[3:10]
         for ref, at in ((g1, 0), (k1, 1)):
             place(ref, 0, before, 9 * at, 9, 9)
             place(ref, 9, own, 10 * at + 1, 8, 8)
             place(ref, 17, after, 9 * at, 9, 9)
     else:
-        k1, d1, k2, d2, ry1, rz1, ry2, rz2 = refs[3:11]
-        out, g1, g2 = refs[11:14]
+        k1, k2, out, g1, g2 = refs[3:8]
         zero = jnp.zeros(g1.shape[1:], F32)
         g1[0], g1[25] = zero, zero
         for ref, at in ((before, 1), (own, 9), (after, 17)):
             place(g1, at, ref, 0, 8, 8)
-    v1, r1, held, w1, v2, r2, w2, part = refs[-8:]
+    v1, r1, held, w1, d1, v2, r2, w2, d2 = refs[-9:]
     w1, w2 = three(w1), three(w2)
     rows = g2.shape[1]
-    if first:
-        zero = jnp.zeros(d1.shape[1:], F32)
-        d1[0], d1[25] = zero, zero
-        weigh(k1, *w1, 1, 25, 0.25, shifts, d1, inside, unroll=U1)
-    else:
-        weigh(k1, *w1, 1, 25, 0.25, shifts, unroll=U1)
+    weigh(k1, *w1, 1, 25, 0.25, shifts, d1, inside, unroll=U1)
     first_sweep(g1, d1, v1, 1, 25, U1)
     residual_of(v1, g1, r1, w1, 2, 24, shifts, d1, unroll=U1)
     zero = jnp.zeros(g2.shape[1:], F32)
     g2[0], g2[11] = zero, zero
+    ry1, rz1 = restriction((24, 40), Y2, Y1), restriction((128, 128), Z1, Z2, True)
     g2[1:11] = restrict(r1, 9, -3, 7, ry1, rz1, held).reshape(10, rows, 128)
     if first:
-        d2[0], d2[11] = zero, zero
+        cy1, cz1 = halving((24, 40), Y2, Y1), halving((128, 128), Z1, Z2, True)
         k2[...] = halve(k1, 9, -4, 8, cy1, cz1, held).reshape(k2.shape)
-        weigh(k2, *w2, 1, 11, 0.25**2, shifts, d2, inside, unroll=U2)
-    else:
-        weigh(k2, *w2, 1, 11, 0.25**2, shifts, unroll=U2)
+    weigh(k2, *w2, 1, 11, 0.25**2, shifts, d2, inside, unroll=U2)
+    if first:
+        below[0], below[1], above[0], above[1] = g2[4], d2[4], g2[7], d2[7]
     first_sweep(g2, d2, v2, 1, 11, U2)
     residual_of(v2, g2, r2, w2, 3, 9, shifts, d2, unroll=U2)
     total = None
     for i in range(2):
         at = 2 * i + 4
         plane = 0.125 * (r2[at - 1] + r2[at + 2]) + 0.375 * (r2[at] + r2[at + 1])
-        value = dot(ry2[i], plane)
+        value = dot(restriction((8, 24), span(4, start=4 * i), Y2), plane)
         total = value if total is None else total + value
-    tile = dot(total, rz2[...])
+    tile = dot(total, restriction((128, 128), Z2, span(16), True))
     if first:
-        total = dot(cy2[0], 0.5 * (k2[4] + k2[5])) + dot(cy2[1], 0.5 * (k2[6] + k2[7]))
-        tile = tile + dot(total, cz2[...])
+        part = [
+            dot(halving((8, 24), span(4, start=4 * i), Y2), 0.5 * (k2[2 * i + 4] + k2[2 * i + 5]))
+            for i in range(2)
+        ]
+        tile = tile + dot(part[0] + part[1], halving((128, 128), Z2, span(16, start=16), True))
     for i in range(out.shape[0]):
         out[i] = tile
 
@@ -321,10 +340,12 @@
                 whole[16 * t + p + 11, 4 * j : 4 * j + 4] = total[4:]
 
 
-def bottom(nz, s, k3, scratch, mats):
+def bottom(nz, s, k3, scratch):
     g3, v3, r3, w3, d3, b3, k4, g4, v4, w4, d4, b4, held, fine4 = scratch
-    ry3, rz3, cy3, cz3, py3, pz3 = mats
     n4 = g4.shape[0]
+    lanes3, lanes4 = span(16 * nz, -3000), span(8 * nz, -9000)
+    rows3, rows4 = span(g3.shape[1]), span(g4.shape[1])
+    tall, wide = (g4.shape[1], g3.shape[1]), (128, 128)
     n3, two = 2 * n4, s.shape[1] == n4 // 4
     rows, lanes = g3.shape[1], g3.shape[2]
     zero = jnp.zeros((rows, lanes), F32)
@@ -338,6 +359,7 @@
     unpack(s, 0, n3 // 16, nz, g3)
     if two:
         unpack(s, n3 // 16, n3 // 16, nz, k3)
+    cy3, cz3 = halving(tall, rows4, rows3), halving(wide, lanes3, lanes4, True)
     k4[1 : n4 + 1] = halve(k3, 3, 0, n4, cy3, cz3, held).reshape(g4.shape)
     shifts3 = Closed((rows, lanes), (rows, 16 * nz))
     shifts4 = Closed((k4.shape[1], lanes), (k4.shape[1], 8 * nz))
@@ -346,6 +368,7 @@
     weigh(k4, *w4, 1, n4 + 1, 0.25**4, shifts4, d4, inside, b4, U3)
     first_sweep(g3, d3, v3, 3, n3 + 3, U3)
     residual_of(v3, g3, r3, w3, 3, n3 + 3, shifts3, b=b3, unroll=U3)
+    ry3, rz3 = restriction(tall, rows4, rows3), restriction(wide, lanes3, lanes4, True)
     g4[...] = restrict(r3, 3, 0, n4, ry3, rz3, held).reshape(g4.shape)
     first_sweep(g4, d4, v4, 1, n4 + 1, U3, by=-1)
 
@@ -358,7 +381,8 @@
     def use(i, value):
         v3[i + 3] = v3[i + 3] + value
 
-    prolong(v4, 0, n4 + 2, py3[...], pz3[...], fine4, use)
+    py3, pz3 = prolongation(tall[::-1], rows3, rows4), prolongation(wide, lanes4, lanes3, True)
+    prolong(v4, 0, n4 + 2, py3, pz3, fine4, use)
     smooth(v3, g3, d3, w3, 3, n3 + 3, shifts3, b3, U3)
     return v3
 
@@ -373,21 +397,20 @@
     return jnp.where(whole == near, 0.75, jnp.where(whole == far, 0.25, 0.0))
 
 
-def upward(index, e3, g2, k2, d2, g1, k1, d1, ends, scratch, mats):
-    v2, w2, m2, v1, w1, fine2, fine1 = scratch
-    py1, pz1 = mats
+def upward(index, e3, g2, k2, g1, k1, ends, scratch):
+    v2, w2, d2, v1, w1, d1, fine2, fine1 = scratch
     shifts, w2, w1 = Open(), three(w2), three(w1)
-    weigh(k2, *w2, 1, 11, 0.25**2, shifts, unroll=U2)
-    weigh(k1, *w1, 6, 20, 0.25, shifts, unroll=U1)
-    first_sweep(g2, d2, v2, 0, 12, U2)
+    weigh(k2, *w2, 1, 11, 0.25**2, shifts, d2, inside, unroll=U2)
+    weigh(k1, *w1, 5, 21, 0.25, shifts, d1, inside, unroll=U1)
+    first_sweep(g2, d2, v2, 1, 11, U2)
     first_sweep(g1, d1, v1, 5, 21, U1)
-    m2[...] = d2[...]
-    if ends is not None:
-        for ref, i in zip(ends, (0, 11)):
-            v2[i], m2[i] = ref[0] * ref[1], ref[1]
+    zero = jnp.zeros(d2.shape[1:], F32)
+    for i, n in ((0, 0), (11, 1)):
+        v2[i] = zero if ends is None else ends[n][0] * ends[n][1]
+        d2[i] = zero if ends is None else ends[n][1]
 
     def use2(i, value):
-        v2[i] = jnp.where(m2[i] > 0.0, v2[i] + value, 0.0)
+        v2[i] = jnp.where(d2[i] > 0.0, v2[i] + value, 0.0)
 
     py2 = spread_matrix((g2.shape[1], e3.shape[1]), 0, index[1] * 4, 8)
     pz2 = spread_matrix((e3.shape[2], g2.shape[2]), 1, index[2] * 16, 32)
@@ -397,45 +420,51 @@
     def use1(i, value):
         v1[i + 5] = jnp.where(d1[i + 5] > 0.0, v1[i + 5] + value, 0.0)
 
-    prolong(v2, 1, 10, py1[...], pz1[...], fine1, use1)
+    py1, pz1 = prolongation((40, 24), Y1, Y2), prolongation((128, 128), Z2, Z1, True)
+    prolong(v2, 1, 10, py1, pz1, fine1, use1)
     smooth(v1, g1, d1, w1, 6, 20, shifts, unroll=U1)
     return v1
 
 
 BOTTOM = 14
-UP = 7
-
-
-def middle(nz, index, f, wx, wy, wz, d, k, s, g2, k2, d2, g1, k1, d1, *refs):
-    ends, m3, m1, (py0, pz0, ry, rz), (v, gn, turned, k3) = refs[:2], refs[2:8], refs[8:10], refs[10:14], refs[14:18]
-    low, mid, (fine0, r, held0) = refs[18:32], refs[32:39], refs[39:]
-    e3 = bottom(nz, s, k3, low, m3)
-    e1 = upward(index, e3, g2, k2, d2, g1, k1, d1, ends, mid, m1)
+UP = 8
+
+
+def middle(nz, index, f, k, s, g2, k2, g1, k1, *refs):
+    ends, (v, gn, turned, k3) = refs[:2], refs[2:6]
+    low, mid, (fine0, r, held0, wx, wy, wz, d) = refs[6:20], refs[20:28], refs[28:]
+    weigh(k, wx, wy, wz, 1, 25, 1.0, Open(), d, inside, unroll=U0)
+    e3 = bottom(nz, s, k3, low)
+    e1 = upward(index, e3, g2, k2, g1, k1, ends, mid)
     w, shifts = (wx, wy, wz), Open()
 
     def use(i, value):
         v[i + 1] = inside(k[i + 1], f[i + 1] * d[i + 1] + value)
 
-    prolong(e1, 6, 14, py0[...], pz0[...], fine0, use)
+    py0, pz0 = prolongation((48, 40), Y0, Y1), prolongation((128, 256), Z1, Z0, True)
+    prolong(e1, 6, 14, py0, pz0, fine0, use)
     smooth(v, f, d, w, 2, 24, shifts, unroll=U0)
     smooth(v, f, d, w, 3, 23, shifts, unroll=U0)
     residual_of(v, f, r, w, 4, 22, shifts, k, unroll=U0)
+    ry, rz = restriction((16, 48), span(16), Y0), restriction((256, 128), Z0, Z1, True)
     value = restrict(r, 5, 0, 8, ry, rz, held0)
     gn[...] = value.reshape(gn.shape)
     turned[...] = pltpu.roll(value, 64, 1).reshape(gn.shape)
 
 
-def final(nz, index, f, wx, wy, wz, d, k, v0, s, g2, k2, d2, g1, k1, d1, *refs):
-    m3, m1, (py0, pz0, k3), (solution_, residual_) = refs[:6], refs[6:8], refs[8:11], refs[11:13]
-    low, mid, (fine0, v) = refs[13:27], refs[27:34], refs[34:]
-    e3 = bottom(nz, s, k3, low, m3)
-    e1 = upward(index, e3, g2, k2, d2, g1, k1, d1, None, mid, m1)
+def final(nz, index, f, k, v0, s, g2, k2, g1, k1, *refs):
+    k3, (solution_, residual_) = refs[0], refs[1:3]
+    low, mid, (fine0, wx, wy, wz, d, v) = refs[3:17], refs[17:25], refs[25:]
+    weigh(k, wx, wy, wz, 3, 22, 1.0, Open(), d, inside, unroll=U0)
+    e3 = bottom(nz, s, k3, low)
+    e1 = upward(index, e3, g2, k2, g1, k1, None, mid)
     w, shifts = (wx, wy, wz), Open()
 
     def use(i, value):
         v[i + 3] = inside(k[i + 3], v0[i + 3] + value)
 
-    prolong(e1, 7, 12, py0[...], pz0[...], fine0, use)
+    py0, pz0 = prolongation((48, 40), Y0, Y1), prolongation((128, 256), Z1, Z0, True)
+    prolong(e1, 7, 12, py0, pz0, fine0, use)
     smooth(v, f, d, w, 4, 22, shifts, unroll=U0)
 
     def last(i, here, im):
@@ -519,33 +548,6 @@
     nx, ny, nz = (lax.axis_size(axis) for axis in ("gx", "gy", "gz"))
     index = jnp.stack([lax.axis_index(axis) for axis in ("gx", "gy", "gz")]).astype(jnp.int32)
 
-    def ends(size, count, away=-1000, start=0):
-        at = np.arange(size)
-        return np.where((at >= start) & (at < start + count), at - start, away)
-
-    y0, z0 = coords(48, 32), coords(256, 128)
-    y1, z1 = coords(40, 16), coords(128, 64)
-    y2, z2 = coords(24, 8), coords(128, 32)
-    rows3, rows4 = np.arange(4 * ny), np.arange(2 * ny)
-    lanes3, lanes4 = ends(128, 16 * nz, -3000), ends(128, 8 * nz, -9000)
-    ry0, rz0 = restriction(np.arange(16), y0), restriction(z1, z0).T
-    cy0, cz0 = halving(np.arange(16), y0), halving(z1, z0).T
-    ry1, rz1 = restriction(y2, y1), restriction(z2, z1).T
-    cy1, cz1 = halving(y2, y1), halving(z2, z1).T
-
-    def both(matrix):
-        zero = np.zeros_like(matrix)
-        return np.stack([np.concatenate([matrix, zero]), np.concatenate([zero, matrix])])
-
-    ry2, rz2 = both(restriction(np.arange(4), y2)), restriction(ends(128, 16), z2).T
-    cy2, cz2 = both(halving(np.arange(4), y2)), halving(ends(128, 16, start=16), z2).T
-    ry3, rz3 = restriction(rows4, rows3), restriction(lanes4, lanes3).T
-    cy3, cz3 = halving(rows4, rows3), halving(lanes4, lanes3).T
-    py0, pz0 = prolongation(y0, y1), prolongation(z0, z1).T
-    py1, pz1 = prolongation(y1, y2), prolongation(z1, z2).T
-    py3, pz3 = prolongation(rows3, rows4), prolongation(lanes3, lanes4).T
-    m3, m1 = (ry3, rz3, cy3, cz3, py3, pz3), (py1, pz1)
-
     wide, l1, l2 = (26, 48, 256), (26, 40, 128), (12, 24, 128)
     n3, n4 = (2 * nx + 6, 4 * ny, 128), (nx + 2, 2 * ny, 128)
     low = [
@@ -553,48 +555,46 @@
         n4, (nx, 2 * ny, 128), n4, (3,) + n4, n4, n4,
         (nx * 2 * ny, 128), (nx + 2, 4 * ny, 128),
     ]
-    mid = [l2, (3,) + l2, l2, l1, (3,) + l1, (8, 24, 128), (10, 40, 128)]
+    mid = [l2, (3,) + l2, l2, l1, (3,) + l1, l1, (8, 24, 128), (10, 40, 128)]
     tiles = nx // 8
 
-    f, k, wx, wy, wz, d, both1 = call(
-        down0, [wide] * 6 + [(20, 16, 128)], [wide] * 2 + [(160, 256)],
-        *finest([right_side, conductivity]), ry0, rz0, cy0, cz0, name="down0", room=6,
+    right_side, conductivity, index = lax.optimization_barrier((right_side, conductivity, index))
+    f, k, both1 = call(
+        down0, [wide] * 2 + [(20, 16, 128)], [wide] * 6 + [(160, 256)],
+        *finest([right_side, conductivity]), name="down0", room=14,
     )
     own = rows1(both1)
     last = jnp.concatenate([own[0:9], own[10:19]])
     initial = jnp.concatenate([own[1:10], own[11:20]])
     before, after = neighbours(last, initial, "gx")
-    inner = [l1, l1, (288, 128), (3,) + l1, l2, l2, (3,) + l2, (8, 128)]
-    pieces, g1, k1, d1, g2, k2, d2 = call(
-        functools.partial(descend, True), [(nx, 8, 128), l1, l1, l1, l2, l2, l2], inner,
-        before, own, after, ry1, rz1, ry2, rz2, cy1, cz1, cy2, cz2, name="descend", room=14,
+    inner = [l1, l1, (288, 128), (3,) + l1, l1, l2, l2, (3,) + l2, l2]
+    pair = (2, 24, 128)
+    pieces, g1, k1, g2, k2, below, above = call(
+        functools.partial(descend, True), [(nx, 8, 128), l1, l1, l2, l2, pair, pair], inner,
+        before, own, after, name="descend", room=10,
     )
-    first, last = jnp.stack([g2[4], d2[4]]), jnp.stack([g2[7], d2[7]])
-    outer = neighbours(first, last, "gx")
     pieces = everyone(pieces, "gx")
     (pieces,) = call(repack, [(ny * nz, 2 * tiles, 8, 128)], [], pieces, name="repack")
+    outer = neighbours(below, above, "gx")
     s = everyone(pieces, ("gy", "gz"))
-    fields = (f, wx, wy, wz, d, k)
     v, value, turned, k3 = call(
         functools.partial(middle, nz), [wide, (8, 16, 128), (8, 16, 128), n3],
-        low + mid + [(14, 48, 256), wide, (128, 256)],
-        index, *fields, s, g2, k2, d2, g1, k1, d1, *outer, *m3, *m1, py0, pz0, ry0, rz0,
-        name="middle", room=14, scalars=1,
+        low + mid + [(14, 48, 256), wide, (128, 256)] + [wide] * 4,
+        index, f, k, s, g2, k2, g1, k1, *outer, name="middle", room=20, scalars=1,
     )
     own = rows1(lanes1(value, turned))
     before, after = neighbours(own, own, "gx")
     pieces, g1, g2 = call(
         functools.partial(descend, False), [(nx, 8, 128), l1, l2], inner,
-        before, own, after, k1, d1, k2, d2, ry1, rz1, ry2, rz2, name="again", room=14,
+        before, own, after, k1, k2, name="again", room=10,
     )
     pieces = everyone(pieces, "gx")
     (pieces,) = call(repack, [(ny * nz, tiles, 8, 128)], [], pieces, name="repack2")
     s = everyone(pieces, ("gy", "gz"))
     return tuple(call(
         functools.partial(final, nz), [(16, 32, 128)] * 2,
-        low + mid + [(12, 48, 256), wide],
-        index, *fields, v, s, g2, k2, d2, g1, k1, d1, *m3, *m1, py0, pz0, k3,
-        name="final", room=14, scalars=1,
+        low + mid + [(12, 48, 256)] + [wide] * 5,
+        index, f, k, v, s, g2, k2, g1, k1, k3, name="final", room=20, scalars=1,
     ))
 
 

time: 236 us -> 211 us (0.89)
  local copies, waits for them, and re-layouts: 30.3 us -> 4.87 us
  blocking collectives: 38.9 us -> 62 us
  starting transfers between devices: 68.5 us -> 54.2 us
  waiting for transfers between devices: 55.5 us -> 48.9 us
  other arithmetic: 3.94 us -> 1.41 us
    unnamed x116 -> x10, local copies, waits for them, and re-layouts: 26.9 us -> 2.78 us
    all_to_all x2 -> x3, blocking collectives: 38.9 us -> 62 us  [everyone(): return lax.all_to_all(pieces, axes, 0, 0)]
    all_to_all x2 -> x1, starting transfers between devices: 26.9 us -> 14.2 us  [everyone(): return lax.all_to_all(pieces, axes, 0, 0)]
    all_to_all x2 -> x1, waiting for transfers between devices: 11.8 us -> 4.15 us  [everyone(): return lax.all_to_all(pieces, axes, 0, 0)]
  transfers between devices with their start and end apart: 20 -> 19, of which waited for: 18 -> 17; matrix products, arithmetic and copies ran while one was open for 2% -> 0% of each run, Pallas kernels for 0% -> 0%
where the time goes in v6:
time: 211 us; the launch traced here: 210 us
  blocking collectives  62 us (29%)
  starting transfers between devices  54.2 us (26%)
  waiting for transfers between devices  48.9 us (23%)
  Pallas kernels  38.1 us (18%)
  local copies, waits for them, and re-layouts  4.87 us (2%)
    all_to_all x3, blocking collectives, everyone(): return lax.all_to_all(pieces, axes, 0, 0)  62 us
    pallas_call x7, Pallas kernels, call(): pl.pallas_call(kernel, out_shape=[jax.ShapeDtypeStruct(o, F32) for o in o...  38.1 us
    ppermute x9, waiting for transfers between devices, neighbours(): after = lax.ppermute(initial, axis, down)  28.4 us
    ppermute x9, starting transfers between devices, neighbours(): before = lax.ppermute(last, axis, up)  26.2 us
    ppermute x9, waiting for transfers between devices, neighbours(): before = lax.ppermute(last, axis, up)  16.3 us
    all_to_all x1, starting transfers between devices, everyone(): return lax.all_to_all(pieces, axes, 0, 0)  14.2 us
    ppermute x9, starting transfers between devices, neighbours(): after = lax.ppermute(initial, axis, down)  13.8 us
  transfers between devices with their start and end apart: 19, of which 17 were waited for; matrix products, arithmetic and copies ran while one was open for 0% of the time, Pallas kernels for 0%

profile of v6, /device:TPU:1, one launch (start us, length us, event | category | flops | bytes accessed | tf_op | source)
XLA Modules:
  0.0 210.5 jit_solution(3916890692692713963)
XLA Ops:
  0.6 0.1 pad_add_fusion.index
  0.7 1.4 fusion.19
  2.1 0.1 pad_maximum_fusion.10
  2.3 2.7 %collective-permute-start.1 = (f32[16,32,50]{2,1,0:T(8,128)S(1)}, f32[16,32,50]{2,1,0:T(8,128)S(1)}, u32[]{:S(2)}, u32[]{:S(2)}) collective-permute-start(f32[16,32,50]{2,1,0:T(8,128)S(1)} %pad_maximum_fusion.10), channel_id=1, source_target_pairs={{0,1},{1,2},{2,3},{3,4},{4,5},{5,6},{6,7},{7,0},{8,9},{9,10},{10,1... | collective-permute-start | bytes 307208 | tf_op jit(solution)/shard_map/ppermute | solution.py:500
  5.0 0.1 pad_maximum_fusion.9
  5.1 4.2 %collective-permute-start = (f32[16,32,50]{2,1,0:T(8,128)S(1)}, f32[16,32,50]{2,1,0:T(8,128)S(1)}, u32[]{:S(2)}, u32[]{:S(2)}) collective-permute-start(f32[16,32,50]{2,1,0:T(8,128)S(1)} %pad_maximum_fusion.9), channel_id=1, source_target_pairs={{1,0},{2,1},{3,2},{4,3},{5,4},{6,5},{7,6},{0,7},{9,8},{10,9},{11,1... | collective-permute-start | bytes 307208 | tf_op jit(solution)/shard_map/ppermute | solution.py:501
  9.3 0.9 collective-permute-done.1
  10.3 0.1 fusion.18
  10.4 0.5 collective-permute-done
  11.0 0.1 fusion.17
  11.1 0.1 copy-done.3
  11.2 0.1 copy-done.4
  11.3 0.3 fusion.8
  11.7 3.0 %collective-permute-start.3 = (f32[32,5,256]{2,1,0:T(8,128)S(1)}, f32[32,5,256]{2,1,0:T(8,128)S(1)}, u32[]{:S(2)}, u32[]{:S(2)}) collective-permute-start(f32[32,5,256]{2,1,0:T(8,128)S(1)} %pad_maximum_fusion.12), channel_id=1, source_target_pairs={{0,8},{8,16},{16,24},{1,9},{9,17},{17,25},{2,10},{10,18},{18,26},{... | collective-permute-start | bytes 491528 | tf_op jit(solution)/shard_map/ppermute | solution.py:500
  14.7 0.1 pad.28.clone
  14.8 1.3 collective-permute-start.2
  16.1 1.9 collective-permute-done.3
  18.0 3.9 %collective-permute-done.2 = f32[32,5,256]{2,1,0:T(8,128)S(1)} collective-permute-done((f32[32,5,256]{2,1,0:T(8,128)S(1)}, f32[32,5,256]{2,1,0:T(8,128)S(1)}, u32[]{:S(2)}, u32[]{:S(2)}) %collective-permute-start.2) | collective-permute-done | bytes 163872 | tf_op jit(solution)/shard_map/ppermute | solution.py:501
  21.9 0.3 fusion.3
  22.4 5.2 %collective-permute-start.4 = (f32[10,48,256]{2,1,0:T(8,128)S(1)}, f32[10,48,256]{2,1,0:T(8,128)S(1)}, u32[]{:S(2)}, u32[]{:S(2)}) collective-permute-start(f32[10,48,256]{2,1,0:T(8,128)S(1)} %pad_maximum_fusion.4), channel_id=1, source_target_pairs={{0,32},{32,64},{64,96},{96,128},{128,160},{160,192},{192,224},{224... | collective-permute-start | bytes 1474568 | tf_op jit(solution)/shard_map/ppermute | solution.py:500
  27.6 1.3 collective-permute-start.5
  28.9 7.2 %collective-permute-done.4.before = f32[10,48,256]{2,1,0:T(8,128)S(1)} collective-permute-done((f32[10,48,256]{2,1,0:T(8,128)S(1)}, f32[10,48,256]{2,1,0:T(8,128)S(1)}, u32[]{:S(2)}, u32[]{:S(2)}) %collective-permute-start.4) | collective-permute-done | bytes 491552 | tf_op jit(solution)/shard_map/ppermute | solution.py:500
  36.1 4.2 %collective-permute-done.5.after = f32[10,48,256]{2,1,0:T(8,128)S(1)} collective-permute-done((f32[10,48,256]{2,1,0:T(8,128)S(1)}, f32[10,48,256]{2,1,0:T(8,128)S(1)}, u32[]{:S(2)}, u32[]{:S(2)}) %collective-permute-start.5) | collective-permute-done | bytes 491552 | tf_op jit(solution)/shard_map/ppermute | solution.py:501
  40.4 4.1 %down0.1 = (f32[26,48,256]{2,1,0:T(8,128)S(1)}, f32[26,48,256]{2,1,0:T(8,128)S(1)}, f32[20,16,128]{2,1,0:T(8,128)S(1)}) custom-call(f32[10,48,256]{2,1,0:T(8,128)S(1)} %collective-permute-done.4.before, f32[16,48,256]{2,1,0:T(8,128)S(1)} %get-tuple-element.54.fo, f32[16,48,256]{2,1,0:T(8,128)S(1)} %get-tuple-element.55.ko, ...), custom_call_target="tpu_custom_call" | custom-call | tf_op jit(solution)/shard_map/down0/pallas_call | solution.py:482
  44.5 3.1 %collective-permute-start.7 = (f32[20,16,128]{2,1,0:T(8,128)S(1)}, f32[20,16,128]{2,1,0:T(8,128)S(1)}, u32[]{:S(2)}, u32[]{:S(2)}) collective-permute-start(f32[20,16,128]{2,1,0:T(8,128)S(1)} %get-tuple-element.27), channel_id=1, source_target_pairs={{0,8},{8,16},{16,24},{1,9},{9,17},{17,25},{2,10},{10,18},{18,26},{... | collective-permute-start | bytes 491528 | tf_op jit(solution)/shard_map/ppermute | solution.py:500
  47.6 1.3 collective-permute-start.6
  48.9 0.1 pad.10.clone
  49.0 0.9 collective-permute-done.7
  49.9 3.8 %collective-permute-done.6 = f32[20,16,128]{2,1,0:T(8,128)S(1)} collective-permute-done((f32[20,16,128]{2,1,0:T(8,128)S(1)}, f32[20,16,128]{2,1,0:T(8,128)S(1)}, u32[]{:S(2)}, u32[]{:S(2)}) %collective-permute-start.6) | collective-permute-done | bytes 163872 | tf_op jit(solution)/shard_map/ppermute | solution.py:501
  53.7 0.1 pad_maximum_fusion.6.refs_1_
  53.8 0.1 fusion.14
  53.9 3.6 %collective-permute-start.8 = (f32[18,40,128]{2,1,0:T(8,128)S(1)}, f32[18,40,128]{2,1,0:T(8,128)S(1)}, u32[]{:S(2)}, u32[]{:S(2)}) collective-permute-start(f32[18,40,128]{2,1,0:T(8,128)S(1)} %pad_maximum_fusion.7), channel_id=1, source_target_pairs={{0,32},{32,64},{64,96},{96,128},{128,160},{160,192},{192,224},{224... | collective-permute-start | bytes 1105928 | tf_op jit(solution)/shard_map/ppermute | solution.py:500
  57.5 1.3 collective-permute-start.9
  58.8 3.1 %collective-permute-done.8.refs_0_ = f32[18,40,128]{2,1,0:T(8,128)S(1)} collective-permute-done((f32[18,40,128]{2,1,0:T(8,128)S(1)}, f32[18,40,128]{2,1,0:T(8,128)S(1)}, u32[]{:S(2)}, u32[]{:S(2)}) %collective-permute-start.8) | collective-permute-done | bytes 368672 | tf_op jit(solution)/shard_map/ppermute | solution.py:500
  61.9 5.3 %collective-permute-done.9.refs_2_ = f32[18,40,128]{2,1,0:T(8,128)S(1)} collective-permute-done((f32[18,40,128]{2,1,0:T(8,128)S(1)}, f32[18,40,128]{2,1,0:T(8,128)S(1)}, u32[]{:S(2)}, u32[]{:S(2)}) %collective-permute-start.9) | collective-permute-done | bytes 368672 | tf_op jit(solution)/shard_map/ppermute | solution.py:501
  67.2 2.9 %descend.1 = (f32[16,8,128]{2,1,0:T(8,128)S(1)}, f32[26,40,128]{2,1,0:T(8,128)S(1)}, f32[26,40,128]{2,1,0:T(8,128)S(1)}, f32[12,24,128]{2,1,0:T(8,128)S(1)}, f32...) custom-call(f32[18,40,128]{2,1,0:T(8,128)S(1)} %collective-permute-done.8.refs_0_, ...), custom_call_target="tpu_custom_call" | custom-call | tf_op jit(solution)/shard_map/descend/pallas_call | solution.py:482
  70.2 0.8 copy-done.1
  71.0 23.9 %all_to_all.20.s = f32[16,8,128]{2,1,0:T(8,128)S(1)} all-to-all(f32[16,8,128]{2,1,0:T(8,128)S(1)} %get-tuple-element.28), channel_id=1, replica_groups=mesh['gx'=16,'gy'=4,'gz'=8] {'gx'}, dimensions={0} | all-to-all | bytes 131072 | tf_op jit(solution)/shard_map/all_to_all | solution.py:544
  94.8 0.2 repack.1
  95.0 0.8 copy-done
  95.8 14.2 %all-to-all-start.1 = ((f32[32,4,8,128]{3,2,1,0:T(8,128)}), f32[32,4,8,128]{3,2,1,0:T(8,128)}, u32[]{:S(2)}, u32[]{:S(2)}) async-start(f32[32,4,8,128]{3,2,1,0:T(8,128)} %copy-done), calls=%async_computation.1 | async-start | bytes 1048576 | tf_op jit(solution)/shard_map/all_to_all | solution.py:544
  110.0 2.5 %collective-permute-start.10 = (f32[2,24,128]{2,1,0:T(8,128)S(1)}, f32[2,24,128]{2,1,0:T(8,128)S(1)}, u32[]{:S(2)}, u32[]{:S(2)}) collective-permute-start(f32[2,24,128]{2,1,0:T(8,128)S(1)} %get-tuple-element.33), channel_id=1, source_target_pairs={{0,32},{32,64},{64,96},{96,128},{128,160},{160,192},{192,224},{224... | collective-permute-start | bytes 73736 | tf_op jit(solution)/shard_map/ppermute | solution.py:500
  112.6 1.5 collective-permute-start.11
  114.1 3.5 %collective-permute-done.11.refs_1_ = f32[2,24,128]{2,1,0:T(8,128)S(1)} collective-permute-done((f32[2,24,128]{2,1,0:T(8,128)S(1)}, f32[2,24,128]{2,1,0:T(8,128)S(1)}, u32[]{:S(2)}, u32[]{:S(2)}) %collective-permute-start.11) | collective-permute-done | bytes 24608 | tf_op jit(solution)/shard_map/ppermute | solution.py:501
  117.6 4.1 %all-to-all-done.1.s = f32[32,4,8,128]{3,2,1,0:T(8,128)} async-done(((f32[32,4,8,128]{3,2,1,0:T(8,128)}), f32[32,4,8,128]{3,2,1,0:T(8,128)}, u32[]{:S(2)}, u32[]{:S(2)}) %all-to-all-start.1) | async-done | bytes 524320 | tf_op jit(solution)/shard_map/all_to_all | solution.py:544
  121.7 1.0 copy-done.2
  122.8 16.3 %middle.1 = (f32[26,48,256]{2,1,0:T(8,128)S(1)}, f32[8,16,128]{2,1,0:T(8,128)S(1)}, f32[8,16,128]{2,1,0:T(8,128)S(1)}, f32[38,16,128]{2,1,0:T(8,128)S(1)}) custom-call(s32[3]{0:T(128)S(1)} %pad_add_fusion.index, f32[26,48,256]{2,1,0:T(8,128)S(1)} %get-tuple-element.25.f, f32[26,48,256]{2,1,0:T(8,128)S(1)} %get-tuple-element.26.k, ...), custom_call_target="tpu_custom_call" | custom-call | tf_op jit(solution)/shard_map/middle/pallas_call | solution.py:482
  139.0 0.2 collective-permute-start.13
  139.2 0.4 collective-permute-start.12
  139.6 1.0 collective-permute-done.13
  140.5 2.7 %collective-permute-done.12 = f32[8,16,128]{2,1,0:T(8,128)S(1)} collective-permute-done((f32[8,16,128]{2,1,0:T(8,128)S(1)}, f32[8,16,128]{2,1,0:T(8,128)S(1)}, u32[]{:S(2)}, u32[]{:S(2)}) %collective-permute-start.12) | collective-permute-done | bytes 65568 | tf_op jit(solution)/shard_map/ppermute | solution.py:501
  143.2 1.9 collective-permute-start.15
  145.1 1.3 collective-permute-start.14
  146.4 3.7 %collective-permute-done.14 = f32[8,16,128]{2,1,0:T(8,128)S(1)} collective-permute-done((f32[8,16,128]{2,1,0:T(8,128)S(1)}, f32[8,16,128]{2,1,0:T(8,128)S(1)}, u32[]{:S(2)}, u32[]{:S(2)}) %collective-permute-start.14) | collective-permute-done | bytes 65568 | tf_op jit(solution)/shard_map/ppermute | solution.py:501
  150.1 0.1 pad_maximum_fusion.13.refs_1_
  150.2 1.3 collective-permute-start.17
  151.5 4.0 %collective-permute-start.16 = (f32[8,40,128]{2,1,0:T(8,128)S(1)}, f32[8,40,128]{2,1,0:T(8,128)S(1)}, u32[]{:S(2)}, u32[]{:S(2)}) collective-permute-start(f32[8,40,128]{2,1,0:T(8,128)S(1)} %pad_maximum_fusion.13.refs_1_), channel_id=1, source_target_pairs={{0,32},{32,64},{64,96},{96,128},{128,160},{160,192},{192,224},{224... | collective-permute-start | bytes 491528 | tf_op jit(solution)/shard_map/ppermute | solution.py:500
  155.5 0.8 collective-permute-done.17.refs_2_
  156.3 1.5 collective-permute-done.16.refs_0_
  157.7 2.1 again.1
  159.8 18.2 %all_to_all.21.s = f32[16,8,128]{2,1,0:T(8,128)S(1)} all-to-all(f32[16,8,128]{2,1,0:T(8,128)S(1)} %get-tuple-element.38), channel_id=1, replica_groups=mesh['gx'=16,'gy'=4,'gz'=8] {'gx'}, dimensions={0} | all-to-all | bytes 131072 | tf_op jit(solution)/shard_map/all_to_all | solution.py:544
  178.1 0.1 repack2.1
  178.2 19.9 %all_to_all.22.s = f32[32,2,8,128]{3,2,1,0:T(8,128)S(1)} all-to-all(f32[32,2,8,128]{3,2,1,0:T(8,128)S(1)} %repack2.1), channel_id=1, replica_groups=mesh['gx'=16,'gy'=4,'gz'=8] {'gy','gz'}, dimensions={0} | all-to-all | bytes 524288 | tf_op jit(solution)/shard_map/all_to_all | solution.py:544
  198.1 12.3 %final.1 = (f32[16,32,128]{2,1,0:T(8,128)}, f32[16,32,128]{2,1,0:T(8,128)}) custom-call(s32[3]{0:T(128)S(1)} %pad_add_fusion.index, f32[26,48,256]{2,1,0:T(8,128)S(1)} %get-tuple-element.25.f, f32[26,48,256]{2,1,0:T(8,128)S(1)} %get-tuple-element.26.k, f32[26,48,256]{2,1,0:T(8,128)S(1)} %get-tuple-element.35.v0, f32[32,2,8,128]{3,2,1,0:T(8,128)S(1)} %all_to_all.22.s, ...), custom_call_target="tpu_custom_call" | custom-call | tf_op jit(solution)/shard_map/final/pallas_call | solution.py:482
  (29 shorter events, 0.5 us)
Async XLA Ops:
  2.3 7.9 %collective-permute-start.1 = (f32[16,32,50]{2,1,0:T(8,128)S(1)}, f32[16,32,50]{2,1,0:T(8,128)S(1)}, u32[]{:S(2)}, u32[]{:S(2)}) collective-permute-start(f32[16,32,50]{2,1,0:T(8,128)S(1)} %pad_maximum_fusion.10), channel_id=1, source_target_pairs={{0,1},{1,2},{2,3},{3,4},{4,5},{5,6},{6,7},{7,0},{8,9},{9,10},{10,1... | collective-permute-start | bytes 307208 | tf_op jit(solution)/shard_map/ppermute | solution.py:500
  5.1 5.8 %collective-permute-start = (f32[16,32,50]{2,1,0:T(8,128)S(1)}, f32[16,32,50]{2,1,0:T(8,128)S(1)}, u32[]{:S(2)}, u32[]{:S(2)}) collective-permute-start(f32[16,32,50]{2,1,0:T(8,128)S(1)} %pad_maximum_fusion.9), channel_id=1, source_target_pairs={{1,0},{2,1},{3,2},{4,3},{5,4},{6,5},{7,6},{0,7},{9,8},{10,9},{11,1... | collective-permute-start | bytes 307208 | tf_op jit(solution)/shard_map/ppermute | solution.py:501
  10.2 1.0 copy-start.3
  10.2 1.0 copy-start.4
  11.7 6.3 %collective-permute-start.3 = (f32[32,5,256]{2,1,0:T(8,128)S(1)}, f32[32,5,256]{2,1,0:T(8,128)S(1)}, u32[]{:S(2)}, u32[]{:S(2)}) collective-permute-start(f32[32,5,256]{2,1,0:T(8,128)S(1)} %pad_maximum_fusion.12), channel_id=1, source_target_pairs={{0,8},{8,16},{16,24},{1,9},{9,17},{17,25},{2,10},{10,18},{18,26},{... | collective-permute-start | bytes 491528 | tf_op jit(solution)/shard_map/ppermute | solution.py:500
  14.8 7.1 %collective-permute-start.2 = (f32[32,5,256]{2,1,0:T(8,128)S(1)}, f32[32,5,256]{2,1,0:T(8,128)S(1)}, u32[]{:S(2)}, u32[]{:S(2)}) collective-permute-start(f32[32,5,256]{2,1,0:T(8,128)S(1)} %pad_maximum_fusion.11), channel_id=1, source_target_pairs={{8,0},{16,8},{24,16},{9,1},{17,9},{25,17},{10,2},{18,10},{26,18},{... | collective-permute-start | bytes 491528 | tf_op jit(solution)/shard_map/ppermute | solution.py:501
  22.4 13.7 %collective-permute-start.4 = (f32[10,48,256]{2,1,0:T(8,128)S(1)}, f32[10,48,256]{2,1,0:T(8,128)S(1)}, u32[]{:S(2)}, u32[]{:S(2)}) collective-permute-start(f32[10,48,256]{2,1,0:T(8,128)S(1)} %pad_maximum_fusion.4), channel_id=1, source_target_pairs={{0,32},{32,64},{64,96},{96,128},{128,160},{160,192},{192,224},{224... | collective-permute-start | bytes 1474568 | tf_op jit(solution)/shard_map/ppermute | solution.py:500
  27.6 12.7 %collective-permute-start.5 = (f32[10,48,256]{2,1,0:T(8,128)S(1)}, f32[10,48,256]{2,1,0:T(8,128)S(1)}, u32[]{:S(2)}, u32[]{:S(2)}) collective-permute-start(f32[10,48,256]{2,1,0:T(8,128)S(1)} %pad_maximum_fusion.5), channel_id=1, source_target_pairs={{32,0},{64,32},{96,64},{128,96},{160,128},{192,160},{224,192},{256... | collective-permute-start | bytes 1474568 | tf_op jit(solution)/shard_map/ppermute | solution.py:501
  44.5 5.4 %collective-permute-start.7 = (f32[20,16,128]{2,1,0:T(8,128)S(1)}, f32[20,16,128]{2,1,0:T(8,128)S(1)}, u32[]{:S(2)}, u32[]{:S(2)}) collective-permute-start(f32[20,16,128]{2,1,0:T(8,128)S(1)} %get-tuple-element.27), channel_id=1, source_target_pairs={{0,8},{8,16},{16,24},{1,9},{9,17},{17,25},{2,10},{10,18},{18,26},{... | collective-permute-start | bytes 491528 | tf_op jit(solution)/shard_map/ppermute | solution.py:500
  47.6 6.1 %collective-permute-start.6 = (f32[20,16,128]{2,1,0:T(8,128)S(1)}, f32[20,16,128]{2,1,0:T(8,128)S(1)}, u32[]{:S(2)}, u32[]{:S(2)}) collective-permute-start(f32[20,16,128]{2,1,0:T(8,128)S(1)} %get-tuple-element.27), channel_id=1, source_target_pairs={{8,0},{16,8},{24,16},{9,1},{17,9},{25,17},{10,2},{18,10},{26,18},{... | collective-permute-start | bytes 491528 | tf_op jit(solution)/shard_map/ppermute | solution.py:501
  53.9 8.0 %collective-permute-start.8 = (f32[18,40,128]{2,1,0:T(8,128)S(1)}, f32[18,40,128]{2,1,0:T(8,128)S(1)}, u32[]{:S(2)}, u32[]{:S(2)}) collective-permute-start(f32[18,40,128]{2,1,0:T(8,128)S(1)} %pad_maximum_fusion.7), channel_id=1, source_target_pairs={{0,32},{32,64},{64,96},{96,128},{128,160},{160,192},{192,224},{224... | collective-permute-start | bytes 1105928 | tf_op jit(solution)/shard_map/ppermute | solution.py:500
  57.5 9.7 %collective-permute-start.9 = (f32[18,40,128]{2,1,0:T(8,128)S(1)}, f32[18,40,128]{2,1,0:T(8,128)S(1)}, u32[]{:S(2)}, u32[]{:S(2)}) collective-permute-start(f32[18,40,128]{2,1,0:T(8,128)S(1)} %pad_maximum_fusion.8), channel_id=1, source_target_pairs={{32,0},{64,32},{96,64},{128,96},{160,128},{192,160},{224,192},{256... | collective-permute-start | bytes 1105928 | tf_op jit(solution)/shard_map/ppermute | solution.py:501
  70.2 0.8 copy-start.1
  95.0 0.8 copy-start
  95.8 25.9 %all-to-all-start.1 = ((f32[32,4,8,128]{3,2,1,0:T(8,128)}), f32[32,4,8,128]{3,2,1,0:T(8,128)}, u32[]{:S(2)}, u32[]{:S(2)}) async-start(f32[32,4,8,128]{3,2,1,0:T(8,128)} %copy-done), calls=%async_computation.1 | async-start | bytes 1048576 | tf_op jit(solution)/shard_map/all_to_all | solution.py:544
  110.0 4.0 %collective-permute-start.10 = (f32[2,24,128]{2,1,0:T(8,128)S(1)}, f32[2,24,128]{2,1,0:T(8,128)S(1)}, u32[]{:S(2)}, u32[]{:S(2)}) collective-permute-start(f32[2,24,128]{2,1,0:T(8,128)S(1)} %get-tuple-element.33), channel_id=1, source_target_pairs={{0,32},{32,64},{64,96},{96,128},{128,160},{160,192},{192,224},{224... | collective-permute-start | bytes 73736 | tf_op jit(solution)/shard_map/ppermute | solution.py:500
  112.6 5.0 %collective-permute-start.11 = (f32[2,24,128]{2,1,0:T(8,128)S(1)}, f32[2,24,128]{2,1,0:T(8,128)S(1)}, u32[]{:S(2)}, u32[]{:S(2)}) collective-permute-start(f32[2,24,128]{2,1,0:T(8,128)S(1)} %get-tuple-element.34), channel_id=1, source_target_pairs={{32,0},{64,32},{96,64},{128,96},{160,128},{192,160},{224,192},{256... | collective-permute-start | bytes 73736 | tf_op jit(solution)/shard_map/ppermute | solution.py:501
  121.7 1.0 copy-start.2
  139.0 1.5 collective-permute-start.13
  139.2 4.0 %collective-permute-start.12 = (f32[8,16,128]{2,1,0:T(8,128)S(1)}, f32[8,16,128]{2,1,0:T(8,128)S(1)}, u32[]{:S(2)}, u32[]{:S(2)}) collective-permute-start(f32[8,16,128]{2,1,0:T(8,128)S(1)} %get-tuple-element.37), channel_id=1, source_target_pairs={{1,0},{2,1},{3,2},{4,3},{5,4},{6,5},{7,6},{0,7},{9,8},{10,9},{11,1... | collective-permute-start | bytes 196616 | tf_op jit(solution)/shard_map/ppermute | solution.py:501
  143.2 3.2 %collective-permute-start.15 = (f32[8,16,128]{2,1,0:T(8,128)S(1)}, f32[8,16,128]{2,1,0:T(8,128)S(1)}, u32[]{:S(2)}, u32[]{:S(2)}) collective-permute-start(f32[8,16,128]{2,1,0:T(8,128)S(1)} %select_select_fusion), channel_id=1, source_target_pairs={{0,8},{8,16},{16,24},{1,9},{9,17},{17,25},{2,10},{10,18},{18,26},{... | collective-permute-start | bytes 196616 | tf_op jit(solution)/shard_map/ppermute | solution.py:500
  145.1 5.0 %collective-permute-start.14 = (f32[8,16,128]{2,1,0:T(8,128)S(1)}, f32[8,16,128]{2,1,0:T(8,128)S(1)}, u32[]{:S(2)}, u32[]{:S(2)}) collective-permute-start(f32[8,16,128]{2,1,0:T(8,128)S(1)} %select_select_fusion), channel_id=1, source_target_pairs={{8,0},{16,8},{24,16},{9,1},{17,9},{25,17},{10,2},{18,10},{26,18},{... | collective-permute-start | bytes 196616 | tf_op jit(solution)/shard_map/ppermute | solution.py:501
  150.2 6.1 %collective-permute-start.17 = (f32[8,40,128]{2,1,0:T(8,128)S(1)}, f32[8,40,128]{2,1,0:T(8,128)S(1)}, u32[]{:S(2)}, u32[]{:S(2)}) collective-permute-start(f32[8,40,128]{2,1,0:T(8,128)S(1)} %pad_maximum_fusion.13.refs_1_), channel_id=1, source_target_pairs={{32,0},{64,32},{96,64},{128,96},{160,128},{192,160},{224,192},{256... | collective-permute-start | bytes 491528 | tf_op jit(solution)/shard_map/ppermute | solution.py:501
  151.5 6.2 %collective-permute-start.16 = (f32[8,40,128]{2,1,0:T(8,128)S(1)}, f32[8,40,128]{2,1,0:T(8,128)S(1)}, u32[]{:S(2)}, u32[]{:S(2)}) collective-permute-start(f32[8,40,128]{2,1,0:T(8,128)S(1)} %pad_maximum_fusion.13.refs_1_), channel_id=1, source_target_pairs={{0,32},{32,64},{64,96},{96,128},{128,160},{160,192},{192,224},{224... | collective-permute-start | bytes 491528 | tf_op jit(solution)/shard_map/ppermute | solution.py:500

commit v7 on v6

--- a/solution.py
+++ b/solution.py
@@ -56,11 +56,27 @@
 Y0, Z0, Y1, Z1, Y2, Z2 = ring(48, 32), ring(256, 128), ring(40, 16), ring(128, 64), ring(24, 8), ring(128, 32)
 
 
-def dot(a, b):
-    return lax.dot_general(
-        a, b, (((1,), (0,)), ((), ())),
-        precision=lax.Precision.HIGHEST, preferred_element_type=F32,
-    )
+def parts(v):
+    high = v.astype(jnp.bfloat16)
+    rest = v - high.astype(F32)
+    middle = rest.astype(jnp.bfloat16)
+    return high, middle, (rest - middle.astype(F32)).astype(jnp.bfloat16)
+
+
+def product(a, b):
+    return lax.dot_general(a, b, (((1,), (0,)), ((), ())), preferred_element_type=F32)
+
+
+def dot_left(m, v):
+    m = m.astype(jnp.bfloat16)
+    high, middle, low = (product(m, part) for part in parts(v))
+    return high + (middle + low)
+
+
+def dot_right(v, m):
+    m = m.astype(jnp.bfloat16)
+    high, middle, low = (product(part, m) for part in parts(v))
+    return high + (middle + low)
 
 
 def planes(lo, hi, step, carry=0, unroll=1):
@@ -192,31 +208,36 @@
     for i in range(lo, hi):
         at = 2 * i + offset
         plane = 0.125 * (r[at - 1] + r[at + 2]) + 0.375 * (r[at] + r[at + 1])
-        held[(i - lo) * size : (i - lo + 1) * size, :] = dot(ry, plane)
-    return dot(held[: (hi - lo) * size, :], rz)
+        held[(i - lo) * size : (i - lo + 1) * size, :] = dot_left(ry, plane)
+    return dot_right(held[: (hi - lo) * size, :], rz)
 
 
 def halve(k, offset, lo, hi, cy, cz, held):
     size = cy.shape[0]
     for i in range(lo, hi):
         plane = 0.5 * (k[2 * i + offset] + k[2 * i + 1 + offset])
-        held[(i - lo) * size : (i - lo + 1) * size, :] = dot(cy, plane)
-    return dot(held[: (hi - lo) * size, :], cz)
-
-
-def prolong(e, first, count, py, pz, finer, use):
+        held[(i - lo) * size : (i - lo + 1) * size, :] = dot_left(cy, plane)
+    return dot_right(held[: (hi - lo) * size, :], cz)
+
+
+def prolong(e, first, count, py, pz, finer, use, put):
     rows = e.shape[1]
-    spread = dot(e[pl.ds(first, count)].reshape(count * rows, e.shape[2]), pz)
+    spread = dot_right(e[pl.ds(first, count)].reshape(count * rows, e.shape[2]), pz)
     for i in range(count):
-        finer[i] = dot(py, spread[i * rows : (i + 1) * rows])
+        finer[i] = dot_left(py, spread[i * rows : (i + 1) * rows])
 
     def step(i, n, carry):
-        below, here, above = finer[i - 1], finer[i], finer[i + 1]
-        use(2 * (i - 1), 0.75 * here + 0.25 * below)
-        use(2 * (i - 1) + 1, 0.75 * here + 0.25 * above)
+        held = [finer[i - 1 + j] for j in range(n + 2)]
+        outs = []
+        for j in range(n):
+            here = 0.75 * held[j + 1]
+            outs.append(use(2 * (i + j - 1), here + 0.25 * held[j]))
+            outs.append(use(2 * (i + j - 1) + 1, here + 0.25 * held[j + 2]))
+        for j, value in enumerate(outs):
+            put(2 * (i - 1) + j, value)
         return carry
 
-    planes(1, count - 1, step)
+    planes(1, count - 1, step, unroll=max(1, 36 // (finer.shape[1] * finer.shape[2] // 1024)))
 
 
 def three(w):
@@ -292,15 +313,15 @@
     for i in range(2):
         at = 2 * i + 4
         plane = 0.125 * (r2[at - 1] + r2[at + 2]) + 0.375 * (r2[at] + r2[at + 1])
-        value = dot(restriction((8, 24), span(4, start=4 * i), Y2), plane)
+        value = dot_left(restriction((8, 24), span(4, start=4 * i), Y2), plane)
         total = value if total is None else total + value
-    tile = dot(total, restriction((128, 128), Z2, span(16), True))
+    tile = dot_right(total, restriction((128, 128), Z2, span(16), True))
     if first:
         part = [
-            dot(halving((8, 24), span(4, start=4 * i), Y2), 0.5 * (k2[2 * i + 4] + k2[2 * i + 5]))
+            dot_left(halving((8, 24), span(4, start=4 * i), Y2), 0.5 * (k2[2 * i + 4] + k2[2 * i + 5]))
             for i in range(2)
         ]
-        tile = tile + dot(part[0] + part[1], halving((128, 128), Z2, span(16, start=16), True))
+        tile = tile + dot_right(part[0] + part[1], halving((128, 128), Z2, span(16, start=16), True))
     for i in range(out.shape[0]):
         out[i] = tile
 
@@ -379,10 +400,10 @@
     lax.fori_loop(0, CSWEEPS - 1, turn, 0)
 
     def use(i, value):
-        v3[i + 3] = v3[i + 3] + value
+        return v3[i + 3] + value
 
     py3, pz3 = prolongation(tall[::-1], rows3, rows4), prolongation(wide, lanes4, lanes3, True)
-    prolong(v4, 0, n4 + 2, py3, pz3, fine4, use)
+    prolong(v4, 0, n4 + 2, py3, pz3, fine4, use, into(v3, 3))
     smooth(v3, g3, d3, w3, 3, n3 + 3, shifts3, b3, U3)
     return v3
 
@@ -410,18 +431,18 @@
         d2[i] = zero if ends is None else ends[n][1]
 
     def use2(i, value):
-        v2[i] = jnp.where(d2[i] > 0.0, v2[i] + value, 0.0)
+        return jnp.where(d2[i] > 0.0, v2[i] + value, 0.0)
 
     py2 = spread_matrix((g2.shape[1], e3.shape[1]), 0, index[1] * 4, 8)
     pz2 = spread_matrix((e3.shape[2], g2.shape[2]), 1, index[2] * 16, 32)
-    prolong(e3, index[0] * 2, 8, py2, pz2, fine2, use2)
+    prolong(e3, index[0] * 2, 8, py2, pz2, fine2, use2, into(v2))
     smooth(v2, g2, d2, w2, 1, 11, shifts, unroll=U2)
 
     def use1(i, value):
-        v1[i + 5] = jnp.where(d1[i + 5] > 0.0, v1[i + 5] + value, 0.0)
+        return jnp.where(d1[i + 5] > 0.0, v1[i + 5] + value, 0.0)
 
     py1, pz1 = prolongation((40, 24), Y1, Y2), prolongation((128, 128), Z2, Z1, True)
-    prolong(v2, 1, 10, py1, pz1, fine1, use1)
+    prolong(v2, 1, 10, py1, pz1, fine1, use1, into(v1, 5))
     smooth(v1, g1, d1, w1, 6, 20, shifts, unroll=U1)
     return v1
 
@@ -439,10 +460,10 @@
     w, shifts = (wx, wy, wz), Open()
 
     def use(i, value):
-        v[i + 1] = inside(k[i + 1], f[i + 1] * d[i + 1] + value)
+        return inside(k[i + 1], f[i + 1] * d[i + 1] + value)
 
     py0, pz0 = prolongation((48, 40), Y0, Y1), prolongation((128, 256), Z1, Z0, True)
-    prolong(e1, 6, 14, py0, pz0, fine0, use)
+    prolong(e1, 6, 14, py0, pz0, fine0, use, into(v, 1))
     smooth(v, f, d, w, 2, 24, shifts, unroll=U0)
     smooth(v, f, d, w, 3, 23, shifts, unroll=U0)
     residual_of(v, f, r, w, 4, 22, shifts, k, unroll=U0)
@@ -461,10 +482,10 @@
     w, shifts = (wx, wy, wz), Open()
 
     def use(i, value):
-        v[i + 3] = inside(k[i + 3], v0[i + 3] + value)
+        return inside(k[i + 3], v0[i + 3] + value)
 
     py0, pz0 = prolongation((48, 40), Y0, Y1), prolongation((128, 256), Z1, Z0, True)
-    prolong(e1, 7, 12, py0, pz0, fine0, use)
+    prolong(e1, 7, 12, py0, pz0, fine0, use, into(v, 3))
     smooth(v, f, d, w, 4, 22, shifts, unroll=U0)
 
     def last(i, here, im):

time: 211 us -> 205 us (0.972)
  Pallas kernels: 38.1 us -> 32.2 us
    pallas_call x7, Pallas kernels: 38.1 us -> 32.2 us  [call(): pl.pallas_call(kernel, out_shape=[jax.ShapeDtypeStruct(o, F32) for o in o...]
where the time goes in v7:
time: 205 us
  blocking collectives  62.1 us (30%)
  starting transfers between devices  54.2 us (26%)
  waiting for transfers between devices  48.9 us (24%)
  Pallas kernels  32.2 us (16%)
  local copies, waits for them, and re-layouts  4.86 us (2%)
    all_to_all x3, blocking collectives, everyone(): return lax.all_to_all(pieces, axes, 0, 0)  62.1 us
    pallas_call x7, Pallas kernels, call(): pl.pallas_call(kernel, out_shape=[jax.ShapeDtypeStruct(o, F32) for o in o...  32.2 us
    ppermute x9, waiting for transfers between devices, neighbours(): after = lax.ppermute(initial, axis, down)  28.4 us
    ppermute x9, starting transfers between devices, neighbours(): before = lax.ppermute(last, axis, up)  26.2 us
    ppermute x9, waiting for transfers between devices, neighbours(): before = lax.ppermute(last, axis, up)  16.3 us
    all_to_all x1, starting transfers between devices, everyone(): return lax.all_to_all(pieces, axes, 0, 0)  14.2 us
    ppermute x9, starting transfers between devices, neighbours(): after = lax.ppermute(initial, axis, down)  13.8 us
    all_to_all x1, waiting for transfers between devices, everyone(): return lax.all_to_all(pieces, axes, 0, 0)  4.15 us
  transfers between devices with their start and end apart: 19, of which 17 were waited for; matrix products, arithmetic and copies ran while one was open for 0% of the time, Pallas kernels for 0%

profile of v7, /device:TPU:1, one launch (start us, length us, event | category | flops | bytes accessed | tf_op | source)
XLA Modules:
  0.0 204.6 jit_solution(3670305860986517395)
XLA Ops:
  0.6 0.1 pad_add_fusion.index
  0.7 1.4 fusion.19
  2.1 0.1 pad_maximum_fusion.10
  2.3 2.7 %collective-permute-start.1 = (f32[16,32,50]{2,1,0:T(8,128)S(1)}, f32[16,32,50]{2,1,0:T(8,128)S(1)}, u32[]{:S(2)}, u32[]{:S(2)}) collective-permute-start(f32[16,32,50]{2,1,0:T(8,128)S(1)} %pad_maximum_fusion.10), channel_id=1, source_target_pairs={{0,1},{1,2},{2,3},{3,4},{4,5},{5,6},{6,7},{7,0},{8,9},{9,10},{10,1... | collective-permute-start | bytes 307208 | tf_op jit(solution)/shard_map/ppermute | solution.py:521
  5.0 0.1 pad_maximum_fusion.9
  5.1 4.2 %collective-permute-start = (f32[16,32,50]{2,1,0:T(8,128)S(1)}, f32[16,32,50]{2,1,0:T(8,128)S(1)}, u32[]{:S(2)}, u32[]{:S(2)}) collective-permute-start(f32[16,32,50]{2,1,0:T(8,128)S(1)} %pad_maximum_fusion.9), channel_id=1, source_target_pairs={{1,0},{2,1},{3,2},{4,3},{5,4},{6,5},{7,6},{0,7},{9,8},{10,9},{11,1... | collective-permute-start | bytes 307208 | tf_op jit(solution)/shard_map/ppermute | solution.py:522
  9.3 0.9 collective-permute-done.1
  10.2 0.1 fusion.18
  10.4 0.5 collective-permute-done
  10.9 0.1 fusion.17
  11.1 0.1 copy-done.3
  11.2 0.1 copy-done.4
  11.3 0.3 fusion.8
  11.6 3.0 %collective-permute-start.3 = (f32[32,5,256]{2,1,0:T(8,128)S(1)}, f32[32,5,256]{2,1,0:T(8,128)S(1)}, u32[]{:S(2)}, u32[]{:S(2)}) collective-permute-start(f32[32,5,256]{2,1,0:T(8,128)S(1)} %pad_maximum_fusion.12), channel_id=1, source_target_pairs={{0,8},{8,16},{16,24},{1,9},{9,17},{17,25},{2,10},{10,18},{18,26},{... | collective-permute-start | bytes 491528 | tf_op jit(solution)/shard_map/ppermute | solution.py:521
  14.7 0.1 pad.28.clone
  14.8 1.3 collective-permute-start.2
  16.1 1.9 collective-permute-done.3
  18.0 3.9 %collective-permute-done.2 = f32[32,5,256]{2,1,0:T(8,128)S(1)} collective-permute-done((f32[32,5,256]{2,1,0:T(8,128)S(1)}, f32[32,5,256]{2,1,0:T(8,128)S(1)}, u32[]{:S(2)}, u32[]{:S(2)}) %collective-permute-start.2) | collective-permute-done | bytes 163872 | tf_op jit(solution)/shard_map/ppermute | solution.py:522
  21.9 0.3 fusion.3
  22.4 5.2 %collective-permute-start.4 = (f32[10,48,256]{2,1,0:T(8,128)S(1)}, f32[10,48,256]{2,1,0:T(8,128)S(1)}, u32[]{:S(2)}, u32[]{:S(2)}) collective-permute-start(f32[10,48,256]{2,1,0:T(8,128)S(1)} %pad_maximum_fusion.4), channel_id=1, source_target_pairs={{0,32},{32,64},{64,96},{96,128},{128,160},{160,192},{192,224},{224... | collective-permute-start | bytes 1474568 | tf_op jit(solution)/shard_map/ppermute | solution.py:521
  27.6 1.3 collective-permute-start.5
  28.9 7.2 %collective-permute-done.4.before = f32[10,48,256]{2,1,0:T(8,128)S(1)} collective-permute-done((f32[10,48,256]{2,1,0:T(8,128)S(1)}, f32[10,48,256]{2,1,0:T(8,128)S(1)}, u32[]{:S(2)}, u32[]{:S(2)}) %collective-permute-start.4) | collective-permute-done | bytes 491552 | tf_op jit(solution)/shard_map/ppermute | solution.py:521
  36.1 4.2 %collective-permute-done.5.after = f32[10,48,256]{2,1,0:T(8,128)S(1)} collective-permute-done((f32[10,48,256]{2,1,0:T(8,128)S(1)}, f32[10,48,256]{2,1,0:T(8,128)S(1)}, u32[]{:S(2)}, u32[]{:S(2)}) %collective-permute-start.5) | collective-permute-done | bytes 491552 | tf_op jit(solution)/shard_map/ppermute | solution.py:522
  40.3 3.5 %down0.1 = (f32[26,48,256]{2,1,0:T(8,128)S(1)}, f32[26,48,256]{2,1,0:T(8,128)S(1)}, f32[20,16,128]{2,1,0:T(8,128)S(1)}) custom-call(f32[10,48,256]{2,1,0:T(8,128)S(1)} %collective-permute-done.4.before, f32[16,48,256]{2,1,0:T(8,128)S(1)} %get-tuple-element.54.fo, f32[16,48,256]{2,1,0:T(8,128)S(1)} %get-tuple-element.55.ko, ...), custom_call_target="tpu_custom_call" | custom-call | tf_op jit(solution)/shard_map/down0/pallas_call | solution.py:503
  43.9 3.1 %collective-permute-start.7 = (f32[20,16,128]{2,1,0:T(8,128)S(1)}, f32[20,16,128]{2,1,0:T(8,128)S(1)}, u32[]{:S(2)}, u32[]{:S(2)}) collective-permute-start(f32[20,16,128]{2,1,0:T(8,128)S(1)} %get-tuple-element.27), channel_id=1, source_target_pairs={{0,8},{8,16},{16,24},{1,9},{9,17},{17,25},{2,10},{10,18},{18,26},{... | collective-permute-start | bytes 491528 | tf_op jit(solution)/shard_map/ppermute | solution.py:521
  47.0 1.3 collective-permute-start.6
  48.3 0.1 pad.10.clone
  48.4 0.9 collective-permute-done.7
  49.2 3.8 %collective-permute-done.6 = f32[20,16,128]{2,1,0:T(8,128)S(1)} collective-permute-done((f32[20,16,128]{2,1,0:T(8,128)S(1)}, f32[20,16,128]{2,1,0:T(8,128)S(1)}, u32[]{:S(2)}, u32[]{:S(2)}) %collective-permute-start.6) | collective-permute-done | bytes 163872 | tf_op jit(solution)/shard_map/ppermute | solution.py:522
  53.0 0.1 pad_maximum_fusion.6.refs_1_
  53.1 0.1 fusion.14
  53.2 3.6 %collective-permute-start.8 = (f32[18,40,128]{2,1,0:T(8,128)S(1)}, f32[18,40,128]{2,1,0:T(8,128)S(1)}, u32[]{:S(2)}, u32[]{:S(2)}) collective-permute-start(f32[18,40,128]{2,1,0:T(8,128)S(1)} %pad_maximum_fusion.7), channel_id=1, source_target_pairs={{0,32},{32,64},{64,96},{96,128},{128,160},{160,192},{192,224},{224... | collective-permute-start | bytes 1105928 | tf_op jit(solution)/shard_map/ppermute | solution.py:521
  56.9 1.3 collective-permute-start.9
  58.2 3.1 %collective-permute-done.8.refs_0_ = f32[18,40,128]{2,1,0:T(8,128)S(1)} collective-permute-done((f32[18,40,128]{2,1,0:T(8,128)S(1)}, f32[18,40,128]{2,1,0:T(8,128)S(1)}, u32[]{:S(2)}, u32[]{:S(2)}) %collective-permute-start.8) | collective-permute-done | bytes 368672 | tf_op jit(solution)/shard_map/ppermute | solution.py:521
  61.2 5.3 %collective-permute-done.9.refs_2_ = f32[18,40,128]{2,1,0:T(8,128)S(1)} collective-permute-done((f32[18,40,128]{2,1,0:T(8,128)S(1)}, f32[18,40,128]{2,1,0:T(8,128)S(1)}, u32[]{:S(2)}, u32[]{:S(2)}) %collective-permute-start.9) | collective-permute-done | bytes 368672 | tf_op jit(solution)/shard_map/ppermute | solution.py:522
  66.6 2.5 %descend.1 = (f32[16,8,128]{2,1,0:T(8,128)S(1)}, f32[26,40,128]{2,1,0:T(8,128)S(1)}, f32[26,40,128]{2,1,0:T(8,128)S(1)}, f32[12,24,128]{2,1,0:T(8,128)S(1)}, f32...) custom-call(f32[18,40,128]{2,1,0:T(8,128)S(1)} %collective-permute-done.8.refs_0_, ...), custom_call_target="tpu_custom_call" | custom-call | tf_op jit(solution)/shard_map/descend/pallas_call | solution.py:503
  69.1 0.8 copy-done.1
  69.9 23.9 %all_to_all.20.s = f32[16,8,128]{2,1,0:T(8,128)S(1)} all-to-all(f32[16,8,128]{2,1,0:T(8,128)S(1)} %get-tuple-element.28), channel_id=1, replica_groups=mesh['gx'=16,'gy'=4,'gz'=8] {'gx'}, dimensions={0} | all-to-all | bytes 131072 | tf_op jit(solution)/shard_map/all_to_all | solution.py:565
  93.7 0.2 repack.1
  93.9 0.8 copy-done
  94.7 14.2 %all-to-all-start.1 = ((f32[32,4,8,128]{3,2,1,0:T(8,128)}), f32[32,4,8,128]{3,2,1,0:T(8,128)}, u32[]{:S(2)}, u32[]{:S(2)}) async-start(f32[32,4,8,128]{3,2,1,0:T(8,128)} %copy-done), calls=%async_computation.1 | async-start | bytes 1048576 | tf_op jit(solution)/shard_map/all_to_all | solution.py:565
  109.0 2.5 %collective-permute-start.10 = (f32[2,24,128]{2,1,0:T(8,128)S(1)}, f32[2,24,128]{2,1,0:T(8,128)S(1)}, u32[]{:S(2)}, u32[]{:S(2)}) collective-permute-start(f32[2,24,128]{2,1,0:T(8,128)S(1)} %get-tuple-element.33), channel_id=1, source_target_pairs={{0,32},{32,64},{64,96},{96,128},{128,160},{160,192},{192,224},{224... | collective-permute-start | bytes 73736 | tf_op jit(solution)/shard_map/ppermute | solution.py:521
  111.5 1.5 collective-permute-start.11
  113.0 3.5 %collective-permute-done.11.refs_1_ = f32[2,24,128]{2,1,0:T(8,128)S(1)} collective-permute-done((f32[2,24,128]{2,1,0:T(8,128)S(1)}, f32[2,24,128]{2,1,0:T(8,128)S(1)}, u32[]{:S(2)}, u32[]{:S(2)}) %collective-permute-start.11) | collective-permute-done | bytes 24608 | tf_op jit(solution)/shard_map/ppermute | solution.py:522
  116.5 4.1 %all-to-all-done.1.s = f32[32,4,8,128]{3,2,1,0:T(8,128)} async-done(((f32[32,4,8,128]{3,2,1,0:T(8,128)}), f32[32,4,8,128]{3,2,1,0:T(8,128)}, u32[]{:S(2)}, u32[]{:S(2)}) %all-to-all-start.1) | async-done | bytes 524320 | tf_op jit(solution)/shard_map/all_to_all | solution.py:565
  120.6 1.0 copy-done.2
  121.7 13.8 %middle.1 = (f32[26,48,256]{2,1,0:T(8,128)S(1)}, f32[8,16,128]{2,1,0:T(8,128)S(1)}, f32[8,16,128]{2,1,0:T(8,128)S(1)}, f32[38,16,128]{2,1,0:T(8,128)S(1)}) custom-call(s32[3]{0:T(128)S(1)} %pad_add_fusion.index, f32[26,48,256]{2,1,0:T(8,128)S(1)} %get-tuple-element.25.f, f32[26,48,256]{2,1,0:T(8,128)S(1)} %get-tuple-element.26.k, ...), custom_call_target="tpu_custom_call" | custom-call | tf_op jit(solution)/shard_map/middle/pallas_call | solution.py:503
  135.5 0.2 collective-permute-start.13
  135.7 0.3 collective-permute-start.12
  136.0 1.0 collective-permute-done.13
  137.0 2.7 %collective-permute-done.12 = f32[8,16,128]{2,1,0:T(8,128)S(1)} collective-permute-done((f32[8,16,128]{2,1,0:T(8,128)S(1)}, f32[8,16,128]{2,1,0:T(8,128)S(1)}, u32[]{:S(2)}, u32[]{:S(2)}) %collective-permute-start.12) | collective-permute-done | bytes 65568 | tf_op jit(solution)/shard_map/ppermute | solution.py:522
  139.7 1.9 collective-permute-start.15
  141.6 1.3 collective-permute-start.14
  142.9 3.7 %collective-permute-done.14 = f32[8,16,128]{2,1,0:T(8,128)S(1)} collective-permute-done((f32[8,16,128]{2,1,0:T(8,128)S(1)}, f32[8,16,128]{2,1,0:T(8,128)S(1)}, u32[]{:S(2)}, u32[]{:S(2)}) %collective-permute-start.14) | collective-permute-done | bytes 65568 | tf_op jit(solution)/shard_map/ppermute | solution.py:522
  146.6 0.1 pad_maximum_fusion.13.refs_1_
  146.7 1.3 collective-permute-start.17
  148.0 4.0 %collective-permute-start.16 = (f32[8,40,128]{2,1,0:T(8,128)S(1)}, f32[8,40,128]{2,1,0:T(8,128)S(1)}, u32[]{:S(2)}, u32[]{:S(2)}) collective-permute-start(f32[8,40,128]{2,1,0:T(8,128)S(1)} %pad_maximum_fusion.13.refs_1_), channel_id=1, source_target_pairs={{0,32},{32,64},{64,96},{96,128},{128,160},{160,192},{192,224},{224... | collective-permute-start | bytes 491528 | tf_op jit(solution)/shard_map/ppermute | solution.py:521
  152.0 0.8 collective-permute-done.17.refs_2_
  152.7 1.5 collective-permute-done.16.refs_0_
  154.2 1.8 again.1
  156.1 18.2 %all_to_all.21.s = f32[16,8,128]{2,1,0:T(8,128)S(1)} all-to-all(f32[16,8,128]{2,1,0:T(8,128)S(1)} %get-tuple-element.38), channel_id=1, replica_groups=mesh['gx'=16,'gy'=4,'gz'=8] {'gx'}, dimensions={0} | all-to-all | bytes 131072 | tf_op jit(solution)/shard_map/all_to_all | solution.py:565
  174.3 0.1 repack2.1
  174.4 20.0 %all_to_all.22.s = f32[32,2,8,128]{3,2,1,0:T(8,128)S(1)} all-to-all(f32[32,2,8,128]{3,2,1,0:T(8,128)S(1)} %repack2.1), channel_id=1, replica_groups=mesh['gx'=16,'gy'=4,'gz'=8] {'gy','gz'}, dimensions={0} | all-to-all | bytes 524288 | tf_op jit(solution)/shard_map/all_to_all | solution.py:565
  194.4 10.2 %final.1 = (f32[16,32,128]{2,1,0:T(8,128)}, f32[16,32,128]{2,1,0:T(8,128)}) custom-call(s32[3]{0:T(128)S(1)} %pad_add_fusion.index, f32[26,48,256]{2,1,0:T(8,128)S(1)} %get-tuple-element.25.f, f32[26,48,256]{2,1,0:T(8,128)S(1)} %get-tuple-element.26.k, f32[26,48,256]{2,1,0:T(8,128)S(1)} %get-tuple-element.35.v0, f32[32,2,8,128]{3,2,1,0:T(8,128)S(1)} %all_to_all.22.s, ...), custom_call_target="tpu_custom_call" | custom-call | tf_op jit(solution)/shard_map/final/pallas_call | solution.py:503
  (29 shorter events, 0.5 us)
Async XLA Ops:
  2.3 7.9 %collective-permute-start.1 = (f32[16,32,50]{2,1,0:T(8,128)S(1)}, f32[16,32,50]{2,1,0:T(8,128)S(1)}, u32[]{:S(2)}, u32[]{:S(2)}) collective-permute-start(f32[16,32,50]{2,1,0:T(8,128)S(1)} %pad_maximum_fusion.10), channel_id=1, source_target_pairs={{0,1},{1,2},{2,3},{3,4},{4,5},{5,6},{6,7},{7,0},{8,9},{9,10},{10,1... | collective-permute-start | bytes 307208 | tf_op jit(solution)/shard_map/ppermute | solution.py:521
  5.1 5.8 %collective-permute-start = (f32[16,32,50]{2,1,0:T(8,128)S(1)}, f32[16,32,50]{2,1,0:T(8,128)S(1)}, u32[]{:S(2)}, u32[]{:S(2)}) collective-permute-start(f32[16,32,50]{2,1,0:T(8,128)S(1)} %pad_maximum_fusion.9), channel_id=1, source_target_pairs={{1,0},{2,1},{3,2},{4,3},{5,4},{6,5},{7,6},{0,7},{9,8},{10,9},{11,1... | collective-permute-start | bytes 307208 | tf_op jit(solution)/shard_map/ppermute | solution.py:522
  10.2 1.0 copy-start.3
  10.2 1.0 copy-start.4
  11.6 6.3 %collective-permute-start.3 = (f32[32,5,256]{2,1,0:T(8,128)S(1)}, f32[32,5,256]{2,1,0:T(8,128)S(1)}, u32[]{:S(2)}, u32[]{:S(2)}) collective-permute-start(f32[32,5,256]{2,1,0:T(8,128)S(1)} %pad_maximum_fusion.12), channel_id=1, source_target_pairs={{0,8},{8,16},{16,24},{1,9},{9,17},{17,25},{2,10},{10,18},{18,26},{... | collective-permute-start | bytes 491528 | tf_op jit(solution)/shard_map/ppermute | solution.py:521
  14.8 7.1 %collective-permute-start.2 = (f32[32,5,256]{2,1,0:T(8,128)S(1)}, f32[32,5,256]{2,1,0:T(8,128)S(1)}, u32[]{:S(2)}, u32[]{:S(2)}) collective-permute-start(f32[32,5,256]{2,1,0:T(8,128)S(1)} %pad_maximum_fusion.11), channel_id=1, source_target_pairs={{8,0},{16,8},{24,16},{9,1},{17,9},{25,17},{10,2},{18,10},{26,18},{... | collective-permute-start | bytes 491528 | tf_op jit(solution)/shard_map/ppermute | solution.py:522
  22.4 13.7 %collective-permute-start.4 = (f32[10,48,256]{2,1,0:T(8,128)S(1)}, f32[10,48,256]{2,1,0:T(8,128)S(1)}, u32[]{:S(2)}, u32[]{:S(2)}) collective-permute-start(f32[10,48,256]{2,1,0:T(8,128)S(1)} %pad_maximum_fusion.4), channel_id=1, source_target_pairs={{0,32},{32,64},{64,96},{96,128},{128,160},{160,192},{192,224},{224... | collective-permute-start | bytes 1474568 | tf_op jit(solution)/shard_map/ppermute | solution.py:521
  27.6 12.7 %collective-permute-start.5 = (f32[10,48,256]{2,1,0:T(8,128)S(1)}, f32[10,48,256]{2,1,0:T(8,128)S(1)}, u32[]{:S(2)}, u32[]{:S(2)}) collective-permute-start(f32[10,48,256]{2,1,0:T(8,128)S(1)} %pad_maximum_fusion.5), channel_id=1, source_target_pairs={{32,0},{64,32},{96,64},{128,96},{160,128},{192,160},{224,192},{256... | collective-permute-start | bytes 1474568 | tf_op jit(solution)/shard_map/ppermute | solution.py:522
  43.9 5.4 %collective-permute-start.7 = (f32[20,16,128]{2,1,0:T(8,128)S(1)}, f32[20,16,128]{2,1,0:T(8,128)S(1)}, u32[]{:S(2)}, u32[]{:S(2)}) collective-permute-start(f32[20,16,128]{2,1,0:T(8,128)S(1)} %get-tuple-element.27), channel_id=1, source_target_pairs={{0,8},{8,16},{16,24},{1,9},{9,17},{17,25},{2,10},{10,18},{18,26},{... | collective-permute-start | bytes 491528 | tf_op jit(solution)/shard_map/ppermute | solution.py:521
  47.0 6.1 %collective-permute-start.6 = (f32[20,16,128]{2,1,0:T(8,128)S(1)}, f32[20,16,128]{2,1,0:T(8,128)S(1)}, u32[]{:S(2)}, u32[]{:S(2)}) collective-permute-start(f32[20,16,128]{2,1,0:T(8,128)S(1)} %get-tuple-element.27), channel_id=1, source_target_pairs={{8,0},{16,8},{24,16},{9,1},{17,9},{25,17},{10,2},{18,10},{26,18},{... | collective-permute-start | bytes 491528 | tf_op jit(solution)/shard_map/ppermute | solution.py:522
  53.2 8.0 %collective-permute-start.8 = (f32[18,40,128]{2,1,0:T(8,128)S(1)}, f32[18,40,128]{2,1,0:T(8,128)S(1)}, u32[]{:S(2)}, u32[]{:S(2)}) collective-permute-start(f32[18,40,128]{2,1,0:T(8,128)S(1)} %pad_maximum_fusion.7), channel_id=1, source_target_pairs={{0,32},{32,64},{64,96},{96,128},{128,160},{160,192},{192,224},{224... | collective-permute-start | bytes 1105928 | tf_op jit(solution)/shard_map/ppermute | solution.py:521
  56.9 9.7 %collective-permute-start.9 = (f32[18,40,128]{2,1,0:T(8,128)S(1)}, f32[18,40,128]{2,1,0:T(8,128)S(1)}, u32[]{:S(2)}, u32[]{:S(2)}) collective-permute-start(f32[18,40,128]{2,1,0:T(8,128)S(1)} %pad_maximum_fusion.8), channel_id=1, source_target_pairs={{32,0},{64,32},{96,64},{128,96},{160,128},{192,160},{224,192},{256... | collective-permute-start | bytes 1105928 | tf_op jit(solution)/shard_map/ppermute | solution.py:522
  69.1 0.8 copy-start.1
  93.9 0.8 copy-start
  94.7 25.9 %all-to-all-start.1 = ((f32[32,4,8,128]{3,2,1,0:T(8,128)}), f32[32,4,8,128]{3,2,1,0:T(8,128)}, u32[]{:S(2)}, u32[]{:S(2)}) async-start(f32[32,4,8,128]{3,2,1,0:T(8,128)} %copy-done), calls=%async_computation.1 | async-start | bytes 1048576 | tf_op jit(solution)/shard_map/all_to_all | solution.py:565
  109.0 4.0 %collective-permute-start.10 = (f32[2,24,128]{2,1,0:T(8,128)S(1)}, f32[2,24,128]{2,1,0:T(8,128)S(1)}, u32[]{:S(2)}, u32[]{:S(2)}) collective-permute-start(f32[2,24,128]{2,1,0:T(8,128)S(1)} %get-tuple-element.33), channel_id=1, source_target_pairs={{0,32},{32,64},{64,96},{96,128},{128,160},{160,192},{192,224},{224... | collective-permute-start | bytes 73736 | tf_op jit(solution)/shard_map/ppermute | solution.py:521
  111.5 5.0 %collective-permute-start.11 = (f32[2,24,128]{2,1,0:T(8,128)S(1)}, f32[2,24,128]{2,1,0:T(8,128)S(1)}, u32[]{:S(2)}, u32[]{:S(2)}) collective-permute-start(f32[2,24,128]{2,1,0:T(8,128)S(1)} %get-tuple-element.34), channel_id=1, source_target_pairs={{32,0},{64,32},{96,64},{128,96},{160,128},{192,160},{224,192},{256... | collective-permute-start | bytes 73736 | tf_op jit(solution)/shard_map/ppermute | solution.py:522
  120.6 1.0 copy-start.2
  135.5 1.5 collective-permute-start.13
  135.7 4.0 %collective-permute-start.12 = (f32[8,16,128]{2,1,0:T(8,128)S(1)}, f32[8,16,128]{2,1,0:T(8,128)S(1)}, u32[]{:S(2)}, u32[]{:S(2)}) collective-permute-start(f32[8,16,128]{2,1,0:T(8,128)S(1)} %get-tuple-element.37), channel_id=1, source_target_pairs={{1,0},{2,1},{3,2},{4,3},{5,4},{6,5},{7,6},{0,7},{9,8},{10,9},{11,1... | collective-permute-start | bytes 196616 | tf_op jit(solution)/shard_map/ppermute | solution.py:522
  139.7 3.2 %collective-permute-start.15 = (f32[8,16,128]{2,1,0:T(8,128)S(1)}, f32[8,16,128]{2,1,0:T(8,128)S(1)}, u32[]{:S(2)}, u32[]{:S(2)}) collective-permute-start(f32[8,16,128]{2,1,0:T(8,128)S(1)} %select_select_fusion), channel_id=1, source_target_pairs={{0,8},{8,16},{16,24},{1,9},{9,17},{17,25},{2,10},{10,18},{18,26},{... | collective-permute-start | bytes 196616 | tf_op jit(solution)/shard_map/ppermute | solution.py:521
  141.6 5.0 %collective-permute-start.14 = (f32[8,16,128]{2,1,0:T(8,128)S(1)}, f32[8,16,128]{2,1,0:T(8,128)S(1)}, u32[]{:S(2)}, u32[]{:S(2)}) collective-permute-start(f32[8,16,128]{2,1,0:T(8,128)S(1)} %select_select_fusion), channel_id=1, source_target_pairs={{8,0},{16,8},{24,16},{9,1},{17,9},{25,17},{10,2},{18,10},{26,18},{... | collective-permute-start | bytes 196616 | tf_op jit(solution)/shard_map/ppermute | solution.py:522
  146.7 6.1 %collective-permute-start.17 = (f32[8,40,128]{2,1,0:T(8,128)S(1)}, f32[8,40,128]{2,1,0:T(8,128)S(1)}, u32[]{:S(2)}, u32[]{:S(2)}) collective-permute-start(f32[8,40,128]{2,1,0:T(8,128)S(1)} %pad_maximum_fusion.13.refs_1_), channel_id=1, source_target_pairs={{32,0},{64,32},{96,64},{128,96},{160,128},{192,160},{224,192},{256... | collective-permute-start | bytes 491528 | tf_op jit(solution)/shard_map/ppermute | solution.py:522
  148.0 6.2 %collective-permute-start.16 = (f32[8,40,128]{2,1,0:T(8,128)S(1)}, f32[8,40,128]{2,1,0:T(8,128)S(1)}, u32[]{:S(2)}, u32[]{:S(2)}) collective-permute-start(f32[8,40,128]{2,1,0:T(8,128)S(1)} %pad_maximum_fusion.13.refs_1_), channel_id=1, source_target_pairs={{0,32},{32,64},{64,96},{96,128},{128,160},{160,192},{192,224},{224... | collective-permute-start | bytes 491528 | tf_op jit(solution)/shard_map/ppermute | solution.py:521

commit v8 on v7

--- a/solution.py
+++ b/solution.py
@@ -263,10 +263,19 @@
 
 def down0(before, fo, ko, after, f, k, out, wx, wy, wz, d, v, r, held):
     shifts = Open()
-    for ref, own, at in ((f, fo, 0), (k, ko, 5)):
-        place(ref, 0, before, at, 5, 5)
-        place(ref, 5, own, 0, 16)
-        place(ref, 21, after, at, 5, 5)
+    place(f, 5, fo, 0, 16)
+    place(k, 5, ko, 0, 16)
+    lane = lax.broadcasted_iota(jnp.int32, (48, 128), 1)
+    ours = (lane < 25) | (lane >= 103)
+    f[0] = f[25] = jnp.zeros((48, 256), F32)
+    for ref, at, shift in ((before, 0, 1), (after, 21, 0)):
+        for j in range(5):
+            tail = ref[9 + j]
+            k[at + j, :, :128] = ref[4 + j]
+            k[at + j, :, 128:] = jnp.where(ours, pltpu.roll(tail, 78, 1), 0.0)
+            if 0 <= j - shift < 4:
+                f[at + j, :, :128] = ref[j - shift]
+                f[at + j, :, 128:] = jnp.where(ours, tail, 0.0)
     weigh(k, wx, wy, wz, 1, 25, 1.0, shifts, d, inside, unroll=U0)
     first_sweep(f, d, v, 1, 25, U0)
     residual_of(v, f, r, (wx, wy, wz), 2, 24, shifts, k, unroll=U0)
@@ -542,10 +551,18 @@
         fields = [
             jnp.concatenate([v, a, gap, b], dim) for b, v, a in zip(before, fields, after)
         ]
-    last = jnp.concatenate([v[11:] for v in fields])
-    initial = jnp.concatenate([v[:5] for v in fields])
-    before, after = neighbours(last, initial, "gx")
-    return before, *fields, after
+    f, k = fields
+    lane = jnp.arange(128)
+    ours = (lane < 25) | (lane >= 103)
+
+    def packed(at, shift):
+        start = at + shift
+        tail = jnp.pad(f[start : start + 4, :, 128:], ((shift, 1 - shift), (0, 0), (0, 0)))
+        tail = jnp.where(ours, tail, jnp.roll(k[at : at + 5, :, 128:], 50, 2))
+        return jnp.concatenate([f[start : start + 4, :, :128], k[at : at + 5, :, :128], tail])
+
+    before, after = neighbours(packed(11, 1), packed(0, 0), "gx")
+    return before, f, k, after
 
 
 def rows1(values):

time: 205 us -> 203 us (level)
  waiting for transfers between devices: 48.9 us -> 45.7 us
    ppermute x9, waiting for transfers between devices: 16.3 us -> 13.2 us  [neighbours(): before = lax.ppermute(last, axis, up)]
where the time goes in v8:
time: 203 us; the launch traced here: 202 us
  blocking collectives  62.1 us (31%)
  starting transfers between devices  54.2 us (27%)
  waiting for transfers between devices  45.7 us (23%)
  Pallas kernels  32.3 us (16%)
  local copies, waits for them, and re-layouts  4.99 us (2%)
    all_to_all x3, blocking collectives, everyone(): return lax.all_to_all(pieces, axes, 0, 0)  62.1 us
    pallas_call x7, Pallas kernels, call(): pl.pallas_call(kernel, out_shape=[jax.ShapeDtypeStruct(o, F32) for o in o...  32.3 us
    ppermute x9, waiting for transfers between devices, neighbours(): after = lax.ppermute(initial, axis, down)  28.4 us
    ppermute x9, starting transfers between devices, neighbours(): before = lax.ppermute(last, axis, up)  26.1 us
    all_to_all x1, starting transfers between devices, everyone(): return lax.all_to_all(pieces, axes, 0, 0)  14.2 us
    ppermute x9, starting transfers between devices, neighbours(): after = lax.ppermute(initial, axis, down)  13.8 us
    ppermute x9, waiting for transfers between devices, neighbours(): before = lax.ppermute(last, axis, up)  13.2 us
    all_to_all x1, waiting for transfers between devices, everyone(): return lax.all_to_all(pieces, axes, 0, 0)  4.15 us
  transfers between devices with their start and end apart: 19, of which 17 were waited for; matrix products, arithmetic and copies ran while one was open for 0% of the time, Pallas kernels for 0%

profile of v8, /device:TPU:1, one launch (start us, length us, event | category | flops | bytes accessed | tf_op | source)
XLA Modules:
  0.0 201.8 jit_solution(4963209220633052817)
XLA Ops:
  0.6 0.1 pad_add_fusion.index
  0.7 1.4 fusion.21
  2.1 0.1 pad_maximum_fusion.10
  2.3 2.7 %collective-permute-start.1 = (f32[16,32,50]{2,1,0:T(8,128)S(1)}, f32[16,32,50]{2,1,0:T(8,128)S(1)}, u32[]{:S(2)}, u32[]{:S(2)}) collective-permute-start(f32[16,32,50]{2,1,0:T(8,128)S(1)} %pad_maximum_fusion.10), channel_id=1, source_target_pairs={{0,1},{1,2},{2,3},{3,4},{4,5},{5,6},{6,7},{7,0},{8,9},{9,10},{10,1... | collective-permute-start | bytes 307208 | tf_op jit(solution)/shard_map/ppermute | solution.py:530
  5.0 0.1 pad_maximum_fusion.9
  5.1 4.2 %collective-permute-start = (f32[16,32,50]{2,1,0:T(8,128)S(1)}, f32[16,32,50]{2,1,0:T(8,128)S(1)}, u32[]{:S(2)}, u32[]{:S(2)}) collective-permute-start(f32[16,32,50]{2,1,0:T(8,128)S(1)} %pad_maximum_fusion.9), channel_id=1, source_target_pairs={{1,0},{2,1},{3,2},{4,3},{5,4},{6,5},{7,6},{0,7},{9,8},{10,9},{11,1... | collective-permute-start | bytes 307208 | tf_op jit(solution)/shard_map/ppermute | solution.py:531
  9.3 0.9 collective-permute-done.1
  10.2 0.1 fusion.20
  10.4 0.5 collective-permute-done
  10.9 0.1 fusion.19
  11.2 0.1 copy-done.4
  11.3 0.3 fusion.8
  11.6 3.0 %collective-permute-start.3 = (f32[32,5,256]{2,1,0:T(8,128)S(1)}, f32[32,5,256]{2,1,0:T(8,128)S(1)}, u32[]{:S(2)}, u32[]{:S(2)}) collective-permute-start(f32[32,5,256]{2,1,0:T(8,128)S(1)} %pad_maximum_fusion.12), channel_id=1, source_target_pairs={{0,8},{8,16},{16,24},{1,9},{9,17},{17,25},{2,10},{10,18},{18,26},{... | collective-permute-start | bytes 491528 | tf_op jit(solution)/shard_map/ppermute | solution.py:530
  14.7 0.1 pad.44.clone
  14.8 1.3 collective-permute-start.2
  16.1 1.9 collective-permute-done.3
  18.0 3.9 %collective-permute-done.2 = f32[32,5,256]{2,1,0:T(8,128)S(1)} collective-permute-done((f32[32,5,256]{2,1,0:T(8,128)S(1)}, f32[32,5,256]{2,1,0:T(8,128)S(1)}, u32[]{:S(2)}, u32[]{:S(2)}) %collective-permute-start.2) | collective-permute-done | bytes 163872 | tf_op jit(solution)/shard_map/ppermute | solution.py:531
  21.9 0.3 fusion.3
  22.3 0.1 fusion.12
  22.5 0.1 maximum_select_fusion.1
  22.7 5.1 %collective-permute-start.4 = (f32[14,48,128]{2,1,0:T(8,128)S(1)}, f32[14,48,128]{2,1,0:T(8,128)S(1)}, u32[]{:S(2)}, u32[]{:S(2)}) collective-permute-start(f32[14,48,128]{2,1,0:T(8,128)S(1)} %pad_maximum_fusion.7), channel_id=1, source_target_pairs={{0,32},{32,64},{64,96},{96,128},{128,160},{160,192},{192,224},{224... | collective-permute-start | bytes 1032200 | tf_op jit(solution)/shard_map/ppermute | solution.py:530
  27.8 1.3 collective-permute-start.5
  29.1 4.1 %collective-permute-done.4.before = f32[14,48,128]{2,1,0:T(8,128)S(1)} collective-permute-done((f32[14,48,128]{2,1,0:T(8,128)S(1)}, f32[14,48,128]{2,1,0:T(8,128)S(1)}, u32[]{:S(2)}, u32[]{:S(2)}) %collective-permute-start.4) | collective-permute-done | bytes 344096 | tf_op jit(solution)/shard_map/ppermute | solution.py:530
  33.2 4.2 %collective-permute-done.5.after = f32[14,48,128]{2,1,0:T(8,128)S(1)} collective-permute-done((f32[14,48,128]{2,1,0:T(8,128)S(1)}, f32[14,48,128]{2,1,0:T(8,128)S(1)}, u32[]{:S(2)}, u32[]{:S(2)}) %collective-permute-start.5) | collective-permute-done | bytes 344096 | tf_op jit(solution)/shard_map/ppermute | solution.py:531
  37.4 3.7 %down0.1 = (f32[26,48,256]{2,1,0:T(8,128)S(1)}, f32[26,48,256]{2,1,0:T(8,128)S(1)}, f32[20,16,128]{2,1,0:T(8,128)S(1)}) custom-call(f32[14,48,128]{2,1,0:T(8,128)S(1)} %collective-permute-done.4.before, f32[16,48,256]{2,1,0:T(8,128)S(1)} %get-tuple-element.60.fo, f32[16,48,256]{2,1,0:T(8,128)S(1)} %get-tuple-element.61.ko, ...), custom_call_target="tpu_custom_call" | custom-call | tf_op jit(solution)/shard_map/down0/pallas_call | solution.py:512
  41.1 3.1 %collective-permute-start.7 = (f32[20,16,128]{2,1,0:T(8,128)S(1)}, f32[20,16,128]{2,1,0:T(8,128)S(1)}, u32[]{:S(2)}, u32[]{:S(2)}) collective-permute-start(f32[20,16,128]{2,1,0:T(8,128)S(1)} %get-tuple-element.27), channel_id=1, source_target_pairs={{0,8},{8,16},{16,24},{1,9},{9,17},{17,25},{2,10},{10,18},{18,26},{... | collective-permute-start | bytes 491528 | tf_op jit(solution)/shard_map/ppermute | solution.py:530
  44.2 1.3 collective-permute-start.6
  45.5 0.1 pad.20.clone
  45.6 0.9 collective-permute-done.7
  46.5 3.8 %collective-permute-done.6 = f32[20,16,128]{2,1,0:T(8,128)S(1)} collective-permute-done((f32[20,16,128]{2,1,0:T(8,128)S(1)}, f32[20,16,128]{2,1,0:T(8,128)S(1)}, u32[]{:S(2)}, u32[]{:S(2)}) %collective-permute-start.6) | collective-permute-done | bytes 163872 | tf_op jit(solution)/shard_map/ppermute | solution.py:531
  50.3 0.1 pad_maximum_fusion.4.refs_1_
  50.5 3.6 %collective-permute-start.8 = (f32[18,40,128]{2,1,0:T(8,128)S(1)}, f32[18,40,128]{2,1,0:T(8,128)S(1)}, u32[]{:S(2)}, u32[]{:S(2)}) collective-permute-start(f32[18,40,128]{2,1,0:T(8,128)S(1)} %pad_maximum_fusion.5), channel_id=1, source_target_pairs={{0,32},{32,64},{64,96},{96,128},{128,160},{160,192},{192,224},{224... | collective-permute-start | bytes 1105928 | tf_op jit(solution)/shard_map/ppermute | solution.py:530
  54.1 1.3 collective-permute-start.9
  55.4 3.1 %collective-permute-done.8.refs_0_ = f32[18,40,128]{2,1,0:T(8,128)S(1)} collective-permute-done((f32[18,40,128]{2,1,0:T(8,128)S(1)}, f32[18,40,128]{2,1,0:T(8,128)S(1)}, u32[]{:S(2)}, u32[]{:S(2)}) %collective-permute-start.8) | collective-permute-done | bytes 368672 | tf_op jit(solution)/shard_map/ppermute | solution.py:530
  58.5 5.3 %collective-permute-done.9.refs_2_ = f32[18,40,128]{2,1,0:T(8,128)S(1)} collective-permute-done((f32[18,40,128]{2,1,0:T(8,128)S(1)}, f32[18,40,128]{2,1,0:T(8,128)S(1)}, u32[]{:S(2)}, u32[]{:S(2)}) %collective-permute-start.9) | collective-permute-done | bytes 368672 | tf_op jit(solution)/shard_map/ppermute | solution.py:531
  63.8 2.5 %descend.1 = (f32[16,8,128]{2,1,0:T(8,128)S(1)}, f32[26,40,128]{2,1,0:T(8,128)S(1)}, f32[26,40,128]{2,1,0:T(8,128)S(1)}, f32[12,24,128]{2,1,0:T(8,128)S(1)}, f32...) custom-call(f32[18,40,128]{2,1,0:T(8,128)S(1)} %collective-permute-done.8.refs_0_, ...), custom_call_target="tpu_custom_call" | custom-call | tf_op jit(solution)/shard_map/descend/pallas_call | solution.py:512
  66.4 0.8 copy-done.1
  67.2 23.9 %all_to_all.20.s = f32[16,8,128]{2,1,0:T(8,128)S(1)} all-to-all(f32[16,8,128]{2,1,0:T(8,128)S(1)} %get-tuple-element.28), channel_id=1, replica_groups=mesh['gx'=16,'gy'=4,'gz'=8] {'gx'}, dimensions={0} | all-to-all | bytes 131072 | tf_op jit(solution)/shard_map/all_to_all | solution.py:582
  91.0 0.2 repack.1
  91.2 0.8 copy-done
  92.0 14.2 %all-to-all-start.1 = ((f32[32,4,8,128]{3,2,1,0:T(8,128)}), f32[32,4,8,128]{3,2,1,0:T(8,128)}, u32[]{:S(2)}, u32[]{:S(2)}) async-start(f32[32,4,8,128]{3,2,1,0:T(8,128)} %copy-done), calls=%async_computation.1 | async-start | bytes 1048576 | tf_op jit(solution)/shard_map/all_to_all | solution.py:582
  106.2 2.5 %collective-permute-start.10 = (f32[2,24,128]{2,1,0:T(8,128)S(1)}, f32[2,24,128]{2,1,0:T(8,128)S(1)}, u32[]{:S(2)}, u32[]{:S(2)}) collective-permute-start(f32[2,24,128]{2,1,0:T(8,128)S(1)} %get-tuple-element.33), channel_id=1, source_target_pairs={{0,32},{32,64},{64,96},{96,128},{128,160},{160,192},{192,224},{224... | collective-permute-start | bytes 73736 | tf_op jit(solution)/shard_map/ppermute | solution.py:530
  108.8 1.5 collective-permute-start.11
  110.3 3.5 %collective-permute-done.11.refs_1_ = f32[2,24,128]{2,1,0:T(8,128)S(1)} collective-permute-done((f32[2,24,128]{2,1,0:T(8,128)S(1)}, f32[2,24,128]{2,1,0:T(8,128)S(1)}, u32[]{:S(2)}, u32[]{:S(2)}) %collective-permute-start.11) | collective-permute-done | bytes 24608 | tf_op jit(solution)/shard_map/ppermute | solution.py:531
  113.8 4.1 %all-to-all-done.1.s = f32[32,4,8,128]{3,2,1,0:T(8,128)} async-done(((f32[32,4,8,128]{3,2,1,0:T(8,128)}), f32[32,4,8,128]{3,2,1,0:T(8,128)}, u32[]{:S(2)}, u32[]{:S(2)}) %all-to-all-start.1) | async-done | bytes 524320 | tf_op jit(solution)/shard_map/all_to_all | solution.py:582
  117.9 1.0 copy-done.2
  119.0 13.8 %middle.1 = (f32[26,48,256]{2,1,0:T(8,128)S(1)}, f32[8,16,128]{2,1,0:T(8,128)S(1)}, f32[8,16,128]{2,1,0:T(8,128)S(1)}, f32[38,16,128]{2,1,0:T(8,128)S(1)}) custom-call(s32[3]{0:T(128)S(1)} %pad_add_fusion.index, f32[26,48,256]{2,1,0:T(8,128)S(1)} %get-tuple-element.25.f, f32[26,48,256]{2,1,0:T(8,128)S(1)} %get-tuple-element.26.k, ...), custom_call_target="tpu_custom_call" | custom-call | tf_op jit(solution)/shard_map/middle/pallas_call | solution.py:512
  132.7 0.2 collective-permute-start.13
  132.9 0.4 collective-permute-start.12
  133.3 1.0 collective-permute-done.13
  134.2 2.7 %collective-permute-done.12 = f32[8,16,128]{2,1,0:T(8,128)S(1)} collective-permute-done((f32[8,16,128]{2,1,0:T(8,128)S(1)}, f32[8,16,128]{2,1,0:T(8,128)S(1)}, u32[]{:S(2)}, u32[]{:S(2)}) %collective-permute-start.12) | collective-permute-done | bytes 65568 | tf_op jit(solution)/shard_map/ppermute | solution.py:531
  136.9 1.9 collective-permute-start.15
  138.8 1.3 collective-permute-start.14
  140.1 3.7 %collective-permute-done.14 = f32[8,16,128]{2,1,0:T(8,128)S(1)} collective-permute-done((f32[8,16,128]{2,1,0:T(8,128)S(1)}, f32[8,16,128]{2,1,0:T(8,128)S(1)}, u32[]{:S(2)}, u32[]{:S(2)}) %collective-permute-start.14) | collective-permute-done | bytes 65568 | tf_op jit(solution)/shard_map/ppermute | solution.py:531
  143.8 0.1 pad_maximum_fusion.13.refs_1_
  143.9 1.3 collective-permute-start.17
  145.2 4.0 %collective-permute-start.16 = (f32[8,40,128]{2,1,0:T(8,128)S(1)}, f32[8,40,128]{2,1,0:T(8,128)S(1)}, u32[]{:S(2)}, u32[]{:S(2)}) collective-permute-start(f32[8,40,128]{2,1,0:T(8,128)S(1)} %pad_maximum_fusion.13.refs_1_), channel_id=1, source_target_pairs={{0,32},{32,64},{64,96},{96,128},{128,160},{160,192},{192,224},{224... | collective-permute-start | bytes 491528 | tf_op jit(solution)/shard_map/ppermute | solution.py:530
  149.2 0.8 collective-permute-done.17.refs_2_
  150.0 1.5 collective-permute-done.16.refs_0_
  151.4 1.9 again.1
  153.3 18.2 %all_to_all.21.s = f32[16,8,128]{2,1,0:T(8,128)S(1)} all-to-all(f32[16,8,128]{2,1,0:T(8,128)S(1)} %get-tuple-element.38), channel_id=1, replica_groups=mesh['gx'=16,'gy'=4,'gz'=8] {'gx'}, dimensions={0} | all-to-all | bytes 131072 | tf_op jit(solution)/shard_map/all_to_all | solution.py:582
  171.5 0.1 repack2.1
  171.7 20.0 %all_to_all.22.s = f32[32,2,8,128]{3,2,1,0:T(8,128)S(1)} all-to-all(f32[32,2,8,128]{3,2,1,0:T(8,128)S(1)} %repack2.1), channel_id=1, replica_groups=mesh['gx'=16,'gy'=4,'gz'=8] {'gy','gz'}, dimensions={0} | all-to-all | bytes 524288 | tf_op jit(solution)/shard_map/all_to_all | solution.py:582
  191.6 10.2 %final.1 = (f32[16,32,128]{2,1,0:T(8,128)}, f32[16,32,128]{2,1,0:T(8,128)}) custom-call(s32[3]{0:T(128)S(1)} %pad_add_fusion.index, f32[26,48,256]{2,1,0:T(8,128)S(1)} %get-tuple-element.25.f, f32[26,48,256]{2,1,0:T(8,128)S(1)} %get-tuple-element.26.k, f32[26,48,256]{2,1,0:T(8,128)S(1)} %get-tuple-element.35.v0, f32[32,2,8,128]{3,2,1,0:T(8,128)S(1)} %all_to_all.22.s, ...), custom_call_target="tpu_custom_call" | custom-call | tf_op jit(solution)/shard_map/final/pallas_call | solution.py:512
  (33 shorter events, 0.6 us)
Async XLA Ops:
  2.3 7.9 %collective-permute-start.1 = (f32[16,32,50]{2,1,0:T(8,128)S(1)}, f32[16,32,50]{2,1,0:T(8,128)S(1)}, u32[]{:S(2)}, u32[]{:S(2)}) collective-permute-start(f32[16,32,50]{2,1,0:T(8,128)S(1)} %pad_maximum_fusion.10), channel_id=1, source_target_pairs={{0,1},{1,2},{2,3},{3,4},{4,5},{5,6},{6,7},{7,0},{8,9},{9,10},{10,1... | collective-permute-start | bytes 307208 | tf_op jit(solution)/shard_map/ppermute | solution.py:530
  5.1 5.8 %collective-permute-start = (f32[16,32,50]{2,1,0:T(8,128)S(1)}, f32[16,32,50]{2,1,0:T(8,128)S(1)}, u32[]{:S(2)}, u32[]{:S(2)}) collective-permute-start(f32[16,32,50]{2,1,0:T(8,128)S(1)} %pad_maximum_fusion.9), channel_id=1, source_target_pairs={{1,0},{2,1},{3,2},{4,3},{5,4},{6,5},{7,6},{0,7},{9,8},{10,9},{11,1... | collective-permute-start | bytes 307208 | tf_op jit(solution)/shard_map/ppermute | solution.py:531
  10.2 1.0 copy-start.3
  10.2 1.0 copy-start.4
  11.6 6.3 %collective-permute-start.3 = (f32[32,5,256]{2,1,0:T(8,128)S(1)}, f32[32,5,256]{2,1,0:T(8,128)S(1)}, u32[]{:S(2)}, u32[]{:S(2)}) collective-permute-start(f32[32,5,256]{2,1,0:T(8,128)S(1)} %pad_maximum_fusion.12), channel_id=1, source_target_pairs={{0,8},{8,16},{16,24},{1,9},{9,17},{17,25},{2,10},{10,18},{18,26},{... | collective-permute-start | bytes 491528 | tf_op jit(solution)/shard_map/ppermute | solution.py:530
  14.8 7.1 %collective-permute-start.2 = (f32[32,5,256]{2,1,0:T(8,128)S(1)}, f32[32,5,256]{2,1,0:T(8,128)S(1)}, u32[]{:S(2)}, u32[]{:S(2)}) collective-permute-start(f32[32,5,256]{2,1,0:T(8,128)S(1)} %pad_maximum_fusion.11), channel_id=1, source_target_pairs={{8,0},{16,8},{24,16},{9,1},{17,9},{25,17},{10,2},{18,10},{26,18},{... | collective-permute-start | bytes 491528 | tf_op jit(solution)/shard_map/ppermute | solution.py:531
  22.7 10.5 %collective-permute-start.4 = (f32[14,48,128]{2,1,0:T(8,128)S(1)}, f32[14,48,128]{2,1,0:T(8,128)S(1)}, u32[]{:S(2)}, u32[]{:S(2)}) collective-permute-start(f32[14,48,128]{2,1,0:T(8,128)S(1)} %pad_maximum_fusion.7), channel_id=1, source_target_pairs={{0,32},{32,64},{64,96},{96,128},{128,160},{160,192},{192,224},{224... | collective-permute-start | bytes 1032200 | tf_op jit(solution)/shard_map/ppermute | solution.py:530
  27.8 9.6 %collective-permute-start.5 = (f32[14,48,128]{2,1,0:T(8,128)S(1)}, f32[14,48,128]{2,1,0:T(8,128)S(1)}, u32[]{:S(2)}, u32[]{:S(2)}) collective-permute-start(f32[14,48,128]{2,1,0:T(8,128)S(1)} %pad_maximum_fusion.8), channel_id=1, source_target_pairs={{32,0},{64,32},{96,64},{128,96},{160,128},{192,160},{224,192},{256... | collective-permute-start | bytes 1032200 | tf_op jit(solution)/shard_map/ppermute | solution.py:531
  41.1 5.4 %collective-permute-start.7 = (f32[20,16,128]{2,1,0:T(8,128)S(1)}, f32[20,16,128]{2,1,0:T(8,128)S(1)}, u32[]{:S(2)}, u32[]{:S(2)}) collective-permute-start(f32[20,16,128]{2,1,0:T(8,128)S(1)} %get-tuple-element.27), channel_id=1, source_target_pairs={{0,8},{8,16},{16,24},{1,9},{9,17},{17,25},{2,10},{10,18},{18,26},{... | collective-permute-start | bytes 491528 | tf_op jit(solution)/shard_map/ppermute | solution.py:530
  44.2 6.1 %collective-permute-start.6 = (f32[20,16,128]{2,1,0:T(8,128)S(1)}, f32[20,16,128]{2,1,0:T(8,128)S(1)}, u32[]{:S(2)}, u32[]{:S(2)}) collective-permute-start(f32[20,16,128]{2,1,0:T(8,128)S(1)} %get-tuple-element.27), channel_id=1, source_target_pairs={{8,0},{16,8},{24,16},{9,1},{17,9},{25,17},{10,2},{18,10},{26,18},{... | collective-permute-start | bytes 491528 | tf_op jit(solution)/shard_map/ppermute | solution.py:531
  50.5 8.0 %collective-permute-start.8 = (f32[18,40,128]{2,1,0:T(8,128)S(1)}, f32[18,40,128]{2,1,0:T(8,128)S(1)}, u32[]{:S(2)}, u32[]{:S(2)}) collective-permute-start(f32[18,40,128]{2,1,0:T(8,128)S(1)} %pad_maximum_fusion.5), channel_id=1, source_target_pairs={{0,32},{32,64},{64,96},{96,128},{128,160},{160,192},{192,224},{224... | collective-permute-start | bytes 1105928 | tf_op jit(solution)/shard_map/ppermute | solution.py:530
  54.1 9.7 %collective-permute-start.9 = (f32[18,40,128]{2,1,0:T(8,128)S(1)}, f32[18,40,128]{2,1,0:T(8,128)S(1)}, u32[]{:S(2)}, u32[]{:S(2)}) collective-permute-start(f32[18,40,128]{2,1,0:T(8,128)S(1)} %pad_maximum_fusion.6), channel_id=1, source_target_pairs={{32,0},{64,32},{96,64},{128,96},{160,128},{192,160},{224,192},{256... | collective-permute-start | bytes 1105928 | tf_op jit(solution)/shard_map/ppermute | solution.py:531
  66.3 0.8 copy-start.1
  91.2 0.8 copy-start
  92.0 25.9 %all-to-all-start.1 = ((f32[32,4,8,128]{3,2,1,0:T(8,128)}), f32[32,4,8,128]{3,2,1,0:T(8,128)}, u32[]{:S(2)}, u32[]{:S(2)}) async-start(f32[32,4,8,128]{3,2,1,0:T(8,128)} %copy-done), calls=%async_computation.1 | async-start | bytes 1048576 | tf_op jit(solution)/shard_map/all_to_all | solution.py:582
  106.2 4.0 %collective-permute-start.10 = (f32[2,24,128]{2,1,0:T(8,128)S(1)}, f32[2,24,128]{2,1,0:T(8,128)S(1)}, u32[]{:S(2)}, u32[]{:S(2)}) collective-permute-start(f32[2,24,128]{2,1,0:T(8,128)S(1)} %get-tuple-element.33), channel_id=1, source_target_pairs={{0,32},{32,64},{64,96},{96,128},{128,160},{160,192},{192,224},{224... | collective-permute-start | bytes 73736 | tf_op jit(solution)/shard_map/ppermute | solution.py:530
  108.8 5.0 %collective-permute-start.11 = (f32[2,24,128]{2,1,0:T(8,128)S(1)}, f32[2,24,128]{2,1,0:T(8,128)S(1)}, u32[]{:S(2)}, u32[]{:S(2)}) collective-permute-start(f32[2,24,128]{2,1,0:T(8,128)S(1)} %get-tuple-element.34), channel_id=1, source_target_pairs={{32,0},{64,32},{96,64},{128,96},{160,128},{192,160},{224,192},{256... | collective-permute-start | bytes 73736 | tf_op jit(solution)/shard_map/ppermute | solution.py:531
  117.9 1.0 copy-start.2
  132.7 1.5 collective-permute-start.13
  132.9 4.0 %collective-permute-start.12 = (f32[8,16,128]{2,1,0:T(8,128)S(1)}, f32[8,16,128]{2,1,0:T(8,128)S(1)}, u32[]{:S(2)}, u32[]{:S(2)}) collective-permute-start(f32[8,16,128]{2,1,0:T(8,128)S(1)} %get-tuple-element.37), channel_id=1, source_target_pairs={{1,0},{2,1},{3,2},{4,3},{5,4},{6,5},{7,6},{0,7},{9,8},{10,9},{11,1... | collective-permute-start | bytes 196616 | tf_op jit(solution)/shard_map/ppermute | solution.py:531
  136.9 3.2 %collective-permute-start.15 = (f32[8,16,128]{2,1,0:T(8,128)S(1)}, f32[8,16,128]{2,1,0:T(8,128)S(1)}, u32[]{:S(2)}, u32[]{:S(2)}) collective-permute-start(f32[8,16,128]{2,1,0:T(8,128)S(1)} %select_select_fusion), channel_id=1, source_target_pairs={{0,8},{8,16},{16,24},{1,9},{9,17},{17,25},{2,10},{10,18},{18,26},{... | collective-permute-start | bytes 196616 | tf_op jit(solution)/shard_map/ppermute | solution.py:530
  138.8 5.0 %collective-permute-start.14 = (f32[8,16,128]{2,1,0:T(8,128)S(1)}, f32[8,16,128]{2,1,0:T(8,128)S(1)}, u32[]{:S(2)}, u32[]{:S(2)}) collective-permute-start(f32[8,16,128]{2,1,0:T(8,128)S(1)} %select_select_fusion), channel_id=1, source_target_pairs={{8,0},{16,8},{24,16},{9,1},{17,9},{25,17},{10,2},{18,10},{26,18},{... | collective-permute-start | bytes 196616 | tf_op jit(solution)/shard_map/ppermute | solution.py:531
  143.9 6.1 %collective-permute-start.17 = (f32[8,40,128]{2,1,0:T(8,128)S(1)}, f32[8,40,128]{2,1,0:T(8,128)S(1)}, u32[]{:S(2)}, u32[]{:S(2)}) collective-permute-start(f32[8,40,128]{2,1,0:T(8,128)S(1)} %pad_maximum_fusion.13.refs_1_), channel_id=1, source_target_pairs={{32,0},{64,32},{96,64},{128,96},{160,128},{192,160},{224,192},{256... | collective-permute-start | bytes 491528 | tf_op jit(solution)/shard_map/ppermute | solution.py:531
  145.2 6.2 %collective-permute-start.16 = (f32[8,40,128]{2,1,0:T(8,128)S(1)}, f32[8,40,128]{2,1,0:T(8,128)S(1)}, u32[]{:S(2)}, u32[]{:S(2)}) collective-permute-start(f32[8,40,128]{2,1,0:T(8,128)S(1)} %pad_maximum_fusion.13.refs_1_), channel_id=1, source_target_pairs={{0,32},{32,64},{64,96},{96,128},{128,160},{160,192},{192,224},{224... | collective-permute-start | bytes 491528 | tf_op jit(solution)/shard_map/ppermute | solution.py:530

commit v9 on v8

--- a/solution.py
+++ b/solution.py
@@ -248,7 +248,7 @@
     return jnp.where(k > 0.0, value, 0.0)
 
 
-U0, U1, U2, U3 = 6, 12, 10, 16
+U0, U1, U2, U3 = 6, 12, 10, 32
 
 
 def place(target, at, source, start, count, unroll=4):

time: 203 us -> 201 us (level)
  no operation moved by 1% of the time
where the time goes in v9:
time: 201 us; the launch traced here: 200 us
  blocking collectives  62.1 us (31%)
  starting transfers between devices  54.2 us (27%)
  waiting for transfers between devices  45.7 us (23%)
  Pallas kernels  30.5 us (15%)
  local copies, waits for them, and re-layouts  4.99 us (2%)
    all_to_all x3, blocking collectives, everyone(): return lax.all_to_all(pieces, axes, 0, 0)  62.1 us
    pallas_call x7, Pallas kernels, call(): pl.pallas_call(kernel, out_shape=[jax.ShapeDtypeStruct(o, F32) for o in o...  30.5 us
    ppermute x9, waiting for transfers between devices, neighbours(): after = lax.ppermute(initial, axis, down)  28.4 us
    ppermute x9, starting transfers between devices, neighbours(): before = lax.ppermute(last, axis, up)  26.1 us
    all_to_all x1, starting transfers between devices, everyone(): return lax.all_to_all(pieces, axes, 0, 0)  14.2 us
    ppermute x9, starting transfers between devices, neighbours(): after = lax.ppermute(initial, axis, down)  13.8 us
    ppermute x9, waiting for transfers between devices, neighbours(): before = lax.ppermute(last, axis, up)  13.2 us
    all_to_all x1, waiting for transfers between devices, everyone(): return lax.all_to_all(pieces, axes, 0, 0)  4.15 us
  transfers between devices with their start and end apart: 19, of which 17 were waited for; matrix products, arithmetic and copies ran while one was open for 0% of the time, Pallas kernels for 0%

profile of v9, /device:TPU:1, one launch (start us, length us, event | category | flops | bytes accessed | tf_op | source)
XLA Modules:
  0.0 200.0 jit_solution(3316378137090305028)
XLA Ops:
  0.6 0.1 pad_add_fusion.index
  0.7 1.4 fusion.21
  2.1 0.1 pad_maximum_fusion.10
  2.3 2.7 %collective-permute-start.1 = (f32[16,32,50]{2,1,0:T(8,128)S(1)}, f32[16,32,50]{2,1,0:T(8,128)S(1)}, u32[]{:S(2)}, u32[]{:S(2)}) collective-permute-start(f32[16,32,50]{2,1,0:T(8,128)S(1)} %pad_maximum_fusion.10), channel_id=1, source_target_pairs={{0,1},{1,2},{2,3},{3,4},{4,5},{5,6},{6,7},{7,0},{8,9},{9,10},{10,1... | collective-permute-start | bytes 307208 | tf_op jit(solution)/shard_map/ppermute | solution.py:530
  5.0 0.1 pad_maximum_fusion.9
  5.1 4.2 %collective-permute-start = (f32[16,32,50]{2,1,0:T(8,128)S(1)}, f32[16,32,50]{2,1,0:T(8,128)S(1)}, u32[]{:S(2)}, u32[]{:S(2)}) collective-permute-start(f32[16,32,50]{2,1,0:T(8,128)S(1)} %pad_maximum_fusion.9), channel_id=1, source_target_pairs={{1,0},{2,1},{3,2},{4,3},{5,4},{6,5},{7,6},{0,7},{9,8},{10,9},{11,1... | collective-permute-start | bytes 307208 | tf_op jit(solution)/shard_map/ppermute | solution.py:531
  9.3 0.9 collective-permute-done.1
  10.2 0.1 fusion.20
  10.4 0.5 collective-permute-done
  10.9 0.1 fusion.19
  11.2 0.1 copy-done.4
  11.3 0.3 fusion.8
  11.6 3.0 %collective-permute-start.3 = (f32[32,5,256]{2,1,0:T(8,128)S(1)}, f32[32,5,256]{2,1,0:T(8,128)S(1)}, u32[]{:S(2)}, u32[]{:S(2)}) collective-permute-start(f32[32,5,256]{2,1,0:T(8,128)S(1)} %pad_maximum_fusion.12), channel_id=1, source_target_pairs={{0,8},{8,16},{16,24},{1,9},{9,17},{17,25},{2,10},{10,18},{18,26},{... | collective-permute-start | bytes 491528 | tf_op jit(solution)/shard_map/ppermute | solution.py:530
  14.7 0.1 pad.44.clone
  14.8 1.3 collective-permute-start.2
  16.1 1.9 collective-permute-done.3
  18.0 3.9 %collective-permute-done.2 = f32[32,5,256]{2,1,0:T(8,128)S(1)} collective-permute-done((f32[32,5,256]{2,1,0:T(8,128)S(1)}, f32[32,5,256]{2,1,0:T(8,128)S(1)}, u32[]{:S(2)}, u32[]{:S(2)}) %collective-permute-start.2) | collective-permute-done | bytes 163872 | tf_op jit(solution)/shard_map/ppermute | solution.py:531
  21.9 0.3 fusion.3
  22.3 0.1 fusion.12
  22.5 0.1 maximum_select_fusion.1
  22.7 5.1 %collective-permute-start.4 = (f32[14,48,128]{2,1,0:T(8,128)S(1)}, f32[14,48,128]{2,1,0:T(8,128)S(1)}, u32[]{:S(2)}, u32[]{:S(2)}) collective-permute-start(f32[14,48,128]{2,1,0:T(8,128)S(1)} %pad_maximum_fusion.7), channel_id=1, source_target_pairs={{0,32},{32,64},{64,96},{96,128},{128,160},{160,192},{192,224},{224... | collective-permute-start | bytes 1032200 | tf_op jit(solution)/shard_map/ppermute | solution.py:530
  27.8 1.3 collective-permute-start.5
  29.1 4.1 %collective-permute-done.4.before = f32[14,48,128]{2,1,0:T(8,128)S(1)} collective-permute-done((f32[14,48,128]{2,1,0:T(8,128)S(1)}, f32[14,48,128]{2,1,0:T(8,128)S(1)}, u32[]{:S(2)}, u32[]{:S(2)}) %collective-permute-start.4) | collective-permute-done | bytes 344096 | tf_op jit(solution)/shard_map/ppermute | solution.py:530
  33.2 4.2 %collective-permute-done.5.after = f32[14,48,128]{2,1,0:T(8,128)S(1)} collective-permute-done((f32[14,48,128]{2,1,0:T(8,128)S(1)}, f32[14,48,128]{2,1,0:T(8,128)S(1)}, u32[]{:S(2)}, u32[]{:S(2)}) %collective-permute-start.5) | collective-permute-done | bytes 344096 | tf_op jit(solution)/shard_map/ppermute | solution.py:531
  37.4 3.7 %down0.1 = (f32[26,48,256]{2,1,0:T(8,128)S(1)}, f32[26,48,256]{2,1,0:T(8,128)S(1)}, f32[20,16,128]{2,1,0:T(8,128)S(1)}) custom-call(f32[14,48,128]{2,1,0:T(8,128)S(1)} %collective-permute-done.4.before, f32[16,48,256]{2,1,0:T(8,128)S(1)} %get-tuple-element.60.fo, f32[16,48,256]{2,1,0:T(8,128)S(1)} %get-tuple-element.61.ko, ...), custom_call_target="tpu_custom_call" | custom-call | tf_op jit(solution)/shard_map/down0/pallas_call | solution.py:512
  41.1 3.1 %collective-permute-start.7 = (f32[20,16,128]{2,1,0:T(8,128)S(1)}, f32[20,16,128]{2,1,0:T(8,128)S(1)}, u32[]{:S(2)}, u32[]{:S(2)}) collective-permute-start(f32[20,16,128]{2,1,0:T(8,128)S(1)} %get-tuple-element.27), channel_id=1, source_target_pairs={{0,8},{8,16},{16,24},{1,9},{9,17},{17,25},{2,10},{10,18},{18,26},{... | collective-permute-start | bytes 491528 | tf_op jit(solution)/shard_map/ppermute | solution.py:530
  44.2 1.3 collective-permute-start.6
  45.5 0.1 pad.20.clone
  45.6 0.9 collective-permute-done.7
  46.5 3.8 %collective-permute-done.6 = f32[20,16,128]{2,1,0:T(8,128)S(1)} collective-permute-done((f32[20,16,128]{2,1,0:T(8,128)S(1)}, f32[20,16,128]{2,1,0:T(8,128)S(1)}, u32[]{:S(2)}, u32[]{:S(2)}) %collective-permute-start.6) | collective-permute-done | bytes 163872 | tf_op jit(solution)/shard_map/ppermute | solution.py:531
  50.3 0.1 pad_maximum_fusion.4.refs_1_
  50.5 3.6 %collective-permute-start.8 = (f32[18,40,128]{2,1,0:T(8,128)S(1)}, f32[18,40,128]{2,1,0:T(8,128)S(1)}, u32[]{:S(2)}, u32[]{:S(2)}) collective-permute-start(f32[18,40,128]{2,1,0:T(8,128)S(1)} %pad_maximum_fusion.5), channel_id=1, source_target_pairs={{0,32},{32,64},{64,96},{96,128},{128,160},{160,192},{192,224},{224... | collective-permute-start | bytes 1105928 | tf_op jit(solution)/shard_map/ppermute | solution.py:530
  54.1 1.3 collective-permute-start.9
  55.4 3.1 %collective-permute-done.8.refs_0_ = f32[18,40,128]{2,1,0:T(8,128)S(1)} collective-permute-done((f32[18,40,128]{2,1,0:T(8,128)S(1)}, f32[18,40,128]{2,1,0:T(8,128)S(1)}, u32[]{:S(2)}, u32[]{:S(2)}) %collective-permute-start.8) | collective-permute-done | bytes 368672 | tf_op jit(solution)/shard_map/ppermute | solution.py:530
  58.5 5.3 %collective-permute-done.9.refs_2_ = f32[18,40,128]{2,1,0:T(8,128)S(1)} collective-permute-done((f32[18,40,128]{2,1,0:T(8,128)S(1)}, f32[18,40,128]{2,1,0:T(8,128)S(1)}, u32[]{:S(2)}, u32[]{:S(2)}) %collective-permute-start.9) | collective-permute-done | bytes 368672 | tf_op jit(solution)/shard_map/ppermute | solution.py:531
  63.8 2.5 %descend.1 = (f32[16,8,128]{2,1,0:T(8,128)S(1)}, f32[26,40,128]{2,1,0:T(8,128)S(1)}, f32[26,40,128]{2,1,0:T(8,128)S(1)}, f32[12,24,128]{2,1,0:T(8,128)S(1)}, f32...) custom-call(f32[18,40,128]{2,1,0:T(8,128)S(1)} %collective-permute-done.8.refs_0_, ...), custom_call_target="tpu_custom_call" | custom-call | tf_op jit(solution)/shard_map/descend/pallas_call | solution.py:512
  66.4 0.8 copy-done.1
  67.2 23.9 %all_to_all.20.s = f32[16,8,128]{2,1,0:T(8,128)S(1)} all-to-all(f32[16,8,128]{2,1,0:T(8,128)S(1)} %get-tuple-element.28), channel_id=1, replica_groups=mesh['gx'=16,'gy'=4,'gz'=8] {'gx'}, dimensions={0} | all-to-all | bytes 131072 | tf_op jit(solution)/shard_map/all_to_all | solution.py:582
  91.0 0.2 repack.1
  91.2 0.8 copy-done
  92.0 14.2 %all-to-all-start.1 = ((f32[32,4,8,128]{3,2,1,0:T(8,128)}), f32[32,4,8,128]{3,2,1,0:T(8,128)}, u32[]{:S(2)}, u32[]{:S(2)}) async-start(f32[32,4,8,128]{3,2,1,0:T(8,128)} %copy-done), calls=%async_computation.1 | async-start | bytes 1048576 | tf_op jit(solution)/shard_map/all_to_all | solution.py:582
  106.2 2.5 %collective-permute-start.10 = (f32[2,24,128]{2,1,0:T(8,128)S(1)}, f32[2,24,128]{2,1,0:T(8,128)S(1)}, u32[]{:S(2)}, u32[]{:S(2)}) collective-permute-start(f32[2,24,128]{2,1,0:T(8,128)S(1)} %get-tuple-element.33), channel_id=1, source_target_pairs={{0,32},{32,64},{64,96},{96,128},{128,160},{160,192},{192,224},{224... | collective-permute-start | bytes 73736 | tf_op jit(solution)/shard_map/ppermute | solution.py:530
  108.8 1.5 collective-permute-start.11
  110.3 3.5 %collective-permute-done.11.refs_1_ = f32[2,24,128]{2,1,0:T(8,128)S(1)} collective-permute-done((f32[2,24,128]{2,1,0:T(8,128)S(1)}, f32[2,24,128]{2,1,0:T(8,128)S(1)}, u32[]{:S(2)}, u32[]{:S(2)}) %collective-permute-start.11) | collective-permute-done | bytes 24608 | tf_op jit(solution)/shard_map/ppermute | solution.py:531
  113.8 4.1 %all-to-all-done.1.s = f32[32,4,8,128]{3,2,1,0:T(8,128)} async-done(((f32[32,4,8,128]{3,2,1,0:T(8,128)}), f32[32,4,8,128]{3,2,1,0:T(8,128)}, u32[]{:S(2)}, u32[]{:S(2)}) %all-to-all-start.1) | async-done | bytes 524320 | tf_op jit(solution)/shard_map/all_to_all | solution.py:582
  117.9 1.0 copy-done.2
  119.0 12.8 %middle.1 = (f32[26,48,256]{2,1,0:T(8,128)S(1)}, f32[8,16,128]{2,1,0:T(8,128)S(1)}, f32[8,16,128]{2,1,0:T(8,128)S(1)}, f32[38,16,128]{2,1,0:T(8,128)S(1)}) custom-call(s32[3]{0:T(128)S(1)} %pad_add_fusion.index, f32[26,48,256]{2,1,0:T(8,128)S(1)} %get-tuple-element.25.f, f32[26,48,256]{2,1,0:T(8,128)S(1)} %get-tuple-element.26.k, ...), custom_call_target="tpu_custom_call" | custom-call | tf_op jit(solution)/shard_map/middle/pallas_call | solution.py:512
  131.7 0.2 collective-permute-start.13
  131.9 0.4 collective-permute-start.12
  132.2 1.0 collective-permute-done.13
  133.2 2.7 %collective-permute-done.12 = f32[8,16,128]{2,1,0:T(8,128)S(1)} collective-permute-done((f32[8,16,128]{2,1,0:T(8,128)S(1)}, f32[8,16,128]{2,1,0:T(8,128)S(1)}, u32[]{:S(2)}, u32[]{:S(2)}) %collective-permute-start.12) | collective-permute-done | bytes 65568 | tf_op jit(solution)/shard_map/ppermute | solution.py:531
  135.9 1.9 collective-permute-start.15
  137.8 1.3 collective-permute-start.14
  139.1 3.7 %collective-permute-done.14 = f32[8,16,128]{2,1,0:T(8,128)S(1)} collective-permute-done((f32[8,16,128]{2,1,0:T(8,128)S(1)}, f32[8,16,128]{2,1,0:T(8,128)S(1)}, u32[]{:S(2)}, u32[]{:S(2)}) %collective-permute-start.14) | collective-permute-done | bytes 65568 | tf_op jit(solution)/shard_map/ppermute | solution.py:531
  142.8 0.1 pad_maximum_fusion.13.refs_1_
  142.9 1.3 collective-permute-start.17
  144.2 4.0 %collective-permute-start.16 = (f32[8,40,128]{2,1,0:T(8,128)S(1)}, f32[8,40,128]{2,1,0:T(8,128)S(1)}, u32[]{:S(2)}, u32[]{:S(2)}) collective-permute-start(f32[8,40,128]{2,1,0:T(8,128)S(1)} %pad_maximum_fusion.13.refs_1_), channel_id=1, source_target_pairs={{0,32},{32,64},{64,96},{96,128},{128,160},{160,192},{192,224},{224... | collective-permute-start | bytes 491528 | tf_op jit(solution)/shard_map/ppermute | solution.py:530
  148.2 0.8 collective-permute-done.17.refs_2_
  148.9 1.5 collective-permute-done.16.refs_0_
  150.4 1.9 again.1
  152.3 18.2 %all_to_all.21.s = f32[16,8,128]{2,1,0:T(8,128)S(1)} all-to-all(f32[16,8,128]{2,1,0:T(8,128)S(1)} %get-tuple-element.38), channel_id=1, replica_groups=mesh['gx'=16,'gy'=4,'gz'=8] {'gx'}, dimensions={0} | all-to-all | bytes 131072 | tf_op jit(solution)/shard_map/all_to_all | solution.py:582
  170.5 0.1 repack2.1
  170.6 20.0 %all_to_all.22.s = f32[32,2,8,128]{3,2,1,0:T(8,128)S(1)} all-to-all(f32[32,2,8,128]{3,2,1,0:T(8,128)S(1)} %repack2.1), channel_id=1, replica_groups=mesh['gx'=16,'gy'=4,'gz'=8] {'gy','gz'}, dimensions={0} | all-to-all | bytes 524288 | tf_op jit(solution)/shard_map/all_to_all | solution.py:582
  190.6 9.4 %final.1 = (f32[16,32,128]{2,1,0:T(8,128)}, f32[16,32,128]{2,1,0:T(8,128)}) custom-call(s32[3]{0:T(128)S(1)} %pad_add_fusion.index, f32[26,48,256]{2,1,0:T(8,128)S(1)} %get-tuple-element.25.f, f32[26,48,256]{2,1,0:T(8,128)S(1)} %get-tuple-element.26.k, f32[26,48,256]{2,1,0:T(8,128)S(1)} %get-tuple-element.35.v0, f32[32,2,8,128]{3,2,1,0:T(8,128)S(1)} %all_to_all.22.s, ...), custom_call_target="tpu_custom_call" | custom-call | tf_op jit(solution)/shard_map/final/pallas_call | solution.py:512
  (33 shorter events, 0.6 us)
Async XLA Ops:
  2.3 7.9 %collective-permute-start.1 = (f32[16,32,50]{2,1,0:T(8,128)S(1)}, f32[16,32,50]{2,1,0:T(8,128)S(1)}, u32[]{:S(2)}, u32[]{:S(2)}) collective-permute-start(f32[16,32,50]{2,1,0:T(8,128)S(1)} %pad_maximum_fusion.10), channel_id=1, source_target_pairs={{0,1},{1,2},{2,3},{3,4},{4,5},{5,6},{6,7},{7,0},{8,9},{9,10},{10,1... | collective-permute-start | bytes 307208 | tf_op jit(solution)/shard_map/ppermute | solution.py:530
  5.1 5.8 %collective-permute-start = (f32[16,32,50]{2,1,0:T(8,128)S(1)}, f32[16,32,50]{2,1,0:T(8,128)S(1)}, u32[]{:S(2)}, u32[]{:S(2)}) collective-permute-start(f32[16,32,50]{2,1,0:T(8,128)S(1)} %pad_maximum_fusion.9), channel_id=1, source_target_pairs={{1,0},{2,1},{3,2},{4,3},{5,4},{6,5},{7,6},{0,7},{9,8},{10,9},{11,1... | collective-permute-start | bytes 307208 | tf_op jit(solution)/shard_map/ppermute | solution.py:531
  10.2 1.0 copy-start.3
  10.2 1.0 copy-start.4
  11.6 6.3 %collective-permute-start.3 = (f32[32,5,256]{2,1,0:T(8,128)S(1)}, f32[32,5,256]{2,1,0:T(8,128)S(1)}, u32[]{:S(2)}, u32[]{:S(2)}) collective-permute-start(f32[32,5,256]{2,1,0:T(8,128)S(1)} %pad_maximum_fusion.12), channel_id=1, source_target_pairs={{0,8},{8,16},{16,24},{1,9},{9,17},{17,25},{2,10},{10,18},{18,26},{... | collective-permute-start | bytes 491528 | tf_op jit(solution)/shard_map/ppermute | solution.py:530
  14.8 7.1 %collective-permute-start.2 = (f32[32,5,256]{2,1,0:T(8,128)S(1)}, f32[32,5,256]{2,1,0:T(8,128)S(1)}, u32[]{:S(2)}, u32[]{:S(2)}) collective-permute-start(f32[32,5,256]{2,1,0:T(8,128)S(1)} %pad_maximum_fusion.11), channel_id=1, source_target_pairs={{8,0},{16,8},{24,16},{9,1},{17,9},{25,17},{10,2},{18,10},{26,18},{... | collective-permute-start | bytes 491528 | tf_op jit(solution)/shard_map/ppermute | solution.py:531
  22.7 10.5 %collective-permute-start.4 = (f32[14,48,128]{2,1,0:T(8,128)S(1)}, f32[14,48,128]{2,1,0:T(8,128)S(1)}, u32[]{:S(2)}, u32[]{:S(2)}) collective-permute-start(f32[14,48,128]{2,1,0:T(8,128)S(1)} %pad_maximum_fusion.7), channel_id=1, source_target_pairs={{0,32},{32,64},{64,96},{96,128},{128,160},{160,192},{192,224},{224... | collective-permute-start | bytes 1032200 | tf_op jit(solution)/shard_map/ppermute | solution.py:530
  27.8 9.6 %collective-permute-start.5 = (f32[14,48,128]{2,1,0:T(8,128)S(1)}, f32[14,48,128]{2,1,0:T(8,128)S(1)}, u32[]{:S(2)}, u32[]{:S(2)}) collective-permute-start(f32[14,48,128]{2,1,0:T(8,128)S(1)} %pad_maximum_fusion.8), channel_id=1, source_target_pairs={{32,0},{64,32},{96,64},{128,96},{160,128},{192,160},{224,192},{256... | collective-permute-start | bytes 1032200 | tf_op jit(solution)/shard_map/ppermute | solution.py:531
  41.1 5.4 %collective-permute-start.7 = (f32[20,16,128]{2,1,0:T(8,128)S(1)}, f32[20,16,128]{2,1,0:T(8,128)S(1)}, u32[]{:S(2)}, u32[]{:S(2)}) collective-permute-start(f32[20,16,128]{2,1,0:T(8,128)S(1)} %get-tuple-element.27), channel_id=1, source_target_pairs={{0,8},{8,16},{16,24},{1,9},{9,17},{17,25},{2,10},{10,18},{18,26},{... | collective-permute-start | bytes 491528 | tf_op jit(solution)/shard_map/ppermute | solution.py:530
  44.2 6.1 %collective-permute-start.6 = (f32[20,16,128]{2,1,0:T(8,128)S(1)}, f32[20,16,128]{2,1,0:T(8,128)S(1)}, u32[]{:S(2)}, u32[]{:S(2)}) collective-permute-start(f32[20,16,128]{2,1,0:T(8,128)S(1)} %get-tuple-element.27), channel_id=1, source_target_pairs={{8,0},{16,8},{24,16},{9,1},{17,9},{25,17},{10,2},{18,10},{26,18},{... | collective-permute-start | bytes 491528 | tf_op jit(solution)/shard_map/ppermute | solution.py:531
  50.5 8.0 %collective-permute-start.8 = (f32[18,40,128]{2,1,0:T(8,128)S(1)}, f32[18,40,128]{2,1,0:T(8,128)S(1)}, u32[]{:S(2)}, u32[]{:S(2)}) collective-permute-start(f32[18,40,128]{2,1,0:T(8,128)S(1)} %pad_maximum_fusion.5), channel_id=1, source_target_pairs={{0,32},{32,64},{64,96},{96,128},{128,160},{160,192},{192,224},{224... | collective-permute-start | bytes 1105928 | tf_op jit(solution)/shard_map/ppermute | solution.py:530
  54.1 9.7 %collective-permute-start.9 = (f32[18,40,128]{2,1,0:T(8,128)S(1)}, f32[18,40,128]{2,1,0:T(8,128)S(1)}, u32[]{:S(2)}, u32[]{:S(2)}) collective-permute-start(f32[18,40,128]{2,1,0:T(8,128)S(1)} %pad_maximum_fusion.6), channel_id=1, source_target_pairs={{32,0},{64,32},{96,64},{128,96},{160,128},{192,160},{224,192},{256... | collective-permute-start | bytes 1105928 | tf_op jit(solution)/shard_map/ppermute | solution.py:531
  66.3 0.8 copy-start.1
  91.2 0.8 copy-start
  92.0 25.9 %all-to-all-start.1 = ((f32[32,4,8,128]{3,2,1,0:T(8,128)}), f32[32,4,8,128]{3,2,1,0:T(8,128)}, u32[]{:S(2)}, u32[]{:S(2)}) async-start(f32[32,4,8,128]{3,2,1,0:T(8,128)} %copy-done), calls=%async_computation.1 | async-start | bytes 1048576 | tf_op jit(solution)/shard_map/all_to_all | solution.py:582
  106.2 4.0 %collective-permute-start.10 = (f32[2,24,128]{2,1,0:T(8,128)S(1)}, f32[2,24,128]{2,1,0:T(8,128)S(1)}, u32[]{:S(2)}, u32[]{:S(2)}) collective-permute-start(f32[2,24,128]{2,1,0:T(8,128)S(1)} %get-tuple-element.33), channel_id=1, source_target_pairs={{0,32},{32,64},{64,96},{96,128},{128,160},{160,192},{192,224},{224... | collective-permute-start | bytes 73736 | tf_op jit(solution)/shard_map/ppermute | solution.py:530
  108.8 5.0 %collective-permute-start.11 = (f32[2,24,128]{2,1,0:T(8,128)S(1)}, f32[2,24,128]{2,1,0:T(8,128)S(1)}, u32[]{:S(2)}, u32[]{:S(2)}) collective-permute-start(f32[2,24,128]{2,1,0:T(8,128)S(1)} %get-tuple-element.34), channel_id=1, source_target_pairs={{32,0},{64,32},{96,64},{128,96},{160,128},{192,160},{224,192},{256... | collective-permute-start | bytes 73736 | tf_op jit(solution)/shard_map/ppermute | solution.py:531
  117.9 1.0 copy-start.2
  131.7 1.5 collective-permute-start.13
  131.9 4.0 %collective-permute-start.12 = (f32[8,16,128]{2,1,0:T(8,128)S(1)}, f32[8,16,128]{2,1,0:T(8,128)S(1)}, u32[]{:S(2)}, u32[]{:S(2)}) collective-permute-start(f32[8,16,128]{2,1,0:T(8,128)S(1)} %get-tuple-element.37), channel_id=1, source_target_pairs={{1,0},{2,1},{3,2},{4,3},{5,4},{6,5},{7,6},{0,7},{9,8},{10,9},{11,1... | collective-permute-start | bytes 196616 | tf_op jit(solution)/shard_map/ppermute | solution.py:531
  135.9 3.2 %collective-permute-start.15 = (f32[8,16,128]{2,1,0:T(8,128)S(1)}, f32[8,16,128]{2,1,0:T(8,128)S(1)}, u32[]{:S(2)}, u32[]{:S(2)}) collective-permute-start(f32[8,16,128]{2,1,0:T(8,128)S(1)} %select_select_fusion), channel_id=1, source_target_pairs={{0,8},{8,16},{16,24},{1,9},{9,17},{17,25},{2,10},{10,18},{18,26},{... | collective-permute-start | bytes 196616 | tf_op jit(solution)/shard_map/ppermute | solution.py:530
  137.8 5.0 %collective-permute-start.14 = (f32[8,16,128]{2,1,0:T(8,128)S(1)}, f32[8,16,128]{2,1,0:T(8,128)S(1)}, u32[]{:S(2)}, u32[]{:S(2)}) collective-permute-start(f32[8,16,128]{2,1,0:T(8,128)S(1)} %select_select_fusion), channel_id=1, source_target_pairs={{8,0},{16,8},{24,16},{9,1},{17,9},{25,17},{10,2},{18,10},{26,18},{... | collective-permute-start | bytes 196616 | tf_op jit(solution)/shard_map/ppermute | solution.py:531
  142.9 6.1 %collective-permute-start.17 = (f32[8,40,128]{2,1,0:T(8,128)S(1)}, f32[8,40,128]{2,1,0:T(8,128)S(1)}, u32[]{:S(2)}, u32[]{:S(2)}) collective-permute-start(f32[8,40,128]{2,1,0:T(8,128)S(1)} %pad_maximum_fusion.13.refs_1_), channel_id=1, source_target_pairs={{32,0},{64,32},{96,64},{128,96},{160,128},{192,160},{224,192},{256... | collective-permute-start | bytes 491528 | tf_op jit(solution)/shard_map/ppermute | solution.py:531
  144.2 6.2 %collective-permute-start.16 = (f32[8,40,128]{2,1,0:T(8,128)S(1)}, f32[8,40,128]{2,1,0:T(8,128)S(1)}, u32[]{:S(2)}, u32[]{:S(2)}) collective-permute-start(f32[8,40,128]{2,1,0:T(8,128)S(1)} %pad_maximum_fusion.13.refs_1_), channel_id=1, source_target_pairs={{0,32},{32,64},{64,96},{96,128},{128,160},{160,192},{192,224},{224... | collective-permute-start | bytes 491528 | tf_op jit(solution)/shard_map/ppermute | solution.py:530

commit v10 on v9

--- a/solution.py
+++ b/solution.py
@@ -237,7 +237,7 @@
             put(2 * (i - 1) + j, value)
         return carry
 
-    planes(1, count - 1, step, unroll=max(1, 36 // (finer.shape[1] * finer.shape[2] // 1024)))
+    planes(1, count - 1, step, unroll=max(1, 60 // (finer.shape[1] * finer.shape[2] // 1024)))
 
 
 def three(w):

time: 201 us -> 201 us (level)
  no operation moved by 1% of the time
where the time goes in v10:
time: 201 us; the launch traced here: 200 us
  blocking collectives  62.1 us (31%)
  starting transfers between devices  54.2 us (27%)
  waiting for transfers between devices  45.7 us (23%)
  Pallas kernels  30.4 us (15%)
  local copies, waits for them, and re-layouts  4.99 us (2%)
    all_to_all x3, blocking collectives, everyone(): return lax.all_to_all(pieces, axes, 0, 0)  62.1 us
    pallas_call x7, Pallas kernels, call(): pl.pallas_call(kernel, out_shape=[jax.ShapeDtypeStruct(o, F32) for o in o...  30.4 us
    ppermute x9, waiting for transfers between devices, neighbours(): after = lax.ppermute(initial, axis, down)  28.4 us
    ppermute x9, starting transfers between devices, neighbours(): before = lax.ppermute(last, axis, up)  26.1 us
    all_to_all x1, starting transfers between devices, everyone(): return lax.all_to_all(pieces, axes, 0, 0)  14.2 us
    ppermute x9, starting transfers between devices, neighbours(): after = lax.ppermute(initial, axis, down)  13.8 us
    ppermute x9, waiting for transfers between devices, neighbours(): before = lax.ppermute(last, axis, up)  13.2 us
    all_to_all x1, waiting for transfers between devices, everyone(): return lax.all_to_all(pieces, axes, 0, 0)  4.15 us
  transfers between devices with their start and end apart: 19, of which 17 were waited for; matrix products, arithmetic and copies ran while one was open for 0% of the time, Pallas kernels for 0%

profile of v10, /device:TPU:1, one launch (start us, length us, event | category | flops | bytes accessed | tf_op | source)
XLA Modules:
  0.0 200.0 jit_solution(11717265225685101060)
XLA Ops:
  0.6 0.1 pad_add_fusion.index
  0.7 1.4 fusion.21
  2.1 0.1 pad_maximum_fusion.10
  2.3 2.7 %collective-permute-start.1 = (f32[16,32,50]{2,1,0:T(8,128)S(1)}, f32[16,32,50]{2,1,0:T(8,128)S(1)}, u32[]{:S(2)}, u32[]{:S(2)}) collective-permute-start(f32[16,32,50]{2,1,0:T(8,128)S(1)} %pad_maximum_fusion.10), channel_id=1, source_target_pairs={{0,1},{1,2},{2,3},{3,4},{4,5},{5,6},{6,7},{7,0},{8,9},{9,10},{10,1... | collective-permute-start | bytes 307208 | tf_op jit(solution)/shard_map/ppermute | solution.py:530
  5.0 0.1 pad_maximum_fusion.9
  5.1 4.2 %collective-permute-start = (f32[16,32,50]{2,1,0:T(8,128)S(1)}, f32[16,32,50]{2,1,0:T(8,128)S(1)}, u32[]{:S(2)}, u32[]{:S(2)}) collective-permute-start(f32[16,32,50]{2,1,0:T(8,128)S(1)} %pad_maximum_fusion.9), channel_id=1, source_target_pairs={{1,0},{2,1},{3,2},{4,3},{5,4},{6,5},{7,6},{0,7},{9,8},{10,9},{11,1... | collective-permute-start | bytes 307208 | tf_op jit(solution)/shard_map/ppermute | solution.py:531
  9.3 0.9 collective-permute-done.1
  10.2 0.1 fusion.20
  10.4 0.5 collective-permute-done
  10.9 0.1 fusion.19
  11.2 0.1 copy-done.4
  11.3 0.3 fusion.8
  11.6 3.0 %collective-permute-start.3 = (f32[32,5,256]{2,1,0:T(8,128)S(1)}, f32[32,5,256]{2,1,0:T(8,128)S(1)}, u32[]{:S(2)}, u32[]{:S(2)}) collective-permute-start(f32[32,5,256]{2,1,0:T(8,128)S(1)} %pad_maximum_fusion.12), channel_id=1, source_target_pairs={{0,8},{8,16},{16,24},{1,9},{9,17},{17,25},{2,10},{10,18},{18,26},{... | collective-permute-start | bytes 491528 | tf_op jit(solution)/shard_map/ppermute | solution.py:530
  14.7 0.1 pad.44.clone
  14.8 1.3 collective-permute-start.2
  16.1 1.9 collective-permute-done.3
  18.0 3.9 %collective-permute-done.2 = f32[32,5,256]{2,1,0:T(8,128)S(1)} collective-permute-done((f32[32,5,256]{2,1,0:T(8,128)S(1)}, f32[32,5,256]{2,1,0:T(8,128)S(1)}, u32[]{:S(2)}, u32[]{:S(2)}) %collective-permute-start.2) | collective-permute-done | bytes 163872 | tf_op jit(solution)/shard_map/ppermute | solution.py:531
  21.9 0.3 fusion.3
  22.3 0.1 fusion.12
  22.5 0.1 maximum_select_fusion.1
  22.7 5.1 %collective-permute-start.4 = (f32[14,48,128]{2,1,0:T(8,128)S(1)}, f32[14,48,128]{2,1,0:T(8,128)S(1)}, u32[]{:S(2)}, u32[]{:S(2)}) collective-permute-start(f32[14,48,128]{2,1,0:T(8,128)S(1)} %pad_maximum_fusion.7), channel_id=1, source_target_pairs={{0,32},{32,64},{64,96},{96,128},{128,160},{160,192},{192,224},{224... | collective-permute-start | bytes 1032200 | tf_op jit(solution)/shard_map/ppermute | solution.py:530
  27.8 1.3 collective-permute-start.5
  29.1 4.1 %collective-permute-done.4.before = f32[14,48,128]{2,1,0:T(8,128)S(1)} collective-permute-done((f32[14,48,128]{2,1,0:T(8,128)S(1)}, f32[14,48,128]{2,1,0:T(8,128)S(1)}, u32[]{:S(2)}, u32[]{:S(2)}) %collective-permute-start.4) | collective-permute-done | bytes 344096 | tf_op jit(solution)/shard_map/ppermute | solution.py:530
  33.2 4.2 %collective-permute-done.5.after = f32[14,48,128]{2,1,0:T(8,128)S(1)} collective-permute-done((f32[14,48,128]{2,1,0:T(8,128)S(1)}, f32[14,48,128]{2,1,0:T(8,128)S(1)}, u32[]{:S(2)}, u32[]{:S(2)}) %collective-permute-start.5) | collective-permute-done | bytes 344096 | tf_op jit(solution)/shard_map/ppermute | solution.py:531
  37.4 3.7 %down0.1 = (f32[26,48,256]{2,1,0:T(8,128)S(1)}, f32[26,48,256]{2,1,0:T(8,128)S(1)}, f32[20,16,128]{2,1,0:T(8,128)S(1)}) custom-call(f32[14,48,128]{2,1,0:T(8,128)S(1)} %collective-permute-done.4.before, f32[16,48,256]{2,1,0:T(8,128)S(1)} %get-tuple-element.60.fo, f32[16,48,256]{2,1,0:T(8,128)S(1)} %get-tuple-element.61.ko, ...), custom_call_target="tpu_custom_call" | custom-call | tf_op jit(solution)/shard_map/down0/pallas_call | solution.py:512
  41.1 3.1 %collective-permute-start.7 = (f32[20,16,128]{2,1,0:T(8,128)S(1)}, f32[20,16,128]{2,1,0:T(8,128)S(1)}, u32[]{:S(2)}, u32[]{:S(2)}) collective-permute-start(f32[20,16,128]{2,1,0:T(8,128)S(1)} %get-tuple-element.27), channel_id=1, source_target_pairs={{0,8},{8,16},{16,24},{1,9},{9,17},{17,25},{2,10},{10,18},{18,26},{... | collective-permute-start | bytes 491528 | tf_op jit(solution)/shard_map/ppermute | solution.py:530
  44.2 1.3 collective-permute-start.6
  45.5 0.1 pad.20.clone
  45.6 0.9 collective-permute-done.7
  46.5 3.8 %collective-permute-done.6 = f32[20,16,128]{2,1,0:T(8,128)S(1)} collective-permute-done((f32[20,16,128]{2,1,0:T(8,128)S(1)}, f32[20,16,128]{2,1,0:T(8,128)S(1)}, u32[]{:S(2)}, u32[]{:S(2)}) %collective-permute-start.6) | collective-permute-done | bytes 163872 | tf_op jit(solution)/shard_map/ppermute | solution.py:531
  50.3 0.1 pad_maximum_fusion.4.refs_1_
  50.5 3.6 %collective-permute-start.8 = (f32[18,40,128]{2,1,0:T(8,128)S(1)}, f32[18,40,128]{2,1,0:T(8,128)S(1)}, u32[]{:S(2)}, u32[]{:S(2)}) collective-permute-start(f32[18,40,128]{2,1,0:T(8,128)S(1)} %pad_maximum_fusion.5), channel_id=1, source_target_pairs={{0,32},{32,64},{64,96},{96,128},{128,160},{160,192},{192,224},{224... | collective-permute-start | bytes 1105928 | tf_op jit(solution)/shard_map/ppermute | solution.py:530
  54.1 1.3 collective-permute-start.9
  55.4 3.1 %collective-permute-done.8.refs_0_ = f32[18,40,128]{2,1,0:T(8,128)S(1)} collective-permute-done((f32[18,40,128]{2,1,0:T(8,128)S(1)}, f32[18,40,128]{2,1,0:T(8,128)S(1)}, u32[]{:S(2)}, u32[]{:S(2)}) %collective-permute-start.8) | collective-permute-done | bytes 368672 | tf_op jit(solution)/shard_map/ppermute | solution.py:530
  58.5 5.3 %collective-permute-done.9.refs_2_ = f32[18,40,128]{2,1,0:T(8,128)S(1)} collective-permute-done((f32[18,40,128]{2,1,0:T(8,128)S(1)}, f32[18,40,128]{2,1,0:T(8,128)S(1)}, u32[]{:S(2)}, u32[]{:S(2)}) %collective-permute-start.9) | collective-permute-done | bytes 368672 | tf_op jit(solution)/shard_map/ppermute | solution.py:531
  63.8 2.5 %descend.1 = (f32[16,8,128]{2,1,0:T(8,128)S(1)}, f32[26,40,128]{2,1,0:T(8,128)S(1)}, f32[26,40,128]{2,1,0:T(8,128)S(1)}, f32[12,24,128]{2,1,0:T(8,128)S(1)}, f32...) custom-call(f32[18,40,128]{2,1,0:T(8,128)S(1)} %collective-permute-done.8.refs_0_, ...), custom_call_target="tpu_custom_call" | custom-call | tf_op jit(solution)/shard_map/descend/pallas_call | solution.py:512
  66.4 0.8 copy-done.1
  67.2 23.9 %all_to_all.20.s = f32[16,8,128]{2,1,0:T(8,128)S(1)} all-to-all(f32[16,8,128]{2,1,0:T(8,128)S(1)} %get-tuple-element.28), channel_id=1, replica_groups=mesh['gx'=16,'gy'=4,'gz'=8] {'gx'}, dimensions={0} | all-to-all | bytes 131072 | tf_op jit(solution)/shard_map/all_to_all | solution.py:582
  91.0 0.2 repack.1
  91.2 0.8 copy-done
  92.0 14.2 %all-to-all-start.1 = ((f32[32,4,8,128]{3,2,1,0:T(8,128)}), f32[32,4,8,128]{3,2,1,0:T(8,128)}, u32[]{:S(2)}, u32[]{:S(2)}) async-start(f32[32,4,8,128]{3,2,1,0:T(8,128)} %copy-done), calls=%async_computation.1 | async-start | bytes 1048576 | tf_op jit(solution)/shard_map/all_to_all | solution.py:582
  106.2 2.5 %collective-permute-start.10 = (f32[2,24,128]{2,1,0:T(8,128)S(1)}, f32[2,24,128]{2,1,0:T(8,128)S(1)}, u32[]{:S(2)}, u32[]{:S(2)}) collective-permute-start(f32[2,24,128]{2,1,0:T(8,128)S(1)} %get-tuple-element.33), channel_id=1, source_target_pairs={{0,32},{32,64},{64,96},{96,128},{128,160},{160,192},{192,224},{224... | collective-permute-start | bytes 73736 | tf_op jit(solution)/shard_map/ppermute | solution.py:530
  108.8 1.5 collective-permute-start.11
  110.3 3.5 %collective-permute-done.11.refs_1_ = f32[2,24,128]{2,1,0:T(8,128)S(1)} collective-permute-done((f32[2,24,128]{2,1,0:T(8,128)S(1)}, f32[2,24,128]{2,1,0:T(8,128)S(1)}, u32[]{:S(2)}, u32[]{:S(2)}) %collective-permute-start.11) | collective-permute-done | bytes 24608 | tf_op jit(solution)/shard_map/ppermute | solution.py:531
  113.8 4.1 %all-to-all-done.1.s = f32[32,4,8,128]{3,2,1,0:T(8,128)} async-done(((f32[32,4,8,128]{3,2,1,0:T(8,128)}), f32[32,4,8,128]{3,2,1,0:T(8,128)}, u32[]{:S(2)}, u32[]{:S(2)}) %all-to-all-start.1) | async-done | bytes 524320 | tf_op jit(solution)/shard_map/all_to_all | solution.py:582
  117.9 1.0 copy-done.2
  119.0 12.7 %middle.1 = (f32[26,48,256]{2,1,0:T(8,128)S(1)}, f32[8,16,128]{2,1,0:T(8,128)S(1)}, f32[8,16,128]{2,1,0:T(8,128)S(1)}, f32[38,16,128]{2,1,0:T(8,128)S(1)}) custom-call(s32[3]{0:T(128)S(1)} %pad_add_fusion.index, f32[26,48,256]{2,1,0:T(8,128)S(1)} %get-tuple-element.25.f, f32[26,48,256]{2,1,0:T(8,128)S(1)} %get-tuple-element.26.k, ...), custom_call_target="tpu_custom_call" | custom-call | tf_op jit(solution)/shard_map/middle/pallas_call | solution.py:512
  131.7 0.2 collective-permute-start.13
  131.9 0.4 collective-permute-start.12
  132.2 1.0 collective-permute-done.13
  133.2 2.7 %collective-permute-done.12 = f32[8,16,128]{2,1,0:T(8,128)S(1)} collective-permute-done((f32[8,16,128]{2,1,0:T(8,128)S(1)}, f32[8,16,128]{2,1,0:T(8,128)S(1)}, u32[]{:S(2)}, u32[]{:S(2)}) %collective-permute-start.12) | collective-permute-done | bytes 65568 | tf_op jit(solution)/shard_map/ppermute | solution.py:531
  135.9 1.9 collective-permute-start.15
  137.8 1.3 collective-permute-start.14
  139.1 3.7 %collective-permute-done.14 = f32[8,16,128]{2,1,0:T(8,128)S(1)} collective-permute-done((f32[8,16,128]{2,1,0:T(8,128)S(1)}, f32[8,16,128]{2,1,0:T(8,128)S(1)}, u32[]{:S(2)}, u32[]{:S(2)}) %collective-permute-start.14) | collective-permute-done | bytes 65568 | tf_op jit(solution)/shard_map/ppermute | solution.py:531
  142.8 0.1 pad_maximum_fusion.13.refs_1_
  142.9 1.3 collective-permute-start.17
  144.2 4.0 %collective-permute-start.16 = (f32[8,40,128]{2,1,0:T(8,128)S(1)}, f32[8,40,128]{2,1,0:T(8,128)S(1)}, u32[]{:S(2)}, u32[]{:S(2)}) collective-permute-start(f32[8,40,128]{2,1,0:T(8,128)S(1)} %pad_maximum_fusion.13.refs_1_), channel_id=1, source_target_pairs={{0,32},{32,64},{64,96},{96,128},{128,160},{160,192},{192,224},{224... | collective-permute-start | bytes 491528 | tf_op jit(solution)/shard_map/ppermute | solution.py:530
  148.2 0.8 collective-permute-done.17.refs_2_
  148.9 1.5 collective-permute-done.16.refs_0_
  150.4 1.9 again.1
  152.3 18.2 %all_to_all.21.s = f32[16,8,128]{2,1,0:T(8,128)S(1)} all-to-all(f32[16,8,128]{2,1,0:T(8,128)S(1)} %get-tuple-element.38), channel_id=1, replica_groups=mesh['gx'=16,'gy'=4,'gz'=8] {'gx'}, dimensions={0} | all-to-all | bytes 131072 | tf_op jit(solution)/shard_map/all_to_all | solution.py:582
  170.5 0.1 repack2.1
  170.6 20.0 %all_to_all.22.s = f32[32,2,8,128]{3,2,1,0:T(8,128)S(1)} all-to-all(f32[32,2,8,128]{3,2,1,0:T(8,128)S(1)} %repack2.1), channel_id=1, replica_groups=mesh['gx'=16,'gy'=4,'gz'=8] {'gy','gz'}, dimensions={0} | all-to-all | bytes 524288 | tf_op jit(solution)/shard_map/all_to_all | solution.py:582
  190.6 9.4 %final.1 = (f32[16,32,128]{2,1,0:T(8,128)}, f32[16,32,128]{2,1,0:T(8,128)}) custom-call(s32[3]{0:T(128)S(1)} %pad_add_fusion.index, f32[26,48,256]{2,1,0:T(8,128)S(1)} %get-tuple-element.25.f, f32[26,48,256]{2,1,0:T(8,128)S(1)} %get-tuple-element.26.k, f32[26,48,256]{2,1,0:T(8,128)S(1)} %get-tuple-element.35.v0, f32[32,2,8,128]{3,2,1,0:T(8,128)S(1)} %all_to_all.22.s, ...), custom_call_target="tpu_custom_call" | custom-call | tf_op jit(solution)/shard_map/final/pallas_call | solution.py:512
  (33 shorter events, 0.6 us)
Async XLA Ops:
  2.3 7.9 %collective-permute-start.1 = (f32[16,32,50]{2,1,0:T(8,128)S(1)}, f32[16,32,50]{2,1,0:T(8,128)S(1)}, u32[]{:S(2)}, u32[]{:S(2)}) collective-permute-start(f32[16,32,50]{2,1,0:T(8,128)S(1)} %pad_maximum_fusion.10), channel_id=1, source_target_pairs={{0,1},{1,2},{2,3},{3,4},{4,5},{5,6},{6,7},{7,0},{8,9},{9,10},{10,1... | collective-permute-start | bytes 307208 | tf_op jit(solution)/shard_map/ppermute | solution.py:530
  5.1 5.8 %collective-permute-start = (f32[16,32,50]{2,1,0:T(8,128)S(1)}, f32[16,32,50]{2,1,0:T(8,128)S(1)}, u32[]{:S(2)}, u32[]{:S(2)}) collective-permute-start(f32[16,32,50]{2,1,0:T(8,128)S(1)} %pad_maximum_fusion.9), channel_id=1, source_target_pairs={{1,0},{2,1},{3,2},{4,3},{5,4},{6,5},{7,6},{0,7},{9,8},{10,9},{11,1... | collective-permute-start | bytes 307208 | tf_op jit(solution)/shard_map/ppermute | solution.py:531
  10.2 1.0 copy-start.3
  10.2 1.0 copy-start.4
  11.6 6.3 %collective-permute-start.3 = (f32[32,5,256]{2,1,0:T(8,128)S(1)}, f32[32,5,256]{2,1,0:T(8,128)S(1)}, u32[]{:S(2)}, u32[]{:S(2)}) collective-permute-start(f32[32,5,256]{2,1,0:T(8,128)S(1)} %pad_maximum_fusion.12), channel_id=1, source_target_pairs={{0,8},{8,16},{16,24},{1,9},{9,17},{17,25},{2,10},{10,18},{18,26},{... | collective-permute-start | bytes 491528 | tf_op jit(solution)/shard_map/ppermute | solution.py:530
  14.8 7.1 %collective-permute-start.2 = (f32[32,5,256]{2,1,0:T(8,128)S(1)}, f32[32,5,256]{2,1,0:T(8,128)S(1)}, u32[]{:S(2)}, u32[]{:S(2)}) collective-permute-start(f32[32,5,256]{2,1,0:T(8,128)S(1)} %pad_maximum_fusion.11), channel_id=1, source_target_pairs={{8,0},{16,8},{24,16},{9,1},{17,9},{25,17},{10,2},{18,10},{26,18},{... | collective-permute-start | bytes 491528 | tf_op jit(solution)/shard_map/ppermute | solution.py:531
  22.7 10.5 %collective-permute-start.4 = (f32[14,48,128]{2,1,0:T(8,128)S(1)}, f32[14,48,128]{2,1,0:T(8,128)S(1)}, u32[]{:S(2)}, u32[]{:S(2)}) collective-permute-start(f32[14,48,128]{2,1,0:T(8,128)S(1)} %pad_maximum_fusion.7), channel_id=1, source_target_pairs={{0,32},{32,64},{64,96},{96,128},{128,160},{160,192},{192,224},{224... | collective-permute-start | bytes 1032200 | tf_op jit(solution)/shard_map/ppermute | solution.py:530
  27.8 9.6 %collective-permute-start.5 = (f32[14,48,128]{2,1,0:T(8,128)S(1)}, f32[14,48,128]{2,1,0:T(8,128)S(1)}, u32[]{:S(2)}, u32[]{:S(2)}) collective-permute-start(f32[14,48,128]{2,1,0:T(8,128)S(1)} %pad_maximum_fusion.8), channel_id=1, source_target_pairs={{32,0},{64,32},{96,64},{128,96},{160,128},{192,160},{224,192},{256... | collective-permute-start | bytes 1032200 | tf_op jit(solution)/shard_map/ppermute | solution.py:531
  41.1 5.4 %collective-permute-start.7 = (f32[20,16,128]{2,1,0:T(8,128)S(1)}, f32[20,16,128]{2,1,0:T(8,128)S(1)}, u32[]{:S(2)}, u32[]{:S(2)}) collective-permute-start(f32[20,16,128]{2,1,0:T(8,128)S(1)} %get-tuple-element.27), channel_id=1, source_target_pairs={{0,8},{8,16},{16,24},{1,9},{9,17},{17,25},{2,10},{10,18},{18,26},{... | collective-permute-start | bytes 491528 | tf_op jit(solution)/shard_map/ppermute | solution.py:530
  44.2 6.1 %collective-permute-start.6 = (f32[20,16,128]{2,1,0:T(8,128)S(1)}, f32[20,16,128]{2,1,0:T(8,128)S(1)}, u32[]{:S(2)}, u32[]{:S(2)}) collective-permute-start(f32[20,16,128]{2,1,0:T(8,128)S(1)} %get-tuple-element.27), channel_id=1, source_target_pairs={{8,0},{16,8},{24,16},{9,1},{17,9},{25,17},{10,2},{18,10},{26,18},{... | collective-permute-start | bytes 491528 | tf_op jit(solution)/shard_map/ppermute | solution.py:531
  50.5 8.0 %collective-permute-start.8 = (f32[18,40,128]{2,1,0:T(8,128)S(1)}, f32[18,40,128]{2,1,0:T(8,128)S(1)}, u32[]{:S(2)}, u32[]{:S(2)}) collective-permute-start(f32[18,40,128]{2,1,0:T(8,128)S(1)} %pad_maximum_fusion.5), channel_id=1, source_target_pairs={{0,32},{32,64},{64,96},{96,128},{128,160},{160,192},{192,224},{224... | collective-permute-start | bytes 1105928 | tf_op jit(solution)/shard_map/ppermute | solution.py:530
  54.1 9.7 %collective-permute-start.9 = (f32[18,40,128]{2,1,0:T(8,128)S(1)}, f32[18,40,128]{2,1,0:T(8,128)S(1)}, u32[]{:S(2)}, u32[]{:S(2)}) collective-permute-start(f32[18,40,128]{2,1,0:T(8,128)S(1)} %pad_maximum_fusion.6), channel_id=1, source_target_pairs={{32,0},{64,32},{96,64},{128,96},{160,128},{192,160},{224,192},{256... | collective-permute-start | bytes 1105928 | tf_op jit(solution)/shard_map/ppermute | solution.py:531
  66.3 0.8 copy-start.1
  91.2 0.8 copy-start
  92.0 25.9 %all-to-all-start.1 = ((f32[32,4,8,128]{3,2,1,0:T(8,128)}), f32[32,4,8,128]{3,2,1,0:T(8,128)}, u32[]{:S(2)}, u32[]{:S(2)}) async-start(f32[32,4,8,128]{3,2,1,0:T(8,128)} %copy-done), calls=%async_computation.1 | async-start | bytes 1048576 | tf_op jit(solution)/shard_map/all_to_all | solution.py:582
  106.2 4.0 %collective-permute-start.10 = (f32[2,24,128]{2,1,0:T(8,128)S(1)}, f32[2,24,128]{2,1,0:T(8,128)S(1)}, u32[]{:S(2)}, u32[]{:S(2)}) collective-permute-start(f32[2,24,128]{2,1,0:T(8,128)S(1)} %get-tuple-element.33), channel_id=1, source_target_pairs={{0,32},{32,64},{64,96},{96,128},{128,160},{160,192},{192,224},{224... | collective-permute-start | bytes 73736 | tf_op jit(solution)/shard_map/ppermute | solution.py:530
  108.8 5.0 %collective-permute-start.11 = (f32[2,24,128]{2,1,0:T(8,128)S(1)}, f32[2,24,128]{2,1,0:T(8,128)S(1)}, u32[]{:S(2)}, u32[]{:S(2)}) collective-permute-start(f32[2,24,128]{2,1,0:T(8,128)S(1)} %get-tuple-element.34), channel_id=1, source_target_pairs={{32,0},{64,32},{96,64},{128,96},{160,128},{192,160},{224,192},{256... | collective-permute-start | bytes 73736 | tf_op jit(solution)/shard_map/ppermute | solution.py:531
  117.9 1.0 copy-start.2
  131.7 1.5 collective-permute-start.13
  131.9 4.0 %collective-permute-start.12 = (f32[8,16,128]{2,1,0:T(8,128)S(1)}, f32[8,16,128]{2,1,0:T(8,128)S(1)}, u32[]{:S(2)}, u32[]{:S(2)}) collective-permute-start(f32[8,16,128]{2,1,0:T(8,128)S(1)} %get-tuple-element.37), channel_id=1, source_target_pairs={{1,0},{2,1},{3,2},{4,3},{5,4},{6,5},{7,6},{0,7},{9,8},{10,9},{11,1... | collective-permute-start | bytes 196616 | tf_op jit(solution)/shard_map/ppermute | solution.py:531
  135.9 3.2 %collective-permute-start.15 = (f32[8,16,128]{2,1,0:T(8,128)S(1)}, f32[8,16,128]{2,1,0:T(8,128)S(1)}, u32[]{:S(2)}, u32[]{:S(2)}) collective-permute-start(f32[8,16,128]{2,1,0:T(8,128)S(1)} %select_select_fusion), channel_id=1, source_target_pairs={{0,8},{8,16},{16,24},{1,9},{9,17},{17,25},{2,10},{10,18},{18,26},{... | collective-permute-start | bytes 196616 | tf_op jit(solution)/shard_map/ppermute | solution.py:530
  137.8 5.0 %collective-permute-start.14 = (f32[8,16,128]{2,1,0:T(8,128)S(1)}, f32[8,16,128]{2,1,0:T(8,128)S(1)}, u32[]{:S(2)}, u32[]{:S(2)}) collective-permute-start(f32[8,16,128]{2,1,0:T(8,128)S(1)} %select_select_fusion), channel_id=1, source_target_pairs={{8,0},{16,8},{24,16},{9,1},{17,9},{25,17},{10,2},{18,10},{26,18},{... | collective-permute-start | bytes 196616 | tf_op jit(solution)/shard_map/ppermute | solution.py:531
  142.9 6.1 %collective-permute-start.17 = (f32[8,40,128]{2,1,0:T(8,128)S(1)}, f32[8,40,128]{2,1,0:T(8,128)S(1)}, u32[]{:S(2)}, u32[]{:S(2)}) collective-permute-start(f32[8,40,128]{2,1,0:T(8,128)S(1)} %pad_maximum_fusion.13.refs_1_), channel_id=1, source_target_pairs={{32,0},{64,32},{96,64},{128,96},{160,128},{192,160},{224,192},{256... | collective-permute-start | bytes 491528 | tf_op jit(solution)/shard_map/ppermute | solution.py:531
  144.2 6.2 %collective-permute-start.16 = (f32[8,40,128]{2,1,0:T(8,128)S(1)}, f32[8,40,128]{2,1,0:T(8,128)S(1)}, u32[]{:S(2)}, u32[]{:S(2)}) collective-permute-start(f32[8,40,128]{2,1,0:T(8,128)S(1)} %pad_maximum_fusion.13.refs_1_), channel_id=1, source_target_pairs={{0,32},{32,64},{64,96},{96,128},{128,160},{160,192},{192,224},{224... | collective-permute-start | bytes 491528 | tf_op jit(solution)/shard_map/ppermute | solution.py:530
